TPU v7x, 32 devices: a whole 2x2x4 slice. The times are simulated.
32 devices in a mesh: dp: 8 (over y, x, core), fsdp: 4 (over z).
Axes of the slice: x: 2, y: 2, z: 4, core: 2. Of those that a mesh axis runs over, the one named last changes fastest.
Arguments:
- teacher_in: bfloat16 [8, 512, 4096], P('dp', 'fsdp'), may hold values from -6 to 6
- teacher_out: bfloat16 [8, 512, 4096], P('dp', 'fsdp'), may hold values from -6 to 6
- owner_section: int32 [4], P('fsdp'), may hold values from 0 to 7
- gate_blocks: bfloat16 [32, 10, 128, 128], P('dp', None, 'fsdp'), may hold values from -0.15625 to 0.15625
- up_blocks: bfloat16 [32, 10, 128, 128], P('dp', None, 'fsdp'), may hold values from -0.15625 to 0.15625
- down_blocks: bfloat16 [32, 10, 128, 128], P('dp', None, 'fsdp'), may hold values from -0.15625 to 0.15625
- input_lists: int32 [32, 10], P('dp'), may hold values from 0 to 31, as said below
- input_counts: int32 [32], P('dp'), may hold values from 6 to 10, as said below
- output_lists: int32 [32, 10], P('dp'), may hold values from 0 to 31, as said below
- output_counts: int32 [32], P('dp'), may hold values from 6 to 10, as said below
Outputs:
- grad_gate: bfloat16 [32, 10, 128, 128], P('dp', None, 'fsdp')
- grad_up: bfloat16 [32, 10, 128, 128], P('dp', None, 'fsdp')
- grad_down: bfloat16 [32, 10, 128, 128], P('dp', None, 'fsdp')
Inputs may be any that keep to these rules, and one draw needn't show every extreme that they name: `input_lists`: the first 10 entries of each row are distinct; entries at dead slots are ignored. `input_counts`: among the hidden blocks of one index of dp, one block has exactly 10 live slots. `output_lists`: the first 10 entries of each row are distinct; entries at dead slots are ignored. `output_counts`: among the hidden blocks of one index of dp, one block has exactly 10 live slots.
All inputs are finite; a program needn't handle non-finite values.
Results may differ from a plain program's by a relative error of at most 0.025.
Values may be sent and summed in bfloat16 or wider, within the bound.
No kernel may reach another device: no remote copies, remote signals or barrier semaphores. Data moves between devices by JAX's collectives and lax.ppermute only.
A program may use at most 64 MiB of HBM per device.

v0:
```python
import functools

import jax
import jax.numpy as jnp
from jax import lax
from jax.experimental import pallas as pl
from jax.experimental.pallas import tpu as pltpu
from jax.sharding import PartitionSpec as P


F32 = jnp.float32
BF16 = jnp.bfloat16
VM = pl.BlockSpec(memory_space=pltpu.VMEM)
SM = pl.BlockSpec(memory_space=pltpu.SMEM)
TN = (((0,), (0,)), ((), ()))
NT = (((1,), (1,)), ((), ()))


def call(kernel, outs, scratch, smem, *args):
    nbytes = sum(a.size * a.dtype.itemsize for a in args) + sum(
        o.size * o.dtype.itemsize for o in outs
    )
    return pl.pallas_call(
        kernel,
        out_shape=tuple(outs),
        in_specs=[SM] * smem + [VM] * (len(args) - smem),
        out_specs=tuple(VM for _ in outs),
        scratch_shapes=scratch,
        compiler_params=pltpu.CompilerParams(vmem_limit_bytes=56 << 20),
        cost_estimate=pl.CostEstimate(flops=1 << 27, bytes_accessed=nbytes, transcendentals=0),
    )(*args)


def sds(shape, dtype=BF16):
    return jax.ShapeDtypeStruct(shape, dtype)


def turn_kernel(tin, *outs, pieces, nb, edge):
    d = lax.axis_index("dp")
    for r in range(pieces):
        out = outs[r % 2]
        base = lax.bitwise_xor(d, r) * (nb * edge)
        for j in range(nb):
            lanes = pl.ds(pl.multiple_of(base + j * edge, edge), edge)
            out[r // 2, j * edge : (j + 1) * edge, :] = tin[:, lanes].T


def relative_block(block, d, nb):
    return lax.bitwise_xor(block // nb, d) * nb + lax.rem(block, nb)


def front_kernel(lists, counts, *refs, pieces, zs, nb, rows, edge, slots, blocks):
    xs = refs[:pieces]
    gate, up = refs[pieces : pieces + 2]
    outs = refs[pieces + 2 : pieces + 2 + zs]
    gathered = refs[pieces + 2 + zs]
    xall, weights = refs[pieces + 3 + zs :]
    d = lax.axis_index("dp")
    tok = xs[0].shape[-1]
    for r in range(pieces):
        for s in range(zs):
            xall[r * nb * rows : (r + 1) * nb * rows, s * tok : (s + 1) * tok] = xs[r][s]
    for f in range(blocks):
        count = counts[f]
        for k in range(slots):
            b = relative_block(lists[f, k], d, nb)
            dst = slice(k * rows, (k + 1) * rows)
            gathered[f, dst, :] = xall[pl.ds(pl.multiple_of(b * rows, rows), rows), :]
            live = k < count
            weights[dst, :edge] = jnp.where(live, gate[f, k], jnp.zeros_like(gate[f, k]))
            weights[dst, edge:] = jnp.where(live, up[f, k], jnp.zeros_like(up[f, k]))
        both = lax.dot_general(gathered[f], weights[...], TN, preferred_element_type=F32)
        lanes = slice(f * edge, (f + 1) * edge)
        for s in range(zs):
            mine = both[((zs - s) % zs) * tok : ((zs - s) % zs + 1) * tok]
            outs[s][0, :, lanes] = mine[:, :edge].astype(outs[s].dtype)
            outs[s][1, :, lanes] = mine[:, edge:].astype(outs[s].dtype)


def middle_kernel(
    owners, lists, counts, *refs, pieces, zs, nb, rows, edge, slots, blocks
):
    parts = refs[:zs]
    downs = refs[zs : 2 * zs]
    tout = refs[2 * zs]
    outs = refs[2 * zs + 1 :]
    factors, hidden_out, keep, send, down_all = outs[0], outs[1 : 1 + zs], *outs[1 + zs : 4 + zs]
    acc, hidden_t = outs[4 + zs :]
    d, z, owner = lax.axis_index("dp"), lax.axis_index("fsdp"), owners[0]
    own = owner == d
    for b in range(pieces * nb):
        term = tout[:, b * edge : (b + 1) * edge].astype(F32)
        acc[b] = jnp.where(own, -term, jnp.zeros_like(term))
    for f in range(blocks):
        count = counts[f]
        for k in range(slots):
            live = k < count
            for s in range(zs):
                at = pl.multiple_of(lax.rem(z - s + zs, zs) * rows, rows)
                block = downs[s][f, k]
                down_all[f, pl.ds(at, rows), k * edge : (k + 1) * edge] = jnp.where(
                    live, block, jnp.zeros_like(block)
                )
    for f in range(blocks):
        lanes = slice(f * edge, (f + 1) * edge)
        g = parts[0][0, :, lanes].astype(F32)
        u = parts[0][1, :, lanes].astype(F32)
        for s in range(1, zs):
            g += parts[s][0, :, lanes].astype(F32)
            u += parts[s][1, :, lanes].astype(F32)
        sig = jax.nn.sigmoid(g)
        act = g * sig
        hidden = (act * u).astype(BF16)
        factors[0, :, lanes] = (u * sig * (1.0 + g * (1.0 - sig))).astype(BF16)
        factors[1, :, lanes] = act.astype(BF16)
        hidden_t[lanes, :] = hidden.T
        prod = jnp.dot(hidden, down_all[f], preferred_element_type=F32)
        for k in range(slots):
            acc[lists[f, k]] += prod[:, k * edge : (k + 1) * edge]
        for s in range(zs):
            at = pl.multiple_of(f * edge + lax.rem(z + s, zs) * rows, rows)
            hidden_out[s][f * rows : (f + 1) * rows, :] = hidden_t[pl.ds(at, rows), :]
    for r in range(pieces):
        for j in range(nb):
            value = acc[lax.bitwise_xor(d, r) * nb + j]
            if r % 2:
                send[r // 2, j] = value.astype(BF16)
            else:
                keep[r // 2, j] = value


def back_kernel(lists, *refs, pieces, nb, edge, slots, blocks):
    es = refs[:pieces]
    down_all, out, eall, ecat = refs[pieces:]
    d = lax.axis_index("dp")
    for r in range(pieces):
        eall[r * nb : (r + 1) * nb] = es[r][...]
    for f in range(blocks):
        for k in range(slots):
            ecat[:, k * edge : (k + 1) * edge] = eall[relative_block(lists[f, k], d, nb)]
        out[:, f * edge : (f + 1) * edge] = lax.dot_general(
            ecat[...], down_all[f], NT, preferred_element_type=F32
        ).astype(BF16)


def down_grad_kernel(lists, counts, *refs, pieces, zs, nb, rows, edge, slots, blocks):
    own = refs[:pieces]
    far = refs[pieces : 2 * pieces]
    hidden = refs[2 * pieces : 2 * pieces + zs]
    out, eall, hid = refs[2 * pieces + zs :]
    d = lax.axis_index("dp")
    tok = hidden[0].shape[-1]
    for r in range(pieces):
        for j in range(nb):
            eall[r * nb + j, :tok, :] = own[r][j]
            for s in range(1, zs):
                eall[r * nb + j, s * tok : (s + 1) * tok, :] = far[r][s - 1, j]
    for s in range(zs):
        hid[:, s * tok : (s + 1) * tok] = hidden[s][...]
    for f in range(blocks):
        count = counts[f]
        for k in range(slots):
            grad = jnp.dot(
                hid[f * rows : (f + 1) * rows, :],
                eall[relative_block(lists[f, k], d, nb)],
                preferred_element_type=F32,
            )
            out[f, k] = jnp.where(k < count, grad, jnp.zeros_like(grad)).astype(BF16)


def up_grad_kernel(counts, *refs, zs, rows, edge, slots, blocks):
    gathered = refs[0]
    factors = refs[1 : 1 + zs]
    errors = refs[1 + zs : 1 + 2 * zs]
    gate_out, up_out, both = refs[1 + 2 * zs :]
    tok = errors[0].shape[0]
    for f in range(blocks):
        count = counts[f]
        lanes = slice(f * edge, (f + 1) * edge)
        for s in range(zs):
            dh = errors[s][:, lanes].astype(F32)
            at = slice(s * tok, (s + 1) * tok)
            both[at, :edge] = (dh * factors[s][0, :, lanes].astype(F32)).astype(BF16)
            both[at, edge:] = (dh * factors[s][1, :, lanes].astype(F32)).astype(BF16)
        grad = jnp.dot(gathered[f], both[...], preferred_element_type=F32)
        for k in range(slots):
            part = grad[k * rows : (k + 1) * rows]
            part = jnp.where(k < count, part, jnp.zeros_like(part)).astype(BF16)
            gate_out[f, k] = part[:, :edge]
            up_out[f, k] = part[:, edge:]


def broadcast(shard, axis, root):
    mine = lax.axis_index(axis) == root
    return lax.psum(jnp.where(mine, shard, jnp.zeros_like(shard)), axis)


def live_mask(counts, slot_count):
    positions = jnp.arange(slot_count, dtype=jnp.int32)
    return (positions[None, :] < counts[:, None])[:, :, None, None]


def plain_shards(
    teacher_in,
    teacher_out,
    owner_section,
    gate_blocks,
    up_blocks,
    down_blocks,
    input_lists,
    input_counts,
    output_lists,
    output_counts,
):
    root_section = owner_section[0]
    local_in = teacher_in[0]
    local_out = teacher_out[0]
    micro_count = lax.axis_size("fsdp")
    rows_in = broadcast(local_in, "dp", root_section)
    gate_full, up_full, down_full = (
        lax.all_gather(gate_blocks, "fsdp", axis=2, tiled=True),
        lax.all_gather(up_blocks, "fsdp", axis=2, tiled=True),
        lax.all_gather(down_blocks, "fsdp", axis=2, tiled=True),
    )
    slot_count = input_lists.shape[1]
    block_edge = gate_full.shape[3]
    tok_rows = rows_in.shape[0]
    model_width = rows_in.shape[1]
    row_blocks = model_width // block_edge
    input_live = live_mask(input_counts, slot_count)
    output_live = live_mask(output_counts, slot_count)
    zero_value = jnp.zeros((), jnp.bfloat16)
    gate_live = jnp.where(input_live, gate_full, zero_value)
    up_live = jnp.where(input_live, up_full, zero_value)
    down_live = jnp.where(output_live, down_full, zero_value)
    picked = rows_in.reshape(tok_rows, row_blocks, block_edge)[:, input_lists]
    gate_pre = jnp.einsum("tfki,fkio->tfo", picked, gate_live, preferred_element_type=jnp.float32)
    up_pre = jnp.einsum("tfki,fkio->tfo", picked, up_live, preferred_element_type=jnp.float32)
    sigmoid_gate = jax.nn.sigmoid(gate_pre)
    activated = gate_pre * sigmoid_gate
    hidden = (activated * up_pre).astype(jnp.bfloat16)
    pieces = jnp.einsum("tfi,fkio->tfko", hidden, down_live, preferred_element_type=jnp.float32)
    blank_out = jnp.zeros((tok_rows, row_blocks, block_edge), jnp.float32)
    partial_out = blank_out.at[:, output_lists].add(pieces).reshape(tok_rows, model_width)
    is_owner = lax.axis_index("dp") == root_section
    own_term = jnp.where(is_owner, local_out.astype(jnp.float32), jnp.float32(0.0))
    residual_rows = lax.psum((partial_out - own_term).astype(jnp.bfloat16), "dp").astype(
        jnp.float32
    )
    scaled_error = (residual_rows / micro_count).astype(jnp.bfloat16)
    error_picked = scaled_error.reshape(tok_rows, row_blocks, block_edge)[:, output_lists]
    output_scale = output_live.astype(jnp.float32)
    input_scale = input_live.astype(jnp.float32)
    down_grad = (
        jnp.einsum("tfi,tfko->fkio", hidden, error_picked, preferred_element_type=jnp.float32)
        * output_scale
    )
    hidden_grad = jnp.einsum(
        "tfko,fkio->tfi", error_picked, down_live, preferred_element_type=jnp.float32
    )
    gate_error = (
        hidden_grad * up_pre * sigmoid_gate * (1.0 + gate_pre * (1.0 - sigmoid_gate))
    ).astype(jnp.bfloat16)
    up_error = (hidden_grad * activated).astype(jnp.bfloat16)
    gate_grad = (
        jnp.einsum("tfki,tfo->fkio", picked, gate_error, preferred_element_type=jnp.float32)
        * input_scale
    )
    up_grad = (
        jnp.einsum("tfki,tfo->fkio", picked, up_error, preferred_element_type=jnp.float32)
        * input_scale
    )
    gate_sum, up_sum, down_sum = (
        lax.psum_scatter(
            gate_grad.astype(jnp.bfloat16), "fsdp", scatter_dimension=2, tiled=True
        ).astype(jnp.float32),
        lax.psum_scatter(
            up_grad.astype(jnp.bfloat16), "fsdp", scatter_dimension=2, tiled=True
        ).astype(jnp.float32),
        lax.psum_scatter(
            down_grad.astype(jnp.bfloat16), "fsdp", scatter_dimension=2, tiled=True
        ).astype(jnp.float32),
    )
    return (
        gate_sum.astype(jnp.bfloat16),
        up_sum.astype(jnp.bfloat16),
        down_sum.astype(jnp.bfloat16),
    )


def shards(
    teacher_in,
    teacher_out,
    owner_section,
    gate_blocks,
    up_blocks,
    down_blocks,
    input_lists,
    input_counts,
    output_lists,
    output_counts,
):
    pieces, zs = lax.axis_size("dp"), lax.axis_size("fsdp")
    d, z = lax.axis_index("dp"), lax.axis_index("fsdp")
    owner = owner_section[0]
    tin, tout = teacher_in[0], teacher_out[0]
    blocks, slots, rows, edge = gate_blocks.shape
    tok, width = tin.shape
    row_blocks = width // edge
    nb = row_blocks // pieces
    chips = pieces // 2
    dims = dict(pieces=pieces, nb=nb, edge=edge)
    more = dict(zs=zs, rows=rows, slots=slots, blocks=blocks)

    def partner(a):
        return lax.ppermute(a, "dp", [(i, i ^ 1) for i in range(pieces)])

    def chip_swap(a, c):
        return lax.ppermute(a, "dp", [(i, i ^ (2 * c)) for i in range(pieces)])

    def shift(a, s):
        return lax.ppermute(a, "fsdp", [(i, (i + s) % zs) for i in range(zs)])

    def spread(a):
        per_chip = [a] + [chip_swap(a, c) for c in range(1, chips)]
        out = []
        for p in per_chip:
            out += [p, partner(p)]
        return out

    downs = [down_blocks] + [shift(down_blocks, s) for s in range(1, zs)]

    half = sds((chips, nb * edge, tok))
    kept, sent = call(functools.partial(turn_kernel, **dims), [half, half], [], 0, tin)
    met = partner(sent)
    is_owner = owner == d
    own_chip = lax.bitwise_xor(owner // 2, d // 2)
    piece = jnp.where(is_owner, kept[0], met[0])
    for c in range(1, chips):
        got = chip_swap(jnp.where(is_owner, kept[c], met[c]), c)
        piece = jnp.where(own_chip == c, got, piece)
    piece = piece.reshape(nb, zs, rows, tok)
    cut = [
        lax.dynamic_index_in_dim(piece, (z + s) % zs, 1, keepdims=False) for s in range(zs)
    ]
    mixed = jnp.stack([cut[0]] + [shift(cut[s], s) for s in range(1, zs)])
    xs = spread(mixed.reshape(zs, nb * rows, tok))

    part = sds((2, tok, blocks * edge))
    front = call(
        functools.partial(front_kernel, **dims, **more),
        [sds(part.shape, F32)] + [part] * (zs - 1) + [sds((blocks, slots * rows, zs * tok))],
        [pltpu.VMEM((row_blocks * rows, zs * tok), BF16), pltpu.VMEM((slots * rows, 2 * edge), BF16)],
        2,
        input_lists,
        input_counts,
        *xs,
        gate_blocks,
        up_blocks,
    )
    gathered = front[zs]
    parts = [front[0]] + [shift(front[s], s) for s in range(1, zs)]

    middle = call(
        functools.partial(middle_kernel, **dims, **more),
        [part]
        + [sds((blocks * rows, tok))] * zs
        + [sds((chips, nb, tok, edge), F32), sds((chips, nb, tok, edge)), sds((blocks, edge, slots * edge))],
        [pltpu.VMEM((row_blocks, tok, edge), F32), pltpu.VMEM((blocks * edge, tok), BF16)],
        3,
        owner_section,
        output_lists,
        output_counts,
        *parts,
        *downs,
        tout,
    )
    keep, send, down_all = middle[1 + zs :]
    factors = [middle[0]] + [shift(middle[0], s) for s in range(1, zs)]
    hidden = [middle[1]] + [shift(middle[1 + s], s) for s in range(1, zs)]

    summed = keep + partner(send).astype(F32)
    total = summed[0]
    for c in range(1, chips):
        total = total + chip_swap(summed[c].astype(BF16), c).astype(F32)
    error = (total / zs).astype(BF16)
    near = spread(error)
    arrived = [shift(error, s) for s in range(1, zs)]
    packed = jnp.stack(arrived)
    far = spread(packed)

    (hidden_grad,) = call(
        functools.partial(back_kernel, **dims, slots=slots, blocks=blocks),
        [sds((tok, blocks * edge))],
        [pltpu.VMEM((row_blocks, tok, edge), BF16), pltpu.VMEM((tok, slots * edge), BF16)],
        1,
        output_lists,
        *near,
        down_all,
    )
    grads = [hidden_grad] + [shift(hidden_grad, s) for s in range(1, zs)]

    (down_grad,) = call(
        functools.partial(down_grad_kernel, **dims, **more),
        [sds(down_blocks.shape)],
        [pltpu.VMEM((row_blocks, zs * tok, edge), BF16), pltpu.VMEM((blocks * rows, zs * tok), BF16)],
        2,
        output_lists,
        output_counts,
        *near,
        *far,
        *hidden,
    )
    gate_grad, up_grad = call(
        functools.partial(up_grad_kernel, edge=edge, **more),
        [sds(gate_blocks.shape)] * 2,
        [pltpu.VMEM((zs * tok, 2 * edge), BF16)],
        1,
        input_counts,
        gathered,
        *factors,
        *grads,
    )
    return gate_grad, up_grad, down_grad


def solution(mesh):
    weights = P("dp", None, "fsdp", None)
    rows = P("dp", "fsdp", None)

    def step(*args):
        block_rows = args[3].shape[2]
        if block_rows % 16:
            return plain_shards(*args)
        return shards(*args)

    return jax.shard_map(
        step,
        mesh=mesh,
        in_specs=(
            rows,
            rows,
            P("fsdp"),
            weights,
            weights,
            weights,
            P("dp", None),
            P("dp"),
            P("dp", None),
            P("dp"),
        ),
        out_specs=(weights, weights, weights),
        check_vma=False,
    )
```

profile of v0, /device:TPU:0, one launch (start us, length us, event | category | flops | bytes accessed | tf_op | source)
XLA Modules:
  0.0 179.0 jit_solution(10894883590977614813)
XLA Ops:
  0.6 2.5 %shard_map.121 = (bf16[4,512,128]{2,1,0:T(8,128)(2,1)}, bf16[4,512,128]{2,1,0:T(8,128)(2,1)}) custom-call(bf16[128,4096]{1,0:T(8,128)(2,1)} %bitcast.56), custom_call_target="tpu_custom_call" | custom-call | flops 134217728 | bytes 2097152 | tf_op jit(solution)/shard_map/pallas_call | solution.py:23
  3.1 0.5 collective-permute-start
  4.3 1.1 collective-permute-done
  5.4 1.1 fusion.9
  6.5 2.9 %collective-permute-start.3 = (bf16[512,128]{1,0:T(8,128)(2,1)S(1)}, bf16[512,128]{1,0:T(8,128)(2,1)S(1)}, u32[]{:S(2)}, u32[]{:S(2)}) collective-permute-start(bf16[512,128]{1,0:T(8,128)(2,1)S(1)} %get-tuple-element.39), channel_id=1, source_target_pairs={{0,8},{4,12},{8,0},{12,4},{16,24},{20,28},{24,16},{28,20},{1,9},{5... | collective-permute-start | bytes 393224 | tf_op jit(solution)/shard_map/ppermute | solution.py:319
  9.4 1.5 collective-permute-start.2
  10.9 2.4 %collective-permute-done.3 = bf16[512,128]{1,0:T(8,128)(2,1)S(1)} collective-permute-done((bf16[512,128]{1,0:T(8,128)(2,1)S(1)}, bf16[512,128]{1,0:T(8,128)(2,1)S(1)}, u32[]{:S(2)}, u32[]{:S(2)}) %collective-permute-start.3) | collective-permute-done | bytes 131104 | tf_op jit(solution)/shard_map/ppermute | solution.py:319
  13.4 4.1 %collective-permute-done.2 = bf16[512,128]{1,0:T(8,128)(2,1)S(1)} collective-permute-done((bf16[512,128]{1,0:T(8,128)(2,1)S(1)}, bf16[512,128]{1,0:T(8,128)(2,1)S(1)}, u32[]{:S(2)}, u32[]{:S(2)}) %collective-permute-start.2) | collective-permute-done | bytes 131104 | tf_op jit(solution)/shard_map/ppermute | solution.py:319
  17.5 0.9 fusion.8
  18.4 3.7 %collective-permute-start.6 = (bf16[4,32,128]{2,1,0:T(8,128)(2,1)S(1)}, bf16[4,32,128]{2,1,0:T(8,128)(2,1)S(1)}, u32[]{:S(2)}, u32[]{:S(2)}) collective-permute-start(bf16[4,32,128]{2,1,0:T(8,128)(2,1)S(1)} %get-tuple-element.46), channel_id=1, source_target_pairs={{0,3},{1,0},{2,1},{3,2},{4,7},{5,4},{6,5},{7,6},{8,11},{9,8},{10,9... | collective-permute-start | bytes 98312 | tf_op jit(solution)/shard_map/ppermute | solution.py:322
  22.1 1.0 collective-permute-start.4
  23.1 0.6 collective-permute-done.6
  23.7 3.2 %collective-permute-done.5 = bf16[4,32,128]{2,1,0:T(8,128)(2,1)S(1)} collective-permute-done((bf16[4,32,128]{2,1,0:T(8,128)(2,1)S(1)}, bf16[4,32,128]{2,1,0:T(8,128)(2,1)S(1)}, u32[]{:S(2)}, u32[]{:S(2)}) %collective-permute-start.5) | collective-permute-done | bytes 32800 | tf_op jit(solution)/shard_map/ppermute | solution.py:322
  26.9 0.9 collective-permute-done.4
  27.8 1.6 collective-permute-start.12
  29.4 1.1 collective-permute-start.18
  30.5 1.2 collective-permute-start.10
  31.7 0.8 collective-permute-start.8
  32.5 2.6 %collective-permute-done.12.refs_6_ = bf16[4,128,128]{2,1,0:T(8,128)(2,1)S(1)} collective-permute-done((bf16[4,128,128]{2,1,0:T(8,128)(2,1)S(1)}, bf16[4,128,128]{2,1,0:T(8,128)(2,1)S(1)}, u32[]{:S(2)}, u32[]{:S(2)}) %collective-permute-start.12) | collective-permute-done | bytes 131104 | tf_op jit(solution)/shard_map/ppermute | solution.py:319
  35.1 0.9 collective-permute-done.10.refs_4_
  36.0 0.7 collective-permute-done.8.refs_2_
  36.8 3.8 %collective-permute-start.19 = (bf16[4,10,32,128]{3,2,1,0:T(8,128)(2,1)S(1)}, bf16[4,10,32,128]{3,2,1,0:T(8,128)(2,1)S(1)}, u32[]{:S(2)}, u32[]{:S(2)}) collective-permute-start(bf16[4,10,32,128]{3,2,1,0:T(8,128)(2,1)S(1)} %copy-done.17), channel_id=1, source_target_pairs={{0,3},{1,0},{2,1},{3,2},{4,7},{5,4},{6,5},{7,6},{8,11},{9,8},{10,9... | collective-permute-start | bytes 983048 | tf_op jit(solution)/shard_map/ppermute | solution.py:322
  40.7 0.6 copy-done.34
  41.2 0.6 copy-done.35
  41.9 4.0 %shard_map.122 = (f32[2,128,512]{2,1,0:T(8,128)}, bf16[2,128,512]{2,1,0:T(8,128)(2,1)}, bf16[2,128,512]{2,1,0:T(8,128)(2,1)}, bf16[2,128,512]{2,1,0:T(8,128)(2,1)}, bf16[4,320,512]{2,1,0:T(8,128)(2,1)}) custom-call(s32[4,10]{1,0:T(4,128)} %lists.4, s32[4]{0:T(128)} %counts.6, bf16[4,128,128]{2,1,0:T(8,128)(2,1)} %copy-done.9, ...), custom_call_target="tpu_custom_call" | custom-call | flops 134217728 | bytes 4325552 | tf_op jit(solution)/shard_map/pallas_call | solution.py:23
  45.9 0.6 collective-permute-start.15
  46.6 3.8 %collective-permute-done.18.refs_6_ = bf16[4,10,32,128]{3,2,1,0:T(8,128)(2,1)S(1)} collective-permute-done((bf16[4,10,32,128]{3,2,1,0:T(8,128)(2,1)S(1)}, bf16[4,10,32,128]{3,2,1,0:T(8,128)(2,1)S(1)}, u32[]{:S(2)}, u32[]{:S(2)}) %collective-permute-start.18) | collective-permute-done | bytes 327712 | tf_op jit(solution)/shard_map/ppermute | solution.py:322
  50.4 12.5 %collective-permute-done.19.refs_7_ = bf16[4,10,32,128]{3,2,1,0:T(8,128)(2,1)S(1)} collective-permute-done((bf16[4,10,32,128]{3,2,1,0:T(8,128)(2,1)S(1)}, bf16[4,10,32,128]{3,2,1,0:T(8,128)(2,1)S(1)}, u32[]{:S(2)}, u32[]{:S(2)}) %collective-permute-start.19) | collective-permute-done | bytes 327712 | tf_op jit(solution)/shard_map/ppermute | solution.py:322
  62.9 11.3 %collective-permute-done.15.refs_2_ = bf16[2,128,512]{2,1,0:T(8,128)(2,1)S(1)} collective-permute-done((bf16[2,128,512]{2,1,0:T(8,128)(2,1)}, bf16[2,128,512]{2,1,0:T(8,128)(2,1)S(1)}, u32[]{:S(2)}, u32[]{:S(2)}) %collective-permute-start.15) | collective-permute-done | bytes 262176 | tf_op jit(solution)/shard_map/ppermute | solution.py:322
  74.3 0.7 copy-done.26
  75.0 4.9 %shard_map.123 = (bf16[2,128,512]{2,1,0:T(8,128)(2,1)}, bf16[128,128]{1,0:T(8,128)(2,1)}, bf16[128,128]{1,0:T(8,128)(2,1)}, bf16[128,128]{1,0:T(8,128)(2,1)}, bf...) custom-call(s32[1]{0:T(128)} %copy.15.owners, ...), custom_call_target="tpu_custom_call" | custom-call | flops 134217728 | bytes 6946996 | tf_op jit(solution)/shard_map/pallas_call | solution.py:23
  79.9 2.1 %collective-permute-done.23 = bf16[4,4,128,128]{3,2,1,0:T(8,128)(2,1)S(1)} collective-permute-done((bf16[4,4,128,128]{3,2,1,0:T(8,128)(2,1)}, bf16[4,4,128,128]{3,2,1,0:T(8,128)(2,1)S(1)}, u32[]{:S(2)}, u32[]{:S(2)}) %collective-permute-start.23) | collective-permute-done | bytes 524320 | tf_op jit(solution)/shard_map/ppermute | solution.py:316
  82.0 1.4 fusion.12
  83.5 1.5 collective-permute-start.24
  85.0 1.4 collective-permute-start.26
  86.4 0.6 collective-permute-start.25
  87.0 2.9 %collective-permute-done.24 = bf16[4,128,128]{2,1,0:T(8,128)(2,1)S(1)} collective-permute-done((bf16[4,128,128]{2,1,0:T(8,128)(2,1)S(1)}, bf16[4,128,128]{2,1,0:T(8,128)(2,1)S(1)}, u32[]{:S(2)}, u32[]{:S(2)}) %collective-permute-start.24) | collective-permute-done | bytes 131104 | tf_op jit(solution)/shard_map/ppermute | solution.py:319
  89.9 2.9 %collective-permute-done.26 = bf16[4,128,128]{2,1,0:T(8,128)(2,1)S(1)} collective-permute-done((bf16[4,128,128]{2,1,0:T(8,128)(2,1)S(1)}, bf16[4,128,128]{2,1,0:T(8,128)(2,1)S(1)}, u32[]{:S(2)}, u32[]{:S(2)}) %collective-permute-start.26) | collective-permute-done | bytes 131104 | tf_op jit(solution)/shard_map/ppermute | solution.py:319
  92.9 1.4 collective-permute-done.25
  94.3 7.3 %collective-permute-start.39 = (bf16[4,128,128]{2,1,0:T(8,128)(2,1)S(1)}, bf16[4,128,128]{2,1,0:T(8,128)(2,1)S(1)}, u32[]{:S(2)}, u32[]{:S(2)}) collective-permute-start(bf16[4,128,128]{2,1,0:T(8,128)(2,1)S(1)} %fusion.4.refs_0_), channel_id=1, source_target_pairs={{0,3},{1,0},{2,1},{3,2},{4,7},{5,4},{6,5},{7,6},{8,11},{9,8},{10,9... | collective-permute-start | bytes 393224 | tf_op jit(solution)/shard_map/ppermute | solution.py:322
  101.8 0.4 collective-permute-start.47
  102.3 2.4 %collective-permute-start.48 = (bf16[128,128]{1,0:T(8,128)(2,1)S(1)}, bf16[128,128]{1,0:T(8,128)(2,1)S(1)}, u32[]{:S(2)}, u32[]{:S(2)}) collective-permute-start(bf16[128,128]{1,0:T(8,128)(2,1)S(1)} %copy-done.42), channel_id=1, source_target_pairs={{0,2},{1,3},{2,0},{3,1},{4,6},{5,7},{6,4},{7,5},{8,10},{9,11},{10,... | collective-permute-start | bytes 98312 | tf_op jit(solution)/shard_map/ppermute | solution.py:322
  104.6 2.9 %collective-permute-start.22 = (bf16[2,128,512]{2,1,0:T(8,128)(2,1)S(1)}, bf16[2,128,512]{2,1,0:T(8,128)(2,1)S(1)}, u32[]{:S(2)}, u32[]{:S(2)}) collective-permute-start(bf16[2,128,512]{2,1,0:T(8,128)(2,1)S(1)} %copy-done.21), channel_id=1, source_target_pairs={{0,3},{1,0},{2,1},{3,2},{4,7},{5,4},{6,5},{7,6},{8,11},{9,8},{10,9... | collective-permute-start | bytes 786440 | tf_op jit(solution)/shard_map/ppermute | solution.py:322
  107.5 2.0 %collective-permute-done.47.refs_17_ = bf16[128,128]{1,0:T(8,128)(2,1)S(1)} collective-permute-done((bf16[128,128]{1,0:T(8,128)(2,1)S(1)}, bf16[128,128]{1,0:T(8,128)(2,1)S(1)}, u32[]{:S(2)}, u32[]{:S(2)}) %collective-permute-start.47) | collective-permute-done | bytes 32800 | tf_op jit(solution)/shard_map/ppermute | solution.py:322
  109.5 7.8 %collective-permute-start.37 = (bf16[4,128,128]{2,1,0:T(8,128)(2,1)S(1)}, bf16[4,128,128]{2,1,0:T(8,128)(2,1)S(1)}, u32[]{:S(2)}, u32[]{:S(2)}) collective-permute-start(bf16[4,128,128]{2,1,0:T(8,128)(2,1)S(1)} %fusion.4.refs_0_), channel_id=1, source_target_pairs={{0,1},{1,2},{2,3},{3,0},{4,5},{5,6},{6,7},{7,4},{8,9},{9,10},{10,1... | collective-permute-start | bytes 393224 | tf_op jit(solution)/shard_map/ppermute | solution.py:322
  117.3 1.5 collective-permute-start.32
  119.2 1.6 collective-permute-start.28
  120.8 2.9 %collective-permute-done.32.refs_6_ = bf16[4,128,128]{2,1,0:T(8,128)(2,1)S(1)} collective-permute-done((bf16[4,128,128]{2,1,0:T(8,128)(2,1)S(1)}, bf16[4,128,128]{2,1,0:T(8,128)(2,1)S(1)}, u32[]{:S(2)}, u32[]{:S(2)}) %collective-permute-start.32) | collective-permute-done | bytes 131104 | tf_op jit(solution)/shard_map/ppermute | solution.py:319
  123.8 1.2 collective-permute-done.30.refs_4_
  125.0 0.5 collective-permute-start.29
  125.6 1.5 collective-permute-start.45
  127.6 1.6 collective-permute-start.41
  129.2 2.0 %collective-permute-start.21 = (bf16[2,128,512]{2,1,0:T(8,128)(2,1)S(1)}, bf16[2,128,512]{2,1,0:T(8,128)(2,1)S(1)}, u32[]{:S(2)}, u32[]{:S(2)}) collective-permute-start(bf16[2,128,512]{2,1,0:T(8,128)(2,1)S(1)} %copy-done.21), channel_id=1, source_target_pairs={{0,2},{1,3},{2,0},{3,1},{4,6},{5,7},{6,4},{7,5},{8,10},{9,11},{10,... | collective-permute-start | bytes 786440 | tf_op jit(solution)/shard_map/ppermute | solution.py:322
  131.2 2.4 %collective-permute-start.20 = (bf16[2,128,512]{2,1,0:T(8,128)(2,1)S(1)}, bf16[2,128,512]{2,1,0:T(8,128)(2,1)S(1)}, u32[]{:S(2)}, u32[]{:S(2)}) collective-permute-start(bf16[2,128,512]{2,1,0:T(8,128)(2,1)S(1)} %copy-done.21), channel_id=1, source_target_pairs={{0,1},{1,2},{2,3},{3,0},{4,5},{5,6},{6,7},{7,4},{8,9},{9,10},{10,1... | collective-permute-start | bytes 786440 | tf_op jit(solution)/shard_map/ppermute | solution.py:322
  133.6 3.1 %shard_map.124.refs_5_ = bf16[128,512]{1,0:T(8,128)(2,1)} custom-call(s32[4,10]{1,0:T(4,128)} %lists.7, bf16[4,128,128]{2,1,0:T(8,128)(2,1)} %copy-done.1, bf16[4,128,128]{2,1,0:T(8,128)(2,1)} %copy-done.5, bf16[4,128,128]{2,1,0:T(8,128)(2,1)} %copy-done.4, bf16[4,128,128]{2,1,0:T(8,128)(2,1)} %copy-done.8, bf16[4,128,128]{2,1,0:T(8,128)(2,1)} %copy-done.3, ...), custom_call_target="tpu_custom_call" | custom-call | flops 134217728 | bytes 2490528 | tf_op jit(solution)/shard_map/pallas_call | solution.py:23
  136.7 13.1 %collective-permute-done.21.refs_3_ = bf16[2,128,512]{2,1,0:T(8,128)(2,1)S(1)} collective-permute-done((bf16[2,128,512]{2,1,0:T(8,128)(2,1)S(1)}, bf16[2,128,512]{2,1,0:T(8,128)(2,1)S(1)}, u32[]{:S(2)}, u32[]{:S(2)}) %collective-permute-start.21) | collective-permute-done | bytes 262176 | tf_op jit(solution)/shard_map/ppermute | solution.py:322
  149.9 0.5 collective-permute-start.46
  150.9 4.1 %collective-permute-done.36.refs_8_ = bf16[128,512]{1,0:T(8,128)(2,1)S(1)} collective-permute-done((bf16[128,512]{1,0:T(8,128)(2,1)}, bf16[128,512]{1,0:T(8,128)(2,1)S(1)}, u32[]{:S(2)}, u32[]{:S(2)}) %collective-permute-start.36) | collective-permute-done | bytes 131104 | tf_op jit(solution)/shard_map/ppermute | solution.py:322
  155.0 6.7 %collective-permute-done.35.refs_7_ = bf16[128,512]{1,0:T(8,128)(2,1)S(1)} collective-permute-done((bf16[128,512]{1,0:T(8,128)(2,1)}, bf16[128,512]{1,0:T(8,128)(2,1)S(1)}, u32[]{:S(2)}, u32[]{:S(2)}) %collective-permute-start.35) | collective-permute-done | bytes 131104 | tf_op jit(solution)/shard_map/ppermute | solution.py:322
  162.0 6.6 %collective-permute-done.34.refs_6_ = bf16[128,512]{1,0:T(8,128)(2,1)S(1)} collective-permute-done((bf16[128,512]{1,0:T(8,128)(2,1)}, bf16[128,512]{1,0:T(8,128)(2,1)S(1)}, u32[]{:S(2)}, u32[]{:S(2)}) %collective-permute-start.34) | collective-permute-done | bytes 131104 | tf_op jit(solution)/shard_map/ppermute | solution.py:322
  168.7 1.7 collective-permute-start.49
  170.4 3.2 %shard_map.125 = (bf16[4,10,32,128]{3,2,1,0:T(8,128)(2,1)}, bf16[4,10,32,128]{3,2,1,0:T(8,128)(2,1)}) custom-call(s32[4]{0:T(128)} %counts.6, bf16[4,320,512]{2,1,0:T(8,128)(2,1)} %get-tuple-element.22.refs_0_, bf16[2,128,512]{2,1,0:T(8,128)(2,1)} %get-tuple-element.27.refs_1_, bf16[2,128,512]{2,1,0:T(8,128)(2,1)} %copy-done.24, ...), custom_call_target="tpu_custom_call" | custom-call | flops 134217728 | bytes 3538960 | tf_op jit(solution)/shard_map/pallas_call | solution.py:23
  173.8 0.5 copy-done.40
  174.9 4.2 %shard_map.126 = bf16[4,10,32,128]{3,2,1,0:T(8,128)(2,1)} custom-call(s32[4,10]{1,0:T(4,128)} %lists.7, s32[4]{0:T(128)} %counts.7, bf16[4,128,128]{2,1,0:T(8,128)(2,1)} %copy-done.1, bf16[4,128,128]{2,1,0:T(8,128)(2,1)} %copy-done.5, bf16[4,128,128]{2,1,0:T(8,128)(2,1)} %copy-done.4, bf16[4,128,128]{2,1,0:T(8,128)(2,1)} %copy-done.8, ...), custom_call_target="tpu_custom_call" | custom-call | flops 134217728 | bytes 4653232 | tf_op jit(solution)/shard_map/pallas_call | solution.py:23
  (138 shorter events, 3.2 us)
Async XLA Ops:
  3.1 2.2 %collective-permute-start = (bf16[4,512,128]{2,1,0:T(8,128)(2,1)}, bf16[4,512,128]{2,1,0:T(8,128)(2,1)S(1)}, u32[]{:S(2)}, u32[]{:S(2)}) collective-permute-start(bf16[4,512,128]{2,1,0:T(8,128)(2,1)} %get-tuple-element.21), channel_id=1, source_target_pairs={{0,4},{4,0},{8,12},{12,8},{16,20},{20,16},{24,28},{28,24},{1,5},{5... | collective-permute-start | bytes 1572872 | tf_op jit(solution)/shard_map/ppermute | solution.py:316
  5.4 24.0 %copy-start.17 = (bf16[4,10,32,128]{3,2,1,0:T(8,128)(2,1)S(1)}, bf16[4,10,32,128]{3,2,1,0:T(8,128)(2,1)}, u32[]{:S(2)}) copy-start(bf16[4,10,32,128]{3,2,1,0:T(8,128)(2,1)} %refs_4_.1) | copy-start | bytes 983044
  6.5 6.9 %collective-permute-start.3 = (bf16[512,128]{1,0:T(8,128)(2,1)S(1)}, bf16[512,128]{1,0:T(8,128)(2,1)S(1)}, u32[]{:S(2)}, u32[]{:S(2)}) collective-permute-start(bf16[512,128]{1,0:T(8,128)(2,1)S(1)} %get-tuple-element.39), channel_id=1, source_target_pairs={{0,8},{4,12},{8,0},{12,4},{16,24},{20,28},{24,16},{28,20},{1,9},{5... | collective-permute-start | bytes 393224 | tf_op jit(solution)/shard_map/ppermute | solution.py:319
  9.4 8.1 %collective-permute-start.2 = (bf16[512,128]{1,0:T(8,128)(2,1)S(1)}, bf16[512,128]{1,0:T(8,128)(2,1)S(1)}, u32[]{:S(2)}, u32[]{:S(2)}) collective-permute-start(bf16[512,128]{1,0:T(8,128)(2,1)S(1)} %get-tuple-element.40), channel_id=1, source_target_pairs={{0,16},{4,20},{8,24},{12,28},{16,0},{20,4},{24,8},{28,12},{1,17},{... | collective-permute-start | bytes 393224 | tf_op jit(solution)/shard_map/ppermute | solution.py:319
  10.9 6.6 %collective-permute-start.1 = (bf16[512,128]{1,0:T(8,128)(2,1)S(1)}, bf16[512,128]{1,0:T(8,128)(2,1)S(1)}, u32[]{:S(2)}, u32[]{:S(2)}) collective-permute-start(bf16[512,128]{1,0:T(8,128)(2,1)S(1)} %get-tuple-element.41), channel_id=1, source_target_pairs={{0,24},{4,28},{8,16},{12,20},{16,8},{20,12},{24,0},{28,4},{1,25},{... | collective-permute-start | bytes 393224 | tf_op jit(solution)/shard_map/ppermute | solution.py:319
  18.4 5.3 %collective-permute-start.6 = (bf16[4,32,128]{2,1,0:T(8,128)(2,1)S(1)}, bf16[4,32,128]{2,1,0:T(8,128)(2,1)S(1)}, u32[]{:S(2)}, u32[]{:S(2)}) collective-permute-start(bf16[4,32,128]{2,1,0:T(8,128)(2,1)S(1)} %get-tuple-element.46), channel_id=1, source_target_pairs={{0,3},{1,0},{2,1},{3,2},{4,7},{5,4},{6,5},{7,6},{8,11},{9,8},{10,9... | collective-permute-start | bytes 98312 | tf_op jit(solution)/shard_map/ppermute | solution.py:322
  22.1 4.8 %collective-permute-start.5 = (bf16[4,32,128]{2,1,0:T(8,128)(2,1)S(1)}, bf16[4,32,128]{2,1,0:T(8,128)(2,1)S(1)}, u32[]{:S(2)}, u32[]{:S(2)}) collective-permute-start(bf16[4,32,128]{2,1,0:T(8,128)(2,1)S(1)} %get-tuple-element.47), channel_id=1, source_target_pairs={{0,2},{1,3},{2,0},{3,1},{4,6},{5,7},{6,4},{7,5},{8,10},{9,11},{10,... | collective-permute-start | bytes 98312 | tf_op jit(solution)/shard_map/ppermute | solution.py:322
  22.1 5.7 %collective-permute-start.4 = (bf16[4,32,128]{2,1,0:T(8,128)(2,1)S(1)}, bf16[4,32,128]{2,1,0:T(8,128)(2,1)S(1)}, u32[]{:S(2)}, u32[]{:S(2)}) collective-permute-start(bf16[4,32,128]{2,1,0:T(8,128)(2,1)S(1)} %get-tuple-element.48), channel_id=1, source_target_pairs={{0,1},{1,2},{2,3},{3,0},{4,5},{5,6},{6,7},{7,4},{8,9},{9,10},{10,1... | collective-permute-start | bytes 98312 | tf_op jit(solution)/shard_map/ppermute | solution.py:322
  27.8 7.2 %collective-permute-start.12 = (bf16[4,128,128]{2,1,0:T(8,128)(2,1)S(1)}, bf16[4,128,128]{2,1,0:T(8,128)(2,1)S(1)}, u32[]{:S(2)}, u32[]{:S(2)}) collective-permute-start(bf16[4,128,128]{2,1,0:T(8,128)(2,1)S(1)} %pad_maximum_fusion.1.refs_0_), channel_id=1, source_target_pairs={{0,24},{4,28},{8,16},{12,20},{16,8},{20,12},{24,0},{28,4},{1,25},{... | collective-permute-start | bytes 393224 | tf_op jit(solution)/shard_map/ppermute | solution.py:319
  29.4 21.0 %collective-permute-start.18 = (bf16[4,10,32,128]{3,2,1,0:T(8,128)(2,1)S(1)}, bf16[4,10,32,128]{3,2,1,0:T(8,128)(2,1)S(1)}, u32[]{:S(2)}, u32[]{:S(2)}) collective-permute-start(bf16[4,10,32,128]{3,2,1,0:T(8,128)(2,1)S(1)} %copy-done.17), channel_id=1, source_target_pairs={{0,2},{1,3},{2,0},{3,1},{4,6},{5,7},{6,4},{7,5},{8,10},{9,11},{10,... | collective-permute-start | bytes 983048 | tf_op jit(solution)/shard_map/ppermute | solution.py:322
  30.5 5.5 %collective-permute-start.10 = (bf16[4,128,128]{2,1,0:T(8,128)(2,1)S(1)}, bf16[4,128,128]{2,1,0:T(8,128)(2,1)S(1)}, u32[]{:S(2)}, u32[]{:S(2)}) collective-permute-start(bf16[4,128,128]{2,1,0:T(8,128)(2,1)S(1)} %pad_maximum_fusion.1.refs_0_), channel_id=1, source_target_pairs={{0,16},{4,20},{8,24},{12,28},{16,0},{20,4},{24,8},{28,12},{1,17},{... | collective-permute-start | bytes 393224 | tf_op jit(solution)/shard_map/ppermute | solution.py:319
  31.7 5.0 %collective-permute-start.8 = (bf16[4,128,128]{2,1,0:T(8,128)(2,1)S(1)}, bf16[4,128,128]{2,1,0:T(8,128)(2,1)S(1)}, u32[]{:S(2)}, u32[]{:S(2)}) collective-permute-start(bf16[4,128,128]{2,1,0:T(8,128)(2,1)S(1)} %pad_maximum_fusion.1.refs_0_), channel_id=1, source_target_pairs={{0,8},{4,12},{8,0},{12,4},{16,24},{20,28},{24,16},{28,20},{1,9},{5... | collective-permute-start | bytes 393224 | tf_op jit(solution)/shard_map/ppermute | solution.py:319
  32.5 4.2 %collective-permute-start.7 = (bf16[4,128,128]{2,1,0:T(8,128)(2,1)S(1)}, bf16[4,128,128]{2,1,0:T(8,128)(2,1)S(1)}, u32[]{:S(2)}, u32[]{:S(2)}) collective-permute-start(bf16[4,128,128]{2,1,0:T(8,128)(2,1)S(1)} %pad_maximum_fusion.1.refs_0_), channel_id=1, source_target_pairs={{0,4},{4,0},{8,12},{12,8},{16,20},{20,16},{24,28},{28,24},{1,5},{5... | collective-permute-start | bytes 393224 | tf_op jit(solution)/shard_map/ppermute | solution.py:316
  35.1 1.7 collective-permute-start.13
  36.0 4.6 %collective-permute-start.11 = (bf16[4,128,128]{2,1,0:T(8,128)(2,1)S(1)}, bf16[4,128,128]{2,1,0:T(8,128)(2,1)S(1)}, u32[]{:S(2)}, u32[]{:S(2)}) collective-permute-start(bf16[4,128,128]{2,1,0:T(8,128)(2,1)S(1)} %collective-permute-done.10.refs_4_), channel_id=1, source_target_pairs={{0,4},{4,0},{8,12},{12,8},{16,20},{20,16},{24,28},{28,24},{1,5},{5... | collective-permute-start | bytes 393224 | tf_op jit(solution)/shard_map/ppermute | solution.py:316
  36.7 3.9 %collective-permute-start.9 = (bf16[4,128,128]{2,1,0:T(8,128)(2,1)S(1)}, bf16[4,128,128]{2,1,0:T(8,128)(2,1)S(1)}, u32[]{:S(2)}, u32[]{:S(2)}) collective-permute-start(bf16[4,128,128]{2,1,0:T(8,128)(2,1)S(1)} %collective-permute-done.8.refs_2_), channel_id=1, source_target_pairs={{0,4},{4,0},{8,12},{12,8},{16,20},{20,16},{24,28},{28,24},{1,5},{5... | collective-permute-start | bytes 393224 | tf_op jit(solution)/shard_map/ppermute | solution.py:316
  36.7 13.7 %collective-permute-start.17 = (bf16[4,10,32,128]{3,2,1,0:T(8,128)(2,1)S(1)}, bf16[4,10,32,128]{3,2,1,0:T(8,128)(2,1)S(1)}, u32[]{:S(2)}, u32[]{:S(2)}) collective-permute-start(bf16[4,10,32,128]{3,2,1,0:T(8,128)(2,1)S(1)} %copy-done.17), channel_id=1, source_target_pairs={{0,1},{1,2},{2,3},{3,0},{4,5},{5,6},{6,7},{7,4},{8,9},{9,10},{10,1... | collective-permute-start | bytes 983048 | tf_op jit(solution)/shard_map/ppermute | solution.py:322
  36.8 26.1 %collective-permute-start.19 = (bf16[4,10,32,128]{3,2,1,0:T(8,128)(2,1)S(1)}, bf16[4,10,32,128]{3,2,1,0:T(8,128)(2,1)S(1)}, u32[]{:S(2)}, u32[]{:S(2)}) collective-permute-start(bf16[4,10,32,128]{3,2,1,0:T(8,128)(2,1)S(1)} %copy-done.17), channel_id=1, source_target_pairs={{0,3},{1,0},{2,1},{3,2},{4,7},{5,4},{6,5},{7,6},{8,11},{9,8},{10,9... | collective-permute-start | bytes 983048 | tf_op jit(solution)/shard_map/ppermute | solution.py:322
  45.9 17.0 %collective-permute-start.14 = (bf16[2,128,512]{2,1,0:T(8,128)(2,1)}, bf16[2,128,512]{2,1,0:T(8,128)(2,1)S(1)}, u32[]{:S(2)}, u32[]{:S(2)}) collective-permute-start(bf16[2,128,512]{2,1,0:T(8,128)(2,1)} %get-tuple-element.24), channel_id=1, source_target_pairs={{0,1},{1,2},{2,3},{3,0},{4,5},{5,6},{6,7},{7,4},{8,9},{9,10},{10,1... | collective-permute-start | bytes 786440 | tf_op jit(solution)/shard_map/ppermute | solution.py:322
  45.9 28.3 %collective-permute-start.15 = (bf16[2,128,512]{2,1,0:T(8,128)(2,1)}, bf16[2,128,512]{2,1,0:T(8,128)(2,1)S(1)}, u32[]{:S(2)}, u32[]{:S(2)}) collective-permute-start(bf16[2,128,512]{2,1,0:T(8,128)(2,1)} %get-tuple-element.25), channel_id=1, source_target_pairs={{0,2},{1,3},{2,0},{3,1},{4,6},{5,7},{6,4},{7,5},{8,10},{9,11},{10,... | collective-permute-start | bytes 786440 | tf_op jit(solution)/shard_map/ppermute | solution.py:322
  50.4 23.9 %copy-start.18 = (bf16[4,10,32,128]{3,2,1,0:T(8,128)(2,1)}, bf16[4,10,32,128]{3,2,1,0:T(8,128)(2,1)S(1)}, u32[]{:S(2)}) copy-start(bf16[4,10,32,128]{3,2,1,0:T(8,128)(2,1)S(1)} %collective-permute-done.18.refs_6_) | copy-start | bytes 983044
  50.4 23.9 %collective-permute-start.16 = (bf16[2,128,512]{2,1,0:T(8,128)(2,1)}, bf16[2,128,512]{2,1,0:T(8,128)(2,1)S(1)}, u32[]{:S(2)}, u32[]{:S(2)}) collective-permute-start(bf16[2,128,512]{2,1,0:T(8,128)(2,1)} %get-tuple-element.26), channel_id=1, source_target_pairs={{0,3},{1,0},{2,1},{3,2},{4,7},{5,4},{6,5},{7,6},{8,11},{9,8},{10,9... | collective-permute-start | bytes 786440 | tf_op jit(solution)/shard_map/ppermute | solution.py:322
  50.4 23.9 %copy-start.19 = (bf16[4,10,32,128]{3,2,1,0:T(8,128)(2,1)}, bf16[4,10,32,128]{3,2,1,0:T(8,128)(2,1)S(1)}, u32[]{:S(2)}) copy-start(bf16[4,10,32,128]{3,2,1,0:T(8,128)(2,1)S(1)} %collective-permute-done.17.refs_5_) | copy-start | bytes 983044
  79.9 2.1 %collective-permute-start.23 = (bf16[4,4,128,128]{3,2,1,0:T(8,128)(2,1)}, bf16[4,4,128,128]{3,2,1,0:T(8,128)(2,1)S(1)}, u32[]{:S(2)}, u32[]{:S(2)}) collective-permute-start(bf16[4,4,128,128]{3,2,1,0:T(8,128)(2,1)} %get-tuple-element.29), channel_id=1, source_target_pairs={{0,4},{4,0},{8,12},{12,8},{16,20},{20,16},{24,28},{28,24},{1,5},{5... | collective-permute-start | bytes 1572872 | tf_op jit(solution)/shard_map/ppermute | solution.py:316
  83.4 21.2 %copy-start.21 = (bf16[2,128,512]{2,1,0:T(8,128)(2,1)S(1)}, bf16[2,128,512]{2,1,0:T(8,128)(2,1)}, u32[]{:S(2)}) copy-start(bf16[2,128,512]{2,1,0:T(8,128)(2,1)} %get-tuple-element.27.refs_1_) | copy-start | bytes 786436
  83.5 6.4 %collective-permute-start.24 = (bf16[4,128,128]{2,1,0:T(8,128)(2,1)S(1)}, bf16[4,128,128]{2,1,0:T(8,128)(2,1)S(1)}, u32[]{:S(2)}, u32[]{:S(2)}) collective-permute-start(bf16[4,128,128]{2,1,0:T(8,128)(2,1)S(1)} %get-tuple-element.42), channel_id=1, source_target_pairs={{0,8},{4,12},{8,0},{12,4},{16,24},{20,28},{24,16},{28,20},{1,9},{5... | collective-permute-start | bytes 393224 | tf_op jit(solution)/shard_map/ppermute | solution.py:319
  85.0 7.8 %collective-permute-start.26 = (bf16[4,128,128]{2,1,0:T(8,128)(2,1)S(1)}, bf16[4,128,128]{2,1,0:T(8,128)(2,1)S(1)}, u32[]{:S(2)}, u32[]{:S(2)}) collective-permute-start(bf16[4,128,128]{2,1,0:T(8,128)(2,1)S(1)} %get-tuple-element.43), channel_id=1, source_target_pairs={{0,24},{4,28},{8,16},{12,20},{16,8},{20,12},{24,0},{28,4},{1,25},{... | collective-permute-start | bytes 393224 | tf_op jit(solution)/shard_map/ppermute | solution.py:319
  86.4 7.8 %collective-permute-start.25 = (bf16[4,128,128]{2,1,0:T(8,128)(2,1)S(1)}, bf16[4,128,128]{2,1,0:T(8,128)(2,1)S(1)}, u32[]{:S(2)}, u32[]{:S(2)}) collective-permute-start(bf16[4,128,128]{2,1,0:T(8,128)(2,1)S(1)} %get-tuple-element.44), channel_id=1, source_target_pairs={{0,16},{4,20},{8,24},{12,28},{16,0},{20,4},{24,8},{28,12},{1,17},{... | collective-permute-start | bytes 393224 | tf_op jit(solution)/shard_map/ppermute | solution.py:319
  94.3 39.2 %copy-start.1 = (bf16[4,128,128]{2,1,0:T(8,128)(2,1)}, bf16[4,128,128]{2,1,0:T(8,128)(2,1)S(1)}, u32[]{:S(2)}) copy-start(bf16[4,128,128]{2,1,0:T(8,128)(2,1)S(1)} %fusion.4.refs_0_) | copy-start | bytes 393220
  94.3 24.5 %collective-permute-start.39 = (bf16[4,128,128]{2,1,0:T(8,128)(2,1)S(1)}, bf16[4,128,128]{2,1,0:T(8,128)(2,1)S(1)}, u32[]{:S(2)}, u32[]{:S(2)}) collective-permute-start(bf16[4,128,128]{2,1,0:T(8,128)(2,1)S(1)} %fusion.4.refs_0_), channel_id=1, source_target_pairs={{0,3},{1,0},{2,1},{3,2},{4,7},{5,4},{6,5},{7,6},{8,11},{9,8},{10,9... | collective-permute-start | bytes 393224 | tf_op jit(solution)/shard_map/ppermute | solution.py:322
  101.6 17.6 %collective-permute-start.38 = (bf16[4,128,128]{2,1,0:T(8,128)(2,1)S(1)}, bf16[4,128,128]{2,1,0:T(8,128)(2,1)S(1)}, u32[]{:S(2)}, u32[]{:S(2)}) collective-permute-start(bf16[4,128,128]{2,1,0:T(8,128)(2,1)S(1)} %fusion.4.refs_0_), channel_id=1, source_target_pairs={{0,2},{1,3},{2,0},{3,1},{4,6},{5,7},{6,4},{7,5},{8,10},{9,11},{10,... | collective-permute-start | bytes 393224 | tf_op jit(solution)/shard_map/ppermute | solution.py:322
  101.8 7.7 %collective-permute-start.47 = (bf16[128,128]{1,0:T(8,128)(2,1)S(1)}, bf16[128,128]{1,0:T(8,128)(2,1)S(1)}, u32[]{:S(2)}, u32[]{:S(2)}) collective-permute-start(bf16[128,128]{1,0:T(8,128)(2,1)S(1)} %copy-done.43), channel_id=1, source_target_pairs={{0,1},{1,2},{2,3},{3,0},{4,5},{5,6},{6,7},{7,4},{8,9},{9,10},{10,1... | collective-permute-start | bytes 98312 | tf_op jit(solution)/shard_map/ppermute | solution.py:322
  102.3 15.1 %collective-permute-start.48 = (bf16[128,128]{1,0:T(8,128)(2,1)S(1)}, bf16[128,128]{1,0:T(8,128)(2,1)S(1)}, u32[]{:S(2)}, u32[]{:S(2)}) collective-permute-start(bf16[128,128]{1,0:T(8,128)(2,1)S(1)} %copy-done.42), channel_id=1, source_target_pairs={{0,2},{1,3},{2,0},{3,1},{4,6},{5,7},{6,4},{7,5},{8,10},{9,11},{10,... | collective-permute-start | bytes 98312 | tf_op jit(solution)/shard_map/ppermute | solution.py:322
  104.6 21.0 %collective-permute-start.22 = (bf16[2,128,512]{2,1,0:T(8,128)(2,1)S(1)}, bf16[2,128,512]{2,1,0:T(8,128)(2,1)S(1)}, u32[]{:S(2)}, u32[]{:S(2)}) collective-permute-start(bf16[2,128,512]{2,1,0:T(8,128)(2,1)S(1)} %copy-done.21), channel_id=1, source_target_pairs={{0,3},{1,0},{2,1},{3,2},{4,7},{5,4},{6,5},{7,6},{8,11},{9,8},{10,9... | collective-permute-start | bytes 786440 | tf_op jit(solution)/shard_map/ppermute | solution.py:322
  109.5 27.2 %copy-start.38 = (bf16[128,128]{1,0:T(8,128)(2,1)}, bf16[128,128]{1,0:T(8,128)(2,1)S(1)}, u32[]{:S(2)}) copy-start(bf16[128,128]{1,0:T(8,128)(2,1)S(1)} %collective-permute-done.47.refs_17_) | copy-start | bytes 98308
  109.5 11.3 %collective-permute-start.37 = (bf16[4,128,128]{2,1,0:T(8,128)(2,1)S(1)}, bf16[4,128,128]{2,1,0:T(8,128)(2,1)S(1)}, u32[]{:S(2)}, u32[]{:S(2)}) collective-permute-start(bf16[4,128,128]{2,1,0:T(8,128)(2,1)S(1)} %fusion.4.refs_0_), channel_id=1, source_target_pairs={{0,1},{1,2},{2,3},{3,0},{4,5},{5,6},{6,7},{7,4},{8,9},{9,10},{10,1... | collective-permute-start | bytes 393224 | tf_op jit(solution)/shard_map/ppermute | solution.py:322
  117.3 6.4 %collective-permute-start.32 = (bf16[4,128,128]{2,1,0:T(8,128)(2,1)S(1)}, bf16[4,128,128]{2,1,0:T(8,128)(2,1)S(1)}, u32[]{:S(2)}, u32[]{:S(2)}) collective-permute-start(bf16[4,128,128]{2,1,0:T(8,128)(2,1)S(1)} %fusion.4.refs_0_), channel_id=1, source_target_pairs={{0,24},{4,28},{8,16},{12,20},{16,8},{20,12},{24,0},{28,4},{1,25},{... | collective-permute-start | bytes 393224 | tf_op jit(solution)/shard_map/ppermute | solution.py:319
  118.8 6.2 %collective-permute-start.30 = (bf16[4,128,128]{2,1,0:T(8,128)(2,1)S(1)}, bf16[4,128,128]{2,1,0:T(8,128)(2,1)S(1)}, u32[]{:S(2)}, u32[]{:S(2)}) collective-permute-start(bf16[4,128,128]{2,1,0:T(8,128)(2,1)S(1)} %fusion.4.refs_0_), channel_id=1, source_target_pairs={{0,16},{4,20},{8,24},{12,28},{16,0},{20,4},{24,8},{28,12},{1,17},{... | collective-permute-start | bytes 393224 | tf_op jit(solution)/shard_map/ppermute | solution.py:319
  119.2 5.8 %collective-permute-start.28 = (bf16[4,128,128]{2,1,0:T(8,128)(2,1)S(1)}, bf16[4,128,128]{2,1,0:T(8,128)(2,1)S(1)}, u32[]{:S(2)}, u32[]{:S(2)}) collective-permute-start(bf16[4,128,128]{2,1,0:T(8,128)(2,1)S(1)} %fusion.4.refs_0_), channel_id=1, source_target_pairs={{0,8},{4,12},{8,0},{12,4},{16,24},{20,28},{24,16},{28,20},{1,9},{5... | collective-permute-start | bytes 393224 | tf_op jit(solution)/shard_map/ppermute | solution.py:319
  120.8 6.3 %collective-permute-start.27 = (bf16[4,128,128]{2,1,0:T(8,128)(2,1)S(1)}, bf16[4,128,128]{2,1,0:T(8,128)(2,1)S(1)}, u32[]{:S(2)}, u32[]{:S(2)}) collective-permute-start(bf16[4,128,128]{2,1,0:T(8,128)(2,1)S(1)} %fusion.4.refs_0_), channel_id=1, source_target_pairs={{0,4},{4,0},{8,12},{12,8},{16,20},{20,16},{24,28},{28,24},{1,5},{5... | collective-permute-start | bytes 393224 | tf_op jit(solution)/shard_map/ppermute | solution.py:316
  123.8 3.8 %collective-permute-start.33 = (bf16[4,128,128]{2,1,0:T(8,128)(2,1)S(1)}, bf16[4,128,128]{2,1,0:T(8,128)(2,1)S(1)}, u32[]{:S(2)}, u32[]{:S(2)}) collective-permute-start(bf16[4,128,128]{2,1,0:T(8,128)(2,1)S(1)} %collective-permute-done.32.refs_6_), channel_id=1, source_target_pairs={{0,4},{4,0},{8,12},{12,8},{16,20},{20,16},{24,28},{28,24},{1,5},{5... | collective-permute-start | bytes 393224 | tf_op jit(solution)/shard_map/ppermute | solution.py:316
  125.0 4.2 %collective-permute-start.31 = (bf16[4,128,128]{2,1,0:T(8,128)(2,1)S(1)}, bf16[4,128,128]{2,1,0:T(8,128)(2,1)S(1)}, u32[]{:S(2)}, u32[]{:S(2)}) collective-permute-start(bf16[4,128,128]{2,1,0:T(8,128)(2,1)S(1)} %collective-permute-done.30.refs_4_), channel_id=1, source_target_pairs={{0,4},{4,0},{8,12},{12,8},{16,20},{20,16},{24,28},{28,24},{1,5},{5... | collective-permute-start | bytes 393224 | tf_op jit(solution)/shard_map/ppermute | solution.py:316
  125.0 6.1 %collective-permute-start.29 = (bf16[4,128,128]{2,1,0:T(8,128)(2,1)S(1)}, bf16[4,128,128]{2,1,0:T(8,128)(2,1)S(1)}, u32[]{:S(2)}, u32[]{:S(2)}) collective-permute-start(bf16[4,128,128]{2,1,0:T(8,128)(2,1)S(1)} %collective-permute-done.28.refs_2_), channel_id=1, source_target_pairs={{0,4},{4,0},{8,12},{12,8},{16,20},{20,16},{24,28},{28,24},{1,5},{5... | collective-permute-start | bytes 393224 | tf_op jit(solution)/shard_map/ppermute | solution.py:316
  125.6 48.1 %copy-start = (bf16[3,4,128,128]{3,2,1,0:T(8,128)(2,1)}, bf16[3,4,128,128]{3,2,1,0:T(8,128)(2,1)S(1)}, u32[]{:S(2)}) copy-start(bf16[3,4,128,128]{3,2,1,0:T(8,128)(2,1)S(1)} %pad_maximum_fusion.refs_8_) | copy-start | bytes 1179652
  125.6 43.1 %copy-start.41 = (bf16[128,128]{1,0:T(8,128)(2,1)S(1)}, bf16[128,128]{1,0:T(8,128)(2,1)}, u32[]{:S(2)}) copy-start(bf16[128,128]{1,0:T(8,128)(2,1)} %get-tuple-element.36) | copy-start | bytes 98308
  125.6 44.8 %copy-start.22 = (bf16[2,128,512]{2,1,0:T(8,128)(2,1)}, bf16[2,128,512]{2,1,0:T(8,128)(2,1)S(1)}, u32[]{:S(2)}) copy-start(bf16[2,128,512]{2,1,0:T(8,128)(2,1)S(1)} %collective-permute-done.22.refs_4_) | copy-start | bytes 786436
  125.6 24.3 %collective-permute-start.45 = (bf16[3,4,128,128]{3,2,1,0:T(8,128)(2,1)S(1)}, bf16[3,4,128,128]{3,2,1,0:T(8,128)(2,1)S(1)}, u32[]{:S(2)}, u32[]{:S(2)}) collective-permute-start(bf16[3,4,128,128]{3,2,1,0:T(8,128)(2,1)S(1)} %pad_maximum_fusion.refs_8_), channel_id=1, source_target_pairs={{0,24},{4,28},{8,16},{12,20},{16,8},{20,12},{24,0},{28,4},{1,25},{... | collective-permute-start | bytes 1179656 | tf_op jit(solution)/shard_map/ppermute | solution.py:319
  127.2 23.2 %collective-permute-start.43 = (bf16[3,4,128,128]{3,2,1,0:T(8,128)(2,1)S(1)}, bf16[3,4,128,128]{3,2,1,0:T(8,128)(2,1)S(1)}, u32[]{:S(2)}, u32[]{:S(2)}) collective-permute-start(bf16[3,4,128,128]{3,2,1,0:T(8,128)(2,1)S(1)} %pad_maximum_fusion.refs_8_), channel_id=1, source_target_pairs={{0,16},{4,20},{8,24},{12,28},{16,0},{20,4},{24,8},{28,12},{1,17},{... | collective-permute-start | bytes 1179656 | tf_op jit(solution)/shard_map/ppermute | solution.py:319
  127.6 22.9 %collective-permute-start.41 = (bf16[3,4,128,128]{3,2,1,0:T(8,128)(2,1)S(1)}, bf16[3,4,128,128]{3,2,1,0:T(8,128)(2,1)S(1)}, u32[]{:S(2)}, u32[]{:S(2)}) collective-permute-start(bf16[3,4,128,128]{3,2,1,0:T(8,128)(2,1)S(1)} %pad_maximum_fusion.refs_8_), channel_id=1, source_target_pairs={{0,8},{4,12},{8,0},{12,4},{16,24},{20,28},{24,16},{28,20},{1,9},{5... | collective-permute-start | bytes 1179656 | tf_op jit(solution)/shard_map/ppermute | solution.py:319
  129.2 20.6 %collective-permute-start.21 = (bf16[2,128,512]{2,1,0:T(8,128)(2,1)S(1)}, bf16[2,128,512]{2,1,0:T(8,128)(2,1)S(1)}, u32[]{:S(2)}, u32[]{:S(2)}) collective-permute-start(bf16[2,128,512]{2,1,0:T(8,128)(2,1)S(1)} %copy-done.21), channel_id=1, source_target_pairs={{0,2},{1,3},{2,0},{3,1},{4,6},{5,7},{6,4},{7,5},{8,10},{9,11},{10,... | collective-permute-start | bytes 786440 | tf_op jit(solution)/shard_map/ppermute | solution.py:322
  131.2 18.6 %collective-permute-start.20 = (bf16[2,128,512]{2,1,0:T(8,128)(2,1)S(1)}, bf16[2,128,512]{2,1,0:T(8,128)(2,1)S(1)}, u32[]{:S(2)}, u32[]{:S(2)}) collective-permute-start(bf16[2,128,512]{2,1,0:T(8,128)(2,1)S(1)} %copy-done.21), channel_id=1, source_target_pairs={{0,1},{1,2},{2,3},{3,0},{4,5},{5,6},{6,7},{7,4},{8,9},{9,10},{10,1... | collective-permute-start | bytes 786440 | tf_op jit(solution)/shard_map/ppermute | solution.py:322
  149.8 20.6 %copy-start.23 = (bf16[2,128,512]{2,1,0:T(8,128)(2,1)}, bf16[2,128,512]{2,1,0:T(8,128)(2,1)S(1)}, u32[]{:S(2)}) copy-start(bf16[2,128,512]{2,1,0:T(8,128)(2,1)S(1)} %collective-permute-done.21.refs_3_) | copy-start | bytes 786436
  149.8 5.2 %collective-permute-start.36 = (bf16[128,512]{1,0:T(8,128)(2,1)}, bf16[128,512]{1,0:T(8,128)(2,1)S(1)}, u32[]{:S(2)}, u32[]{:S(2)}) collective-permute-start(bf16[128,512]{1,0:T(8,128)(2,1)} %shard_map.124.refs_5_), channel_id=1, source_target_pairs={{0,3},{1,0},{2,1},{3,2},{4,7},{5,4},{6,5},{7,6},{8,11},{9,8},{10,9... | collective-permute-start | bytes 393224 | tf_op jit(solution)/shard_map/ppermute | solution.py:322
  149.8 20.6 %copy-start.24 = (bf16[2,128,512]{2,1,0:T(8,128)(2,1)}, bf16[2,128,512]{2,1,0:T(8,128)(2,1)S(1)}, u32[]{:S(2)}) copy-start(bf16[2,128,512]{2,1,0:T(8,128)(2,1)S(1)} %collective-permute-done.20.refs_2_) | copy-start | bytes 786436
  149.8 23.9 %collective-permute-start.40 = (bf16[3,4,128,128]{3,2,1,0:T(8,128)(2,1)S(1)}, bf16[3,4,128,128]{3,2,1,0:T(8,128)(2,1)S(1)}, u32[]{:S(2)}, u32[]{:S(2)}) collective-permute-start(bf16[3,4,128,128]{3,2,1,0:T(8,128)(2,1)S(1)} %pad_maximum_fusion.refs_8_), channel_id=1, source_target_pairs={{0,4},{4,0},{8,12},{12,8},{16,20},{20,16},{24,28},{28,24},{1,5},{5... | collective-permute-start | bytes 1179656 | tf_op jit(solution)/shard_map/ppermute | solution.py:316
  149.9 23.8 %copy-start.10 = (bf16[3,4,128,128]{3,2,1,0:T(8,128)(2,1)}, bf16[3,4,128,128]{3,2,1,0:T(8,128)(2,1)S(1)}, u32[]{:S(2)}) copy-start(bf16[3,4,128,128]{3,2,1,0:T(8,128)(2,1)S(1)} %collective-permute-done.45.refs_14_) | copy-start | bytes 1179652
  149.9 23.8 %collective-permute-start.46 = (bf16[3,4,128,128]{3,2,1,0:T(8,128)(2,1)S(1)}, bf16[3,4,128,128]{3,2,1,0:T(8,128)(2,1)S(1)}, u32[]{:S(2)}, u32[]{:S(2)}) collective-permute-start(bf16[3,4,128,128]{3,2,1,0:T(8,128)(2,1)S(1)} %collective-permute-done.45.refs_14_), channel_id=1, source_target_pairs={{0,4},{4,0},{8,12},{12,8},{16,20},{20,16},{24,28},{28,24},{1,5},{5... | collective-permute-start | bytes 1179656 | tf_op jit(solution)/shard_map/ppermute | solution.py:316
  150.4 23.3 %copy-start.11 = (bf16[3,4,128,128]{3,2,1,0:T(8,128)(2,1)}, bf16[3,4,128,128]{3,2,1,0:T(8,128)(2,1)S(1)}, u32[]{:S(2)}) copy-start(bf16[3,4,128,128]{3,2,1,0:T(8,128)(2,1)S(1)} %collective-permute-done.43.refs_12_) | copy-start | bytes 1179652
  150.4 23.3 %collective-permute-start.44 = (bf16[3,4,128,128]{3,2,1,0:T(8,128)(2,1)S(1)}, bf16[3,4,128,128]{3,2,1,0:T(8,128)(2,1)S(1)}, u32[]{:S(2)}, u32[]{:S(2)}) collective-permute-start(bf16[3,4,128,128]{3,2,1,0:T(8,128)(2,1)S(1)} %collective-permute-done.43.refs_12_), channel_id=1, source_target_pairs={{0,4},{4,0},{8,12},{12,8},{16,20},{20,16},{24,28},{28,24},{1,5},{5... | collective-permute-start | bytes 1179656 | tf_op jit(solution)/shard_map/ppermute | solution.py:316
  150.5 23.2 %copy-start.12 = (bf16[3,4,128,128]{3,2,1,0:T(8,128)(2,1)}, bf16[3,4,128,128]{3,2,1,0:T(8,128)(2,1)S(1)}, u32[]{:S(2)}) copy-start(bf16[3,4,128,128]{3,2,1,0:T(8,128)(2,1)S(1)} %collective-permute-done.41.refs_10_) | copy-start | bytes 1179652
  150.5 23.3 %collective-permute-start.42 = (bf16[3,4,128,128]{3,2,1,0:T(8,128)(2,1)S(1)}, bf16[3,4,128,128]{3,2,1,0:T(8,128)(2,1)S(1)}, u32[]{:S(2)}, u32[]{:S(2)}) collective-permute-start(bf16[3,4,128,128]{3,2,1,0:T(8,128)(2,1)S(1)} %collective-permute-done.41.refs_10_), channel_id=1, source_target_pairs={{0,4},{4,0},{8,12},{12,8},{16,20},{20,16},{24,28},{28,24},{1,5},{5... | collective-permute-start | bytes 1179656 | tf_op jit(solution)/shard_map/ppermute | solution.py:316
  155.0 6.7 %collective-permute-start.35 = (bf16[128,512]{1,0:T(8,128)(2,1)}, bf16[128,512]{1,0:T(8,128)(2,1)S(1)}, u32[]{:S(2)}, u32[]{:S(2)}) collective-permute-start(bf16[128,512]{1,0:T(8,128)(2,1)} %shard_map.124.refs_5_), channel_id=1, source_target_pairs={{0,2},{1,3},{2,0},{3,1},{4,6},{5,7},{6,4},{7,5},{8,10},{9,11},{10,... | collective-permute-start | bytes 393224 | tf_op jit(solution)/shard_map/ppermute | solution.py:322
  161.7 7.0 %collective-permute-start.34 = (bf16[128,512]{1,0:T(8,128)(2,1)}, bf16[128,512]{1,0:T(8,128)(2,1)S(1)}, u32[]{:S(2)}, u32[]{:S(2)}) collective-permute-start(bf16[128,512]{1,0:T(8,128)(2,1)} %shard_map.124.refs_5_), channel_id=1, source_target_pairs={{0,1},{1,2},{2,3},{3,0},{4,5},{5,6},{6,7},{7,4},{8,9},{9,10},{10,1... | collective-permute-start | bytes 393224 | tf_op jit(solution)/shard_map/ppermute | solution.py:322
  168.7 5.0 %collective-permute-start.49 = (bf16[128,128]{1,0:T(8,128)(2,1)S(1)}, bf16[128,128]{1,0:T(8,128)(2,1)S(1)}, u32[]{:S(2)}, u32[]{:S(2)}) collective-permute-start(bf16[128,128]{1,0:T(8,128)(2,1)S(1)} %copy-done.41), channel_id=1, source_target_pairs={{0,3},{1,0},{2,1},{3,2},{4,7},{5,4},{6,5},{7,6},{8,11},{9,8},{10,9... | collective-permute-start | bytes 98312 | tf_op jit(solution)/shard_map/ppermute | solution.py:322
  (30 other events, 193.2 us)
where the time goes:
time: 179 us
  waiting for transfers between devices  90.2 us (50%)
  starting transfers between devices  58.3 us (33%)
  Pallas kernels  21.8 us (12%)
  other arithmetic  3.6 us (2%)
  local copies, waits for them, and re-layouts  3.28 us (2%)
  between operations  1.8 us (1%)
    ppermute x21, waiting for transfers between devices, shift(): return lax.ppermute(a, 'fsdp', [(i, (i + s) % zs) for i in range(zs)])  64.9 us
    ppermute x21, starting transfers between devices, shift(): return lax.ppermute(a, 'fsdp', [(i, (i + s) % zs) for i in range(zs)])  37.7 us
    ppermute x15, waiting for transfers between devices, chip_swap(): return lax.ppermute(a, 'dp', [(i, i ^ 2 * c) for i in range(pieces)])  22 us
    pallas_call x6, Pallas kernels, call(): pl.pallas_call(kernel, out_shape=tuple(outs), in_specs=[SM] * smem + [VM]...  21.8 us
    ppermute x15, starting transfers between devices, chip_swap(): return lax.ppermute(a, 'dp', [(i, i ^ 2 * c) for i in range(pieces)])  18.6 us
  transfers between devices with their start and end apart: 50, of which 23 were waited for; matrix products, arithmetic and copies ran while one was open for 0% of the time, Pallas kernels for 6%

commit v1 on v0

--- a/solution.py
+++ b/solution.py
@@ -26,13 +26,17 @@
         in_specs=[SM] * smem + [VM] * (len(args) - smem),
         out_specs=tuple(VM for _ in outs),
         scratch_shapes=scratch,
-        compiler_params=pltpu.CompilerParams(vmem_limit_bytes=56 << 20),
+        compiler_params=pltpu.CompilerParams(vmem_limit_bytes=16 << 20),
         cost_estimate=pl.CostEstimate(flops=1 << 27, bytes_accessed=nbytes, transcendentals=0),
     )(*args)
 
 
 def sds(shape, dtype=BF16):
     return jax.ShapeDtypeStruct(shape, dtype)
+
+
+def far_end(z, zs):
+    return jnp.logical_or(z == 0, z == zs - 1)
 
 
 def turn_kernel(tin, *outs, pieces, nb, edge):
@@ -72,7 +76,7 @@
         both = lax.dot_general(gathered[f], weights[...], TN, preferred_element_type=F32)
         lanes = slice(f * edge, (f + 1) * edge)
         for s in range(zs):
-            mine = both[((zs - s) % zs) * tok : ((zs - s) % zs + 1) * tok]
+            mine = both[s * tok : (s + 1) * tok]
             outs[s][0, :, lanes] = mine[:, :edge].astype(outs[s].dtype)
             outs[s][1, :, lanes] = mine[:, edge:].astype(outs[s].dtype)
 
@@ -81,9 +85,9 @@
     owners, lists, counts, *refs, pieces, zs, nb, rows, edge, slots, blocks
 ):
     parts = refs[:zs]
-    downs = refs[zs : 2 * zs]
-    tout = refs[2 * zs]
-    outs = refs[2 * zs + 1 :]
+    downs = refs[zs : 2 * zs + 1]
+    tout = refs[2 * zs + 1]
+    outs = refs[2 * zs + 2 :]
     factors, hidden_out, keep, send, down_all = outs[0], outs[1 : 1 + zs], *outs[1 + zs : 4 + zs]
     acc, hidden_t = outs[4 + zs :]
     d, z, owner = lax.axis_index("dp"), lax.axis_index("fsdp"), owners[0]
@@ -96,8 +100,10 @@
         for k in range(slots):
             live = k < count
             for s in range(zs):
-                at = pl.multiple_of(lax.rem(z - s + zs, zs) * rows, rows)
+                at = pl.multiple_of(lax.bitwise_xor(z, s) * rows, rows)
                 block = downs[s][f, k]
+                if s == zs - 1:
+                    block = jnp.where(far_end(z, zs), downs[zs][f, k], block)
                 down_all[f, pl.ds(at, rows), k * edge : (k + 1) * edge] = jnp.where(
                     live, block, jnp.zeros_like(block)
                 )
@@ -118,7 +124,7 @@
         for k in range(slots):
             acc[lists[f, k]] += prod[:, k * edge : (k + 1) * edge]
         for s in range(zs):
-            at = pl.multiple_of(f * edge + lax.rem(z + s, zs) * rows, rows)
+            at = pl.multiple_of(f * edge + lax.bitwise_xor(z, s) * rows, rows)
             hidden_out[s][f * rows : (f + 1) * rows, :] = hidden_t[pl.ds(at, rows), :]
     for r in range(pieces):
         for j in range(nb):
@@ -170,18 +176,22 @@
 
 def up_grad_kernel(counts, *refs, zs, rows, edge, slots, blocks):
     gathered = refs[0]
-    factors = refs[1 : 1 + zs]
-    errors = refs[1 + zs : 1 + 2 * zs]
-    gate_out, up_out, both = refs[1 + 2 * zs :]
+    factors = refs[1 : 2 + zs]
+    errors = refs[2 + zs : 2 + 2 * zs]
+    gate_out, up_out, both = refs[2 + 2 * zs :]
     tok = errors[0].shape[0]
+    ends = far_end(lax.axis_index("fsdp"), zs)
     for f in range(blocks):
         count = counts[f]
         lanes = slice(f * edge, (f + 1) * edge)
         for s in range(zs):
             dh = errors[s][:, lanes].astype(F32)
             at = slice(s * tok, (s + 1) * tok)
-            both[at, :edge] = (dh * factors[s][0, :, lanes].astype(F32)).astype(BF16)
-            both[at, edge:] = (dh * factors[s][1, :, lanes].astype(F32)).astype(BF16)
+            for side in range(2):
+                factor = factors[s][side, :, lanes]
+                if s == zs - 1:
+                    factor = jnp.where(ends, factors[zs][side, :, lanes], factor)
+                both[at, side * edge : (side + 1) * edge] = (dh * factor.astype(F32)).astype(BF16)
         grad = jnp.dot(gathered[f], both[...], preferred_element_type=F32)
         for k in range(slots):
             part = grad[k * rows : (k + 1) * rows]
@@ -319,7 +329,17 @@
         return lax.ppermute(a, "dp", [(i, i ^ (2 * c)) for i in range(pieces)])
 
     def shift(a, s):
-        return lax.ppermute(a, "fsdp", [(i, (i + s) % zs) for i in range(zs)])
+        return lax.ppermute(a, "fsdp", [(i, i ^ s) for i in range(zs)])
+
+    def gather(a):
+        last = zs - 1
+        out = [a] + [shift(a, s) for s in range(1, last)]
+        if zs != 4:
+            straight = shift(a, last)
+            return out + [straight, straight]
+        out.append(lax.ppermute(a, "fsdp", [(1, 2), (2, 1)]))
+        out.append(lax.ppermute(out[2], "fsdp", [(1, 0), (2, 3)]))
+        return out
 
     def spread(a):
         per_chip = [a] + [chip_swap(a, c) for c in range(1, chips)]
@@ -328,7 +348,7 @@
             out += [p, partner(p)]
         return out
 
-    downs = [down_blocks] + [shift(down_blocks, s) for s in range(1, zs)]
+    downs = gather(down_blocks)
 
     half = sds((chips, nb * edge, tok))
     kept, sent = call(functools.partial(turn_kernel, **dims), [half, half], [], 0, tin)
@@ -341,7 +361,8 @@
         piece = jnp.where(own_chip == c, got, piece)
     piece = piece.reshape(nb, zs, rows, tok)
     cut = [
-        lax.dynamic_index_in_dim(piece, (z + s) % zs, 1, keepdims=False) for s in range(zs)
+        lax.dynamic_index_in_dim(piece, lax.bitwise_xor(z, s), 1, keepdims=False)
+        for s in range(zs)
     ]
     mixed = jnp.stack([cut[0]] + [shift(cut[s], s) for s in range(1, zs)])
     xs = spread(mixed.reshape(zs, nb * rows, tok))
@@ -376,7 +397,7 @@
         tout,
     )
     keep, send, down_all = middle[1 + zs :]
-    factors = [middle[0]] + [shift(middle[0], s) for s in range(1, zs)]
+    factors = gather(middle[0])
     hidden = [middle[1]] + [shift(middle[1 + s], s) for s in range(1, zs)]
 
     summed = keep + partner(send).astype(F32)

time: 179 us -> 163 us (0.911)
  Pallas kernels: 21.8 us -> 9.69 us
  starting transfers between devices: 58.3 us -> 62.8 us
  waiting for transfers between devices: 90.2 us -> 86.8 us
  other arithmetic: 3.6 us -> 0.44 us
  local copies, waits for them, and re-layouts: 3.28 us -> 1.3 us
    pallas_call x6, Pallas kernels: 21.8 us -> 9.69 us  [call(): pl.pallas_call(kernel, out_shape=tuple(outs), in_specs=[SM] * smem + [VM]...]
    ppermute x15, waiting for transfers between devices: 22 us -> 15.1 us  [chip_swap(): return lax.ppermute(a, 'dp', [(i, i ^ 2 * c) for i in range(pieces)])]
    ppermute x21 -> x23, waiting for transfers between devices: 64.9 us -> 68.8 us  [the longest x19 56.8 us: shift(): return lax.ppermute(a, 'fsdp', [(i, i ^ s) for i in range(zs)])]
    ppermute x21 -> x23, starting transfers between devices: 37.7 us -> 41.2 us  [the longest x19 37.3 us: shift(): return lax.ppermute(a, 'fsdp', [(i, i ^ s) for i in range(zs)])]
    unnamed x88 -> x18, local copies, waits for them, and re-layouts: 3.23 us -> 1.26 us
  transfers between devices with their start and end apart: 50 -> 52, of which waited for: 23 -> 24; matrix products, arithmetic and copies ran while one was open for 0% -> 0% of each run, Pallas kernels for 6% -> 3%
where the time goes in v1:
time: 163 us
  waiting for transfers between devices  86.8 us (53%)
  starting transfers between devices  62.8 us (39%)
  Pallas kernels  9.69 us (6%)
    ppermute x19, waiting for transfers between devices, shift(): return lax.ppermute(a, 'fsdp', [(i, i ^ s) for i in range(zs)])  56.8 us
    ppermute x19, starting transfers between devices, shift(): return lax.ppermute(a, 'fsdp', [(i, i ^ s) for i in range(zs)])  37.3 us
    ppermute x15, starting transfers between devices, chip_swap(): return lax.ppermute(a, 'dp', [(i, i ^ 2 * c) for i in range(pieces)])  18.6 us
    ppermute x15, waiting for transfers between devices, chip_swap(): return lax.ppermute(a, 'dp', [(i, i ^ 2 * c) for i in range(pieces)])  15.1 us
    ppermute x2, waiting for transfers between devices, gather(): out.append(lax.ppermute(out[2], 'fsdp', [(1, 0), (2, 3)]))  12 us
    pallas_call x6, Pallas kernels, call(): pl.pallas_call(kernel, out_shape=tuple(outs), in_specs=[SM] * smem + [VM]...  9.69 us
  transfers between devices with their start and end apart: 52, of which 24 were waited for; matrix products, arithmetic and copies ran while one was open for 0% of the time, Pallas kernels for 3%

profile of v1, /device:TPU:0, one launch (start us, length us, event | category | flops | bytes accessed | tf_op | source)
XLA Modules:
  0.0 162.5 jit_solution(11235919480070436484)
XLA Ops:
  0.6 1.2 copy-done
  2.2 0.6 collective-permute-start
  3.4 0.9 collective-permute-done
  4.3 2.9 %collective-permute-start.3 = (bf16[512,128]{1,0:T(8,128)(2,1)S(1)}, bf16[512,128]{1,0:T(8,128)(2,1)S(1)}, u32[]{:S(2)}, u32[]{:S(2)}) collective-permute-start(bf16[512,128]{1,0:T(8,128)(2,1)S(1)} %get-tuple-element.39), channel_id=1, source_target_pairs={{0,8},{4,12},{8,0},{12,4},{16,24},{20,28},{24,16},{28,20},{1,9},{5... | collective-permute-start | bytes 393224 | tf_op jit(solution)/shard_map/ppermute | solution.py:329
  7.3 1.5 collective-permute-start.2
  8.8 3.0 %collective-permute-start.18 = (bf16[4,10,32,128]{3,2,1,0:T(8,128)(2,1)S(1)}, bf16[4,10,32,128]{3,2,1,0:T(8,128)(2,1)S(1)}, u32[]{:S(2)}, u32[]{:S(2)}) collective-permute-start(bf16[4,10,32,128]{3,2,1,0:T(8,128)(2,1)S(1)} %copy-done.2), channel_id=1, source_target_pairs={{0,2},{1,3},{2,0},{3,1},{4,6},{5,7},{6,4},{7,5},{8,10},{9,11},{10,... | collective-permute-start | bytes 983048 | tf_op jit(solution)/shard_map/ppermute | solution.py:332
  11.9 3.5 %collective-permute-done.2 = bf16[512,128]{1,0:T(8,128)(2,1)S(1)} collective-permute-done((bf16[512,128]{1,0:T(8,128)(2,1)S(1)}, bf16[512,128]{1,0:T(8,128)(2,1)S(1)}, u32[]{:S(2)}, u32[]{:S(2)}) %collective-permute-start.2) | collective-permute-done | bytes 131104 | tf_op jit(solution)/shard_map/ppermute | solution.py:329
  15.4 3.7 %collective-permute-start.6 = (bf16[4,32,128]{2,1,0:T(8,128)(2,1)S(1)}, bf16[4,32,128]{2,1,0:T(8,128)(2,1)S(1)}, u32[]{:S(2)}, u32[]{:S(2)}) collective-permute-start(bf16[4,32,128]{2,1,0:T(8,128)(2,1)S(1)} %get-tuple-element.46), channel_id=1, source_target_pairs={{0,3},{1,2},{2,1},{3,0},{4,7},{5,6},{6,5},{7,4},{8,11},{9,10},{10,... | collective-permute-start | bytes 98312 | tf_op jit(solution)/shard_map/ppermute | solution.py:332
  19.1 0.8 collective-permute-start.4
  19.9 1.3 collective-permute-done.6
  21.2 7.6 %collective-permute-done.5 = bf16[4,32,128]{2,1,0:T(8,128)(2,1)S(1)} collective-permute-done((bf16[4,32,128]{2,1,0:T(8,128)(2,1)S(1)}, bf16[4,32,128]{2,1,0:T(8,128)(2,1)S(1)}, u32[]{:S(2)}, u32[]{:S(2)}) %collective-permute-start.5) | collective-permute-done | bytes 32800 | tf_op jit(solution)/shard_map/ppermute | solution.py:332
  28.9 2.6 %collective-permute-start.12 = (bf16[4,128,128]{2,1,0:T(8,128)(2,1)S(1)}, bf16[4,128,128]{2,1,0:T(8,128)(2,1)S(1)}, u32[]{:S(2)}, u32[]{:S(2)}) collective-permute-start(bf16[4,128,128]{2,1,0:T(8,128)(2,1)S(1)} %pad_maximum_fusion.1.refs_0_), channel_id=1, source_target_pairs={{0,24},{4,28},{8,16},{12,20},{16,8},{20,12},{24,0},{28,4},{1,25},{... | collective-permute-start | bytes 393224 | tf_op jit(solution)/shard_map/ppermute | solution.py:329
  31.4 0.7 collective-permute-start.17
  32.1 0.5 collective-permute-start.10
  32.6 0.5 collective-permute-start.8
  33.2 2.1 %collective-permute-done.12.refs_6_ = bf16[4,128,128]{2,1,0:T(8,128)(2,1)S(1)} collective-permute-done((bf16[4,128,128]{2,1,0:T(8,128)(2,1)S(1)}, bf16[4,128,128]{2,1,0:T(8,128)(2,1)S(1)}, u32[]{:S(2)}, u32[]{:S(2)}) %collective-permute-start.12) | collective-permute-done | bytes 131104 | tf_op jit(solution)/shard_map/ppermute | solution.py:329
  35.3 2.4 %collective-permute-done.10.refs_4_ = bf16[4,128,128]{2,1,0:T(8,128)(2,1)S(1)} collective-permute-done((bf16[4,128,128]{2,1,0:T(8,128)(2,1)S(1)}, bf16[4,128,128]{2,1,0:T(8,128)(2,1)S(1)}, u32[]{:S(2)}, u32[]{:S(2)}) %collective-permute-start.10) | collective-permute-done | bytes 131104 | tf_op jit(solution)/shard_map/ppermute | solution.py:329
  37.7 0.4 collective-permute-start.9
  38.1 0.7 collective-permute-start.19
  38.8 1.3 collective-permute-start.20
  40.2 1.7 %shard_map.122 = (f32[2,128,512]{2,1,0:T(8,128)S(1)}, bf16[2,128,512]{2,1,0:T(8,128)(2,1)S(1)}, bf16[2,128,512]{2,1,0:T(8,128)(2,1)S(1)}, bf16[2,128,512]{2,1,0:T(8,128)(2,1)S(1)}, bf16[4,320,512]{2,1,0:T(8,128)(2,1)S(1)}) custom-call(s32[4,10]{1,0:T(4,128)S(1)} %copy-done.6, s32[4]{0:T(128)S(1)} %copy-done.8, ...), custom_call_target="tpu_custom_call" | custom-call | flops 134217728 | bytes 4325552 | tf_op jit(solution)/shard_map/pallas_call | solution.py:23
  41.9 4.7 %collective-permute-start.14 = (bf16[2,128,512]{2,1,0:T(8,128)(2,1)S(1)}, bf16[2,128,512]{2,1,0:T(8,128)(2,1)S(1)}, u32[]{:S(2)}, u32[]{:S(2)}) collective-permute-start(bf16[2,128,512]{2,1,0:T(8,128)(2,1)S(1)} %get-tuple-element.24), channel_id=1, source_target_pairs={{0,1},{1,0},{2,3},{3,2},{4,5},{5,4},{6,7},{7,6},{8,9},{9,8},{10,11... | collective-permute-start | bytes 786440 | tf_op jit(solution)/shard_map/ppermute | solution.py:332
  46.7 0.6 collective-permute-start.15
  47.3 1.8 %collective-permute-start.16 = (bf16[2,128,512]{2,1,0:T(8,128)(2,1)S(1)}, bf16[2,128,512]{2,1,0:T(8,128)(2,1)S(1)}, u32[]{:S(2)}, u32[]{:S(2)}) collective-permute-start(bf16[2,128,512]{2,1,0:T(8,128)(2,1)S(1)} %get-tuple-element.26), channel_id=1, source_target_pairs={{0,3},{1,2},{2,1},{3,0},{4,7},{5,6},{6,5},{7,4},{8,11},{9,10},{10,... | collective-permute-start | bytes 786440 | tf_op jit(solution)/shard_map/ppermute | solution.py:332
  49.1 7.6 %collective-permute-done.20.refs_8_ = bf16[4,10,32,128]{3,2,1,0:T(8,128)(2,1)S(1)} collective-permute-done((bf16[4,10,32,128]{3,2,1,0:T(8,128)(2,1)S(1)}, bf16[4,10,32,128]{3,2,1,0:T(8,128)(2,1)S(1)}, u32[]{:S(2)}, u32[]{:S(2)}) %collective-permute-start.20) | collective-permute-done | bytes 327712 | tf_op jit(solution)/shard_map/ppermute | solution.py:341
  56.7 13.0 %collective-permute-done.14.refs_1_ = bf16[2,128,512]{2,1,0:T(8,128)(2,1)S(1)} collective-permute-done((bf16[2,128,512]{2,1,0:T(8,128)(2,1)S(1)}, bf16[2,128,512]{2,1,0:T(8,128)(2,1)S(1)}, u32[]{:S(2)}, u32[]{:S(2)}) %collective-permute-start.14) | collective-permute-done | bytes 262176 | tf_op jit(solution)/shard_map/ppermute | solution.py:332
  69.7 1.8 %shard_map.123 = (bf16[2,128,512]{2,1,0:T(8,128)(2,1)S(1)}, bf16[128,128]{1,0:T(8,128)(2,1)S(1)}, bf16[128,128]{1,0:T(8,128)(2,1)S(1)}, bf16[128,128]{1,0:T(8,12...) custom-call(s32[1]{0:T(128)} %copy.15.owners, ...), custom_call_target="tpu_custom_call" | custom-call | flops 134217728 | bytes 7274676 | tf_op jit(solution)/shard_map/pallas_call | solution.py:23
  71.6 1.9 %collective-permute-done.25 = bf16[4,4,128,128]{3,2,1,0:T(8,128)(2,1)S(1)} collective-permute-done((bf16[4,4,128,128]{3,2,1,0:T(8,128)(2,1)S(1)}, bf16[4,4,128,128]{3,2,1,0:T(8,128)(2,1)S(1)}, u32[]{:S(2)}, u32[]{:S(2)}) %collective-permute-start.25) | collective-permute-done | bytes 524320 | tf_op jit(solution)/shard_map/ppermute | solution.py:326
  73.8 0.7 collective-permute-start.26
  74.5 2.4 %collective-permute-start.28 = (bf16[4,128,128]{2,1,0:T(8,128)(2,1)S(1)}, bf16[4,128,128]{2,1,0:T(8,128)(2,1)S(1)}, u32[]{:S(2)}, u32[]{:S(2)}) collective-permute-start(bf16[4,128,128]{2,1,0:T(8,128)(2,1)S(1)} %get-tuple-element.43), channel_id=1, source_target_pairs={{0,24},{4,28},{8,16},{12,20},{16,8},{20,12},{24,0},{28,4},{1,25},{... | collective-permute-start | bytes 393224 | tf_op jit(solution)/shard_map/ppermute | solution.py:329
  76.9 0.5 collective-permute-start.27
  77.3 0.7 collective-permute-start.23
  78.0 2.2 %collective-permute-done.26 = bf16[4,128,128]{2,1,0:T(8,128)(2,1)S(1)} collective-permute-done((bf16[4,128,128]{2,1,0:T(8,128)(2,1)S(1)}, bf16[4,128,128]{2,1,0:T(8,128)(2,1)S(1)}, u32[]{:S(2)}, u32[]{:S(2)}) %collective-permute-start.26) | collective-permute-done | bytes 131104 | tf_op jit(solution)/shard_map/ppermute | solution.py:329
  80.2 3.1 %collective-permute-done.28 = bf16[4,128,128]{2,1,0:T(8,128)(2,1)S(1)} collective-permute-done((bf16[4,128,128]{2,1,0:T(8,128)(2,1)S(1)}, bf16[4,128,128]{2,1,0:T(8,128)(2,1)S(1)}, u32[]{:S(2)}, u32[]{:S(2)}) %collective-permute-start.28) | collective-permute-done | bytes 131104 | tf_op jit(solution)/shard_map/ppermute | solution.py:329
  83.3 1.4 collective-permute-done.27
  84.7 1.7 %collective-permute-start.41 = (bf16[4,128,128]{2,1,0:T(8,128)(2,1)S(1)}, bf16[4,128,128]{2,1,0:T(8,128)(2,1)S(1)}, u32[]{:S(2)}, u32[]{:S(2)}) collective-permute-start(bf16[4,128,128]{2,1,0:T(8,128)(2,1)S(1)} %fusion.4.refs_0_), channel_id=1, source_target_pairs={{0,3},{1,2},{2,1},{3,0},{4,7},{5,6},{6,5},{7,4},{8,11},{9,10},{10,... | collective-permute-start | bytes 393224 | tf_op jit(solution)/shard_map/ppermute | solution.py:332
  86.4 4.5 %collective-permute-start.40 = (bf16[4,128,128]{2,1,0:T(8,128)(2,1)S(1)}, bf16[4,128,128]{2,1,0:T(8,128)(2,1)S(1)}, u32[]{:S(2)}, u32[]{:S(2)}) collective-permute-start(bf16[4,128,128]{2,1,0:T(8,128)(2,1)S(1)} %fusion.4.refs_0_), channel_id=1, source_target_pairs={{0,2},{1,3},{2,0},{3,1},{4,6},{5,7},{6,4},{7,5},{8,10},{9,11},{10,... | collective-permute-start | bytes 393224 | tf_op jit(solution)/shard_map/ppermute | solution.py:332
  91.2 2.9 %collective-permute-start.50 = (bf16[128,128]{1,0:T(8,128)(2,1)S(1)}, bf16[128,128]{1,0:T(8,128)(2,1)S(1)}, u32[]{:S(2)}, u32[]{:S(2)}) collective-permute-start(bf16[128,128]{1,0:T(8,128)(2,1)S(1)} %get-tuple-element.35), channel_id=1, source_target_pairs={{0,2},{1,3},{2,0},{3,1},{4,6},{5,7},{6,4},{7,5},{8,10},{9,11},{10,... | collective-permute-start | bytes 98312 | tf_op jit(solution)/shard_map/ppermute | solution.py:332
  94.1 0.7 collective-permute-done.49.refs_17_
  94.8 2.6 %collective-permute-start.22 = (bf16[2,128,512]{2,1,0:T(8,128)(2,1)S(1)}, bf16[2,128,512]{2,1,0:T(8,128)(2,1)S(1)}, u32[]{:S(2)}, u32[]{:S(2)}) collective-permute-start(bf16[2,128,512]{2,1,0:T(8,128)(2,1)S(1)} %get-tuple-element.27.refs_1_), channel_id=1, source_target_pairs={{0,2},{1,3},{2,0},{3,1},{4,6},{5,7},{6,4},{7,5},{8,10},{9,11},{10,... | collective-permute-start | bytes 786440 | tf_op jit(solution)/shard_map/ppermute | solution.py:332
  97.5 13.3 %collective-permute-done.50.refs_18_ = bf16[128,128]{1,0:T(8,128)(2,1)S(1)} collective-permute-done((bf16[128,128]{1,0:T(8,128)(2,1)S(1)}, bf16[128,128]{1,0:T(8,128)(2,1)S(1)}, u32[]{:S(2)}, u32[]{:S(2)}) %collective-permute-start.50) | collective-permute-done | bytes 32800 | tf_op jit(solution)/shard_map/ppermute | solution.py:332
  110.8 1.5 collective-permute-start.34
  112.4 0.5 collective-permute-start.32
  112.9 1.4 collective-permute-start.30
  114.3 3.2 %collective-permute-done.39 = bf16[4,128,128]{2,1,0:T(8,128)(2,1)S(1)} collective-permute-done((bf16[4,128,128]{2,1,0:T(8,128)(2,1)S(1)}, bf16[4,128,128]{2,1,0:T(8,128)(2,1)S(1)}, u32[]{:S(2)}, u32[]{:S(2)}) %collective-permute-start.39) | collective-permute-done | bytes 131104 | tf_op jit(solution)/shard_map/ppermute | solution.py:332
  117.5 0.5 collective-permute-start.35
  118.7 1.7 %collective-permute-start.47 = (bf16[3,4,128,128]{3,2,1,0:T(8,128)(2,1)S(1)}, bf16[3,4,128,128]{3,2,1,0:T(8,128)(2,1)S(1)}, u32[]{:S(2)}, u32[]{:S(2)}) collective-permute-start(bf16[3,4,128,128]{3,2,1,0:T(8,128)(2,1)S(1)} %pad_maximum_fusion.refs_8_), channel_id=1, source_target_pairs={{0,24},{4,28},{8,16},{12,20},{16,8},{20,12},{24,0},{28,4},{1,25},{... | collective-permute-start | bytes 1179656 | tf_op jit(solution)/shard_map/ppermute | solution.py:329
  120.4 0.5 collective-permute-start.45
  120.9 1.3 collective-permute-start.43
  122.2 2.0 %collective-permute-start.21 = (bf16[2,128,512]{2,1,0:T(8,128)(2,1)S(1)}, bf16[2,128,512]{2,1,0:T(8,128)(2,1)S(1)}, u32[]{:S(2)}, u32[]{:S(2)}) collective-permute-start(bf16[2,128,512]{2,1,0:T(8,128)(2,1)S(1)} %get-tuple-element.27.refs_1_), channel_id=1, source_target_pairs={{0,1},{1,0},{2,3},{3,2},{4,5},{5,4},{6,7},{7,6},{8,9},{9,8},{10,11... | collective-permute-start | bytes 786440 | tf_op jit(solution)/shard_map/ppermute | solution.py:332
  124.3 1.3 collective-permute-start.24
  125.6 1.3 shard_map.124.refs_6_
  126.8 4.6 %collective-permute-done.21.refs_2_ = bf16[2,128,512]{2,1,0:T(8,128)(2,1)S(1)} collective-permute-done((bf16[2,128,512]{2,1,0:T(8,128)(2,1)S(1)}, bf16[2,128,512]{2,1,0:T(8,128)(2,1)S(1)}, u32[]{:S(2)}, u32[]{:S(2)}) %collective-permute-start.21) | collective-permute-done | bytes 262176 | tf_op jit(solution)/shard_map/ppermute | solution.py:332
  131.4 2.6 %collective-permute-start.38 = (bf16[128,512]{1,0:T(8,128)(2,1)S(1)}, bf16[128,512]{1,0:T(8,128)(2,1)S(1)}, u32[]{:S(2)}, u32[]{:S(2)}) collective-permute-start(bf16[128,512]{1,0:T(8,128)(2,1)S(1)} %shard_map.124.refs_6_), channel_id=1, source_target_pairs={{0,3},{1,2},{2,1},{3,0},{4,7},{5,6},{6,5},{7,4},{8,11},{9,10},{10,... | collective-permute-start | bytes 393224 | tf_op jit(solution)/shard_map/ppermute | solution.py:332
  134.1 4.4 %collective-permute-done.24.refs_5_ = bf16[2,128,512]{2,1,0:T(8,128)(2,1)S(1)} collective-permute-done((bf16[2,128,512]{2,1,0:T(8,128)(2,1)S(1)}, bf16[2,128,512]{2,1,0:T(8,128)(2,1)S(1)}, u32[]{:S(2)}, u32[]{:S(2)}) %collective-permute-start.24) | collective-permute-done | bytes 262176 | tf_op jit(solution)/shard_map/ppermute | solution.py:341
  138.5 0.5 collective-permute-start.48
  139.3 0.5 collective-permute-start.44
  139.7 3.1 %collective-permute-start.37 = (bf16[128,512]{1,0:T(8,128)(2,1)S(1)}, bf16[128,512]{1,0:T(8,128)(2,1)S(1)}, u32[]{:S(2)}, u32[]{:S(2)}) collective-permute-start(bf16[128,512]{1,0:T(8,128)(2,1)S(1)} %shard_map.124.refs_6_), channel_id=1, source_target_pairs={{0,2},{1,3},{2,0},{3,1},{4,6},{5,7},{6,4},{7,5},{8,10},{9,11},{10,... | collective-permute-start | bytes 393224 | tf_op jit(solution)/shard_map/ppermute | solution.py:332
  142.8 6.5 %collective-permute-done.37.refs_8_ = bf16[128,512]{1,0:T(8,128)(2,1)S(1)} collective-permute-done((bf16[128,512]{1,0:T(8,128)(2,1)S(1)}, bf16[128,512]{1,0:T(8,128)(2,1)S(1)}, u32[]{:S(2)}, u32[]{:S(2)}) %collective-permute-start.37) | collective-permute-done | bytes 131104 | tf_op jit(solution)/shard_map/ppermute | solution.py:332
  149.4 5.0 %collective-permute-done.36.refs_7_ = bf16[128,512]{1,0:T(8,128)(2,1)S(1)} collective-permute-done((bf16[128,512]{1,0:T(8,128)(2,1)S(1)}, bf16[128,512]{1,0:T(8,128)(2,1)S(1)}, u32[]{:S(2)}, u32[]{:S(2)}) %collective-permute-start.36) | collective-permute-done | bytes 131104 | tf_op jit(solution)/shard_map/ppermute | solution.py:332
  154.3 2.1 %collective-permute-start.51 = (bf16[128,128]{1,0:T(8,128)(2,1)S(1)}, bf16[128,128]{1,0:T(8,128)(2,1)S(1)}, u32[]{:S(2)}, u32[]{:S(2)}) collective-permute-start(bf16[128,128]{1,0:T(8,128)(2,1)S(1)} %get-tuple-element.36), channel_id=1, source_target_pairs={{0,3},{1,2},{2,1},{3,0},{4,7},{5,6},{6,5},{7,4},{8,11},{9,10},{10,... | collective-permute-start | bytes 98312 | tf_op jit(solution)/shard_map/ppermute | solution.py:332
  156.4 2.0 %shard_map.125 = (bf16[4,10,32,128]{3,2,1,0:T(8,128)(2,1)}, bf16[4,10,32,128]{3,2,1,0:T(8,128)(2,1)}) custom-call(s32[4]{0:T(128)S(1)} %copy-done.8, bf16[4,320,512]{2,1,0:T(8,128)(2,1)S(1)} %get-tuple-element.22.refs_0_, bf16[2,128,512]{2,1,0:T(8,128)(2,1)S(1)} %get-tuple-element.27.refs_1_, bf16[2,128,512]{2,1,0:T(8,128)(2,1)S(1)} %collective-permute-done.21.refs_2_, ...), custom_call_target="tpu_custom_call" | custom-call | flops 134217728 | bytes 3801104 | tf_op jit(solution)/shard_map/pallas_call | solution.py:23
  158.5 1.6 collective-permute-done.51.refs_19_
  160.1 2.5 %shard_map.126 = bf16[4,10,32,128]{3,2,1,0:T(8,128)(2,1)} custom-call(s32[4,10]{1,0:T(4,128)S(1)} %copy-done.5, s32[4]{0:T(128)S(1)} %copy-done.7, bf16[4,128,128]{2,1,0:T(8,128)(2,1)S(1)} %fusion.4.refs_0_, bf16[4,128,128]{2,1,0:T(8,128)(2,1)S(1)} %collective-permute-done.29.refs_1_, bf16[4,128,128]{2,1,0:T(8,128)(2,1)S(1)} %collective-permute-done.30.refs_2_, ...), custom_call_target="tpu_custom_call" | custom-call | flops 134217728 | bytes 4653232 | tf_op jit(solution)/shard_map/pallas_call | solution.py:23
  (72 shorter events, 2.3 us)
Async XLA Ops:
  0.6 1.2 copy-start
  1.9 7.0 %copy-start.2 = (bf16[4,10,32,128]{3,2,1,0:T(8,128)(2,1)S(1)}, bf16[4,10,32,128]{3,2,1,0:T(8,128)(2,1)}, u32[]{:S(2)}) copy-start(bf16[4,10,32,128]{3,2,1,0:T(8,128)(2,1)} %refs_4_.1) | copy-start | bytes 983044
  2.2 2.1 %collective-permute-start = (bf16[4,512,128]{2,1,0:T(8,128)(2,1)S(1)}, bf16[4,512,128]{2,1,0:T(8,128)(2,1)S(1)}, u32[]{:S(2)}, u32[]{:S(2)}) collective-permute-start(bf16[4,512,128]{2,1,0:T(8,128)(2,1)S(1)} %get-tuple-element.21), channel_id=1, source_target_pairs={{0,4},{4,0},{8,12},{12,8},{16,20},{20,16},{24,28},{28,24},{1,5},{5... | collective-permute-start | bytes 1572872 | tf_op jit(solution)/shard_map/ppermute | solution.py:326
  4.3 35.9 %copy-start.3 = (bf16[4,10,32,128]{3,2,1,0:T(8,128)(2,1)S(1)}, bf16[4,10,32,128]{3,2,1,0:T(8,128)(2,1)}, u32[]{:S(2)}) copy-start(bf16[4,10,32,128]{3,2,1,0:T(8,128)(2,1)} %refs_8_.1) | copy-start | bytes 983044
  4.3 35.9 %copy-start.4 = (bf16[4,10,32,128]{3,2,1,0:T(8,128)(2,1)S(1)}, bf16[4,10,32,128]{3,2,1,0:T(8,128)(2,1)}, u32[]{:S(2)}) copy-start(bf16[4,10,32,128]{3,2,1,0:T(8,128)(2,1)} %refs_9_.1) | copy-start | bytes 983044
  4.3 35.9 %copy-start.6 = (s32[4,10]{1,0:T(4,128)S(1)}, s32[4,10]{1,0:T(4,128)}, u32[]{:S(2)}) copy-start(s32[4,10]{1,0:T(4,128)} %lists.4) | copy-start | bytes 484
  4.3 35.9 %copy-start.8 = (s32[4]{0:T(128)S(1)}, s32[4]{0:T(128)}, u32[]{:S(2)}) copy-start(s32[4]{0:T(128)} %counts.6) | copy-start | bytes 52
  4.3 7.5 %collective-permute-start.3 = (bf16[512,128]{1,0:T(8,128)(2,1)S(1)}, bf16[512,128]{1,0:T(8,128)(2,1)S(1)}, u32[]{:S(2)}, u32[]{:S(2)}) collective-permute-start(bf16[512,128]{1,0:T(8,128)(2,1)S(1)} %get-tuple-element.39), channel_id=1, source_target_pairs={{0,8},{4,12},{8,0},{12,4},{16,24},{20,28},{24,16},{28,20},{1,9},{5... | collective-permute-start | bytes 393224 | tf_op jit(solution)/shard_map/ppermute | solution.py:329
  7.3 8.1 %collective-permute-start.2 = (bf16[512,128]{1,0:T(8,128)(2,1)S(1)}, bf16[512,128]{1,0:T(8,128)(2,1)S(1)}, u32[]{:S(2)}, u32[]{:S(2)}) collective-permute-start(bf16[512,128]{1,0:T(8,128)(2,1)S(1)} %get-tuple-element.40), channel_id=1, source_target_pairs={{0,16},{4,20},{8,24},{12,28},{16,0},{20,4},{24,8},{28,12},{1,17},{... | collective-permute-start | bytes 393224 | tf_op jit(solution)/shard_map/ppermute | solution.py:329
  8.8 6.5 %collective-permute-start.1 = (bf16[512,128]{1,0:T(8,128)(2,1)S(1)}, bf16[512,128]{1,0:T(8,128)(2,1)S(1)}, u32[]{:S(2)}, u32[]{:S(2)}) collective-permute-start(bf16[512,128]{1,0:T(8,128)(2,1)S(1)} %get-tuple-element.41), channel_id=1, source_target_pairs={{0,24},{4,28},{8,16},{12,20},{16,8},{20,12},{24,0},{28,4},{1,25},{... | collective-permute-start | bytes 393224 | tf_op jit(solution)/shard_map/ppermute | solution.py:329
  8.8 24.4 %collective-permute-start.18 = (bf16[4,10,32,128]{3,2,1,0:T(8,128)(2,1)S(1)}, bf16[4,10,32,128]{3,2,1,0:T(8,128)(2,1)S(1)}, u32[]{:S(2)}, u32[]{:S(2)}) collective-permute-start(bf16[4,10,32,128]{3,2,1,0:T(8,128)(2,1)S(1)} %copy-done.2), channel_id=1, source_target_pairs={{0,2},{1,3},{2,0},{3,1},{4,6},{5,7},{6,4},{7,5},{8,10},{9,11},{10,... | collective-permute-start | bytes 983048 | tf_op jit(solution)/shard_map/ppermute | solution.py:332
  15.4 54.3 %copy-start.1 = (bf16[1,128,4096]{2,1,0:T(8,128)(2,1)S(1)}, bf16[1,128,4096]{2,1,0:T(8,128)(2,1)}, u32[]{:S(2)}) copy-start(bf16[1,128,4096]{2,1,0:T(8,128)(2,1)} %param.11) | copy-start | bytes 3145732
  15.4 54.3 %copy-start.5 = (s32[4,10]{1,0:T(4,128)S(1)}, s32[4,10]{1,0:T(4,128)}, u32[]{:S(2)}) copy-start(s32[4,10]{1,0:T(4,128)} %lists.7) | copy-start | bytes 484
  15.4 54.3 %copy-start.7 = (s32[4]{0:T(128)S(1)}, s32[4]{0:T(128)}, u32[]{:S(2)}) copy-start(s32[4]{0:T(128)} %counts.7) | copy-start | bytes 52
  15.4 5.8 %collective-permute-start.6 = (bf16[4,32,128]{2,1,0:T(8,128)(2,1)S(1)}, bf16[4,32,128]{2,1,0:T(8,128)(2,1)S(1)}, u32[]{:S(2)}, u32[]{:S(2)}) collective-permute-start(bf16[4,32,128]{2,1,0:T(8,128)(2,1)S(1)} %get-tuple-element.46), channel_id=1, source_target_pairs={{0,3},{1,2},{2,1},{3,0},{4,7},{5,6},{6,5},{7,4},{8,11},{9,10},{10,... | collective-permute-start | bytes 98312 | tf_op jit(solution)/shard_map/ppermute | solution.py:332
  19.1 9.7 %collective-permute-start.5 = (bf16[4,32,128]{2,1,0:T(8,128)(2,1)S(1)}, bf16[4,32,128]{2,1,0:T(8,128)(2,1)S(1)}, u32[]{:S(2)}, u32[]{:S(2)}) collective-permute-start(bf16[4,32,128]{2,1,0:T(8,128)(2,1)S(1)} %get-tuple-element.47), channel_id=1, source_target_pairs={{0,2},{1,3},{2,0},{3,1},{4,6},{5,7},{6,4},{7,5},{8,10},{9,11},{10,... | collective-permute-start | bytes 98312 | tf_op jit(solution)/shard_map/ppermute | solution.py:332
  19.1 9.7 %collective-permute-start.4 = (bf16[4,32,128]{2,1,0:T(8,128)(2,1)S(1)}, bf16[4,32,128]{2,1,0:T(8,128)(2,1)S(1)}, u32[]{:S(2)}, u32[]{:S(2)}) collective-permute-start(bf16[4,32,128]{2,1,0:T(8,128)(2,1)S(1)} %get-tuple-element.48), channel_id=1, source_target_pairs={{0,1},{1,0},{2,3},{3,2},{4,5},{5,4},{6,7},{7,6},{8,9},{9,8},{10,11... | collective-permute-start | bytes 98312 | tf_op jit(solution)/shard_map/ppermute | solution.py:332
  28.9 6.4 %collective-permute-start.12 = (bf16[4,128,128]{2,1,0:T(8,128)(2,1)S(1)}, bf16[4,128,128]{2,1,0:T(8,128)(2,1)S(1)}, u32[]{:S(2)}, u32[]{:S(2)}) collective-permute-start(bf16[4,128,128]{2,1,0:T(8,128)(2,1)S(1)} %pad_maximum_fusion.1.refs_0_), channel_id=1, source_target_pairs={{0,24},{4,28},{8,16},{12,20},{16,8},{20,12},{24,0},{28,4},{1,25},{... | collective-permute-start | bytes 393224 | tf_op jit(solution)/shard_map/ppermute | solution.py:329
  31.4 15.8 %collective-permute-start.17 = (bf16[4,10,32,128]{3,2,1,0:T(8,128)(2,1)S(1)}, bf16[4,10,32,128]{3,2,1,0:T(8,128)(2,1)S(1)}, u32[]{:S(2)}, u32[]{:S(2)}) collective-permute-start(bf16[4,10,32,128]{3,2,1,0:T(8,128)(2,1)S(1)} %copy-done.2), channel_id=1, source_target_pairs={{0,1},{1,0},{2,3},{3,2},{4,5},{5,4},{6,7},{7,6},{8,9},{9,8},{10,11... | collective-permute-start | bytes 983048 | tf_op jit(solution)/shard_map/ppermute | solution.py:332
  32.1 5.5 %collective-permute-start.10 = (bf16[4,128,128]{2,1,0:T(8,128)(2,1)S(1)}, bf16[4,128,128]{2,1,0:T(8,128)(2,1)S(1)}, u32[]{:S(2)}, u32[]{:S(2)}) collective-permute-start(bf16[4,128,128]{2,1,0:T(8,128)(2,1)S(1)} %pad_maximum_fusion.1.refs_0_), channel_id=1, source_target_pairs={{0,16},{4,20},{8,24},{12,28},{16,0},{20,4},{24,8},{28,12},{1,17},{... | collective-permute-start | bytes 393224 | tf_op jit(solution)/shard_map/ppermute | solution.py:329
  32.6 5.1 %collective-permute-start.8 = (bf16[4,128,128]{2,1,0:T(8,128)(2,1)S(1)}, bf16[4,128,128]{2,1,0:T(8,128)(2,1)S(1)}, u32[]{:S(2)}, u32[]{:S(2)}) collective-permute-start(bf16[4,128,128]{2,1,0:T(8,128)(2,1)S(1)} %pad_maximum_fusion.1.refs_0_), channel_id=1, source_target_pairs={{0,8},{4,12},{8,0},{12,4},{16,24},{20,28},{24,16},{28,20},{1,9},{5... | collective-permute-start | bytes 393224 | tf_op jit(solution)/shard_map/ppermute | solution.py:329
  33.2 5.0 %collective-permute-start.7 = (bf16[4,128,128]{2,1,0:T(8,128)(2,1)S(1)}, bf16[4,128,128]{2,1,0:T(8,128)(2,1)S(1)}, u32[]{:S(2)}, u32[]{:S(2)}) collective-permute-start(bf16[4,128,128]{2,1,0:T(8,128)(2,1)S(1)} %pad_maximum_fusion.1.refs_0_), channel_id=1, source_target_pairs={{0,4},{4,0},{8,12},{12,8},{16,20},{20,16},{24,28},{28,24},{1,5},{5... | collective-permute-start | bytes 393224 | tf_op jit(solution)/shard_map/ppermute | solution.py:326
  35.3 3.6 %collective-permute-start.13 = (bf16[4,128,128]{2,1,0:T(8,128)(2,1)S(1)}, bf16[4,128,128]{2,1,0:T(8,128)(2,1)S(1)}, u32[]{:S(2)}, u32[]{:S(2)}) collective-permute-start(bf16[4,128,128]{2,1,0:T(8,128)(2,1)S(1)} %collective-permute-done.12.refs_6_), channel_id=1, source_target_pairs={{0,4},{4,0},{8,12},{12,8},{16,20},{20,16},{24,28},{28,24},{1,5},{5... | collective-permute-start | bytes 393224 | tf_op jit(solution)/shard_map/ppermute | solution.py:326
  37.6 2.5 %collective-permute-start.11 = (bf16[4,128,128]{2,1,0:T(8,128)(2,1)S(1)}, bf16[4,128,128]{2,1,0:T(8,128)(2,1)S(1)}, u32[]{:S(2)}, u32[]{:S(2)}) collective-permute-start(bf16[4,128,128]{2,1,0:T(8,128)(2,1)S(1)} %collective-permute-done.10.refs_4_), channel_id=1, source_target_pairs={{0,4},{4,0},{8,12},{12,8},{16,20},{20,16},{24,28},{28,24},{1,5},{5... | collective-permute-start | bytes 393224 | tf_op jit(solution)/shard_map/ppermute | solution.py:326
  37.7 2.4 %collective-permute-start.9 = (bf16[4,128,128]{2,1,0:T(8,128)(2,1)S(1)}, bf16[4,128,128]{2,1,0:T(8,128)(2,1)S(1)}, u32[]{:S(2)}, u32[]{:S(2)}) collective-permute-start(bf16[4,128,128]{2,1,0:T(8,128)(2,1)S(1)} %collective-permute-done.8.refs_2_), channel_id=1, source_target_pairs={{0,4},{4,0},{8,12},{12,8},{16,20},{20,16},{24,28},{28,24},{1,5},{5... | collective-permute-start | bytes 393224 | tf_op jit(solution)/shard_map/ppermute | solution.py:326
  38.1 11.0 %collective-permute-start.19 = (bf16[4,10,32,128]{3,2,1,0:T(8,128)(2,1)S(1)}, bf16[4,10,32,128]{3,2,1,0:T(8,128)(2,1)S(1)}, u32[]{:S(2)}, u32[]{:S(2)}) collective-permute-start(bf16[4,10,32,128]{3,2,1,0:T(8,128)(2,1)S(1)} %copy-done.2), channel_id=1, source_target_pairs={{1,2},{2,1},{5,6},{6,5},{9,10},{10,9},{13,14},{14,13},{17,18},{18,... | collective-permute-start | bytes 983048 | tf_op jit(solution)/shard_map/ppermute | solution.py:340
  38.8 17.9 %collective-permute-start.20 = (bf16[4,10,32,128]{3,2,1,0:T(8,128)(2,1)S(1)}, bf16[4,10,32,128]{3,2,1,0:T(8,128)(2,1)S(1)}, u32[]{:S(2)}, u32[]{:S(2)}) collective-permute-start(bf16[4,10,32,128]{3,2,1,0:T(8,128)(2,1)S(1)} %collective-permute-done.18.refs_6_), channel_id=1, source_target_pairs={{1,0},{2,3},{5,4},{6,7},{9,8},{10,11},{13,12},{14,15},{17,16},{18,... | collective-permute-start | bytes 983048 | tf_op jit(solution)/shard_map/ppermute | solution.py:341
  41.9 27.8 %collective-permute-start.14 = (bf16[2,128,512]{2,1,0:T(8,128)(2,1)S(1)}, bf16[2,128,512]{2,1,0:T(8,128)(2,1)S(1)}, u32[]{:S(2)}, u32[]{:S(2)}) collective-permute-start(bf16[2,128,512]{2,1,0:T(8,128)(2,1)S(1)} %get-tuple-element.24), channel_id=1, source_target_pairs={{0,1},{1,0},{2,3},{3,2},{4,5},{5,4},{6,7},{7,6},{8,9},{9,8},{10,11... | collective-permute-start | bytes 786440 | tf_op jit(solution)/shard_map/ppermute | solution.py:332
  46.7 23.0 %collective-permute-start.15 = (bf16[2,128,512]{2,1,0:T(8,128)(2,1)S(1)}, bf16[2,128,512]{2,1,0:T(8,128)(2,1)S(1)}, u32[]{:S(2)}, u32[]{:S(2)}) collective-permute-start(bf16[2,128,512]{2,1,0:T(8,128)(2,1)S(1)} %get-tuple-element.25), channel_id=1, source_target_pairs={{0,2},{1,3},{2,0},{3,1},{4,6},{5,7},{6,4},{7,5},{8,10},{9,11},{10,... | collective-permute-start | bytes 786440 | tf_op jit(solution)/shard_map/ppermute | solution.py:332
  47.3 22.4 %collective-permute-start.16 = (bf16[2,128,512]{2,1,0:T(8,128)(2,1)S(1)}, bf16[2,128,512]{2,1,0:T(8,128)(2,1)S(1)}, u32[]{:S(2)}, u32[]{:S(2)}) collective-permute-start(bf16[2,128,512]{2,1,0:T(8,128)(2,1)S(1)} %get-tuple-element.26), channel_id=1, source_target_pairs={{0,3},{1,2},{2,1},{3,0},{4,7},{5,6},{6,5},{7,4},{8,11},{9,10},{10,... | collective-permute-start | bytes 786440 | tf_op jit(solution)/shard_map/ppermute | solution.py:332
  71.6 2.0 %collective-permute-start.25 = (bf16[4,4,128,128]{3,2,1,0:T(8,128)(2,1)S(1)}, bf16[4,4,128,128]{3,2,1,0:T(8,128)(2,1)S(1)}, u32[]{:S(2)}, u32[]{:S(2)}) collective-permute-start(bf16[4,4,128,128]{3,2,1,0:T(8,128)(2,1)S(1)} %get-tuple-element.29), channel_id=1, source_target_pairs={{0,4},{4,0},{8,12},{12,8},{16,20},{20,16},{24,28},{28,24},{1,5},{5... | collective-permute-start | bytes 1572872 | tf_op jit(solution)/shard_map/ppermute | solution.py:326
  73.8 6.4 %collective-permute-start.26 = (bf16[4,128,128]{2,1,0:T(8,128)(2,1)S(1)}, bf16[4,128,128]{2,1,0:T(8,128)(2,1)S(1)}, u32[]{:S(2)}, u32[]{:S(2)}) collective-permute-start(bf16[4,128,128]{2,1,0:T(8,128)(2,1)S(1)} %get-tuple-element.42), channel_id=1, source_target_pairs={{0,8},{4,12},{8,0},{12,4},{16,24},{20,28},{24,16},{28,20},{1,9},{5... | collective-permute-start | bytes 393224 | tf_op jit(solution)/shard_map/ppermute | solution.py:329
  74.5 8.8 %collective-permute-start.28 = (bf16[4,128,128]{2,1,0:T(8,128)(2,1)S(1)}, bf16[4,128,128]{2,1,0:T(8,128)(2,1)S(1)}, u32[]{:S(2)}, u32[]{:S(2)}) collective-permute-start(bf16[4,128,128]{2,1,0:T(8,128)(2,1)S(1)} %get-tuple-element.43), channel_id=1, source_target_pairs={{0,24},{4,28},{8,16},{12,20},{16,8},{20,12},{24,0},{28,4},{1,25},{... | collective-permute-start | bytes 393224 | tf_op jit(solution)/shard_map/ppermute | solution.py:329
  76.9 7.8 %collective-permute-start.27 = (bf16[4,128,128]{2,1,0:T(8,128)(2,1)S(1)}, bf16[4,128,128]{2,1,0:T(8,128)(2,1)S(1)}, u32[]{:S(2)}, u32[]{:S(2)}) collective-permute-start(bf16[4,128,128]{2,1,0:T(8,128)(2,1)S(1)} %get-tuple-element.44), channel_id=1, source_target_pairs={{0,16},{4,20},{8,24},{12,28},{16,0},{20,4},{24,8},{28,12},{1,17},{... | collective-permute-start | bytes 393224 | tf_op jit(solution)/shard_map/ppermute | solution.py:329
  77.3 33.5 %collective-permute-start.23 = (bf16[2,128,512]{2,1,0:T(8,128)(2,1)S(1)}, bf16[2,128,512]{2,1,0:T(8,128)(2,1)S(1)}, u32[]{:S(2)}, u32[]{:S(2)}) collective-permute-start(bf16[2,128,512]{2,1,0:T(8,128)(2,1)S(1)} %get-tuple-element.27.refs_1_), channel_id=1, source_target_pairs={{1,2},{2,1},{5,6},{6,5},{9,10},{10,9},{13,14},{14,13},{17,18},{18,... | collective-permute-start | bytes 786440 | tf_op jit(solution)/shard_map/ppermute | solution.py:340
  84.7 27.6 %collective-permute-start.41 = (bf16[4,128,128]{2,1,0:T(8,128)(2,1)S(1)}, bf16[4,128,128]{2,1,0:T(8,128)(2,1)S(1)}, u32[]{:S(2)}, u32[]{:S(2)}) collective-permute-start(bf16[4,128,128]{2,1,0:T(8,128)(2,1)S(1)} %fusion.4.refs_0_), channel_id=1, source_target_pairs={{0,3},{1,2},{2,1},{3,0},{4,7},{5,6},{6,5},{7,4},{8,11},{9,10},{10,... | collective-permute-start | bytes 393224 | tf_op jit(solution)/shard_map/ppermute | solution.py:332
  86.4 26.5 %collective-permute-start.40 = (bf16[4,128,128]{2,1,0:T(8,128)(2,1)S(1)}, bf16[4,128,128]{2,1,0:T(8,128)(2,1)S(1)}, u32[]{:S(2)}, u32[]{:S(2)}) collective-permute-start(bf16[4,128,128]{2,1,0:T(8,128)(2,1)S(1)} %fusion.4.refs_0_), channel_id=1, source_target_pairs={{0,2},{1,3},{2,0},{3,1},{4,6},{5,7},{6,4},{7,5},{8,10},{9,11},{10,... | collective-permute-start | bytes 393224 | tf_op jit(solution)/shard_map/ppermute | solution.py:332
  90.9 3.9 %collective-permute-start.49 = (bf16[128,128]{1,0:T(8,128)(2,1)S(1)}, bf16[128,128]{1,0:T(8,128)(2,1)S(1)}, u32[]{:S(2)}, u32[]{:S(2)}) collective-permute-start(bf16[128,128]{1,0:T(8,128)(2,1)S(1)} %get-tuple-element.34), channel_id=1, source_target_pairs={{0,1},{1,0},{2,3},{3,2},{4,5},{5,4},{6,7},{7,6},{8,9},{9,8},{10,11... | collective-permute-start | bytes 98312 | tf_op jit(solution)/shard_map/ppermute | solution.py:332
  91.2 19.6 %collective-permute-start.50 = (bf16[128,128]{1,0:T(8,128)(2,1)S(1)}, bf16[128,128]{1,0:T(8,128)(2,1)S(1)}, u32[]{:S(2)}, u32[]{:S(2)}) collective-permute-start(bf16[128,128]{1,0:T(8,128)(2,1)S(1)} %get-tuple-element.35), channel_id=1, source_target_pairs={{0,2},{1,3},{2,0},{3,1},{4,6},{5,7},{6,4},{7,5},{8,10},{9,11},{10,... | collective-permute-start | bytes 98312 | tf_op jit(solution)/shard_map/ppermute | solution.py:332
  94.8 23.8 %collective-permute-start.22 = (bf16[2,128,512]{2,1,0:T(8,128)(2,1)S(1)}, bf16[2,128,512]{2,1,0:T(8,128)(2,1)S(1)}, u32[]{:S(2)}, u32[]{:S(2)}) collective-permute-start(bf16[2,128,512]{2,1,0:T(8,128)(2,1)S(1)} %get-tuple-element.27.refs_1_), channel_id=1, source_target_pairs={{0,2},{1,3},{2,0},{3,1},{4,6},{5,7},{6,4},{7,5},{8,10},{9,11},{10,... | collective-permute-start | bytes 786440 | tf_op jit(solution)/shard_map/ppermute | solution.py:332
  110.8 6.7 %collective-permute-start.39 = (bf16[4,128,128]{2,1,0:T(8,128)(2,1)S(1)}, bf16[4,128,128]{2,1,0:T(8,128)(2,1)S(1)}, u32[]{:S(2)}, u32[]{:S(2)}) collective-permute-start(bf16[4,128,128]{2,1,0:T(8,128)(2,1)S(1)} %fusion.4.refs_0_), channel_id=1, source_target_pairs={{0,1},{1,0},{2,3},{3,2},{4,5},{5,4},{6,7},{7,6},{8,9},{9,8},{10,11... | collective-permute-start | bytes 393224 | tf_op jit(solution)/shard_map/ppermute | solution.py:332
  110.8 6.7 %collective-permute-start.34 = (bf16[4,128,128]{2,1,0:T(8,128)(2,1)S(1)}, bf16[4,128,128]{2,1,0:T(8,128)(2,1)S(1)}, u32[]{:S(2)}, u32[]{:S(2)}) collective-permute-start(bf16[4,128,128]{2,1,0:T(8,128)(2,1)S(1)} %fusion.4.refs_0_), channel_id=1, source_target_pairs={{0,24},{4,28},{8,16},{12,20},{16,8},{20,12},{24,0},{28,4},{1,25},{... | collective-permute-start | bytes 393224 | tf_op jit(solution)/shard_map/ppermute | solution.py:329
  112.4 5.7 %collective-permute-start.32 = (bf16[4,128,128]{2,1,0:T(8,128)(2,1)S(1)}, bf16[4,128,128]{2,1,0:T(8,128)(2,1)S(1)}, u32[]{:S(2)}, u32[]{:S(2)}) collective-permute-start(bf16[4,128,128]{2,1,0:T(8,128)(2,1)S(1)} %fusion.4.refs_0_), channel_id=1, source_target_pairs={{0,16},{4,20},{8,24},{12,28},{16,0},{20,4},{24,8},{28,12},{1,17},{... | collective-permute-start | bytes 393224 | tf_op jit(solution)/shard_map/ppermute | solution.py:329
  112.9 5.3 %collective-permute-start.30 = (bf16[4,128,128]{2,1,0:T(8,128)(2,1)S(1)}, bf16[4,128,128]{2,1,0:T(8,128)(2,1)S(1)}, u32[]{:S(2)}, u32[]{:S(2)}) collective-permute-start(bf16[4,128,128]{2,1,0:T(8,128)(2,1)S(1)} %fusion.4.refs_0_), channel_id=1, source_target_pairs={{0,8},{4,12},{8,0},{12,4},{16,24},{20,28},{24,16},{28,20},{1,9},{5... | collective-permute-start | bytes 393224 | tf_op jit(solution)/shard_map/ppermute | solution.py:329
  117.5 2.9 %collective-permute-start.29 = (bf16[4,128,128]{2,1,0:T(8,128)(2,1)S(1)}, bf16[4,128,128]{2,1,0:T(8,128)(2,1)S(1)}, u32[]{:S(2)}, u32[]{:S(2)}) collective-permute-start(bf16[4,128,128]{2,1,0:T(8,128)(2,1)S(1)} %fusion.4.refs_0_), channel_id=1, source_target_pairs={{0,4},{4,0},{8,12},{12,8},{16,20},{20,16},{24,28},{28,24},{1,5},{5... | collective-permute-start | bytes 393224 | tf_op jit(solution)/shard_map/ppermute | solution.py:326
  117.5 3.4 %collective-permute-start.35 = (bf16[4,128,128]{2,1,0:T(8,128)(2,1)S(1)}, bf16[4,128,128]{2,1,0:T(8,128)(2,1)S(1)}, u32[]{:S(2)}, u32[]{:S(2)}) collective-permute-start(bf16[4,128,128]{2,1,0:T(8,128)(2,1)S(1)} %collective-permute-done.34.refs_6_), channel_id=1, source_target_pairs={{0,4},{4,0},{8,12},{12,8},{16,20},{20,16},{24,28},{28,24},{1,5},{5... | collective-permute-start | bytes 393224 | tf_op jit(solution)/shard_map/ppermute | solution.py:326
  118.1 4.1 %collective-permute-start.33 = (bf16[4,128,128]{2,1,0:T(8,128)(2,1)S(1)}, bf16[4,128,128]{2,1,0:T(8,128)(2,1)S(1)}, u32[]{:S(2)}, u32[]{:S(2)}) collective-permute-start(bf16[4,128,128]{2,1,0:T(8,128)(2,1)S(1)} %collective-permute-done.32.refs_4_), channel_id=1, source_target_pairs={{0,4},{4,0},{8,12},{12,8},{16,20},{20,16},{24,28},{28,24},{1,5},{5... | collective-permute-start | bytes 393224 | tf_op jit(solution)/shard_map/ppermute | solution.py:326
  118.2 6.0 %collective-permute-start.31 = (bf16[4,128,128]{2,1,0:T(8,128)(2,1)S(1)}, bf16[4,128,128]{2,1,0:T(8,128)(2,1)S(1)}, u32[]{:S(2)}, u32[]{:S(2)}) collective-permute-start(bf16[4,128,128]{2,1,0:T(8,128)(2,1)S(1)} %collective-permute-done.30.refs_2_), channel_id=1, source_target_pairs={{0,4},{4,0},{8,12},{12,8},{16,20},{20,16},{24,28},{28,24},{1,5},{5... | collective-permute-start | bytes 393224 | tf_op jit(solution)/shard_map/ppermute | solution.py:326
  118.7 19.8 %collective-permute-start.47 = (bf16[3,4,128,128]{3,2,1,0:T(8,128)(2,1)S(1)}, bf16[3,4,128,128]{3,2,1,0:T(8,128)(2,1)S(1)}, u32[]{:S(2)}, u32[]{:S(2)}) collective-permute-start(bf16[3,4,128,128]{3,2,1,0:T(8,128)(2,1)S(1)} %pad_maximum_fusion.refs_8_), channel_id=1, source_target_pairs={{0,24},{4,28},{8,16},{12,20},{16,8},{20,12},{24,0},{28,4},{1,25},{... | collective-permute-start | bytes 1179656 | tf_op jit(solution)/shard_map/ppermute | solution.py:329
  120.4 18.8 %collective-permute-start.45 = (bf16[3,4,128,128]{3,2,1,0:T(8,128)(2,1)S(1)}, bf16[3,4,128,128]{3,2,1,0:T(8,128)(2,1)S(1)}, u32[]{:S(2)}, u32[]{:S(2)}) collective-permute-start(bf16[3,4,128,128]{3,2,1,0:T(8,128)(2,1)S(1)} %pad_maximum_fusion.refs_8_), channel_id=1, source_target_pairs={{0,16},{4,20},{8,24},{12,28},{16,0},{20,4},{24,8},{28,12},{1,17},{... | collective-permute-start | bytes 1179656 | tf_op jit(solution)/shard_map/ppermute | solution.py:329
  120.9 18.3 %collective-permute-start.43 = (bf16[3,4,128,128]{3,2,1,0:T(8,128)(2,1)S(1)}, bf16[3,4,128,128]{3,2,1,0:T(8,128)(2,1)S(1)}, u32[]{:S(2)}, u32[]{:S(2)}) collective-permute-start(bf16[3,4,128,128]{3,2,1,0:T(8,128)(2,1)S(1)} %pad_maximum_fusion.refs_8_), channel_id=1, source_target_pairs={{0,8},{4,12},{8,0},{12,4},{16,24},{20,28},{24,16},{28,20},{1,9},{5... | collective-permute-start | bytes 1179656 | tf_op jit(solution)/shard_map/ppermute | solution.py:329
  122.2 9.2 %collective-permute-start.21 = (bf16[2,128,512]{2,1,0:T(8,128)(2,1)S(1)}, bf16[2,128,512]{2,1,0:T(8,128)(2,1)S(1)}, u32[]{:S(2)}, u32[]{:S(2)}) collective-permute-start(bf16[2,128,512]{2,1,0:T(8,128)(2,1)S(1)} %get-tuple-element.27.refs_1_), channel_id=1, source_target_pairs={{0,1},{1,0},{2,3},{3,2},{4,5},{5,4},{6,7},{7,6},{8,9},{9,8},{10,11... | collective-permute-start | bytes 786440 | tf_op jit(solution)/shard_map/ppermute | solution.py:332
  124.3 14.2 %collective-permute-start.24 = (bf16[2,128,512]{2,1,0:T(8,128)(2,1)S(1)}, bf16[2,128,512]{2,1,0:T(8,128)(2,1)S(1)}, u32[]{:S(2)}, u32[]{:S(2)}) collective-permute-start(bf16[2,128,512]{2,1,0:T(8,128)(2,1)S(1)} %collective-permute-done.22.refs_3_), channel_id=1, source_target_pairs={{1,0},{2,3},{5,4},{6,7},{9,8},{10,11},{13,12},{14,15},{17,16},{18,... | collective-permute-start | bytes 786440 | tf_op jit(solution)/shard_map/ppermute | solution.py:341
  131.4 8.3 %collective-permute-start.38 = (bf16[128,512]{1,0:T(8,128)(2,1)S(1)}, bf16[128,512]{1,0:T(8,128)(2,1)S(1)}, u32[]{:S(2)}, u32[]{:S(2)}) collective-permute-start(bf16[128,512]{1,0:T(8,128)(2,1)S(1)} %shard_map.124.refs_6_), channel_id=1, source_target_pairs={{0,3},{1,2},{2,1},{3,0},{4,7},{5,6},{6,5},{7,4},{8,11},{9,10},{10,... | collective-permute-start | bytes 393224 | tf_op jit(solution)/shard_map/ppermute | solution.py:332
  138.4 21.6 %collective-permute-start.42 = (bf16[3,4,128,128]{3,2,1,0:T(8,128)(2,1)S(1)}, bf16[3,4,128,128]{3,2,1,0:T(8,128)(2,1)S(1)}, u32[]{:S(2)}, u32[]{:S(2)}) collective-permute-start(bf16[3,4,128,128]{3,2,1,0:T(8,128)(2,1)S(1)} %pad_maximum_fusion.refs_8_), channel_id=1, source_target_pairs={{0,4},{4,0},{8,12},{12,8},{16,20},{20,16},{24,28},{28,24},{1,5},{5... | collective-permute-start | bytes 1179656 | tf_op jit(solution)/shard_map/ppermute | solution.py:326
  138.5 21.6 %collective-permute-start.48 = (bf16[3,4,128,128]{3,2,1,0:T(8,128)(2,1)S(1)}, bf16[3,4,128,128]{3,2,1,0:T(8,128)(2,1)S(1)}, u32[]{:S(2)}, u32[]{:S(2)}) collective-permute-start(bf16[3,4,128,128]{3,2,1,0:T(8,128)(2,1)S(1)} %collective-permute-done.47.refs_14_), channel_id=1, source_target_pairs={{0,4},{4,0},{8,12},{12,8},{16,20},{20,16},{24,28},{28,24},{1,5},{5... | collective-permute-start | bytes 1179656 | tf_op jit(solution)/shard_map/ppermute | solution.py:326
  139.2 20.8 %collective-permute-start.46 = (bf16[3,4,128,128]{3,2,1,0:T(8,128)(2,1)S(1)}, bf16[3,4,128,128]{3,2,1,0:T(8,128)(2,1)S(1)}, u32[]{:S(2)}, u32[]{:S(2)}) collective-permute-start(bf16[3,4,128,128]{3,2,1,0:T(8,128)(2,1)S(1)} %collective-permute-done.45.refs_12_), channel_id=1, source_target_pairs={{0,4},{4,0},{8,12},{12,8},{16,20},{20,16},{24,28},{28,24},{1,5},{5... | collective-permute-start | bytes 1179656 | tf_op jit(solution)/shard_map/ppermute | solution.py:326
  139.3 20.8 %collective-permute-start.44 = (bf16[3,4,128,128]{3,2,1,0:T(8,128)(2,1)S(1)}, bf16[3,4,128,128]{3,2,1,0:T(8,128)(2,1)S(1)}, u32[]{:S(2)}, u32[]{:S(2)}) collective-permute-start(bf16[3,4,128,128]{3,2,1,0:T(8,128)(2,1)S(1)} %collective-permute-done.43.refs_10_), channel_id=1, source_target_pairs={{0,4},{4,0},{8,12},{12,8},{16,20},{20,16},{24,28},{28,24},{1,5},{5... | collective-permute-start | bytes 1179656 | tf_op jit(solution)/shard_map/ppermute | solution.py:326
  139.7 9.6 %collective-permute-start.37 = (bf16[128,512]{1,0:T(8,128)(2,1)S(1)}, bf16[128,512]{1,0:T(8,128)(2,1)S(1)}, u32[]{:S(2)}, u32[]{:S(2)}) collective-permute-start(bf16[128,512]{1,0:T(8,128)(2,1)S(1)} %shard_map.124.refs_6_), channel_id=1, source_target_pairs={{0,2},{1,3},{2,0},{3,1},{4,6},{5,7},{6,4},{7,5},{8,10},{9,11},{10,... | collective-permute-start | bytes 393224 | tf_op jit(solution)/shard_map/ppermute | solution.py:332
  149.4 5.0 %collective-permute-start.36 = (bf16[128,512]{1,0:T(8,128)(2,1)S(1)}, bf16[128,512]{1,0:T(8,128)(2,1)S(1)}, u32[]{:S(2)}, u32[]{:S(2)}) collective-permute-start(bf16[128,512]{1,0:T(8,128)(2,1)S(1)} %shard_map.124.refs_6_), channel_id=1, source_target_pairs={{0,1},{1,0},{2,3},{3,2},{4,5},{5,4},{6,7},{7,6},{8,9},{9,8},{10,11... | collective-permute-start | bytes 393224 | tf_op jit(solution)/shard_map/ppermute | solution.py:332
  154.3 5.7 %collective-permute-start.51 = (bf16[128,128]{1,0:T(8,128)(2,1)S(1)}, bf16[128,128]{1,0:T(8,128)(2,1)S(1)}, u32[]{:S(2)}, u32[]{:S(2)}) collective-permute-start(bf16[128,128]{1,0:T(8,128)(2,1)S(1)} %get-tuple-element.36), channel_id=1, source_target_pairs={{0,3},{1,2},{2,1},{3,0},{4,7},{5,6},{6,5},{7,4},{8,11},{9,10},{10,... | collective-permute-start | bytes 98312 | tf_op jit(solution)/shard_map/ppermute | solution.py:332

commit v2 on v1

--- a/solution.py
+++ b/solution.py
@@ -84,13 +84,14 @@
 def middle_kernel(
     owners, lists, counts, *refs, pieces, zs, nb, rows, edge, slots, blocks
 ):
-    parts = refs[:zs]
-    downs = refs[zs : 2 * zs + 1]
-    tout = refs[2 * zs + 1]
-    outs = refs[2 * zs + 2 :]
-    factors, hidden_out, keep, send, down_all = outs[0], outs[1 : 1 + zs], *outs[1 + zs : 4 + zs]
-    acc, hidden_t = outs[4 + zs :]
+    terms = len(refs) - zs - 10
+    parts = refs[:terms]
+    downs = refs[terms : terms + zs + 1]
+    tout = refs[terms + zs + 1]
+    outs = refs[terms + zs + 2 :]
+    hidden_own, plain, wide, keep, send, down_all, acc, hidden_t = outs
     d, z, owner = lax.axis_index("dp"), lax.axis_index("fsdp"), owners[0]
+    tok = tout.shape[0]
     own = owner == d
     for b in range(pieces * nb):
         term = tout[:, b * edge : (b + 1) * edge].astype(F32)
@@ -111,21 +112,28 @@
         lanes = slice(f * edge, (f + 1) * edge)
         g = parts[0][0, :, lanes].astype(F32)
         u = parts[0][1, :, lanes].astype(F32)
-        for s in range(1, zs):
-            g += parts[s][0, :, lanes].astype(F32)
-            u += parts[s][1, :, lanes].astype(F32)
+        for part in parts[1:]:
+            g += part[0, :, lanes].astype(F32)
+            u += part[1, :, lanes].astype(F32)
         sig = jax.nn.sigmoid(g)
         act = g * sig
         hidden = (act * u).astype(BF16)
-        factors[0, :, lanes] = (u * sig * (1.0 + g * (1.0 - sig))).astype(BF16)
-        factors[1, :, lanes] = act.astype(BF16)
+        slope = (u * sig * (1.0 + g * (1.0 - sig))).astype(BF16)
+        for message in (plain, wide):
+            message[:tok, lanes] = slope
+            message[tok : 2 * tok, lanes] = act.astype(BF16)
         hidden_t[lanes, :] = hidden.T
         prod = jnp.dot(hidden, down_all[f], preferred_element_type=F32)
         for k in range(slots):
             acc[lists[f, k]] += prod[:, k * edge : (k + 1) * edge]
         for s in range(zs):
             at = pl.multiple_of(f * edge + lax.bitwise_xor(z, s) * rows, rows)
-            hidden_out[s][f * rows : (f + 1) * rows, :] = hidden_t[pl.ds(at, rows), :]
+            cut = hidden_t[pl.ds(at, rows), :]
+            slot = slice(2 * tok + s % 2 * rows, 2 * tok + (s % 2 + 1) * rows)
+            if s < 2:
+                hidden_own[s, f * rows : (f + 1) * rows, :] = cut
+            else:
+                wide[slot, lanes] = cut
     for r in range(pieces):
         for j in range(nb):
             value = acc[lax.bitwise_xor(d, r) * nb + j]
@@ -152,26 +160,30 @@
 def down_grad_kernel(lists, counts, *refs, pieces, zs, nb, rows, edge, slots, blocks):
     own = refs[:pieces]
     far = refs[pieces : 2 * pieces]
-    hidden = refs[2 * pieces : 2 * pieces + zs]
-    out, eall, hid = refs[2 * pieces + zs :]
+    hidden_own, message = refs[2 * pieces : 2 * pieces + 2]
+    keep, send, eall, hid = refs[2 * pieces + 2 :]
     d = lax.axis_index("dp")
-    tok = hidden[0].shape[-1]
+    tok = hidden_own.shape[-1]
     for r in range(pieces):
         for j in range(nb):
             eall[r * nb + j, :tok, :] = own[r][j]
-            for s in range(1, zs):
-                eall[r * nb + j, s * tok : (s + 1) * tok, :] = far[r][s - 1, j]
-    for s in range(zs):
-        hid[:, s * tok : (s + 1) * tok] = hidden[s][...]
-    for f in range(blocks):
+            eall[r * nb + j, tok:, :] = far[r][j]
+    for f in range(blocks):
+        lanes = slice(f * edge, (f + 1) * edge)
+        for side in range(2):
+            dst = slice(side * rows, (side + 1) * rows)
+            hid[dst, :tok] = hidden_own[side, f * rows : (f + 1) * rows, :]
+            hid[dst, tok:] = message[2 * tok + side * rows : 2 * tok + (side + 1) * rows, lanes]
         count = counts[f]
         for k in range(slots):
             grad = jnp.dot(
-                hid[f * rows : (f + 1) * rows, :],
+                hid[...],
                 eall[relative_block(lists[f, k], d, nb)],
                 preferred_element_type=F32,
             )
-            out[f, k] = jnp.where(k < count, grad, jnp.zeros_like(grad)).astype(BF16)
+            grad = jnp.where(k < count, grad, jnp.zeros_like(grad))
+            keep[f, k] = grad[:rows]
+            send[f, k] = grad[rows:].astype(BF16)
 
 
 def up_grad_kernel(counts, *refs, zs, rows, edge, slots, blocks):
@@ -188,9 +200,10 @@
             dh = errors[s][:, lanes].astype(F32)
             at = slice(s * tok, (s + 1) * tok)
             for side in range(2):
-                factor = factors[s][side, :, lanes]
+                span = slice(side * tok, (side + 1) * tok)
+                factor = factors[s][span, lanes]
                 if s == zs - 1:
-                    factor = jnp.where(ends, factors[zs][side, :, lanes], factor)
+                    factor = jnp.where(ends, factors[zs][span, lanes], factor)
                 both[at, side * edge : (side + 1) * edge] = (dh * factor.astype(F32)).astype(BF16)
         grad = jnp.dot(gathered[f], both[...], preferred_element_type=F32)
         for k in range(slots):
@@ -331,15 +344,22 @@
     def shift(a, s):
         return lax.ppermute(a, "fsdp", [(i, i ^ s) for i in range(zs)])
 
-    def gather(a):
-        last = zs - 1
-        out = [a] + [shift(a, s) for s in range(1, last)]
-        if zs != 4:
-            straight = shift(a, last)
-            return out + [straight, straight]
-        out.append(lax.ppermute(a, "fsdp", [(1, 2), (2, 1)]))
-        out.append(lax.ppermute(out[2], "fsdp", [(1, 0), (2, 3)]))
-        return out
+    def move(a, pairs):
+        return lax.ppermute(a, "fsdp", pairs)
+
+    def gather(plain, wide):
+        side = shift(plain, 1)
+        cross = shift(wide, 2)
+        inner = move(plain, [(1, 2), (2, 1)])
+        return [side, cross, inner, move(cross, [(1, 0), (2, 3)])]
+
+    def collect(mine):
+        joined = move(mine[3], [(0, 1), (3, 2)])
+        cross = move(mine[2], [(0, 2), (3, 1)])
+        inner = move(mine[3], [(1, 2), (2, 1)])
+        pair = shift(mine[1], 1)
+        both = (mine[2].astype(F32) + joined.astype(F32)).astype(BF16)
+        return [mine[0], pair, cross, inner, move(both, [(2, 0), (1, 3)])]
 
     def spread(a):
         per_chip = [a] + [chip_swap(a, c) for c in range(1, chips)]
@@ -348,7 +368,7 @@
             out += [p, partner(p)]
         return out
 
-    downs = gather(down_blocks)
+    downs = [down_blocks] + gather(down_blocks, down_blocks)
 
     half = sds((chips, nb * edge, tok))
     kept, sent = call(functools.partial(turn_kernel, **dims), [half, half], [], 0, tin)
@@ -380,12 +400,12 @@
         up_blocks,
     )
     gathered = front[zs]
-    parts = [front[0]] + [shift(front[s], s) for s in range(1, zs)]
+    parts = collect(front[:zs])
 
     middle = call(
         functools.partial(middle_kernel, **dims, **more),
-        [part]
-        + [sds((blocks * rows, tok))] * zs
+        [sds((2, blocks * rows, tok)), sds((2 * tok, blocks * edge))]
+        + [sds((2 * tok + 2 * rows, blocks * edge))]
         + [sds((chips, nb, tok, edge), F32), sds((chips, nb, tok, edge)), sds((blocks, edge, slots * edge))],
         [pltpu.VMEM((row_blocks, tok, edge), F32), pltpu.VMEM((blocks * edge, tok), BF16)],
         3,
@@ -396,9 +416,8 @@
         *downs,
         tout,
     )
-    keep, send, down_all = middle[1 + zs :]
-    factors = gather(middle[0])
-    hidden = [middle[1]] + [shift(middle[1 + s], s) for s in range(1, zs)]
+    hidden_own, plain, wide, keep, send, down_all = middle
+    messages = gather(plain, wide)
 
     summed = keep + partner(send).astype(F32)
     total = summed[0]
@@ -406,9 +425,7 @@
         total = total + chip_swap(summed[c].astype(BF16), c).astype(F32)
     error = (total / zs).astype(BF16)
     near = spread(error)
-    arrived = [shift(error, s) for s in range(1, zs)]
-    packed = jnp.stack(arrived)
-    far = spread(packed)
+    far = spread(shift(error, 2))
 
     (hidden_grad,) = call(
         functools.partial(back_kernel, **dims, slots=slots, blocks=blocks),
@@ -421,17 +438,19 @@
     )
     grads = [hidden_grad] + [shift(hidden_grad, s) for s in range(1, zs)]
 
-    (down_grad,) = call(
+    kept, passed = call(
         functools.partial(down_grad_kernel, **dims, **more),
-        [sds(down_blocks.shape)],
-        [pltpu.VMEM((row_blocks, zs * tok, edge), BF16), pltpu.VMEM((blocks * rows, zs * tok), BF16)],
+        [sds(down_blocks.shape, F32), sds(down_blocks.shape)],
+        [pltpu.VMEM((row_blocks, 2 * tok, edge), BF16), pltpu.VMEM((2 * rows, 2 * tok), BF16)],
         2,
         output_lists,
         output_counts,
         *near,
         *far,
-        *hidden,
-    )
+        hidden_own,
+        messages[1],
+    )
+    down_grad = (kept + shift(passed, 1).astype(F32)).astype(BF16)
     gate_grad, up_grad = call(
         functools.partial(up_grad_kernel, edge=edge, **more),
         [sds(gate_blocks.shape)] * 2,
@@ -439,7 +458,8 @@
         1,
         input_counts,
         gathered,
-        *factors,
+        plain,
+        *messages,
         *grads,
     )
     return gate_grad, up_grad, down_grad
@@ -450,8 +470,8 @@
     rows = P("dp", "fsdp", None)
 
     def step(*args):
-        block_rows = args[3].shape[2]
-        if block_rows % 16:
+        block_rows, block_edge = args[3].shape[2:]
+        if mesh.shape["fsdp"] != 4 or block_rows % 16 or args[0].shape[1] != block_edge:
             return plain_shards(*args)
         return shards(*args)
 

time: 163 us -> 150 us (0.920)
  starting transfers between devices: 62.8 us -> 49.8 us
    ppermute x19 -> x13, starting transfers between devices: 37.3 us -> 17.9 us  [shift(): return lax.ppermute(a, 'fsdp', [(i, i ^ s) for i in range(zs)])]
    ppermute x19 -> x13, waiting for transfers between devices: 56.8 us -> 40.2 us  [shift(): return lax.ppermute(a, 'fsdp', [(i, i ^ s) for i in range(zs)])]
    ppermute x4 -> x8, waiting for transfers between devices: 12 us -> 22 us  [move(): return lax.ppermute(a, 'fsdp', pairs)]
    ppermute x15, waiting for transfers between devices: 15.1 us -> 22.4 us  [chip_swap(): return lax.ppermute(a, 'dp', [(i, i ^ 2 * c) for i in range(pieces)])]
    ppermute x4 -> x8, starting transfers between devices: 3.91 us -> 10.9 us  [move(): return lax.ppermute(a, 'fsdp', pairs)]
  transfers between devices with their start and end apart: 52 -> 50, of which waited for: 24 -> 22; matrix products, arithmetic and copies ran while one was open for 0% -> 0% of each run, Pallas kernels for 3% -> 4%
where the time goes in v2:
time: 150 us
  waiting for transfers between devices  87.5 us (58%)
  starting transfers between devices  49.8 us (33%)
  Pallas kernels  8.61 us (6%)
  between operations  1.61 us (1%)
    ppermute x13, waiting for transfers between devices, shift(): return lax.ppermute(a, 'fsdp', [(i, i ^ s) for i in range(zs)])  40.2 us
    ppermute x15, waiting for transfers between devices, chip_swap(): return lax.ppermute(a, 'dp', [(i, i ^ 2 * c) for i in range(pieces)])  22.4 us
    ppermute x8, waiting for transfers between devices, move(): return lax.ppermute(a, 'fsdp', pairs)  22 us
    ppermute x15, starting transfers between devices, chip_swap(): return lax.ppermute(a, 'dp', [(i, i ^ 2 * c) for i in range(pieces)])  18.6 us
    ppermute x13, starting transfers between devices, shift(): return lax.ppermute(a, 'fsdp', [(i, i ^ s) for i in range(zs)])  17.9 us
    ppermute x8, starting transfers between devices, move(): return lax.ppermute(a, 'fsdp', pairs)  10.9 us
    pallas_call x6, Pallas kernels, call(): pl.pallas_call(kernel, out_shape=tuple(outs), in_specs=[SM] * smem + [VM]...  8.61 us
  transfers between devices with their start and end apart: 50, of which 22 were waited for; matrix products, arithmetic and copies ran while one was open for 0% of the time, Pallas kernels for 4%

profile of v2, /device:TPU:0, one launch (start us, length us, event | category | flops | bytes accessed | tf_op | source)
XLA Modules:
  0.0 150.0 jit_solution(15831905990797479909)
XLA Ops:
  0.6 1.2 copy-done
  1.9 0.3 shard_map.121
  2.2 0.6 collective-permute-start
  3.4 0.9 collective-permute-done
  4.4 2.9 %collective-permute-start.3 = (bf16[512,128]{1,0:T(8,128)(2,1)S(1)}, bf16[512,128]{1,0:T(8,128)(2,1)S(1)}, u32[]{:S(2)}, u32[]{:S(2)}) collective-permute-start(bf16[512,128]{1,0:T(8,128)(2,1)S(1)} %get-tuple-element.39), channel_id=1, source_target_pairs={{0,8},{4,12},{8,0},{12,4},{16,24},{20,28},{24,16},{28,20},{1,9},{5... | collective-permute-start | bytes 393224 | tf_op jit(solution)/shard_map/ppermute | solution.py:342
  7.3 1.5 %collective-permute-start.2 = (bf16[512,128]{1,0:T(8,128)(2,1)S(1)}, bf16[512,128]{1,0:T(8,128)(2,1)S(1)}, u32[]{:S(2)}, u32[]{:S(2)}) collective-permute-start(bf16[512,128]{1,0:T(8,128)(2,1)S(1)} %get-tuple-element.40), channel_id=1, source_target_pairs={{0,16},{4,20},{8,24},{12,28},{16,0},{20,4},{24,8},{28,12},{1,17},{... | collective-permute-start | bytes 393224 | tf_op jit(solution)/shard_map/ppermute | solution.py:342
  8.8 2.4 %collective-permute-done.3 = bf16[512,128]{1,0:T(8,128)(2,1)S(1)} collective-permute-done((bf16[512,128]{1,0:T(8,128)(2,1)S(1)}, bf16[512,128]{1,0:T(8,128)(2,1)S(1)}, u32[]{:S(2)}, u32[]{:S(2)}) %collective-permute-start.3) | collective-permute-done | bytes 131104 | tf_op jit(solution)/shard_map/ppermute | solution.py:342
  11.2 4.1 %collective-permute-done.2 = bf16[512,128]{1,0:T(8,128)(2,1)S(1)} collective-permute-done((bf16[512,128]{1,0:T(8,128)(2,1)S(1)}, bf16[512,128]{1,0:T(8,128)(2,1)S(1)}, u32[]{:S(2)}, u32[]{:S(2)}) %collective-permute-start.2) | collective-permute-done | bytes 131104 | tf_op jit(solution)/shard_map/ppermute | solution.py:342
  15.4 3.7 %collective-permute-start.6 = (bf16[4,32,128]{2,1,0:T(8,128)(2,1)S(1)}, bf16[4,32,128]{2,1,0:T(8,128)(2,1)S(1)}, u32[]{:S(2)}, u32[]{:S(2)}) collective-permute-start(bf16[4,32,128]{2,1,0:T(8,128)(2,1)S(1)} %get-tuple-element.46), channel_id=1, source_target_pairs={{0,3},{1,2},{2,1},{3,0},{4,7},{5,6},{6,5},{7,4},{8,11},{9,10},{10,... | collective-permute-start | bytes 98312 | tf_op jit(solution)/shard_map/ppermute | solution.py:345
  19.1 0.8 collective-permute-start.4
  19.9 1.3 collective-permute-done.6
  21.2 2.7 %collective-permute-done.5 = bf16[4,32,128]{2,1,0:T(8,128)(2,1)S(1)} collective-permute-done((bf16[4,32,128]{2,1,0:T(8,128)(2,1)S(1)}, bf16[4,32,128]{2,1,0:T(8,128)(2,1)S(1)}, u32[]{:S(2)}, u32[]{:S(2)}) %collective-permute-start.5) | collective-permute-done | bytes 32800 | tf_op jit(solution)/shard_map/ppermute | solution.py:345
  24.0 1.6 %collective-permute-start.12 = (bf16[4,128,128]{2,1,0:T(8,128)(2,1)S(1)}, bf16[4,128,128]{2,1,0:T(8,128)(2,1)S(1)}, u32[]{:S(2)}, u32[]{:S(2)}) collective-permute-start(bf16[4,128,128]{2,1,0:T(8,128)(2,1)S(1)} %pad_maximum_fusion.refs_0_), channel_id=1, source_target_pairs={{0,24},{4,28},{8,16},{12,20},{16,8},{20,12},{24,0},{28,4},{1,25},{... | collective-permute-start | bytes 393224 | tf_op jit(solution)/shard_map/ppermute | solution.py:342
  25.5 1.2 collective-permute-start.10
  26.7 0.8 collective-permute-start.8
  27.5 2.5 %collective-permute-done.12.refs_6_ = bf16[4,128,128]{2,1,0:T(8,128)(2,1)S(1)} collective-permute-done((bf16[4,128,128]{2,1,0:T(8,128)(2,1)S(1)}, bf16[4,128,128]{2,1,0:T(8,128)(2,1)S(1)}, u32[]{:S(2)}, u32[]{:S(2)}) %collective-permute-start.12) | collective-permute-done | bytes 131104 | tf_op jit(solution)/shard_map/ppermute | solution.py:342
  30.0 1.3 collective-permute-done.10.refs_4_
  31.3 0.4 collective-permute-done.8.refs_2_
  31.8 2.0 %collective-permute-start.20 = (bf16[4,10,32,128]{3,2,1,0:T(8,128)(2,1)S(1)}, bf16[4,10,32,128]{3,2,1,0:T(8,128)(2,1)S(1)}, u32[]{:S(2)}, u32[]{:S(2)}) collective-permute-start(bf16[4,10,32,128]{3,2,1,0:T(8,128)(2,1)S(1)} %copy-done.2), channel_id=1, source_target_pairs={{0,2},{1,3},{2,0},{3,1},{4,6},{5,7},{6,4},{7,5},{8,10},{9,11},{10,... | collective-permute-start | bytes 983048 | tf_op jit(solution)/shard_map/ppermute | solution.py:345
  33.9 1.7 %shard_map.122 = (f32[2,128,512]{2,1,0:T(8,128)S(1)}, bf16[2,128,512]{2,1,0:T(8,128)(2,1)S(1)}, bf16[2,128,512]{2,1,0:T(8,128)(2,1)S(1)}, bf16[2,128,512]{2,1,0:T(8,128)(2,1)S(1)}, bf16[4,320,512]{2,1,0:T(8,128)(2,1)S(1)}) custom-call(s32[4,10]{1,0:T(4,128)S(1)} %copy-done.6, s32[4]{0:T(128)S(1)} %copy-done.8, ...), custom_call_target="tpu_custom_call" | custom-call | flops 134217728 | bytes 4325552 | tf_op jit(solution)/shard_map/pallas_call | solution.py:23
  35.6 1.9 %collective-permute-start.17 = (bf16[2,128,512]{2,1,0:T(8,128)(2,1)S(1)}, bf16[2,128,512]{2,1,0:T(8,128)(2,1)S(1)}, u32[]{:S(2)}, u32[]{:S(2)}) collective-permute-start(bf16[2,128,512]{2,1,0:T(8,128)(2,1)S(1)} %get-tuple-element.26), channel_id=1, source_target_pairs={{0,1},{3,2},{4,5},{7,6},{8,9},{11,10},{12,13},{15,14},{16,17},{19,... | collective-permute-start | bytes 786440 | tf_op jit(solution)/shard_map/ppermute | solution.py:348
  37.6 0.7 collective-permute-start.21
  38.3 10.8 %collective-permute-done.20.refs_7_ = bf16[4,10,32,128]{3,2,1,0:T(8,128)(2,1)S(1)} collective-permute-done((bf16[4,10,32,128]{3,2,1,0:T(8,128)(2,1)S(1)}, bf16[4,10,32,128]{3,2,1,0:T(8,128)(2,1)S(1)}, u32[]{:S(2)}, u32[]{:S(2)}) %collective-permute-start.20) | collective-permute-done | bytes 327712 | tf_op jit(solution)/shard_map/ppermute | solution.py:345
  49.2 1.3 collective-permute-start.22
  50.4 2.7 %collective-permute-start.14 = (bf16[2,128,512]{2,1,0:T(8,128)(2,1)S(1)}, bf16[2,128,512]{2,1,0:T(8,128)(2,1)S(1)}, u32[]{:S(2)}, u32[]{:S(2)}) collective-permute-start(bf16[2,128,512]{2,1,0:T(8,128)(2,1)S(1)} %get-tuple-element.24), channel_id=1, source_target_pairs={{0,1},{1,0},{2,3},{3,2},{4,5},{5,4},{6,7},{7,6},{8,9},{9,8},{10,11... | collective-permute-start | bytes 786440 | tf_op jit(solution)/shard_map/ppermute | solution.py:345
  53.2 3.1 %collective-permute-start.15 = (bf16[2,128,512]{2,1,0:T(8,128)(2,1)S(1)}, bf16[2,128,512]{2,1,0:T(8,128)(2,1)S(1)}, u32[]{:S(2)}, u32[]{:S(2)}) collective-permute-start(bf16[2,128,512]{2,1,0:T(8,128)(2,1)S(1)} %get-tuple-element.25), channel_id=1, source_target_pairs={{0,2},{3,1},{4,6},{7,5},{8,10},{11,9},{12,14},{15,13},{16,18},{19,... | collective-permute-start | bytes 786440 | tf_op jit(solution)/shard_map/ppermute | solution.py:348
  56.4 0.7 collective-permute-start.16
  57.1 1.3 collective-permute-start.18
  58.4 3.2 %collective-permute-done.22.refs_9_ = bf16[4,10,32,128]{3,2,1,0:T(8,128)(2,1)S(1)} collective-permute-done((bf16[4,10,32,128]{3,2,1,0:T(8,128)(2,1)S(1)}, bf16[4,10,32,128]{3,2,1,0:T(8,128)(2,1)S(1)}, u32[]{:S(2)}, u32[]{:S(2)}) %collective-permute-start.22) | collective-permute-done | bytes 327712 | tf_op jit(solution)/shard_map/ppermute | solution.py:348
  61.6 5.0 %collective-permute-done.14.refs_1_ = bf16[2,128,512]{2,1,0:T(8,128)(2,1)S(1)} collective-permute-done((bf16[2,128,512]{2,1,0:T(8,128)(2,1)S(1)}, bf16[2,128,512]{2,1,0:T(8,128)(2,1)S(1)}, u32[]{:S(2)}, u32[]{:S(2)}) %collective-permute-start.14) | collective-permute-done | bytes 262176 | tf_op jit(solution)/shard_map/ppermute | solution.py:345
  66.6 9.4 %collective-permute-done.18.refs_4_ = bf16[2,128,512]{2,1,0:T(8,128)(2,1)S(1)} collective-permute-done((bf16[2,128,512]{2,1,0:T(8,128)(2,1)S(1)}, bf16[2,128,512]{2,1,0:T(8,128)(2,1)S(1)}, u32[]{:S(2)}, u32[]{:S(2)}) %collective-permute-start.18) | collective-permute-done | bytes 262176 | tf_op jit(solution)/shard_map/ppermute | solution.py:348
  76.0 1.9 %shard_map.123 = (bf16[2,128,128]{2,1,0:T(8,128)(2,1)S(1)}, bf16[256,512]{1,0:T(8,128)(2,1)S(1)}, bf16[320,512]{1,0:T(8,128)(2,1)S(1)}, f32[4,4,128,128]{3,2,1,0...) custom-call(s32[1]{0:T(128)} %copy.15.owners, s32[4,10]{1,0:T(4,128)S(1)} %copy-done.5, ...), custom_call_target="tpu_custom_call" | custom-call | flops 134217728 | bytes 7798964 | tf_op jit(solution)/shard_map/pallas_call | solution.py:23
  78.0 1.9 %collective-permute-done.27 = bf16[4,4,128,128]{3,2,1,0:T(8,128)(2,1)S(1)} collective-permute-done((bf16[4,4,128,128]{3,2,1,0:T(8,128)(2,1)S(1)}, bf16[4,4,128,128]{3,2,1,0:T(8,128)(2,1)S(1)}, u32[]{:S(2)}, u32[]{:S(2)}) %collective-permute-start.27) | collective-permute-done | bytes 524320 | tf_op jit(solution)/shard_map/ppermute | solution.py:339
  80.2 0.5 collective-permute-start.28
  80.7 1.8 %collective-permute-start.30 = (bf16[4,128,128]{2,1,0:T(8,128)(2,1)S(1)}, bf16[4,128,128]{2,1,0:T(8,128)(2,1)S(1)}, u32[]{:S(2)}, u32[]{:S(2)}) collective-permute-start(bf16[4,128,128]{2,1,0:T(8,128)(2,1)S(1)} %get-tuple-element.43), channel_id=1, source_target_pairs={{0,24},{4,28},{8,16},{12,20},{16,8},{20,12},{24,0},{28,4},{1,25},{... | collective-permute-start | bytes 393224 | tf_op jit(solution)/shard_map/ppermute | solution.py:342
  82.4 1.3 collective-permute-start.29
  83.7 2.9 %collective-permute-done.28 = bf16[4,128,128]{2,1,0:T(8,128)(2,1)S(1)} collective-permute-done((bf16[4,128,128]{2,1,0:T(8,128)(2,1)S(1)}, bf16[4,128,128]{2,1,0:T(8,128)(2,1)S(1)}, u32[]{:S(2)}, u32[]{:S(2)}) %collective-permute-start.28) | collective-permute-done | bytes 131104 | tf_op jit(solution)/shard_map/ppermute | solution.py:342
  86.6 2.3 %collective-permute-done.30 = bf16[4,128,128]{2,1,0:T(8,128)(2,1)S(1)} collective-permute-done((bf16[4,128,128]{2,1,0:T(8,128)(2,1)S(1)}, bf16[4,128,128]{2,1,0:T(8,128)(2,1)S(1)}, u32[]{:S(2)}, u32[]{:S(2)}) %collective-permute-start.30) | collective-permute-done | bytes 131104 | tf_op jit(solution)/shard_map/ppermute | solution.py:342
  88.9 1.4 collective-permute-done.29
  90.5 1.5 collective-permute-start.36
  92.0 1.7 %collective-permute-start.34 = (bf16[4,128,128]{2,1,0:T(8,128)(2,1)S(1)}, bf16[4,128,128]{2,1,0:T(8,128)(2,1)S(1)}, u32[]{:S(2)}, u32[]{:S(2)}) collective-permute-start(bf16[4,128,128]{2,1,0:T(8,128)(2,1)S(1)} %fusion.4.refs_0_), channel_id=1, source_target_pairs={{0,16},{4,20},{8,24},{12,28},{16,0},{20,4},{24,8},{28,12},{1,17},{... | collective-permute-start | bytes 393224 | tf_op jit(solution)/shard_map/ppermute | solution.py:342
  93.7 0.4 collective-permute-start.32
  94.1 8.7 %collective-permute-done.24.refs_3_.refs_17_ = bf16[320,512]{1,0:T(8,128)(2,1)S(1)} collective-permute-done((bf16[320,512]{1,0:T(8,128)(2,1)S(1)}, bf16[320,512]{1,0:T(8,128)(2,1)S(1)}, u32[]{:S(2)}, u32[]{:S(2)}) %collective-permute-start.24) | collective-permute-done | bytes 327712 | tf_op jit(solution)/shard_map/ppermute | solution.py:345
  102.8 2.7 %collective-permute-done.41.refs_8_ = bf16[4,128,128]{2,1,0:T(8,128)(2,1)S(1)} collective-permute-done((bf16[4,128,128]{2,1,0:T(8,128)(2,1)S(1)}, bf16[4,128,128]{2,1,0:T(8,128)(2,1)S(1)}, u32[]{:S(2)}, u32[]{:S(2)}) %collective-permute-start.41) | collective-permute-done | bytes 131104 | tf_op jit(solution)/shard_map/ppermute | solution.py:345
  105.5 1.9 %collective-permute-start.47 = (bf16[4,128,128]{2,1,0:T(8,128)(2,1)S(1)}, bf16[4,128,128]{2,1,0:T(8,128)(2,1)S(1)}, u32[]{:S(2)}, u32[]{:S(2)}) collective-permute-start(bf16[4,128,128]{2,1,0:T(8,128)(2,1)S(1)} %collective-permute-done.41.refs_8_), channel_id=1, source_target_pairs={{0,24},{4,28},{8,16},{12,20},{16,8},{20,12},{24,0},{28,4},{1,25},{... | collective-permute-start | bytes 393224 | tf_op jit(solution)/shard_map/ppermute | solution.py:342
  107.4 0.3 collective-permute-start.45
  107.7 1.3 collective-permute-start.43
  109.0 0.5 collective-permute-start.37
  109.5 3.2 %collective-permute-done.47.refs_14_ = bf16[4,128,128]{2,1,0:T(8,128)(2,1)S(1)} collective-permute-done((bf16[4,128,128]{2,1,0:T(8,128)(2,1)S(1)}, bf16[4,128,128]{2,1,0:T(8,128)(2,1)S(1)}, u32[]{:S(2)}, u32[]{:S(2)}) %collective-permute-start.47) | collective-permute-done | bytes 131104 | tf_op jit(solution)/shard_map/ppermute | solution.py:342
  112.8 1.9 %collective-permute-done.45.refs_12_ = bf16[4,128,128]{2,1,0:T(8,128)(2,1)S(1)} collective-permute-done((bf16[4,128,128]{2,1,0:T(8,128)(2,1)S(1)}, bf16[4,128,128]{2,1,0:T(8,128)(2,1)S(1)}, u32[]{:S(2)}, u32[]{:S(2)}) %collective-permute-start.45) | collective-permute-done | bytes 131104 | tf_op jit(solution)/shard_map/ppermute | solution.py:342
  114.7 0.5 collective-permute-start.48
  115.2 0.4 collective-permute-start.44
  115.7 0.7 collective-permute-start.25
  116.4 1.4 collective-permute-start.23
  117.8 1.3 collective-permute-start.26
  119.1 1.3 shard_map.126
  120.4 2.7 %collective-permute-start.49 = (bf16[4,10,32,128]{3,2,1,0:T(8,128)(2,1)S(1)}, bf16[4,10,32,128]{3,2,1,0:T(8,128)(2,1)S(1)}, u32[]{:S(2)}, u32[]{:S(2)}) collective-permute-start(bf16[4,10,32,128]{3,2,1,0:T(8,128)(2,1)S(1)} %get-tuple-element.36), channel_id=1, source_target_pairs={{0,1},{1,0},{2,3},{3,2},{4,5},{5,4},{6,7},{7,6},{8,9},{9,8},{10,11... | collective-permute-start | bytes 983048 | tf_op jit(solution)/shard_map/ppermute | solution.py:345
  123.2 1.3 shard_map.124.refs_6_
  124.4 1.9 %collective-permute-start.40 = (bf16[128,512]{1,0:T(8,128)(2,1)S(1)}, bf16[128,512]{1,0:T(8,128)(2,1)S(1)}, u32[]{:S(2)}, u32[]{:S(2)}) collective-permute-start(bf16[128,512]{1,0:T(8,128)(2,1)S(1)} %shard_map.124.refs_6_), channel_id=1, source_target_pairs={{0,3},{1,2},{2,1},{3,0},{4,7},{5,6},{6,5},{7,4},{8,11},{9,10},{10,... | collective-permute-start | bytes 393224 | tf_op jit(solution)/shard_map/ppermute | solution.py:345
  126.3 2.6 %collective-permute-start.38 = (bf16[128,512]{1,0:T(8,128)(2,1)S(1)}, bf16[128,512]{1,0:T(8,128)(2,1)S(1)}, u32[]{:S(2)}, u32[]{:S(2)}) collective-permute-start(bf16[128,512]{1,0:T(8,128)(2,1)S(1)} %shard_map.124.refs_6_), channel_id=1, source_target_pairs={{0,1},{1,0},{2,3},{3,2},{4,5},{5,4},{6,7},{7,6},{8,9},{9,8},{10,11... | collective-permute-start | bytes 393224 | tf_op jit(solution)/shard_map/ppermute | solution.py:345
  128.9 9.4 %collective-permute-done.26.refs_5_ = bf16[320,512]{1,0:T(8,128)(2,1)S(1)} collective-permute-done((bf16[320,512]{1,0:T(8,128)(2,1)S(1)}, bf16[320,512]{1,0:T(8,128)(2,1)S(1)}, u32[]{:S(2)}, u32[]{:S(2)}) %collective-permute-start.26) | collective-permute-done | bytes 327712 | tf_op jit(solution)/shard_map/ppermute | solution.py:348
  138.3 8.9 %collective-permute-done.38.refs_7_ = bf16[128,512]{1,0:T(8,128)(2,1)S(1)} collective-permute-done((bf16[128,512]{1,0:T(8,128)(2,1)S(1)}, bf16[128,512]{1,0:T(8,128)(2,1)S(1)}, u32[]{:S(2)}, u32[]{:S(2)}) %collective-permute-start.38) | collective-permute-done | bytes 131104 | tf_op jit(solution)/shard_map/ppermute | solution.py:345
  147.2 2.0 %shard_map.125 = (bf16[4,10,32,128]{3,2,1,0:T(8,128)(2,1)}, bf16[4,10,32,128]{3,2,1,0:T(8,128)(2,1)}) custom-call(s32[4]{0:T(128)S(1)} %copy-done.8, bf16[4,320,512]{2,1,0:T(8,128)(2,1)S(1)} %get-tuple-element.22.refs_0_, bf16[256,512]{1,0:T(8,128)(2,1)S(1)} %get-tuple-element.27.refs_1_, bf16[256,512]{1,0:T(8,128)(2,1)S(1)} %collective-permute-done.23.refs_2_, ...), custom_call_target="tpu_custom_call" | custom-call | flops 134217728 | bytes 3932176 | tf_op jit(solution)/shard_map/pallas_call | solution.py:23
  149.2 0.8 add_convert_fusion
  (69 shorter events, 1.1 us)
Async XLA Ops:
  0.6 1.2 copy-start
  2.2 2.1 %collective-permute-start = (bf16[4,512,128]{2,1,0:T(8,128)(2,1)S(1)}, bf16[4,512,128]{2,1,0:T(8,128)(2,1)S(1)}, u32[]{:S(2)}, u32[]{:S(2)}) collective-permute-start(bf16[4,512,128]{2,1,0:T(8,128)(2,1)S(1)} %get-tuple-element.21), channel_id=1, source_target_pairs={{0,4},{4,0},{8,12},{12,8},{16,20},{20,16},{24,28},{28,24},{1,5},{5... | collective-permute-start | bytes 1572872 | tf_op jit(solution)/shard_map/ppermute | solution.py:339
  4.3 27.5 %copy-start.2 = (bf16[4,10,32,128]{3,2,1,0:T(8,128)(2,1)S(1)}, bf16[4,10,32,128]{3,2,1,0:T(8,128)(2,1)}, u32[]{:S(2)}) copy-start(bf16[4,10,32,128]{3,2,1,0:T(8,128)(2,1)} %refs_5_.1) | copy-start | bytes 983044
  4.3 29.6 %copy-start.3 = (bf16[4,10,32,128]{3,2,1,0:T(8,128)(2,1)S(1)}, bf16[4,10,32,128]{3,2,1,0:T(8,128)(2,1)}, u32[]{:S(2)}) copy-start(bf16[4,10,32,128]{3,2,1,0:T(8,128)(2,1)} %refs_8_.1) | copy-start | bytes 983044
  4.3 29.6 %copy-start.4 = (bf16[4,10,32,128]{3,2,1,0:T(8,128)(2,1)S(1)}, bf16[4,10,32,128]{3,2,1,0:T(8,128)(2,1)}, u32[]{:S(2)}) copy-start(bf16[4,10,32,128]{3,2,1,0:T(8,128)(2,1)} %refs_9_.1) | copy-start | bytes 983044
  4.3 29.6 %copy-start.6 = (s32[4,10]{1,0:T(4,128)S(1)}, s32[4,10]{1,0:T(4,128)}, u32[]{:S(2)}) copy-start(s32[4,10]{1,0:T(4,128)} %lists.4) | copy-start | bytes 484
  4.3 29.6 %copy-start.8 = (s32[4]{0:T(128)S(1)}, s32[4]{0:T(128)}, u32[]{:S(2)}) copy-start(s32[4]{0:T(128)} %counts.6) | copy-start | bytes 52
  4.4 6.9 %collective-permute-start.3 = (bf16[512,128]{1,0:T(8,128)(2,1)S(1)}, bf16[512,128]{1,0:T(8,128)(2,1)S(1)}, u32[]{:S(2)}, u32[]{:S(2)}) collective-permute-start(bf16[512,128]{1,0:T(8,128)(2,1)S(1)} %get-tuple-element.39), channel_id=1, source_target_pairs={{0,8},{4,12},{8,0},{12,4},{16,24},{20,28},{24,16},{28,20},{1,9},{5... | collective-permute-start | bytes 393224 | tf_op jit(solution)/shard_map/ppermute | solution.py:342
  7.3 8.1 %collective-permute-start.2 = (bf16[512,128]{1,0:T(8,128)(2,1)S(1)}, bf16[512,128]{1,0:T(8,128)(2,1)S(1)}, u32[]{:S(2)}, u32[]{:S(2)}) collective-permute-start(bf16[512,128]{1,0:T(8,128)(2,1)S(1)} %get-tuple-element.40), channel_id=1, source_target_pairs={{0,16},{4,20},{8,24},{12,28},{16,0},{20,4},{24,8},{28,12},{1,17},{... | collective-permute-start | bytes 393224 | tf_op jit(solution)/shard_map/ppermute | solution.py:342
  8.8 6.5 %collective-permute-start.1 = (bf16[512,128]{1,0:T(8,128)(2,1)S(1)}, bf16[512,128]{1,0:T(8,128)(2,1)S(1)}, u32[]{:S(2)}, u32[]{:S(2)}) collective-permute-start(bf16[512,128]{1,0:T(8,128)(2,1)S(1)} %get-tuple-element.41), channel_id=1, source_target_pairs={{0,24},{4,28},{8,16},{12,20},{16,8},{20,12},{24,0},{28,4},{1,25},{... | collective-permute-start | bytes 393224 | tf_op jit(solution)/shard_map/ppermute | solution.py:342
  15.4 5.8 %collective-permute-start.6 = (bf16[4,32,128]{2,1,0:T(8,128)(2,1)S(1)}, bf16[4,32,128]{2,1,0:T(8,128)(2,1)S(1)}, u32[]{:S(2)}, u32[]{:S(2)}) collective-permute-start(bf16[4,32,128]{2,1,0:T(8,128)(2,1)S(1)} %get-tuple-element.46), channel_id=1, source_target_pairs={{0,3},{1,2},{2,1},{3,0},{4,7},{5,6},{6,5},{7,4},{8,11},{9,10},{10,... | collective-permute-start | bytes 98312 | tf_op jit(solution)/shard_map/ppermute | solution.py:345
  19.1 4.8 %collective-permute-start.5 = (bf16[4,32,128]{2,1,0:T(8,128)(2,1)S(1)}, bf16[4,32,128]{2,1,0:T(8,128)(2,1)S(1)}, u32[]{:S(2)}, u32[]{:S(2)}) collective-permute-start(bf16[4,32,128]{2,1,0:T(8,128)(2,1)S(1)} %get-tuple-element.47), channel_id=1, source_target_pairs={{0,2},{1,3},{2,0},{3,1},{4,6},{5,7},{6,4},{7,5},{8,10},{9,11},{10,... | collective-permute-start | bytes 98312 | tf_op jit(solution)/shard_map/ppermute | solution.py:345
  19.1 4.8 %collective-permute-start.4 = (bf16[4,32,128]{2,1,0:T(8,128)(2,1)S(1)}, bf16[4,32,128]{2,1,0:T(8,128)(2,1)S(1)}, u32[]{:S(2)}, u32[]{:S(2)}) collective-permute-start(bf16[4,32,128]{2,1,0:T(8,128)(2,1)S(1)} %get-tuple-element.48), channel_id=1, source_target_pairs={{0,1},{1,0},{2,3},{3,2},{4,5},{5,4},{6,7},{7,6},{8,9},{9,8},{10,11... | collective-permute-start | bytes 98312 | tf_op jit(solution)/shard_map/ppermute | solution.py:345
  23.9 52.1 %copy-start.1 = (bf16[1,128,4096]{2,1,0:T(8,128)(2,1)S(1)}, bf16[1,128,4096]{2,1,0:T(8,128)(2,1)}, u32[]{:S(2)}) copy-start(bf16[1,128,4096]{2,1,0:T(8,128)(2,1)} %param.11) | copy-start | bytes 3145732
  23.9 52.1 %copy-start.5 = (s32[4,10]{1,0:T(4,128)S(1)}, s32[4,10]{1,0:T(4,128)}, u32[]{:S(2)}) copy-start(s32[4,10]{1,0:T(4,128)} %lists.7) | copy-start | bytes 484
  23.9 52.1 %copy-start.7 = (s32[4]{0:T(128)S(1)}, s32[4]{0:T(128)}, u32[]{:S(2)}) copy-start(s32[4]{0:T(128)} %counts.7) | copy-start | bytes 52
  24.0 6.0 %collective-permute-start.12 = (bf16[4,128,128]{2,1,0:T(8,128)(2,1)S(1)}, bf16[4,128,128]{2,1,0:T(8,128)(2,1)S(1)}, u32[]{:S(2)}, u32[]{:S(2)}) collective-permute-start(bf16[4,128,128]{2,1,0:T(8,128)(2,1)S(1)} %pad_maximum_fusion.refs_0_), channel_id=1, source_target_pairs={{0,24},{4,28},{8,16},{12,20},{16,8},{20,12},{24,0},{28,4},{1,25},{... | collective-permute-start | bytes 393224 | tf_op jit(solution)/shard_map/ppermute | solution.py:342
  25.5 5.8 %collective-permute-start.10 = (bf16[4,128,128]{2,1,0:T(8,128)(2,1)S(1)}, bf16[4,128,128]{2,1,0:T(8,128)(2,1)S(1)}, u32[]{:S(2)}, u32[]{:S(2)}) collective-permute-start(bf16[4,128,128]{2,1,0:T(8,128)(2,1)S(1)} %pad_maximum_fusion.refs_0_), channel_id=1, source_target_pairs={{0,16},{4,20},{8,24},{12,28},{16,0},{20,4},{24,8},{28,12},{1,17},{... | collective-permute-start | bytes 393224 | tf_op jit(solution)/shard_map/ppermute | solution.py:342
  26.7 5.0 %collective-permute-start.8 = (bf16[4,128,128]{2,1,0:T(8,128)(2,1)S(1)}, bf16[4,128,128]{2,1,0:T(8,128)(2,1)S(1)}, u32[]{:S(2)}, u32[]{:S(2)}) collective-permute-start(bf16[4,128,128]{2,1,0:T(8,128)(2,1)S(1)} %pad_maximum_fusion.refs_0_), channel_id=1, source_target_pairs={{0,8},{4,12},{8,0},{12,4},{16,24},{20,28},{24,16},{28,20},{1,9},{5... | collective-permute-start | bytes 393224 | tf_op jit(solution)/shard_map/ppermute | solution.py:342
  27.5 6.3 %collective-permute-start.7 = (bf16[4,128,128]{2,1,0:T(8,128)(2,1)S(1)}, bf16[4,128,128]{2,1,0:T(8,128)(2,1)S(1)}, u32[]{:S(2)}, u32[]{:S(2)}) collective-permute-start(bf16[4,128,128]{2,1,0:T(8,128)(2,1)S(1)} %pad_maximum_fusion.refs_0_), channel_id=1, source_target_pairs={{0,4},{4,0},{8,12},{12,8},{16,20},{20,16},{24,28},{28,24},{1,5},{5... | collective-permute-start | bytes 393224 | tf_op jit(solution)/shard_map/ppermute | solution.py:339
  30.0 3.9 %collective-permute-start.13 = (bf16[4,128,128]{2,1,0:T(8,128)(2,1)S(1)}, bf16[4,128,128]{2,1,0:T(8,128)(2,1)S(1)}, u32[]{:S(2)}, u32[]{:S(2)}) collective-permute-start(bf16[4,128,128]{2,1,0:T(8,128)(2,1)S(1)} %collective-permute-done.12.refs_6_), channel_id=1, source_target_pairs={{0,4},{4,0},{8,12},{12,8},{16,20},{20,16},{24,28},{28,24},{1,5},{5... | collective-permute-start | bytes 393224 | tf_op jit(solution)/shard_map/ppermute | solution.py:339
  31.3 2.5 %collective-permute-start.11 = (bf16[4,128,128]{2,1,0:T(8,128)(2,1)S(1)}, bf16[4,128,128]{2,1,0:T(8,128)(2,1)S(1)}, u32[]{:S(2)}, u32[]{:S(2)}) collective-permute-start(bf16[4,128,128]{2,1,0:T(8,128)(2,1)S(1)} %collective-permute-done.10.refs_4_), channel_id=1, source_target_pairs={{0,4},{4,0},{8,12},{12,8},{16,20},{20,16},{24,28},{28,24},{1,5},{5... | collective-permute-start | bytes 393224 | tf_op jit(solution)/shard_map/ppermute | solution.py:339
  31.7 2.2 %collective-permute-start.9 = (bf16[4,128,128]{2,1,0:T(8,128)(2,1)S(1)}, bf16[4,128,128]{2,1,0:T(8,128)(2,1)S(1)}, u32[]{:S(2)}, u32[]{:S(2)}) collective-permute-start(bf16[4,128,128]{2,1,0:T(8,128)(2,1)S(1)} %collective-permute-done.8.refs_2_), channel_id=1, source_target_pairs={{0,4},{4,0},{8,12},{12,8},{16,20},{20,16},{24,28},{28,24},{1,5},{5... | collective-permute-start | bytes 393224 | tf_op jit(solution)/shard_map/ppermute | solution.py:339
  31.8 17.3 %collective-permute-start.20 = (bf16[4,10,32,128]{3,2,1,0:T(8,128)(2,1)S(1)}, bf16[4,10,32,128]{3,2,1,0:T(8,128)(2,1)S(1)}, u32[]{:S(2)}, u32[]{:S(2)}) collective-permute-start(bf16[4,10,32,128]{3,2,1,0:T(8,128)(2,1)S(1)} %copy-done.2), channel_id=1, source_target_pairs={{0,2},{1,3},{2,0},{3,1},{4,6},{5,7},{6,4},{7,5},{8,10},{9,11},{10,... | collective-permute-start | bytes 983048 | tf_op jit(solution)/shard_map/ppermute | solution.py:345
  35.6 17.5 %collective-permute-start.17 = (bf16[2,128,512]{2,1,0:T(8,128)(2,1)S(1)}, bf16[2,128,512]{2,1,0:T(8,128)(2,1)S(1)}, u32[]{:S(2)}, u32[]{:S(2)}) collective-permute-start(bf16[2,128,512]{2,1,0:T(8,128)(2,1)S(1)} %get-tuple-element.26), channel_id=1, source_target_pairs={{0,1},{3,2},{4,5},{7,6},{8,9},{11,10},{12,13},{15,14},{16,17},{19,... | collective-permute-start | bytes 786440 | tf_op jit(solution)/shard_map/ppermute | solution.py:348
  37.6 18.8 %collective-permute-start.19 = (bf16[4,10,32,128]{3,2,1,0:T(8,128)(2,1)S(1)}, bf16[4,10,32,128]{3,2,1,0:T(8,128)(2,1)S(1)}, u32[]{:S(2)}, u32[]{:S(2)}) collective-permute-start(bf16[4,10,32,128]{3,2,1,0:T(8,128)(2,1)S(1)} %copy-done.2), channel_id=1, source_target_pairs={{0,1},{1,0},{2,3},{3,2},{4,5},{5,4},{6,7},{7,6},{8,9},{9,8},{10,11... | collective-permute-start | bytes 983048 | tf_op jit(solution)/shard_map/ppermute | solution.py:345
  37.6 19.5 %collective-permute-start.21 = (bf16[4,10,32,128]{3,2,1,0:T(8,128)(2,1)S(1)}, bf16[4,10,32,128]{3,2,1,0:T(8,128)(2,1)S(1)}, u32[]{:S(2)}, u32[]{:S(2)}) collective-permute-start(bf16[4,10,32,128]{3,2,1,0:T(8,128)(2,1)S(1)} %copy-done.2), channel_id=1, source_target_pairs={{1,2},{2,1},{5,6},{6,5},{9,10},{10,9},{13,14},{14,13},{17,18},{18,... | collective-permute-start | bytes 983048 | tf_op jit(solution)/shard_map/ppermute | solution.py:348
  49.2 12.5 %collective-permute-start.22 = (bf16[4,10,32,128]{3,2,1,0:T(8,128)(2,1)S(1)}, bf16[4,10,32,128]{3,2,1,0:T(8,128)(2,1)S(1)}, u32[]{:S(2)}, u32[]{:S(2)}) collective-permute-start(bf16[4,10,32,128]{3,2,1,0:T(8,128)(2,1)S(1)} %collective-permute-done.20.refs_7_), channel_id=1, source_target_pairs={{1,0},{2,3},{5,4},{6,7},{9,8},{10,11},{13,12},{14,15},{17,16},{18,... | collective-permute-start | bytes 983048 | tf_op jit(solution)/shard_map/ppermute | solution.py:348
  50.4 16.2 %collective-permute-start.14 = (bf16[2,128,512]{2,1,0:T(8,128)(2,1)S(1)}, bf16[2,128,512]{2,1,0:T(8,128)(2,1)S(1)}, u32[]{:S(2)}, u32[]{:S(2)}) collective-permute-start(bf16[2,128,512]{2,1,0:T(8,128)(2,1)S(1)} %get-tuple-element.24), channel_id=1, source_target_pairs={{0,1},{1,0},{2,3},{3,2},{4,5},{5,4},{6,7},{7,6},{8,9},{9,8},{10,11... | collective-permute-start | bytes 786440 | tf_op jit(solution)/shard_map/ppermute | solution.py:345
  53.2 13.5 %collective-permute-start.15 = (bf16[2,128,512]{2,1,0:T(8,128)(2,1)S(1)}, bf16[2,128,512]{2,1,0:T(8,128)(2,1)S(1)}, u32[]{:S(2)}, u32[]{:S(2)}) collective-permute-start(bf16[2,128,512]{2,1,0:T(8,128)(2,1)S(1)} %get-tuple-element.25), channel_id=1, source_target_pairs={{0,2},{3,1},{4,6},{7,5},{8,10},{11,9},{12,14},{15,13},{16,18},{19,... | collective-permute-start | bytes 786440 | tf_op jit(solution)/shard_map/ppermute | solution.py:348
  56.4 10.2 %collective-permute-start.16 = (bf16[2,128,512]{2,1,0:T(8,128)(2,1)S(1)}, bf16[2,128,512]{2,1,0:T(8,128)(2,1)S(1)}, u32[]{:S(2)}, u32[]{:S(2)}) collective-permute-start(bf16[2,128,512]{2,1,0:T(8,128)(2,1)S(1)} %get-tuple-element.26), channel_id=1, source_target_pairs={{1,2},{2,1},{5,6},{6,5},{9,10},{10,9},{13,14},{14,13},{17,18},{18,... | collective-permute-start | bytes 786440 | tf_op jit(solution)/shard_map/ppermute | solution.py:348
  57.1 18.9 %collective-permute-start.18 = (bf16[2,128,512]{2,1,0:T(8,128)(2,1)S(1)}, bf16[2,128,512]{2,1,0:T(8,128)(2,1)S(1)}, u32[]{:S(2)}, u32[]{:S(2)}) collective-permute-start(bf16[2,128,512]{2,1,0:T(8,128)(2,1)S(1)} %add_convert_fusion.1), channel_id=1, source_target_pairs={{2,0},{1,3},{6,4},{5,7},{10,8},{9,11},{14,12},{13,15},{18,16},{17,... | collective-permute-start | bytes 786440 | tf_op jit(solution)/shard_map/ppermute | solution.py:348
  77.9 2.0 %collective-permute-start.27 = (bf16[4,4,128,128]{3,2,1,0:T(8,128)(2,1)S(1)}, bf16[4,4,128,128]{3,2,1,0:T(8,128)(2,1)S(1)}, u32[]{:S(2)}, u32[]{:S(2)}) collective-permute-start(bf16[4,4,128,128]{3,2,1,0:T(8,128)(2,1)S(1)} %get-tuple-element.30), channel_id=1, source_target_pairs={{0,4},{4,0},{8,12},{12,8},{16,20},{20,16},{24,28},{28,24},{1,5},{5... | collective-permute-start | bytes 1572872 | tf_op jit(solution)/shard_map/ppermute | solution.py:339
  80.2 6.4 %collective-permute-start.28 = (bf16[4,128,128]{2,1,0:T(8,128)(2,1)S(1)}, bf16[4,128,128]{2,1,0:T(8,128)(2,1)S(1)}, u32[]{:S(2)}, u32[]{:S(2)}) collective-permute-start(bf16[4,128,128]{2,1,0:T(8,128)(2,1)S(1)} %get-tuple-element.42), channel_id=1, source_target_pairs={{0,8},{4,12},{8,0},{12,4},{16,24},{20,28},{24,16},{28,20},{1,9},{5... | collective-permute-start | bytes 393224 | tf_op jit(solution)/shard_map/ppermute | solution.py:342
  80.7 8.3 %collective-permute-start.30 = (bf16[4,128,128]{2,1,0:T(8,128)(2,1)S(1)}, bf16[4,128,128]{2,1,0:T(8,128)(2,1)S(1)}, u32[]{:S(2)}, u32[]{:S(2)}) collective-permute-start(bf16[4,128,128]{2,1,0:T(8,128)(2,1)S(1)} %get-tuple-element.43), channel_id=1, source_target_pairs={{0,24},{4,28},{8,16},{12,20},{16,8},{20,12},{24,0},{28,4},{1,25},{... | collective-permute-start | bytes 393224 | tf_op jit(solution)/shard_map/ppermute | solution.py:342
  82.4 8.0 %collective-permute-start.29 = (bf16[4,128,128]{2,1,0:T(8,128)(2,1)S(1)}, bf16[4,128,128]{2,1,0:T(8,128)(2,1)S(1)}, u32[]{:S(2)}, u32[]{:S(2)}) collective-permute-start(bf16[4,128,128]{2,1,0:T(8,128)(2,1)S(1)} %get-tuple-element.44), channel_id=1, source_target_pairs={{0,16},{4,20},{8,24},{12,28},{16,0},{20,4},{24,8},{28,12},{1,17},{... | collective-permute-start | bytes 393224 | tf_op jit(solution)/shard_map/ppermute | solution.py:342
  83.7 19.1 %collective-permute-start.24 = (bf16[320,512]{1,0:T(8,128)(2,1)S(1)}, bf16[320,512]{1,0:T(8,128)(2,1)S(1)}, u32[]{:S(2)}, u32[]{:S(2)}) collective-permute-start(bf16[320,512]{1,0:T(8,128)(2,1)S(1)} %get-tuple-element.28), channel_id=1, source_target_pairs={{0,2},{1,3},{2,0},{3,1},{4,6},{5,7},{6,4},{7,5},{8,10},{9,11},{10,... | collective-permute-start | bytes 983048 | tf_op jit(solution)/shard_map/ppermute | solution.py:345
  90.5 15.1 %collective-permute-start.41 = (bf16[4,128,128]{2,1,0:T(8,128)(2,1)S(1)}, bf16[4,128,128]{2,1,0:T(8,128)(2,1)S(1)}, u32[]{:S(2)}, u32[]{:S(2)}) collective-permute-start(bf16[4,128,128]{2,1,0:T(8,128)(2,1)S(1)} %fusion.4.refs_0_), channel_id=1, source_target_pairs={{0,2},{1,3},{2,0},{3,1},{4,6},{5,7},{6,4},{7,5},{8,10},{9,11},{10,... | collective-permute-start | bytes 393224 | tf_op jit(solution)/shard_map/ppermute | solution.py:345
  90.5 16.9 %collective-permute-start.36 = (bf16[4,128,128]{2,1,0:T(8,128)(2,1)S(1)}, bf16[4,128,128]{2,1,0:T(8,128)(2,1)S(1)}, u32[]{:S(2)}, u32[]{:S(2)}) collective-permute-start(bf16[4,128,128]{2,1,0:T(8,128)(2,1)S(1)} %fusion.4.refs_0_), channel_id=1, source_target_pairs={{0,24},{4,28},{8,16},{12,20},{16,8},{20,12},{24,0},{28,4},{1,25},{... | collective-permute-start | bytes 393224 | tf_op jit(solution)/shard_map/ppermute | solution.py:342
  92.0 15.7 %collective-permute-start.34 = (bf16[4,128,128]{2,1,0:T(8,128)(2,1)S(1)}, bf16[4,128,128]{2,1,0:T(8,128)(2,1)S(1)}, u32[]{:S(2)}, u32[]{:S(2)}) collective-permute-start(bf16[4,128,128]{2,1,0:T(8,128)(2,1)S(1)} %fusion.4.refs_0_), channel_id=1, source_target_pairs={{0,16},{4,20},{8,24},{12,28},{16,0},{20,4},{24,8},{28,12},{1,17},{... | collective-permute-start | bytes 393224 | tf_op jit(solution)/shard_map/ppermute | solution.py:342
  93.7 15.3 %collective-permute-start.32 = (bf16[4,128,128]{2,1,0:T(8,128)(2,1)S(1)}, bf16[4,128,128]{2,1,0:T(8,128)(2,1)S(1)}, u32[]{:S(2)}, u32[]{:S(2)}) collective-permute-start(bf16[4,128,128]{2,1,0:T(8,128)(2,1)S(1)} %fusion.4.refs_0_), channel_id=1, source_target_pairs={{0,8},{4,12},{8,0},{12,4},{16,24},{20,28},{24,16},{28,20},{1,9},{5... | collective-permute-start | bytes 393224 | tf_op jit(solution)/shard_map/ppermute | solution.py:342
  102.8 6.2 %collective-permute-start.31 = (bf16[4,128,128]{2,1,0:T(8,128)(2,1)S(1)}, bf16[4,128,128]{2,1,0:T(8,128)(2,1)S(1)}, u32[]{:S(2)}, u32[]{:S(2)}) collective-permute-start(bf16[4,128,128]{2,1,0:T(8,128)(2,1)S(1)} %fusion.4.refs_0_), channel_id=1, source_target_pairs={{0,4},{4,0},{8,12},{12,8},{16,20},{20,16},{24,28},{28,24},{1,5},{5... | collective-permute-start | bytes 393224 | tf_op jit(solution)/shard_map/ppermute | solution.py:339
  105.5 7.2 %collective-permute-start.47 = (bf16[4,128,128]{2,1,0:T(8,128)(2,1)S(1)}, bf16[4,128,128]{2,1,0:T(8,128)(2,1)S(1)}, u32[]{:S(2)}, u32[]{:S(2)}) collective-permute-start(bf16[4,128,128]{2,1,0:T(8,128)(2,1)S(1)} %collective-permute-done.41.refs_8_), channel_id=1, source_target_pairs={{0,24},{4,28},{8,16},{12,20},{16,8},{20,12},{24,0},{28,4},{1,25},{... | collective-permute-start | bytes 393224 | tf_op jit(solution)/shard_map/ppermute | solution.py:342
  107.4 7.3 %collective-permute-start.45 = (bf16[4,128,128]{2,1,0:T(8,128)(2,1)S(1)}, bf16[4,128,128]{2,1,0:T(8,128)(2,1)S(1)}, u32[]{:S(2)}, u32[]{:S(2)}) collective-permute-start(bf16[4,128,128]{2,1,0:T(8,128)(2,1)S(1)} %collective-permute-done.41.refs_8_), channel_id=1, source_target_pairs={{0,16},{4,20},{8,24},{12,28},{16,0},{20,4},{24,8},{28,12},{1,17},{... | collective-permute-start | bytes 393224 | tf_op jit(solution)/shard_map/ppermute | solution.py:342
  107.7 7.0 %collective-permute-start.43 = (bf16[4,128,128]{2,1,0:T(8,128)(2,1)S(1)}, bf16[4,128,128]{2,1,0:T(8,128)(2,1)S(1)}, u32[]{:S(2)}, u32[]{:S(2)}) collective-permute-start(bf16[4,128,128]{2,1,0:T(8,128)(2,1)S(1)} %collective-permute-done.41.refs_8_), channel_id=1, source_target_pairs={{0,8},{4,12},{8,0},{12,4},{16,24},{20,28},{24,16},{28,20},{1,9},{5... | collective-permute-start | bytes 393224 | tf_op jit(solution)/shard_map/ppermute | solution.py:342
  109.0 6.1 %collective-permute-start.42 = (bf16[4,128,128]{2,1,0:T(8,128)(2,1)S(1)}, bf16[4,128,128]{2,1,0:T(8,128)(2,1)S(1)}, u32[]{:S(2)}, u32[]{:S(2)}) collective-permute-start(bf16[4,128,128]{2,1,0:T(8,128)(2,1)S(1)} %collective-permute-done.41.refs_8_), channel_id=1, source_target_pairs={{0,4},{4,0},{8,12},{12,8},{16,20},{20,16},{24,28},{28,24},{1,5},{5... | collective-permute-start | bytes 393224 | tf_op jit(solution)/shard_map/ppermute | solution.py:339
  109.0 6.2 %collective-permute-start.37 = (bf16[4,128,128]{2,1,0:T(8,128)(2,1)S(1)}, bf16[4,128,128]{2,1,0:T(8,128)(2,1)S(1)}, u32[]{:S(2)}, u32[]{:S(2)}) collective-permute-start(bf16[4,128,128]{2,1,0:T(8,128)(2,1)S(1)} %collective-permute-done.36.refs_6_), channel_id=1, source_target_pairs={{0,4},{4,0},{8,12},{12,8},{16,20},{20,16},{24,28},{28,24},{1,5},{5... | collective-permute-start | bytes 393224 | tf_op jit(solution)/shard_map/ppermute | solution.py:339
  112.8 2.9 %collective-permute-start.35 = (bf16[4,128,128]{2,1,0:T(8,128)(2,1)S(1)}, bf16[4,128,128]{2,1,0:T(8,128)(2,1)S(1)}, u32[]{:S(2)}, u32[]{:S(2)}) collective-permute-start(bf16[4,128,128]{2,1,0:T(8,128)(2,1)S(1)} %collective-permute-done.34.refs_4_), channel_id=1, source_target_pairs={{0,4},{4,0},{8,12},{12,8},{16,20},{20,16},{24,28},{28,24},{1,5},{5... | collective-permute-start | bytes 393224 | tf_op jit(solution)/shard_map/ppermute | solution.py:339
  114.7 1.7 %collective-permute-start.33 = (bf16[4,128,128]{2,1,0:T(8,128)(2,1)S(1)}, bf16[4,128,128]{2,1,0:T(8,128)(2,1)S(1)}, u32[]{:S(2)}, u32[]{:S(2)}) collective-permute-start(bf16[4,128,128]{2,1,0:T(8,128)(2,1)S(1)} %collective-permute-done.32.refs_2_), channel_id=1, source_target_pairs={{0,4},{4,0},{8,12},{12,8},{16,20},{20,16},{24,28},{28,24},{1,5},{5... | collective-permute-start | bytes 393224 | tf_op jit(solution)/shard_map/ppermute | solution.py:339
  114.7 3.1 %collective-permute-start.48 = (bf16[4,128,128]{2,1,0:T(8,128)(2,1)S(1)}, bf16[4,128,128]{2,1,0:T(8,128)(2,1)S(1)}, u32[]{:S(2)}, u32[]{:S(2)}) collective-permute-start(bf16[4,128,128]{2,1,0:T(8,128)(2,1)S(1)} %collective-permute-done.47.refs_14_), channel_id=1, source_target_pairs={{0,4},{4,0},{8,12},{12,8},{16,20},{20,16},{24,28},{28,24},{1,5},{5... | collective-permute-start | bytes 393224 | tf_op jit(solution)/shard_map/ppermute | solution.py:339
  115.2 3.9 %collective-permute-start.46 = (bf16[4,128,128]{2,1,0:T(8,128)(2,1)S(1)}, bf16[4,128,128]{2,1,0:T(8,128)(2,1)S(1)}, u32[]{:S(2)}, u32[]{:S(2)}) collective-permute-start(bf16[4,128,128]{2,1,0:T(8,128)(2,1)S(1)} %collective-permute-done.45.refs_12_), channel_id=1, source_target_pairs={{0,4},{4,0},{8,12},{12,8},{16,20},{20,16},{24,28},{28,24},{1,5},{5... | collective-permute-start | bytes 393224 | tf_op jit(solution)/shard_map/ppermute | solution.py:339
  115.2 3.8 %collective-permute-start.44 = (bf16[4,128,128]{2,1,0:T(8,128)(2,1)S(1)}, bf16[4,128,128]{2,1,0:T(8,128)(2,1)S(1)}, u32[]{:S(2)}, u32[]{:S(2)}) collective-permute-start(bf16[4,128,128]{2,1,0:T(8,128)(2,1)S(1)} %collective-permute-done.43.refs_10_), channel_id=1, source_target_pairs={{0,4},{4,0},{8,12},{12,8},{16,20},{20,16},{24,28},{28,24},{1,5},{5... | collective-permute-start | bytes 393224 | tf_op jit(solution)/shard_map/ppermute | solution.py:339
  115.7 10.6 %collective-permute-start.25 = (bf16[256,512]{1,0:T(8,128)(2,1)S(1)}, bf16[256,512]{1,0:T(8,128)(2,1)S(1)}, u32[]{:S(2)}, u32[]{:S(2)}) collective-permute-start(bf16[256,512]{1,0:T(8,128)(2,1)S(1)} %get-tuple-element.27.refs_1_), channel_id=1, source_target_pairs={{1,2},{2,1},{5,6},{6,5},{9,10},{10,9},{13,14},{14,13},{17,18},{18,... | collective-permute-start | bytes 786440 | tf_op jit(solution)/shard_map/ppermute | solution.py:348
  116.4 10.0 %collective-permute-start.23 = (bf16[256,512]{1,0:T(8,128)(2,1)S(1)}, bf16[256,512]{1,0:T(8,128)(2,1)S(1)}, u32[]{:S(2)}, u32[]{:S(2)}) collective-permute-start(bf16[256,512]{1,0:T(8,128)(2,1)S(1)} %get-tuple-element.27.refs_1_), channel_id=1, source_target_pairs={{0,1},{1,0},{2,3},{3,2},{4,5},{5,4},{6,7},{7,6},{8,9},{9,8},{10,11... | collective-permute-start | bytes 786440 | tf_op jit(solution)/shard_map/ppermute | solution.py:345
  117.8 20.5 %collective-permute-start.26 = (bf16[320,512]{1,0:T(8,128)(2,1)S(1)}, bf16[320,512]{1,0:T(8,128)(2,1)S(1)}, u32[]{:S(2)}, u32[]{:S(2)}) collective-permute-start(bf16[320,512]{1,0:T(8,128)(2,1)S(1)} %collective-permute-done.24.refs_3_.refs_17_), channel_id=1, source_target_pairs={{1,0},{2,3},{5,4},{6,7},{9,8},{10,11},{13,12},{14,15},{17,16},{18,... | collective-permute-start | bytes 983048 | tf_op jit(solution)/shard_map/ppermute | solution.py:348
  120.4 28.8 %collective-permute-start.49 = (bf16[4,10,32,128]{3,2,1,0:T(8,128)(2,1)S(1)}, bf16[4,10,32,128]{3,2,1,0:T(8,128)(2,1)S(1)}, u32[]{:S(2)}, u32[]{:S(2)}) collective-permute-start(bf16[4,10,32,128]{3,2,1,0:T(8,128)(2,1)S(1)} %get-tuple-element.36), channel_id=1, source_target_pairs={{0,1},{1,0},{2,3},{3,2},{4,5},{5,4},{6,7},{7,6},{8,9},{9,8},{10,11... | collective-permute-start | bytes 983048 | tf_op jit(solution)/shard_map/ppermute | solution.py:345
  124.4 13.8 %collective-permute-start.40 = (bf16[128,512]{1,0:T(8,128)(2,1)S(1)}, bf16[128,512]{1,0:T(8,128)(2,1)S(1)}, u32[]{:S(2)}, u32[]{:S(2)}) collective-permute-start(bf16[128,512]{1,0:T(8,128)(2,1)S(1)} %shard_map.124.refs_6_), channel_id=1, source_target_pairs={{0,3},{1,2},{2,1},{3,0},{4,7},{5,6},{6,5},{7,4},{8,11},{9,10},{10,... | collective-permute-start | bytes 393224 | tf_op jit(solution)/shard_map/ppermute | solution.py:345
  126.3 11.9 %collective-permute-start.39 = (bf16[128,512]{1,0:T(8,128)(2,1)S(1)}, bf16[128,512]{1,0:T(8,128)(2,1)S(1)}, u32[]{:S(2)}, u32[]{:S(2)}) collective-permute-start(bf16[128,512]{1,0:T(8,128)(2,1)S(1)} %shard_map.124.refs_6_), channel_id=1, source_target_pairs={{0,2},{1,3},{2,0},{3,1},{4,6},{5,7},{6,4},{7,5},{8,10},{9,11},{10,... | collective-permute-start | bytes 393224 | tf_op jit(solution)/shard_map/ppermute | solution.py:345
  126.3 20.8 %collective-permute-start.38 = (bf16[128,512]{1,0:T(8,128)(2,1)S(1)}, bf16[128,512]{1,0:T(8,128)(2,1)S(1)}, u32[]{:S(2)}, u32[]{:S(2)}) collective-permute-start(bf16[128,512]{1,0:T(8,128)(2,1)S(1)} %shard_map.124.refs_6_), channel_id=1, source_target_pairs={{0,1},{1,0},{2,3},{3,2},{4,5},{5,4},{6,7},{7,6},{8,9},{9,8},{10,11... | collective-permute-start | bytes 393224 | tf_op jit(solution)/shard_map/ppermute | solution.py:345

commit v3 on v2

--- a/solution.py
+++ b/solution.py
@@ -53,27 +53,50 @@
     return lax.bitwise_xor(block // nb, d) * nb + lax.rem(block, nb)
 
 
-def front_kernel(lists, counts, *refs, pieces, zs, nb, rows, edge, slots, blocks):
+def pair_kernel(counts, gate, up, weights, *, rows, edge, slots, blocks):
+    for f in range(blocks):
+        count = counts[f]
+        for k in range(slots):
+            dst = slice(k * rows, (k + 1) * rows)
+            live = k < count
+            weights[f, dst, :edge] = jnp.where(live, gate[f, k], jnp.zeros_like(gate[f, k]))
+            weights[f, dst, edge:] = jnp.where(live, up[f, k], jnp.zeros_like(up[f, k]))
+
+
+def join_kernel(counts, *refs, zs, rows, edge, slots, blocks):
+    downs, down_all = refs[: zs + 1], refs[zs + 1]
+    z = lax.axis_index("fsdp")
+    ends = far_end(z, zs)
+    for f in range(blocks):
+        count = counts[f]
+        for k in range(slots):
+            live = k < count
+            for s in range(zs):
+                at = pl.multiple_of(lax.bitwise_xor(z, s) * rows, rows)
+                block = downs[s][f, k]
+                if s == zs - 1:
+                    block = jnp.where(ends, downs[zs][f, k], block)
+                down_all[f, pl.ds(at, rows), k * edge : (k + 1) * edge] = jnp.where(
+                    live, block, jnp.zeros_like(block)
+                )
+
+
+def front_kernel(lists, *refs, pieces, zs, nb, rows, edge, slots, blocks):
     xs = refs[:pieces]
-    gate, up = refs[pieces : pieces + 2]
-    outs = refs[pieces + 2 : pieces + 2 + zs]
-    gathered = refs[pieces + 2 + zs]
-    xall, weights = refs[pieces + 3 + zs :]
+    weights = refs[pieces]
+    outs = refs[pieces + 1 : pieces + 1 + zs]
+    gathered, xall = refs[pieces + 1 + zs :]
     d = lax.axis_index("dp")
     tok = xs[0].shape[-1]
     for r in range(pieces):
         for s in range(zs):
             xall[r * nb * rows : (r + 1) * nb * rows, s * tok : (s + 1) * tok] = xs[r][s]
     for f in range(blocks):
-        count = counts[f]
         for k in range(slots):
             b = relative_block(lists[f, k], d, nb)
             dst = slice(k * rows, (k + 1) * rows)
             gathered[f, dst, :] = xall[pl.ds(pl.multiple_of(b * rows, rows), rows), :]
-            live = k < count
-            weights[dst, :edge] = jnp.where(live, gate[f, k], jnp.zeros_like(gate[f, k]))
-            weights[dst, edge:] = jnp.where(live, up[f, k], jnp.zeros_like(up[f, k]))
-        both = lax.dot_general(gathered[f], weights[...], TN, preferred_element_type=F32)
+        both = lax.dot_general(gathered[f], weights[f], TN, preferred_element_type=F32)
         lanes = slice(f * edge, (f + 1) * edge)
         for s in range(zs):
             mine = both[s * tok : (s + 1) * tok]
@@ -82,32 +105,16 @@
 
 
 def middle_kernel(
-    owners, lists, counts, *refs, pieces, zs, nb, rows, edge, slots, blocks
+    owners, lists, *refs, pieces, zs, nb, rows, edge, slots, blocks
 ):
-    terms = len(refs) - zs - 10
-    parts = refs[:terms]
-    downs = refs[terms : terms + zs + 1]
-    tout = refs[terms + zs + 1]
-    outs = refs[terms + zs + 2 :]
-    hidden_own, plain, wide, keep, send, down_all, acc, hidden_t = outs
+    parts = refs[:-9]
+    down_all, tout, hidden_own, plain, wide, keep, send, acc, hidden_t = refs[-9:]
     d, z, owner = lax.axis_index("dp"), lax.axis_index("fsdp"), owners[0]
     tok = tout.shape[0]
     own = owner == d
     for b in range(pieces * nb):
         term = tout[:, b * edge : (b + 1) * edge].astype(F32)
         acc[b] = jnp.where(own, -term, jnp.zeros_like(term))
-    for f in range(blocks):
-        count = counts[f]
-        for k in range(slots):
-            live = k < count
-            for s in range(zs):
-                at = pl.multiple_of(lax.bitwise_xor(z, s) * rows, rows)
-                block = downs[s][f, k]
-                if s == zs - 1:
-                    block = jnp.where(far_end(z, zs), downs[zs][f, k], block)
-                down_all[f, pl.ds(at, rows), k * edge : (k + 1) * edge] = jnp.where(
-                    live, block, jnp.zeros_like(block)
-                )
     for f in range(blocks):
         lanes = slice(f * edge, (f + 1) * edge)
         g = parts[0][0, :, lanes].astype(F32)
@@ -351,7 +358,8 @@
         side = shift(plain, 1)
         cross = shift(wide, 2)
         inner = move(plain, [(1, 2), (2, 1)])
-        return [side, cross, inner, move(cross, [(1, 0), (2, 3)])]
+        core = cross[: plain.shape[0]]
+        return [side, cross, inner, move(core, [(1, 0), (2, 3)])]
 
     def collect(mine):
         joined = move(mine[3], [(0, 1), (3, 2)])
@@ -388,35 +396,49 @@
     xs = spread(mixed.reshape(zs, nb * rows, tok))
 
     part = sds((2, tok, blocks * edge))
+    inner_sizes = dict(rows=rows, edge=edge, slots=slots, blocks=blocks)
+    (weights,) = call(
+        functools.partial(pair_kernel, **inner_sizes),
+        [sds((blocks, slots * rows, 2 * edge))],
+        [],
+        1,
+        input_counts,
+        gate_blocks,
+        up_blocks,
+    )
     front = call(
         functools.partial(front_kernel, **dims, **more),
         [sds(part.shape, F32)] + [part] * (zs - 1) + [sds((blocks, slots * rows, zs * tok))],
-        [pltpu.VMEM((row_blocks * rows, zs * tok), BF16), pltpu.VMEM((slots * rows, 2 * edge), BF16)],
-        2,
+        [pltpu.VMEM((row_blocks * rows, zs * tok), BF16)],
+        1,
         input_lists,
-        input_counts,
         *xs,
-        gate_blocks,
-        up_blocks,
+        weights,
     )
     gathered = front[zs]
     parts = collect(front[:zs])
 
-    middle = call(
+    (down_all,) = call(
+        functools.partial(join_kernel, zs=zs, **inner_sizes),
+        [sds((blocks, edge, slots * edge))],
+        [],
+        1,
+        output_counts,
+        *downs,
+    )
+    hidden_own, plain, wide, keep, send = call(
         functools.partial(middle_kernel, **dims, **more),
         [sds((2, blocks * rows, tok)), sds((2 * tok, blocks * edge))]
         + [sds((2 * tok + 2 * rows, blocks * edge))]
-        + [sds((chips, nb, tok, edge), F32), sds((chips, nb, tok, edge)), sds((blocks, edge, slots * edge))],
+        + [sds((chips, nb, tok, edge), F32), sds((chips, nb, tok, edge))],
         [pltpu.VMEM((row_blocks, tok, edge), F32), pltpu.VMEM((blocks * edge, tok), BF16)],
-        3,
+        2,
         owner_section,
         output_lists,
-        output_counts,
         *parts,
-        *downs,
+        down_all,
         tout,
     )
-    hidden_own, plain, wide, keep, send, down_all = middle
     messages = gather(plain, wide)
 
     summed = keep + partner(send).astype(F32)

time: 150 us -> 148 us (0.987)
  waiting for transfers between devices: 87.5 us -> 83 us
    ppermute x13, waiting for transfers between devices: 40.2 us -> 31.6 us  [shift(): return lax.ppermute(a, 'fsdp', [(i, i ^ s) for i in range(zs)])]
    ppermute x8, waiting for transfers between devices: 22 us -> 26.1 us  [move(): return lax.ppermute(a, 'fsdp', pairs)]
    ppermute x8, starting transfers between devices: 10.9 us -> 12.6 us  [move(): return lax.ppermute(a, 'fsdp', pairs)]
    pallas_call x6 -> x8, Pallas kernels: 8.61 us -> 9.75 us  [call(): pl.pallas_call(kernel, out_shape=tuple(outs), in_specs=[SM] * smem + [VM]...]
  transfers between devices with their start and end apart: 50 -> 50, of which waited for: 22 -> 24; matrix products, arithmetic and copies ran while one was open for 0% -> 0% of each run, Pallas kernels for 4% -> 5%
where the time goes in v3:
time: 148 us
  waiting for transfers between devices  83 us (56%)
  starting transfers between devices  50.9 us (34%)
  Pallas kernels  9.75 us (7%)
  between operations  1.6 us (1%)
    ppermute x13, waiting for transfers between devices, shift(): return lax.ppermute(a, 'fsdp', [(i, i ^ s) for i in range(zs)])  31.6 us
    ppermute x8, waiting for transfers between devices, move(): return lax.ppermute(a, 'fsdp', pairs)  26.1 us
    ppermute x15, waiting for transfers between devices, chip_swap(): return lax.ppermute(a, 'dp', [(i, i ^ 2 * c) for i in range(pieces)])  22.2 us
    ppermute x15, starting transfers between devices, chip_swap(): return lax.ppermute(a, 'dp', [(i, i ^ 2 * c) for i in range(pieces)])  18.7 us
    ppermute x13, starting transfers between devices, shift(): return lax.ppermute(a, 'fsdp', [(i, i ^ s) for i in range(zs)])  17.4 us
    ppermute x8, starting transfers between devices, move(): return lax.ppermute(a, 'fsdp', pairs)  12.6 us
    pallas_call x8, Pallas kernels, call(): pl.pallas_call(kernel, out_shape=tuple(outs), in_specs=[SM] * smem + [VM]...  9.75 us
    ppermute x14, waiting for transfers between devices, partner(): return lax.ppermute(a, 'dp', [(i, i ^ 1) for i in range(pieces)])  3.13 us
  transfers between devices with their start and end apart: 50, of which 24 were waited for; matrix products, arithmetic and copies ran while one was open for 0% of the time, Pallas kernels for 5%

profile of v3, /device:TPU:0, one launch (start us, length us, event | category | flops | bytes accessed | tf_op | source)
XLA Modules:
  0.0 147.8 jit_solution(12063779786819485961)
XLA Ops:
  0.6 1.2 copy-done
  2.2 0.6 collective-permute-start
  3.4 0.9 collective-permute-done
  4.3 3.9 %collective-permute-start.1 = (bf16[512,128]{1,0:T(8,128)(2,1)S(1)}, bf16[512,128]{1,0:T(8,128)(2,1)S(1)}, u32[]{:S(2)}, u32[]{:S(2)}) collective-permute-start(bf16[512,128]{1,0:T(8,128)(2,1)S(1)} %get-tuple-element.39), channel_id=1, source_target_pairs={{0,24},{4,28},{8,16},{12,20},{16,8},{20,12},{24,0},{28,4},{1,25},{... | collective-permute-start | bytes 393224 | tf_op jit(solution)/shard_map/ppermute | solution.py:349
  8.2 0.5 collective-permute-start.2
  8.9 3.3 %collective-permute-done.1 = bf16[512,128]{1,0:T(8,128)(2,1)S(1)} collective-permute-done((bf16[512,128]{1,0:T(8,128)(2,1)S(1)}, bf16[512,128]{1,0:T(8,128)(2,1)S(1)}, u32[]{:S(2)}, u32[]{:S(2)}) %collective-permute-start.1) | collective-permute-done | bytes 131104 | tf_op jit(solution)/shard_map/ppermute | solution.py:349
  12.2 2.6 %collective-permute-done.2 = bf16[512,128]{1,0:T(8,128)(2,1)S(1)} collective-permute-done((bf16[512,128]{1,0:T(8,128)(2,1)S(1)}, bf16[512,128]{1,0:T(8,128)(2,1)S(1)}, u32[]{:S(2)}, u32[]{:S(2)}) %collective-permute-start.2) | collective-permute-done | bytes 131104 | tf_op jit(solution)/shard_map/ppermute | solution.py:349
  15.2 2.7 %collective-permute-start.5 = (bf16[4,32,128]{2,1,0:T(8,128)(2,1)S(1)}, bf16[4,32,128]{2,1,0:T(8,128)(2,1)S(1)}, u32[]{:S(2)}, u32[]{:S(2)}) collective-permute-start(bf16[4,32,128]{2,1,0:T(8,128)(2,1)S(1)} %get-tuple-element.45), channel_id=1, source_target_pairs={{0,2},{1,3},{2,0},{3,1},{4,6},{5,7},{6,4},{7,5},{8,10},{9,11},{10,... | collective-permute-start | bytes 98312 | tf_op jit(solution)/shard_map/ppermute | solution.py:352
  17.8 1.3 collective-permute-start.6
  19.4 1.0 collective-permute-done.5
  20.4 3.2 %collective-permute-done.6 = bf16[4,32,128]{2,1,0:T(8,128)(2,1)S(1)} collective-permute-done((bf16[4,32,128]{2,1,0:T(8,128)(2,1)S(1)}, bf16[4,32,128]{2,1,0:T(8,128)(2,1)S(1)}, u32[]{:S(2)}, u32[]{:S(2)}) %collective-permute-start.6) | collective-permute-done | bytes 32800 | tf_op jit(solution)/shard_map/ppermute | solution.py:352
  23.6 1.5 %collective-permute-start.10 = (bf16[4,128,128]{2,1,0:T(8,128)(2,1)S(1)}, bf16[4,128,128]{2,1,0:T(8,128)(2,1)S(1)}, u32[]{:S(2)}, u32[]{:S(2)}) collective-permute-start(bf16[4,128,128]{2,1,0:T(8,128)(2,1)S(1)} %pad_maximum_fusion.refs_0_), channel_id=1, source_target_pairs={{0,16},{4,20},{8,24},{12,28},{16,0},{20,4},{24,8},{28,12},{1,17},{... | collective-permute-start | bytes 393224 | tf_op jit(solution)/shard_map/ppermute | solution.py:349
  25.1 1.5 %collective-permute-start.12 = (bf16[4,128,128]{2,1,0:T(8,128)(2,1)S(1)}, bf16[4,128,128]{2,1,0:T(8,128)(2,1)S(1)}, u32[]{:S(2)}, u32[]{:S(2)}) collective-permute-start(bf16[4,128,128]{2,1,0:T(8,128)(2,1)S(1)} %pad_maximum_fusion.refs_0_), channel_id=1, source_target_pairs={{0,24},{4,28},{8,16},{12,20},{16,8},{20,12},{24,0},{28,4},{1,25},{... | collective-permute-start | bytes 393224 | tf_op jit(solution)/shard_map/ppermute | solution.py:349
  26.6 0.5 collective-permute-start.8
  27.1 2.7 %collective-permute-done.10.refs_4_ = bf16[4,128,128]{2,1,0:T(8,128)(2,1)S(1)} collective-permute-done((bf16[4,128,128]{2,1,0:T(8,128)(2,1)S(1)}, bf16[4,128,128]{2,1,0:T(8,128)(2,1)S(1)}, u32[]{:S(2)}, u32[]{:S(2)}) %collective-permute-start.10) | collective-permute-done | bytes 131104 | tf_op jit(solution)/shard_map/ppermute | solution.py:349
  29.8 1.3 collective-permute-done.12.refs_6_
  31.1 0.5 collective-permute-done.8.refs_2_
  31.6 1.2 collective-permute-start.20
  32.8 0.7 shard_map.122.refs_8_
  33.6 1.6 %shard_map.123 = (f32[2,128,512]{2,1,0:T(8,128)S(1)}, bf16[2,128,512]{2,1,0:T(8,128)(2,1)S(1)}, bf16[2,128,512]{2,1,0:T(8,128)(2,1)S(1)}, bf16[2,128,512]{2,1,0:T(8,128)(2,1)S(1)}, bf16[4,320,512]{2,1,0:T(8,128)(2,1)S(1)}) custom-call(s32[4,10]{1,0:T(4,128)S(1)} %copy-done.6, bf16[4,128,128]{2,1,0:T(8,128)(2,1)S(1)} %pad_maximum_fusion.refs_0_, ...), custom_call_target="tpu_custom_call" | custom-call | flops 134217728 | bytes 4325536 | tf_op jit(solution)/shard_map/pallas_call | solution.py:23
  35.2 3.9 %collective-permute-start.17 = (bf16[2,128,512]{2,1,0:T(8,128)(2,1)S(1)}, bf16[2,128,512]{2,1,0:T(8,128)(2,1)S(1)}, u32[]{:S(2)}, u32[]{:S(2)}) collective-permute-start(bf16[2,128,512]{2,1,0:T(8,128)(2,1)S(1)} %get-tuple-element.25), channel_id=1, source_target_pairs={{0,1},{3,2},{4,5},{7,6},{8,9},{11,10},{12,13},{15,14},{16,17},{19,... | collective-permute-start | bytes 786440 | tf_op jit(solution)/shard_map/ppermute | solution.py:355
  39.2 0.7 collective-permute-start.21
  39.9 9.7 %collective-permute-done.20.refs_2_ = bf16[4,10,32,128]{3,2,1,0:T(8,128)(2,1)S(1)} collective-permute-done((bf16[4,10,32,128]{3,2,1,0:T(8,128)(2,1)S(1)}, bf16[4,10,32,128]{3,2,1,0:T(8,128)(2,1)S(1)}, u32[]{:S(2)}, u32[]{:S(2)}) %collective-permute-start.20) | collective-permute-done | bytes 327712 | tf_op jit(solution)/shard_map/ppermute | solution.py:352
  49.6 1.3 collective-permute-start.22
  50.9 2.7 %collective-permute-start.14 = (bf16[2,128,512]{2,1,0:T(8,128)(2,1)S(1)}, bf16[2,128,512]{2,1,0:T(8,128)(2,1)S(1)}, u32[]{:S(2)}, u32[]{:S(2)}) collective-permute-start(bf16[2,128,512]{2,1,0:T(8,128)(2,1)S(1)} %get-tuple-element.23), channel_id=1, source_target_pairs={{0,1},{1,0},{2,3},{3,2},{4,5},{5,4},{6,7},{7,6},{8,9},{9,8},{10,11... | collective-permute-start | bytes 786440 | tf_op jit(solution)/shard_map/ppermute | solution.py:352
  53.7 2.7 %collective-permute-start.15 = (bf16[2,128,512]{2,1,0:T(8,128)(2,1)S(1)}, bf16[2,128,512]{2,1,0:T(8,128)(2,1)S(1)}, u32[]{:S(2)}, u32[]{:S(2)}) collective-permute-start(bf16[2,128,512]{2,1,0:T(8,128)(2,1)S(1)} %get-tuple-element.24), channel_id=1, source_target_pairs={{0,2},{3,1},{4,6},{7,5},{8,10},{11,9},{12,14},{15,13},{16,18},{19,... | collective-permute-start | bytes 786440 | tf_op jit(solution)/shard_map/ppermute | solution.py:355
  56.5 0.8 collective-permute-start.16
  57.3 1.3 collective-permute-start.18
  58.6 4.9 %collective-permute-done.22.refs_4_ = bf16[4,10,32,128]{3,2,1,0:T(8,128)(2,1)S(1)} collective-permute-done((bf16[4,10,32,128]{3,2,1,0:T(8,128)(2,1)S(1)}, bf16[4,10,32,128]{3,2,1,0:T(8,128)(2,1)S(1)}, u32[]{:S(2)}, u32[]{:S(2)}) %collective-permute-start.22) | collective-permute-done | bytes 327712 | tf_op jit(solution)/shard_map/ppermute | solution.py:355
  63.5 0.9 shard_map.124.refs_5_.refs_8_
  64.5 3.8 %collective-permute-done.14.refs_1_ = bf16[2,128,512]{2,1,0:T(8,128)(2,1)S(1)} collective-permute-done((bf16[2,128,512]{2,1,0:T(8,128)(2,1)S(1)}, bf16[2,128,512]{2,1,0:T(8,128)(2,1)S(1)}, u32[]{:S(2)}, u32[]{:S(2)}) %collective-permute-start.14) | collective-permute-done | bytes 262176 | tf_op jit(solution)/shard_map/ppermute | solution.py:352
  68.2 7.8 %collective-permute-done.18.refs_4_ = bf16[2,128,512]{2,1,0:T(8,128)(2,1)S(1)} collective-permute-done((bf16[2,128,512]{2,1,0:T(8,128)(2,1)S(1)}, bf16[2,128,512]{2,1,0:T(8,128)(2,1)S(1)}, u32[]{:S(2)}, u32[]{:S(2)}) %collective-permute-start.18) | collective-permute-done | bytes 262176 | tf_op jit(solution)/shard_map/ppermute | solution.py:355
  76.0 1.5 %shard_map.125 = (bf16[2,128,128]{2,1,0:T(8,128)(2,1)S(1)}, bf16[256,512]{1,0:T(8,128)(2,1)S(1)}, bf16[320,512]{1,0:T(8,128)(2,1)S(1)}, f32[4,4,128,128]{3,2,1,0:T(8,128)S(1)}, bf16[4,4,128,128]{3,2,1,0:T(8,128)(2,1)S(1)}) custom-call(s32[1]{0:T(128)} %copy.15.owners, s32[4,10]{1,0:T(4,128)S(1)} %copy-done.5, f32[2,128,512]{2,1,0:T(8,128)S(1)} %get-tuple-element.22.refs_0_, ...), custom_call_target="tpu_custom_call" | custom-call | flops 134217728 | bytes 6160548 | tf_op jit(solution)/shard_map/pallas_call | solution.py:23
  77.7 1.9 %collective-permute-done.27 = bf16[4,4,128,128]{3,2,1,0:T(8,128)(2,1)S(1)} collective-permute-done((bf16[4,4,128,128]{3,2,1,0:T(8,128)(2,1)S(1)}, bf16[4,4,128,128]{3,2,1,0:T(8,128)(2,1)S(1)}, u32[]{:S(2)}, u32[]{:S(2)}) %collective-permute-start.27) | collective-permute-done | bytes 524320 | tf_op jit(solution)/shard_map/ppermute | solution.py:346
  79.8 1.5 collective-permute-start.28
  81.3 0.7 collective-permute-start.29
  82.0 1.4 collective-permute-start.30
  83.4 2.5 %collective-permute-done.28 = bf16[4,128,128]{2,1,0:T(8,128)(2,1)S(1)} collective-permute-done((bf16[4,128,128]{2,1,0:T(8,128)(2,1)S(1)}, bf16[4,128,128]{2,1,0:T(8,128)(2,1)S(1)}, u32[]{:S(2)}, u32[]{:S(2)}) %collective-permute-start.28) | collective-permute-done | bytes 131104 | tf_op jit(solution)/shard_map/ppermute | solution.py:349
  85.9 3.4 %collective-permute-done.29 = bf16[4,128,128]{2,1,0:T(8,128)(2,1)S(1)} collective-permute-done((bf16[4,128,128]{2,1,0:T(8,128)(2,1)S(1)}, bf16[4,128,128]{2,1,0:T(8,128)(2,1)S(1)}, u32[]{:S(2)}, u32[]{:S(2)}) %collective-permute-start.29) | collective-permute-done | bytes 131104 | tf_op jit(solution)/shard_map/ppermute | solution.py:349
  89.5 0.7 collective-permute-start.32
  90.2 1.3 collective-permute-start.34
  91.5 1.5 %collective-permute-start.36 = (bf16[4,128,128]{2,1,0:T(8,128)(2,1)S(1)}, bf16[4,128,128]{2,1,0:T(8,128)(2,1)S(1)}, u32[]{:S(2)}, u32[]{:S(2)}) collective-permute-start(bf16[4,128,128]{2,1,0:T(8,128)(2,1)S(1)} %fusion.4.refs_0_), channel_id=1, source_target_pairs={{0,24},{4,28},{8,16},{12,20},{16,8},{20,12},{24,0},{28,4},{1,25},{... | collective-permute-start | bytes 393224 | tf_op jit(solution)/shard_map/ppermute | solution.py:349
  93.1 9.3 %collective-permute-done.24.refs_3_.refs_17_ = bf16[320,512]{1,0:T(8,128)(2,1)S(1)} collective-permute-done((bf16[320,512]{1,0:T(8,128)(2,1)S(1)}, bf16[320,512]{1,0:T(8,128)(2,1)S(1)}, u32[]{:S(2)}, u32[]{:S(2)}) %collective-permute-start.24) | collective-permute-done | bytes 327712 | tf_op jit(solution)/shard_map/ppermute | solution.py:352
  102.4 2.7 %collective-permute-done.41.refs_8_ = bf16[4,128,128]{2,1,0:T(8,128)(2,1)S(1)} collective-permute-done((bf16[4,128,128]{2,1,0:T(8,128)(2,1)S(1)}, bf16[4,128,128]{2,1,0:T(8,128)(2,1)S(1)}, u32[]{:S(2)}, u32[]{:S(2)}) %collective-permute-start.41) | collective-permute-done | bytes 131104 | tf_op jit(solution)/shard_map/ppermute | solution.py:352
  105.1 1.5 %collective-permute-start.43 = (bf16[4,128,128]{2,1,0:T(8,128)(2,1)S(1)}, bf16[4,128,128]{2,1,0:T(8,128)(2,1)S(1)}, u32[]{:S(2)}, u32[]{:S(2)}) collective-permute-start(bf16[4,128,128]{2,1,0:T(8,128)(2,1)S(1)} %collective-permute-done.41.refs_8_), channel_id=1, source_target_pairs={{0,8},{4,12},{8,0},{12,4},{16,24},{20,28},{24,16},{28,20},{1,9},{5... | collective-permute-start | bytes 393224 | tf_op jit(solution)/shard_map/ppermute | solution.py:349
  106.6 0.6 collective-permute-start.45
  107.2 1.4 collective-permute-start.47
  108.6 0.5 collective-permute-start.35
  109.1 1.8 %collective-permute-done.43.refs_10_ = bf16[4,128,128]{2,1,0:T(8,128)(2,1)S(1)} collective-permute-done((bf16[4,128,128]{2,1,0:T(8,128)(2,1)S(1)}, bf16[4,128,128]{2,1,0:T(8,128)(2,1)S(1)}, u32[]{:S(2)}, u32[]{:S(2)}) %collective-permute-start.43) | collective-permute-done | bytes 131104 | tf_op jit(solution)/shard_map/ppermute | solution.py:349
  110.9 3.6 %collective-permute-done.45.refs_12_ = bf16[4,128,128]{2,1,0:T(8,128)(2,1)S(1)} collective-permute-done((bf16[4,128,128]{2,1,0:T(8,128)(2,1)S(1)}, bf16[4,128,128]{2,1,0:T(8,128)(2,1)S(1)}, u32[]{:S(2)}, u32[]{:S(2)}) %collective-permute-start.45) | collective-permute-done | bytes 131104 | tf_op jit(solution)/shard_map/ppermute | solution.py:349
  114.5 0.5 collective-permute-start.44
  115.1 0.4 collective-permute-start.48
  115.9 0.7 collective-permute-start.25
  116.6 1.3 shard_map.128
  117.9 3.9 %collective-permute-start.49 = (bf16[4,10,32,128]{3,2,1,0:T(8,128)(2,1)S(1)}, bf16[4,10,32,128]{3,2,1,0:T(8,128)(2,1)S(1)}, u32[]{:S(2)}, u32[]{:S(2)}) collective-permute-start(bf16[4,10,32,128]{3,2,1,0:T(8,128)(2,1)S(1)} %get-tuple-element.34), channel_id=1, source_target_pairs={{0,1},{1,0},{2,3},{3,2},{4,5},{5,4},{6,7},{7,6},{8,9},{9,8},{10,11... | collective-permute-start | bytes 983048 | tf_op jit(solution)/shard_map/ppermute | solution.py:352
  121.9 1.3 collective-permute-start.26
  123.2 1.3 shard_map.126.refs_6_
  124.5 2.7 %collective-permute-start.38 = (bf16[128,512]{1,0:T(8,128)(2,1)S(1)}, bf16[128,512]{1,0:T(8,128)(2,1)S(1)}, u32[]{:S(2)}, u32[]{:S(2)}) collective-permute-start(bf16[128,512]{1,0:T(8,128)(2,1)S(1)} %shard_map.126.refs_6_), channel_id=1, source_target_pairs={{0,1},{1,0},{2,3},{3,2},{4,5},{5,4},{6,7},{7,6},{8,9},{9,8},{10,11... | collective-permute-start | bytes 393224 | tf_op jit(solution)/shard_map/ppermute | solution.py:352
  127.2 0.6 collective-permute-start.39
  127.8 1.8 %collective-permute-start.40 = (bf16[128,512]{1,0:T(8,128)(2,1)S(1)}, bf16[128,512]{1,0:T(8,128)(2,1)S(1)}, u32[]{:S(2)}, u32[]{:S(2)}) collective-permute-start(bf16[128,512]{1,0:T(8,128)(2,1)S(1)} %shard_map.126.refs_6_), channel_id=1, source_target_pairs={{0,3},{1,2},{2,1},{3,0},{4,7},{5,6},{6,5},{7,4},{8,11},{9,10},{10,... | collective-permute-start | bytes 393224 | tf_op jit(solution)/shard_map/ppermute | solution.py:352
  129.6 13.4 %collective-permute-done.26.refs_5_ = bf16[256,512]{1,0:T(8,128)(2,1)S(1)} collective-permute-done((bf16[256,512]{1,0:T(8,128)(2,1)S(1)}, bf16[256,512]{1,0:T(8,128)(2,1)S(1)}, u32[]{:S(2)}, u32[]{:S(2)}) %collective-permute-start.26) | collective-permute-done | bytes 262176 | tf_op jit(solution)/shard_map/ppermute | solution.py:355
  143.0 1.9 %collective-permute-done.38.refs_7_ = bf16[128,512]{1,0:T(8,128)(2,1)S(1)} collective-permute-done((bf16[128,512]{1,0:T(8,128)(2,1)S(1)}, bf16[128,512]{1,0:T(8,128)(2,1)S(1)}, u32[]{:S(2)}, u32[]{:S(2)}) %collective-permute-start.38) | collective-permute-done | bytes 131104 | tf_op jit(solution)/shard_map/ppermute | solution.py:352
  144.9 2.0 %shard_map.127 = (bf16[4,10,32,128]{3,2,1,0:T(8,128)(2,1)}, bf16[4,10,32,128]{3,2,1,0:T(8,128)(2,1)}) custom-call(s32[4]{0:T(128)S(1)} %copy-done.8, bf16[4,320,512]{2,1,0:T(8,128)(2,1)S(1)} %get-tuple-element.21.refs_0_, bf16[256,512]{1,0:T(8,128)(2,1)S(1)} %get-tuple-element.26.refs_1_, bf16[256,512]{1,0:T(8,128)(2,1)S(1)} %collective-permute-done.23.refs_2_, ...), custom_call_target="tpu_custom_call" | custom-call | flops 134217728 | bytes 3866640 | tf_op jit(solution)/shard_map/pallas_call | solution.py:23
  147.0 0.8 add_convert_fusion
  (72 shorter events, 2.3 us)
Async XLA Ops:
  0.6 1.2 copy-start
  2.2 2.1 %collective-permute-start = (bf16[4,512,128]{2,1,0:T(8,128)(2,1)S(1)}, bf16[4,512,128]{2,1,0:T(8,128)(2,1)S(1)}, u32[]{:S(2)}, u32[]{:S(2)}) collective-permute-start(bf16[4,512,128]{2,1,0:T(8,128)(2,1)S(1)} %get-tuple-element.20), channel_id=1, source_target_pairs={{0,4},{4,0},{8,12},{12,8},{16,20},{20,16},{24,28},{28,24},{1,5},{5... | collective-permute-start | bytes 1572872 | tf_op jit(solution)/shard_map/ppermute | solution.py:346
  4.3 27.4 %copy-start.2 = (bf16[4,10,32,128]{3,2,1,0:T(8,128)(2,1)S(1)}, bf16[4,10,32,128]{3,2,1,0:T(8,128)(2,1)}, u32[]{:S(2)}) copy-start(bf16[4,10,32,128]{3,2,1,0:T(8,128)(2,1)} %refs_0_.1) | copy-start | bytes 983044
  4.3 28.5 %copy-start.3 = (bf16[4,10,32,128]{3,2,1,0:T(8,128)(2,1)S(1)}, bf16[4,10,32,128]{3,2,1,0:T(8,128)(2,1)}, u32[]{:S(2)}) copy-start(bf16[4,10,32,128]{3,2,1,0:T(8,128)(2,1)} %gate.1) | copy-start | bytes 983044
  4.3 28.5 %copy-start.4 = (bf16[4,10,32,128]{3,2,1,0:T(8,128)(2,1)S(1)}, bf16[4,10,32,128]{3,2,1,0:T(8,128)(2,1)}, u32[]{:S(2)}) copy-start(bf16[4,10,32,128]{3,2,1,0:T(8,128)(2,1)} %up.1) | copy-start | bytes 983044
  4.3 28.5 %copy-start.8 = (s32[4]{0:T(128)S(1)}, s32[4]{0:T(128)}, u32[]{:S(2)}) copy-start(s32[4]{0:T(128)} %counts.6) | copy-start | bytes 52
  4.3 7.8 %collective-permute-start.1 = (bf16[512,128]{1,0:T(8,128)(2,1)S(1)}, bf16[512,128]{1,0:T(8,128)(2,1)S(1)}, u32[]{:S(2)}, u32[]{:S(2)}) collective-permute-start(bf16[512,128]{1,0:T(8,128)(2,1)S(1)} %get-tuple-element.39), channel_id=1, source_target_pairs={{0,24},{4,28},{8,16},{12,20},{16,8},{20,12},{24,0},{28,4},{1,25},{... | collective-permute-start | bytes 393224 | tf_op jit(solution)/shard_map/ppermute | solution.py:349
  8.2 6.6 %collective-permute-start.2 = (bf16[512,128]{1,0:T(8,128)(2,1)S(1)}, bf16[512,128]{1,0:T(8,128)(2,1)S(1)}, u32[]{:S(2)}, u32[]{:S(2)}) collective-permute-start(bf16[512,128]{1,0:T(8,128)(2,1)S(1)} %get-tuple-element.38), channel_id=1, source_target_pairs={{0,16},{4,20},{8,24},{12,28},{16,0},{20,4},{24,8},{28,12},{1,17},{... | collective-permute-start | bytes 393224 | tf_op jit(solution)/shard_map/ppermute | solution.py:349
  8.7 6.4 %collective-permute-start.3 = (bf16[512,128]{1,0:T(8,128)(2,1)S(1)}, bf16[512,128]{1,0:T(8,128)(2,1)S(1)}, u32[]{:S(2)}, u32[]{:S(2)}) collective-permute-start(bf16[512,128]{1,0:T(8,128)(2,1)S(1)} %get-tuple-element.37), channel_id=1, source_target_pairs={{0,8},{4,12},{8,0},{12,4},{16,24},{20,28},{24,16},{28,20},{1,9},{5... | collective-permute-start | bytes 393224 | tf_op jit(solution)/shard_map/ppermute | solution.py:349
  8.9 24.7 %copy-start.6 = (s32[4,10]{1,0:T(4,128)S(1)}, s32[4,10]{1,0:T(4,128)}, u32[]{:S(2)}) copy-start(s32[4,10]{1,0:T(4,128)} %lists.4) | copy-start | bytes 484
  15.2 5.2 %collective-permute-start.5 = (bf16[4,32,128]{2,1,0:T(8,128)(2,1)S(1)}, bf16[4,32,128]{2,1,0:T(8,128)(2,1)S(1)}, u32[]{:S(2)}, u32[]{:S(2)}) collective-permute-start(bf16[4,32,128]{2,1,0:T(8,128)(2,1)S(1)} %get-tuple-element.45), channel_id=1, source_target_pairs={{0,2},{1,3},{2,0},{3,1},{4,6},{5,7},{6,4},{7,5},{8,10},{9,11},{10,... | collective-permute-start | bytes 98312 | tf_op jit(solution)/shard_map/ppermute | solution.py:352
  17.8 5.7 %collective-permute-start.6 = (bf16[4,32,128]{2,1,0:T(8,128)(2,1)S(1)}, bf16[4,32,128]{2,1,0:T(8,128)(2,1)S(1)}, u32[]{:S(2)}, u32[]{:S(2)}) collective-permute-start(bf16[4,32,128]{2,1,0:T(8,128)(2,1)S(1)} %get-tuple-element.44), channel_id=1, source_target_pairs={{0,3},{1,2},{2,1},{3,0},{4,7},{5,6},{6,5},{7,4},{8,11},{9,10},{10,... | collective-permute-start | bytes 98312 | tf_op jit(solution)/shard_map/ppermute | solution.py:352
  19.2 4.4 %collective-permute-start.4 = (bf16[4,32,128]{2,1,0:T(8,128)(2,1)S(1)}, bf16[4,32,128]{2,1,0:T(8,128)(2,1)S(1)}, u32[]{:S(2)}, u32[]{:S(2)}) collective-permute-start(bf16[4,32,128]{2,1,0:T(8,128)(2,1)S(1)} %get-tuple-element.46), channel_id=1, source_target_pairs={{0,1},{1,0},{2,3},{3,2},{4,5},{5,4},{6,7},{7,6},{8,9},{9,8},{10,11... | collective-permute-start | bytes 98312 | tf_op jit(solution)/shard_map/ppermute | solution.py:352
  23.6 6.3 %collective-permute-start.10 = (bf16[4,128,128]{2,1,0:T(8,128)(2,1)S(1)}, bf16[4,128,128]{2,1,0:T(8,128)(2,1)S(1)}, u32[]{:S(2)}, u32[]{:S(2)}) collective-permute-start(bf16[4,128,128]{2,1,0:T(8,128)(2,1)S(1)} %pad_maximum_fusion.refs_0_), channel_id=1, source_target_pairs={{0,16},{4,20},{8,24},{12,28},{16,0},{20,4},{24,8},{28,12},{1,17},{... | collective-permute-start | bytes 393224 | tf_op jit(solution)/shard_map/ppermute | solution.py:349
  25.1 6.0 %collective-permute-start.12 = (bf16[4,128,128]{2,1,0:T(8,128)(2,1)S(1)}, bf16[4,128,128]{2,1,0:T(8,128)(2,1)S(1)}, u32[]{:S(2)}, u32[]{:S(2)}) collective-permute-start(bf16[4,128,128]{2,1,0:T(8,128)(2,1)S(1)} %pad_maximum_fusion.refs_0_), channel_id=1, source_target_pairs={{0,24},{4,28},{8,16},{12,20},{16,8},{20,12},{24,0},{28,4},{1,25},{... | collective-permute-start | bytes 393224 | tf_op jit(solution)/shard_map/ppermute | solution.py:349
  26.6 5.0 %collective-permute-start.8 = (bf16[4,128,128]{2,1,0:T(8,128)(2,1)S(1)}, bf16[4,128,128]{2,1,0:T(8,128)(2,1)S(1)}, u32[]{:S(2)}, u32[]{:S(2)}) collective-permute-start(bf16[4,128,128]{2,1,0:T(8,128)(2,1)S(1)} %pad_maximum_fusion.refs_0_), channel_id=1, source_target_pairs={{0,8},{4,12},{8,0},{12,4},{16,24},{20,28},{24,16},{28,20},{1,9},{5... | collective-permute-start | bytes 393224 | tf_op jit(solution)/shard_map/ppermute | solution.py:349
  27.1 6.4 %collective-permute-start.7 = (bf16[4,128,128]{2,1,0:T(8,128)(2,1)S(1)}, bf16[4,128,128]{2,1,0:T(8,128)(2,1)S(1)}, u32[]{:S(2)}, u32[]{:S(2)}) collective-permute-start(bf16[4,128,128]{2,1,0:T(8,128)(2,1)S(1)} %pad_maximum_fusion.refs_0_), channel_id=1, source_target_pairs={{0,4},{4,0},{8,12},{12,8},{16,20},{20,16},{24,28},{28,24},{1,5},{5... | collective-permute-start | bytes 393224 | tf_op jit(solution)/shard_map/ppermute | solution.py:346
  29.8 3.7 %collective-permute-start.11 = (bf16[4,128,128]{2,1,0:T(8,128)(2,1)S(1)}, bf16[4,128,128]{2,1,0:T(8,128)(2,1)S(1)}, u32[]{:S(2)}, u32[]{:S(2)}) collective-permute-start(bf16[4,128,128]{2,1,0:T(8,128)(2,1)S(1)} %collective-permute-done.10.refs_4_), channel_id=1, source_target_pairs={{0,4},{4,0},{8,12},{12,8},{16,20},{20,16},{24,28},{28,24},{1,5},{5... | collective-permute-start | bytes 393224 | tf_op jit(solution)/shard_map/ppermute | solution.py:346
  31.1 2.5 %collective-permute-start.13 = (bf16[4,128,128]{2,1,0:T(8,128)(2,1)S(1)}, bf16[4,128,128]{2,1,0:T(8,128)(2,1)S(1)}, u32[]{:S(2)}, u32[]{:S(2)}) collective-permute-start(bf16[4,128,128]{2,1,0:T(8,128)(2,1)S(1)} %collective-permute-done.12.refs_6_), channel_id=1, source_target_pairs={{0,4},{4,0},{8,12},{12,8},{16,20},{20,16},{24,28},{28,24},{1,5},{5... | collective-permute-start | bytes 393224 | tf_op jit(solution)/shard_map/ppermute | solution.py:346
  31.6 2.0 %collective-permute-start.9 = (bf16[4,128,128]{2,1,0:T(8,128)(2,1)S(1)}, bf16[4,128,128]{2,1,0:T(8,128)(2,1)S(1)}, u32[]{:S(2)}, u32[]{:S(2)}) collective-permute-start(bf16[4,128,128]{2,1,0:T(8,128)(2,1)S(1)} %collective-permute-done.8.refs_2_), channel_id=1, source_target_pairs={{0,4},{4,0},{8,12},{12,8},{16,20},{20,16},{24,28},{28,24},{1,5},{5... | collective-permute-start | bytes 393224 | tf_op jit(solution)/shard_map/ppermute | solution.py:346
  31.6 18.0 %collective-permute-start.20 = (bf16[4,10,32,128]{3,2,1,0:T(8,128)(2,1)S(1)}, bf16[4,10,32,128]{3,2,1,0:T(8,128)(2,1)S(1)}, u32[]{:S(2)}, u32[]{:S(2)}) collective-permute-start(bf16[4,10,32,128]{3,2,1,0:T(8,128)(2,1)S(1)} %copy-done.2), channel_id=1, source_target_pairs={{0,2},{1,3},{2,0},{3,1},{4,6},{5,7},{6,4},{7,5},{8,10},{9,11},{10,... | collective-permute-start | bytes 983048 | tf_op jit(solution)/shard_map/ppermute | solution.py:352
  33.5 30.0 %copy-start.7 = (s32[4]{0:T(128)S(1)}, s32[4]{0:T(128)}, u32[]{:S(2)}) copy-start(s32[4]{0:T(128)} %counts.7) | copy-start | bytes 52
  35.2 18.4 %collective-permute-start.17 = (bf16[2,128,512]{2,1,0:T(8,128)(2,1)S(1)}, bf16[2,128,512]{2,1,0:T(8,128)(2,1)S(1)}, u32[]{:S(2)}, u32[]{:S(2)}) collective-permute-start(bf16[2,128,512]{2,1,0:T(8,128)(2,1)S(1)} %get-tuple-element.25), channel_id=1, source_target_pairs={{0,1},{3,2},{4,5},{7,6},{8,9},{11,10},{12,13},{15,14},{16,17},{19,... | collective-permute-start | bytes 786440 | tf_op jit(solution)/shard_map/ppermute | solution.py:355
  39.2 17.4 %collective-permute-start.19 = (bf16[4,10,32,128]{3,2,1,0:T(8,128)(2,1)S(1)}, bf16[4,10,32,128]{3,2,1,0:T(8,128)(2,1)S(1)}, u32[]{:S(2)}, u32[]{:S(2)}) collective-permute-start(bf16[4,10,32,128]{3,2,1,0:T(8,128)(2,1)S(1)} %copy-done.2), channel_id=1, source_target_pairs={{0,1},{1,0},{2,3},{3,2},{4,5},{5,4},{6,7},{7,6},{8,9},{9,8},{10,11... | collective-permute-start | bytes 983048 | tf_op jit(solution)/shard_map/ppermute | solution.py:352
  39.2 18.1 %collective-permute-start.21 = (bf16[4,10,32,128]{3,2,1,0:T(8,128)(2,1)S(1)}, bf16[4,10,32,128]{3,2,1,0:T(8,128)(2,1)S(1)}, u32[]{:S(2)}, u32[]{:S(2)}) collective-permute-start(bf16[4,10,32,128]{3,2,1,0:T(8,128)(2,1)S(1)} %copy-done.2), channel_id=1, source_target_pairs={{1,2},{2,1},{5,6},{6,5},{9,10},{10,9},{13,14},{14,13},{17,18},{18,... | collective-permute-start | bytes 983048 | tf_op jit(solution)/shard_map/ppermute | solution.py:355
  49.6 13.9 %collective-permute-start.22 = (bf16[4,10,32,128]{3,2,1,0:T(8,128)(2,1)S(1)}, bf16[4,10,32,128]{3,2,1,0:T(8,128)(2,1)S(1)}, u32[]{:S(2)}, u32[]{:S(2)}) collective-permute-start(bf16[4,10,32,128]{3,2,1,0:T(8,128)(2,1)S(1)} %collective-permute-done.20.refs_2_), channel_id=1, source_target_pairs={{1,0},{2,3},{5,4},{6,7},{9,8},{10,11},{13,12},{14,15},{17,16},{18,... | collective-permute-start | bytes 983048 | tf_op jit(solution)/shard_map/ppermute | solution.py:355
  50.9 17.3 %collective-permute-start.14 = (bf16[2,128,512]{2,1,0:T(8,128)(2,1)S(1)}, bf16[2,128,512]{2,1,0:T(8,128)(2,1)S(1)}, u32[]{:S(2)}, u32[]{:S(2)}) collective-permute-start(bf16[2,128,512]{2,1,0:T(8,128)(2,1)S(1)} %get-tuple-element.23), channel_id=1, source_target_pairs={{0,1},{1,0},{2,3},{3,2},{4,5},{5,4},{6,7},{7,6},{8,9},{9,8},{10,11... | collective-permute-start | bytes 786440 | tf_op jit(solution)/shard_map/ppermute | solution.py:352
  53.7 14.6 %collective-permute-start.15 = (bf16[2,128,512]{2,1,0:T(8,128)(2,1)S(1)}, bf16[2,128,512]{2,1,0:T(8,128)(2,1)S(1)}, u32[]{:S(2)}, u32[]{:S(2)}) collective-permute-start(bf16[2,128,512]{2,1,0:T(8,128)(2,1)S(1)} %get-tuple-element.24), channel_id=1, source_target_pairs={{0,2},{3,1},{4,6},{7,5},{8,10},{11,9},{12,14},{15,13},{16,18},{19,... | collective-permute-start | bytes 786440 | tf_op jit(solution)/shard_map/ppermute | solution.py:355
  56.4 19.6 %copy-start.1 = (bf16[1,128,4096]{2,1,0:T(8,128)(2,1)S(1)}, bf16[1,128,4096]{2,1,0:T(8,128)(2,1)}, u32[]{:S(2)}) copy-start(bf16[1,128,4096]{2,1,0:T(8,128)(2,1)} %param.11) | copy-start | bytes 3145732
  56.4 19.6 %copy-start.5 = (s32[4,10]{1,0:T(4,128)S(1)}, s32[4,10]{1,0:T(4,128)}, u32[]{:S(2)}) copy-start(s32[4,10]{1,0:T(4,128)} %lists.7) | copy-start | bytes 484
  56.5 11.7 %collective-permute-start.16 = (bf16[2,128,512]{2,1,0:T(8,128)(2,1)S(1)}, bf16[2,128,512]{2,1,0:T(8,128)(2,1)S(1)}, u32[]{:S(2)}, u32[]{:S(2)}) collective-permute-start(bf16[2,128,512]{2,1,0:T(8,128)(2,1)S(1)} %get-tuple-element.25), channel_id=1, source_target_pairs={{1,2},{2,1},{5,6},{6,5},{9,10},{10,9},{13,14},{14,13},{17,18},{18,... | collective-permute-start | bytes 786440 | tf_op jit(solution)/shard_map/ppermute | solution.py:355
  57.3 18.7 %collective-permute-start.18 = (bf16[2,128,512]{2,1,0:T(8,128)(2,1)S(1)}, bf16[2,128,512]{2,1,0:T(8,128)(2,1)S(1)}, u32[]{:S(2)}, u32[]{:S(2)}) collective-permute-start(bf16[2,128,512]{2,1,0:T(8,128)(2,1)S(1)} %add_convert_fusion.1), channel_id=1, source_target_pairs={{2,0},{1,3},{6,4},{5,7},{10,8},{9,11},{14,12},{13,15},{18,16},{17,... | collective-permute-start | bytes 786440 | tf_op jit(solution)/shard_map/ppermute | solution.py:355
  77.6 2.0 %collective-permute-start.27 = (bf16[4,4,128,128]{3,2,1,0:T(8,128)(2,1)S(1)}, bf16[4,4,128,128]{3,2,1,0:T(8,128)(2,1)S(1)}, u32[]{:S(2)}, u32[]{:S(2)}) collective-permute-start(bf16[4,4,128,128]{3,2,1,0:T(8,128)(2,1)S(1)} %get-tuple-element.29), channel_id=1, source_target_pairs={{0,4},{4,0},{8,12},{12,8},{16,20},{20,16},{24,28},{28,24},{1,5},{5... | collective-permute-start | bytes 1572872 | tf_op jit(solution)/shard_map/ppermute | solution.py:346
  79.8 6.1 %collective-permute-start.28 = (bf16[4,128,128]{2,1,0:T(8,128)(2,1)S(1)}, bf16[4,128,128]{2,1,0:T(8,128)(2,1)S(1)}, u32[]{:S(2)}, u32[]{:S(2)}) collective-permute-start(bf16[4,128,128]{2,1,0:T(8,128)(2,1)S(1)} %get-tuple-element.40), channel_id=1, source_target_pairs={{0,8},{4,12},{8,0},{12,4},{16,24},{20,28},{24,16},{28,20},{1,9},{5... | collective-permute-start | bytes 393224 | tf_op jit(solution)/shard_map/ppermute | solution.py:349
  81.3 8.1 %collective-permute-start.29 = (bf16[4,128,128]{2,1,0:T(8,128)(2,1)S(1)}, bf16[4,128,128]{2,1,0:T(8,128)(2,1)S(1)}, u32[]{:S(2)}, u32[]{:S(2)}) collective-permute-start(bf16[4,128,128]{2,1,0:T(8,128)(2,1)S(1)} %get-tuple-element.42), channel_id=1, source_target_pairs={{0,16},{4,20},{8,24},{12,28},{16,0},{20,4},{24,8},{28,12},{1,17},{... | collective-permute-start | bytes 393224 | tf_op jit(solution)/shard_map/ppermute | solution.py:349
  82.0 7.3 %collective-permute-start.30 = (bf16[4,128,128]{2,1,0:T(8,128)(2,1)S(1)}, bf16[4,128,128]{2,1,0:T(8,128)(2,1)S(1)}, u32[]{:S(2)}, u32[]{:S(2)}) collective-permute-start(bf16[4,128,128]{2,1,0:T(8,128)(2,1)S(1)} %get-tuple-element.41), channel_id=1, source_target_pairs={{0,24},{4,28},{8,16},{12,20},{16,8},{20,12},{24,0},{28,4},{1,25},{... | collective-permute-start | bytes 393224 | tf_op jit(solution)/shard_map/ppermute | solution.py:349
  83.4 19.0 %collective-permute-start.24 = (bf16[320,512]{1,0:T(8,128)(2,1)S(1)}, bf16[320,512]{1,0:T(8,128)(2,1)S(1)}, u32[]{:S(2)}, u32[]{:S(2)}) collective-permute-start(bf16[320,512]{1,0:T(8,128)(2,1)S(1)} %get-tuple-element.27), channel_id=1, source_target_pairs={{0,2},{1,3},{2,0},{3,1},{4,6},{5,7},{6,4},{7,5},{8,10},{9,11},{10,... | collective-permute-start | bytes 983048 | tf_op jit(solution)/shard_map/ppermute | solution.py:352
  89.4 15.6 %collective-permute-start.41 = (bf16[4,128,128]{2,1,0:T(8,128)(2,1)S(1)}, bf16[4,128,128]{2,1,0:T(8,128)(2,1)S(1)}, u32[]{:S(2)}, u32[]{:S(2)}) collective-permute-start(bf16[4,128,128]{2,1,0:T(8,128)(2,1)S(1)} %fusion.4.refs_0_), channel_id=1, source_target_pairs={{0,2},{1,3},{2,0},{3,1},{4,6},{5,7},{6,4},{7,5},{8,10},{9,11},{10,... | collective-permute-start | bytes 393224 | tf_op jit(solution)/shard_map/ppermute | solution.py:352
  89.5 17.1 %collective-permute-start.32 = (bf16[4,128,128]{2,1,0:T(8,128)(2,1)S(1)}, bf16[4,128,128]{2,1,0:T(8,128)(2,1)S(1)}, u32[]{:S(2)}, u32[]{:S(2)}) collective-permute-start(bf16[4,128,128]{2,1,0:T(8,128)(2,1)S(1)} %fusion.4.refs_0_), channel_id=1, source_target_pairs={{0,8},{4,12},{8,0},{12,4},{16,24},{20,28},{24,16},{28,20},{1,9},{5... | collective-permute-start | bytes 393224 | tf_op jit(solution)/shard_map/ppermute | solution.py:349
  90.2 17.0 %collective-permute-start.34 = (bf16[4,128,128]{2,1,0:T(8,128)(2,1)S(1)}, bf16[4,128,128]{2,1,0:T(8,128)(2,1)S(1)}, u32[]{:S(2)}, u32[]{:S(2)}) collective-permute-start(bf16[4,128,128]{2,1,0:T(8,128)(2,1)S(1)} %fusion.4.refs_0_), channel_id=1, source_target_pairs={{0,16},{4,20},{8,24},{12,28},{16,0},{20,4},{24,8},{28,12},{1,17},{... | collective-permute-start | bytes 393224 | tf_op jit(solution)/shard_map/ppermute | solution.py:349
  91.5 17.0 %collective-permute-start.36 = (bf16[4,128,128]{2,1,0:T(8,128)(2,1)S(1)}, bf16[4,128,128]{2,1,0:T(8,128)(2,1)S(1)}, u32[]{:S(2)}, u32[]{:S(2)}) collective-permute-start(bf16[4,128,128]{2,1,0:T(8,128)(2,1)S(1)} %fusion.4.refs_0_), channel_id=1, source_target_pairs={{0,24},{4,28},{8,16},{12,20},{16,8},{20,12},{24,0},{28,4},{1,25},{... | collective-permute-start | bytes 393224 | tf_op jit(solution)/shard_map/ppermute | solution.py:349
  102.4 6.2 %collective-permute-start.31 = (bf16[4,128,128]{2,1,0:T(8,128)(2,1)S(1)}, bf16[4,128,128]{2,1,0:T(8,128)(2,1)S(1)}, u32[]{:S(2)}, u32[]{:S(2)}) collective-permute-start(bf16[4,128,128]{2,1,0:T(8,128)(2,1)S(1)} %fusion.4.refs_0_), channel_id=1, source_target_pairs={{0,4},{4,0},{8,12},{12,8},{16,20},{20,16},{24,28},{28,24},{1,5},{5... | collective-permute-start | bytes 393224 | tf_op jit(solution)/shard_map/ppermute | solution.py:346
  105.1 5.8 %collective-permute-start.43 = (bf16[4,128,128]{2,1,0:T(8,128)(2,1)S(1)}, bf16[4,128,128]{2,1,0:T(8,128)(2,1)S(1)}, u32[]{:S(2)}, u32[]{:S(2)}) collective-permute-start(bf16[4,128,128]{2,1,0:T(8,128)(2,1)S(1)} %collective-permute-done.41.refs_8_), channel_id=1, source_target_pairs={{0,8},{4,12},{8,0},{12,4},{16,24},{20,28},{24,16},{28,20},{1,9},{5... | collective-permute-start | bytes 393224 | tf_op jit(solution)/shard_map/ppermute | solution.py:349
  106.6 7.9 %collective-permute-start.45 = (bf16[4,128,128]{2,1,0:T(8,128)(2,1)S(1)}, bf16[4,128,128]{2,1,0:T(8,128)(2,1)S(1)}, u32[]{:S(2)}, u32[]{:S(2)}) collective-permute-start(bf16[4,128,128]{2,1,0:T(8,128)(2,1)S(1)} %collective-permute-done.41.refs_8_), channel_id=1, source_target_pairs={{0,16},{4,20},{8,24},{12,28},{16,0},{20,4},{24,8},{28,12},{1,17},{... | collective-permute-start | bytes 393224 | tf_op jit(solution)/shard_map/ppermute | solution.py:349
  107.2 7.3 %collective-permute-start.47 = (bf16[4,128,128]{2,1,0:T(8,128)(2,1)S(1)}, bf16[4,128,128]{2,1,0:T(8,128)(2,1)S(1)}, u32[]{:S(2)}, u32[]{:S(2)}) collective-permute-start(bf16[4,128,128]{2,1,0:T(8,128)(2,1)S(1)} %collective-permute-done.41.refs_8_), channel_id=1, source_target_pairs={{0,24},{4,28},{8,16},{12,20},{16,8},{20,12},{24,0},{28,4},{1,25},{... | collective-permute-start | bytes 393224 | tf_op jit(solution)/shard_map/ppermute | solution.py:349
  108.6 6.5 %collective-permute-start.33 = (bf16[4,128,128]{2,1,0:T(8,128)(2,1)S(1)}, bf16[4,128,128]{2,1,0:T(8,128)(2,1)S(1)}, u32[]{:S(2)}, u32[]{:S(2)}) collective-permute-start(bf16[4,128,128]{2,1,0:T(8,128)(2,1)S(1)} %collective-permute-done.32.refs_2_), channel_id=1, source_target_pairs={{0,4},{4,0},{8,12},{12,8},{16,20},{20,16},{24,28},{28,24},{1,5},{5... | collective-permute-start | bytes 393224 | tf_op jit(solution)/shard_map/ppermute | solution.py:346
  108.6 6.5 %collective-permute-start.35 = (bf16[4,128,128]{2,1,0:T(8,128)(2,1)S(1)}, bf16[4,128,128]{2,1,0:T(8,128)(2,1)S(1)}, u32[]{:S(2)}, u32[]{:S(2)}) collective-permute-start(bf16[4,128,128]{2,1,0:T(8,128)(2,1)S(1)} %collective-permute-done.34.refs_4_), channel_id=1, source_target_pairs={{0,4},{4,0},{8,12},{12,8},{16,20},{20,16},{24,28},{28,24},{1,5},{5... | collective-permute-start | bytes 393224 | tf_op jit(solution)/shard_map/ppermute | solution.py:346
  110.9 4.7 %collective-permute-start.37 = (bf16[4,128,128]{2,1,0:T(8,128)(2,1)S(1)}, bf16[4,128,128]{2,1,0:T(8,128)(2,1)S(1)}, u32[]{:S(2)}, u32[]{:S(2)}) collective-permute-start(bf16[4,128,128]{2,1,0:T(8,128)(2,1)S(1)} %collective-permute-done.36.refs_6_), channel_id=1, source_target_pairs={{0,4},{4,0},{8,12},{12,8},{16,20},{20,16},{24,28},{28,24},{1,5},{5... | collective-permute-start | bytes 393224 | tf_op jit(solution)/shard_map/ppermute | solution.py:346
  114.5 1.3 collective-permute-start.42
  114.5 2.0 %collective-permute-start.44 = (bf16[4,128,128]{2,1,0:T(8,128)(2,1)S(1)}, bf16[4,128,128]{2,1,0:T(8,128)(2,1)S(1)}, u32[]{:S(2)}, u32[]{:S(2)}) collective-permute-start(bf16[4,128,128]{2,1,0:T(8,128)(2,1)S(1)} %collective-permute-done.43.refs_10_), channel_id=1, source_target_pairs={{0,4},{4,0},{8,12},{12,8},{16,20},{20,16},{24,28},{28,24},{1,5},{5... | collective-permute-start | bytes 393224 | tf_op jit(solution)/shard_map/ppermute | solution.py:346
  115.1 1.5 %collective-permute-start.46 = (bf16[4,128,128]{2,1,0:T(8,128)(2,1)S(1)}, bf16[4,128,128]{2,1,0:T(8,128)(2,1)S(1)}, u32[]{:S(2)}, u32[]{:S(2)}) collective-permute-start(bf16[4,128,128]{2,1,0:T(8,128)(2,1)S(1)} %collective-permute-done.45.refs_12_), channel_id=1, source_target_pairs={{0,4},{4,0},{8,12},{12,8},{16,20},{20,16},{24,28},{28,24},{1,5},{5... | collective-permute-start | bytes 393224 | tf_op jit(solution)/shard_map/ppermute | solution.py:346
  115.1 1.5 collective-permute-start.48
  115.6 11.6 %collective-permute-start.23 = (bf16[256,512]{1,0:T(8,128)(2,1)S(1)}, bf16[256,512]{1,0:T(8,128)(2,1)S(1)}, u32[]{:S(2)}, u32[]{:S(2)}) collective-permute-start(bf16[256,512]{1,0:T(8,128)(2,1)S(1)} %get-tuple-element.26.refs_1_), channel_id=1, source_target_pairs={{0,1},{1,0},{2,3},{3,2},{4,5},{5,4},{6,7},{7,6},{8,9},{9,8},{10,11... | collective-permute-start | bytes 786440 | tf_op jit(solution)/shard_map/ppermute | solution.py:352
  115.9 11.9 %collective-permute-start.25 = (bf16[256,512]{1,0:T(8,128)(2,1)S(1)}, bf16[256,512]{1,0:T(8,128)(2,1)S(1)}, u32[]{:S(2)}, u32[]{:S(2)}) collective-permute-start(bf16[256,512]{1,0:T(8,128)(2,1)S(1)} %get-tuple-element.26.refs_1_), channel_id=1, source_target_pairs={{1,2},{2,1},{5,6},{6,5},{9,10},{10,9},{13,14},{14,13},{17,18},{18,... | collective-permute-start | bytes 786440 | tf_op jit(solution)/shard_map/ppermute | solution.py:355
  117.9 29.0 %collective-permute-start.49 = (bf16[4,10,32,128]{3,2,1,0:T(8,128)(2,1)S(1)}, bf16[4,10,32,128]{3,2,1,0:T(8,128)(2,1)S(1)}, u32[]{:S(2)}, u32[]{:S(2)}) collective-permute-start(bf16[4,10,32,128]{3,2,1,0:T(8,128)(2,1)S(1)} %get-tuple-element.34), channel_id=1, source_target_pairs={{0,1},{1,0},{2,3},{3,2},{4,5},{5,4},{6,7},{7,6},{8,9},{9,8},{10,11... | collective-permute-start | bytes 983048 | tf_op jit(solution)/shard_map/ppermute | solution.py:352
  121.9 21.1 %collective-permute-start.26 = (bf16[256,512]{1,0:T(8,128)(2,1)S(1)}, bf16[256,512]{1,0:T(8,128)(2,1)S(1)}, u32[]{:S(2)}, u32[]{:S(2)}) collective-permute-start(bf16[256,512]{1,0:T(8,128)(2,1)S(1)} %slice.59), channel_id=1, source_target_pairs={{1,0},{2,3},{5,4},{6,7},{9,8},{10,11},{13,12},{14,15},{17,16},{18,... | collective-permute-start | bytes 786440 | tf_op jit(solution)/shard_map/ppermute | solution.py:355
  124.5 20.5 %collective-permute-start.38 = (bf16[128,512]{1,0:T(8,128)(2,1)S(1)}, bf16[128,512]{1,0:T(8,128)(2,1)S(1)}, u32[]{:S(2)}, u32[]{:S(2)}) collective-permute-start(bf16[128,512]{1,0:T(8,128)(2,1)S(1)} %shard_map.126.refs_6_), channel_id=1, source_target_pairs={{0,1},{1,0},{2,3},{3,2},{4,5},{5,4},{6,7},{7,6},{8,9},{9,8},{10,11... | collective-permute-start | bytes 393224 | tf_op jit(solution)/shard_map/ppermute | solution.py:352
  127.2 17.7 %collective-permute-start.39 = (bf16[128,512]{1,0:T(8,128)(2,1)S(1)}, bf16[128,512]{1,0:T(8,128)(2,1)S(1)}, u32[]{:S(2)}, u32[]{:S(2)}) collective-permute-start(bf16[128,512]{1,0:T(8,128)(2,1)S(1)} %shard_map.126.refs_6_), channel_id=1, source_target_pairs={{0,2},{1,3},{2,0},{3,1},{4,6},{5,7},{6,4},{7,5},{8,10},{9,11},{10,... | collective-permute-start | bytes 393224 | tf_op jit(solution)/shard_map/ppermute | solution.py:352
  127.8 17.1 %collective-permute-start.40 = (bf16[128,512]{1,0:T(8,128)(2,1)S(1)}, bf16[128,512]{1,0:T(8,128)(2,1)S(1)}, u32[]{:S(2)}, u32[]{:S(2)}) collective-permute-start(bf16[128,512]{1,0:T(8,128)(2,1)S(1)} %shard_map.126.refs_6_), channel_id=1, source_target_pairs={{0,3},{1,2},{2,1},{3,0},{4,7},{5,6},{6,5},{7,4},{8,11},{9,10},{10,... | collective-permute-start | bytes 393224 | tf_op jit(solution)/shard_map/ppermute | solution.py:352

commit v4 on v3

--- a/solution.py
+++ b/solution.py
@@ -81,11 +81,23 @@
                 )
 
 
+def partials(gathered, weights, outs, numbers, tok, edge, blocks):
+    for f in range(blocks):
+        lanes = slice(f * edge, (f + 1) * edge)
+        for s, out in zip(numbers, outs):
+            both = lax.dot_general(
+                gathered[f, :, s * tok : (s + 1) * tok],
+                weights[f],
+                TN,
+                preferred_element_type=F32,
+            )
+            out[0, :, lanes] = both[:, :edge].astype(out.dtype)
+            out[1, :, lanes] = both[:, edge:].astype(out.dtype)
+
+
 def front_kernel(lists, *refs, pieces, zs, nb, rows, edge, slots, blocks):
     xs = refs[:pieces]
-    weights = refs[pieces]
-    outs = refs[pieces + 1 : pieces + 1 + zs]
-    gathered, xall = refs[pieces + 1 + zs :]
+    weights, last, gathered, xall = refs[pieces:]
     d = lax.axis_index("dp")
     tok = xs[0].shape[-1]
     for r in range(pieces):
@@ -96,12 +108,12 @@
             b = relative_block(lists[f, k], d, nb)
             dst = slice(k * rows, (k + 1) * rows)
             gathered[f, dst, :] = xall[pl.ds(pl.multiple_of(b * rows, rows), rows), :]
-        both = lax.dot_general(gathered[f], weights[f], TN, preferred_element_type=F32)
-        lanes = slice(f * edge, (f + 1) * edge)
-        for s in range(zs):
-            mine = both[s * tok : (s + 1) * tok]
-            outs[s][0, :, lanes] = mine[:, :edge].astype(outs[s].dtype)
-            outs[s][1, :, lanes] = mine[:, edge:].astype(outs[s].dtype)
+    partials(gathered, weights, [last], [zs - 1], tok, edge, blocks)
+
+
+def rest_kernel(gathered, weights, *outs, edge, blocks):
+    numbers = list(range(len(outs)))
+    partials(gathered, weights, outs, numbers, outs[0].shape[1], edge, blocks)
 
 
 def middle_kernel(
@@ -406,17 +418,24 @@
         gate_blocks,
         up_blocks,
     )
-    front = call(
+    last, gathered = call(
         functools.partial(front_kernel, **dims, **more),
-        [sds(part.shape, F32)] + [part] * (zs - 1) + [sds((blocks, slots * rows, zs * tok))],
+        [part, sds((blocks, slots * rows, zs * tok))],
         [pltpu.VMEM((row_blocks * rows, zs * tok), BF16)],
         1,
         input_lists,
         *xs,
         weights,
     )
-    gathered = front[zs]
-    parts = collect(front[:zs])
+    rest = call(
+        functools.partial(rest_kernel, edge=edge, blocks=blocks),
+        [sds(part.shape, F32)] + [part] * (zs - 2),
+        [],
+        0,
+        gathered,
+        weights,
+    )
+    parts = collect([*rest, last])
 
     (down_all,) = call(
         functools.partial(join_kernel, zs=zs, **inner_sizes),

time: 148 us -> 149 us (level)
    pallas_call x8 -> x9, Pallas kernels: 9.75 us -> 10.1 us  [call(): pl.pallas_call(kernel, out_shape=tuple(outs), in_specs=[SM] * smem + [VM]...]
  transfers between devices with their start and end apart: 50 -> 50, of which waited for: 24 -> 23; matrix products, arithmetic and copies ran while one was open for 0% -> 0% of each run, Pallas kernels for 5% -> 6%
where the time goes in v4:
time: 149 us; the launch traced here: 148 us
  waiting for transfers between devices  83.4 us (56%)
  starting transfers between devices  50.7 us (34%)
  Pallas kernels  10.1 us (7%)
  between operations  1.61 us (1%)
    ppermute x13, waiting for transfers between devices, shift(): return lax.ppermute(a, 'fsdp', [(i, i ^ s) for i in range(zs)])  32 us
    ppermute x8, waiting for transfers between devices, move(): return lax.ppermute(a, 'fsdp', pairs)  26.2 us
    ppermute x15, waiting for transfers between devices, chip_swap(): return lax.ppermute(a, 'dp', [(i, i ^ 2 * c) for i in range(pieces)])  22.1 us
    ppermute x15, starting transfers between devices, chip_swap(): return lax.ppermute(a, 'dp', [(i, i ^ 2 * c) for i in range(pieces)])  18.7 us
    ppermute x13, starting transfers between devices, shift(): return lax.ppermute(a, 'fsdp', [(i, i ^ s) for i in range(zs)])  17.2 us
    ppermute x8, starting transfers between devices, move(): return lax.ppermute(a, 'fsdp', pairs)  12.6 us
    pallas_call x9, Pallas kernels, call(): pl.pallas_call(kernel, out_shape=tuple(outs), in_specs=[SM] * smem + [VM]...  10.1 us
    ppermute x14, waiting for transfers between devices, partner(): return lax.ppermute(a, 'dp', [(i, i ^ 1) for i in range(pieces)])  3.13 us
  transfers between devices with their start and end apart: 50, of which 23 were waited for; matrix products, arithmetic and copies ran while one was open for 0% of the time, Pallas kernels for 6%

profile of v4, /device:TPU:0, one launch (start us, length us, event | category | flops | bytes accessed | tf_op | source)
XLA Modules:
  0.0 148.3 jit_solution(9210050214644895326)
XLA Ops:
  0.6 1.2 copy-done
  2.2 0.6 collective-permute-start
  3.4 0.9 collective-permute-done
  4.3 3.9 %collective-permute-start.1 = (bf16[512,128]{1,0:T(8,128)(2,1)S(1)}, bf16[512,128]{1,0:T(8,128)(2,1)S(1)}, u32[]{:S(2)}, u32[]{:S(2)}) collective-permute-start(bf16[512,128]{1,0:T(8,128)(2,1)S(1)} %get-tuple-element.39), channel_id=1, source_target_pairs={{0,24},{4,28},{8,16},{12,20},{16,8},{20,12},{24,0},{28,4},{1,25},{... | collective-permute-start | bytes 393224 | tf_op jit(solution)/shard_map/ppermute | solution.py:361
  8.2 0.5 collective-permute-start.2
  8.9 3.3 %collective-permute-done.1 = bf16[512,128]{1,0:T(8,128)(2,1)S(1)} collective-permute-done((bf16[512,128]{1,0:T(8,128)(2,1)S(1)}, bf16[512,128]{1,0:T(8,128)(2,1)S(1)}, u32[]{:S(2)}, u32[]{:S(2)}) %collective-permute-start.1) | collective-permute-done | bytes 131104 | tf_op jit(solution)/shard_map/ppermute | solution.py:361
  12.2 2.6 %collective-permute-done.2 = bf16[512,128]{1,0:T(8,128)(2,1)S(1)} collective-permute-done((bf16[512,128]{1,0:T(8,128)(2,1)S(1)}, bf16[512,128]{1,0:T(8,128)(2,1)S(1)}, u32[]{:S(2)}, u32[]{:S(2)}) %collective-permute-start.2) | collective-permute-done | bytes 131104 | tf_op jit(solution)/shard_map/ppermute | solution.py:361
  15.2 2.7 %collective-permute-start.5 = (bf16[4,32,128]{2,1,0:T(8,128)(2,1)S(1)}, bf16[4,32,128]{2,1,0:T(8,128)(2,1)S(1)}, u32[]{:S(2)}, u32[]{:S(2)}) collective-permute-start(bf16[4,32,128]{2,1,0:T(8,128)(2,1)S(1)} %get-tuple-element.45), channel_id=1, source_target_pairs={{0,2},{1,3},{2,0},{3,1},{4,6},{5,7},{6,4},{7,5},{8,10},{9,11},{10,... | collective-permute-start | bytes 98312 | tf_op jit(solution)/shard_map/ppermute | solution.py:364
  17.8 1.3 collective-permute-start.6
  19.4 1.0 collective-permute-done.5
  20.4 3.2 %collective-permute-done.6 = bf16[4,32,128]{2,1,0:T(8,128)(2,1)S(1)} collective-permute-done((bf16[4,32,128]{2,1,0:T(8,128)(2,1)S(1)}, bf16[4,32,128]{2,1,0:T(8,128)(2,1)S(1)}, u32[]{:S(2)}, u32[]{:S(2)}) %collective-permute-start.6) | collective-permute-done | bytes 32800 | tf_op jit(solution)/shard_map/ppermute | solution.py:364
  23.6 1.5 %collective-permute-start.10 = (bf16[4,128,128]{2,1,0:T(8,128)(2,1)S(1)}, bf16[4,128,128]{2,1,0:T(8,128)(2,1)S(1)}, u32[]{:S(2)}, u32[]{:S(2)}) collective-permute-start(bf16[4,128,128]{2,1,0:T(8,128)(2,1)S(1)} %pad_maximum_fusion.refs_0_), channel_id=1, source_target_pairs={{0,16},{4,20},{8,24},{12,28},{16,0},{20,4},{24,8},{28,12},{1,17},{... | collective-permute-start | bytes 393224 | tf_op jit(solution)/shard_map/ppermute | solution.py:361
  25.1 1.5 %collective-permute-start.12 = (bf16[4,128,128]{2,1,0:T(8,128)(2,1)S(1)}, bf16[4,128,128]{2,1,0:T(8,128)(2,1)S(1)}, u32[]{:S(2)}, u32[]{:S(2)}) collective-permute-start(bf16[4,128,128]{2,1,0:T(8,128)(2,1)S(1)} %pad_maximum_fusion.refs_0_), channel_id=1, source_target_pairs={{0,24},{4,28},{8,16},{12,20},{16,8},{20,12},{24,0},{28,4},{1,25},{... | collective-permute-start | bytes 393224 | tf_op jit(solution)/shard_map/ppermute | solution.py:361
  26.6 0.5 collective-permute-start.8
  27.1 2.7 %collective-permute-done.10.refs_4_ = bf16[4,128,128]{2,1,0:T(8,128)(2,1)S(1)} collective-permute-done((bf16[4,128,128]{2,1,0:T(8,128)(2,1)S(1)}, bf16[4,128,128]{2,1,0:T(8,128)(2,1)S(1)}, u32[]{:S(2)}, u32[]{:S(2)}) %collective-permute-start.10) | collective-permute-done | bytes 131104 | tf_op jit(solution)/shard_map/ppermute | solution.py:361
  29.8 1.3 collective-permute-done.12.refs_6_
  31.1 0.5 collective-permute-done.8.refs_2_
  31.6 1.2 collective-permute-start.20
  32.8 0.7 shard_map.122.refs_8_.weights
  33.6 1.3 shard_map.123
  34.9 3.9 %collective-permute-start.17 = (bf16[2,128,512]{2,1,0:T(8,128)(2,1)S(1)}, bf16[2,128,512]{2,1,0:T(8,128)(2,1)S(1)}, u32[]{:S(2)}, u32[]{:S(2)}) collective-permute-start(bf16[2,128,512]{2,1,0:T(8,128)(2,1)S(1)} %get-tuple-element.25), channel_id=1, source_target_pairs={{0,1},{3,2},{4,5},{7,6},{8,9},{11,10},{12,13},{15,14},{16,17},{19,... | collective-permute-start | bytes 786440 | tf_op jit(solution)/shard_map/ppermute | solution.py:367
  38.9 0.7 collective-permute-start.21
  39.6 10.1 %collective-permute-done.20.refs_2_ = bf16[4,10,32,128]{3,2,1,0:T(8,128)(2,1)S(1)} collective-permute-done((bf16[4,10,32,128]{3,2,1,0:T(8,128)(2,1)S(1)}, bf16[4,10,32,128]{3,2,1,0:T(8,128)(2,1)S(1)}, u32[]{:S(2)}, u32[]{:S(2)}) %collective-permute-start.20) | collective-permute-done | bytes 327712 | tf_op jit(solution)/shard_map/ppermute | solution.py:364
  49.6 1.3 collective-permute-start.22
  50.9 0.6 shard_map.124
  51.6 2.7 %collective-permute-start.14 = (bf16[2,128,512]{2,1,0:T(8,128)(2,1)S(1)}, bf16[2,128,512]{2,1,0:T(8,128)(2,1)S(1)}, u32[]{:S(2)}, u32[]{:S(2)}) collective-permute-start(bf16[2,128,512]{2,1,0:T(8,128)(2,1)S(1)} %get-tuple-element.23), channel_id=1, source_target_pairs={{0,1},{1,0},{2,3},{3,2},{4,5},{5,4},{6,7},{7,6},{8,9},{9,8},{10,11... | collective-permute-start | bytes 786440 | tf_op jit(solution)/shard_map/ppermute | solution.py:364
  54.3 2.7 %collective-permute-start.15 = (bf16[2,128,512]{2,1,0:T(8,128)(2,1)S(1)}, bf16[2,128,512]{2,1,0:T(8,128)(2,1)S(1)}, u32[]{:S(2)}, u32[]{:S(2)}) collective-permute-start(bf16[2,128,512]{2,1,0:T(8,128)(2,1)S(1)} %get-tuple-element.24), channel_id=1, source_target_pairs={{0,2},{3,1},{4,6},{7,5},{8,10},{11,9},{12,14},{15,13},{16,18},{19,... | collective-permute-start | bytes 786440 | tf_op jit(solution)/shard_map/ppermute | solution.py:367
  57.1 0.8 collective-permute-start.16
  57.9 1.3 collective-permute-start.18
  59.2 4.1 %collective-permute-done.22.refs_4_ = bf16[4,10,32,128]{3,2,1,0:T(8,128)(2,1)S(1)} collective-permute-done((bf16[4,10,32,128]{3,2,1,0:T(8,128)(2,1)S(1)}, bf16[4,10,32,128]{3,2,1,0:T(8,128)(2,1)S(1)}, u32[]{:S(2)}, u32[]{:S(2)}) %collective-permute-start.22) | collective-permute-done | bytes 327712 | tf_op jit(solution)/shard_map/ppermute | solution.py:367
  63.4 0.9 shard_map.125.refs_5_.refs_8_
  64.3 3.6 %collective-permute-done.14.refs_1_ = bf16[2,128,512]{2,1,0:T(8,128)(2,1)S(1)} collective-permute-done((bf16[2,128,512]{2,1,0:T(8,128)(2,1)S(1)}, bf16[2,128,512]{2,1,0:T(8,128)(2,1)S(1)}, u32[]{:S(2)}, u32[]{:S(2)}) %collective-permute-start.14) | collective-permute-done | bytes 262176 | tf_op jit(solution)/shard_map/ppermute | solution.py:364
  67.9 8.5 %collective-permute-done.18.refs_4_ = bf16[2,128,512]{2,1,0:T(8,128)(2,1)S(1)} collective-permute-done((bf16[2,128,512]{2,1,0:T(8,128)(2,1)S(1)}, bf16[2,128,512]{2,1,0:T(8,128)(2,1)S(1)}, u32[]{:S(2)}, u32[]{:S(2)}) %collective-permute-start.18) | collective-permute-done | bytes 262176 | tf_op jit(solution)/shard_map/ppermute | solution.py:367
  76.4 1.5 %shard_map.126 = (bf16[2,128,128]{2,1,0:T(8,128)(2,1)S(1)}, bf16[256,512]{1,0:T(8,128)(2,1)S(1)}, bf16[320,512]{1,0:T(8,128)(2,1)S(1)}, f32[4,4,128,128]{3,2,1,0:T(8,128)S(1)}, bf16[4,4,128,128]{3,2,1,0:T(8,128)(2,1)S(1)}) custom-call(s32[1]{0:T(128)} %copy.15.owners, s32[4,10]{1,0:T(4,128)S(1)} %copy-done.5, f32[2,128,512]{2,1,0:T(8,128)S(1)} %get-tuple-element.22.refs_0_, ...), custom_call_target="tpu_custom_call" | custom-call | flops 134217728 | bytes 6160548 | tf_op jit(solution)/shard_map/pallas_call | solution.py:23
  78.0 1.9 %collective-permute-done.27 = bf16[4,4,128,128]{3,2,1,0:T(8,128)(2,1)S(1)} collective-permute-done((bf16[4,4,128,128]{3,2,1,0:T(8,128)(2,1)S(1)}, bf16[4,4,128,128]{3,2,1,0:T(8,128)(2,1)S(1)}, u32[]{:S(2)}, u32[]{:S(2)}) %collective-permute-start.27) | collective-permute-done | bytes 524320 | tf_op jit(solution)/shard_map/ppermute | solution.py:358
  80.2 1.5 %collective-permute-start.28 = (bf16[4,128,128]{2,1,0:T(8,128)(2,1)S(1)}, bf16[4,128,128]{2,1,0:T(8,128)(2,1)S(1)}, u32[]{:S(2)}, u32[]{:S(2)}) collective-permute-start(bf16[4,128,128]{2,1,0:T(8,128)(2,1)S(1)} %get-tuple-element.40), channel_id=1, source_target_pairs={{0,8},{4,12},{8,0},{12,4},{16,24},{20,28},{24,16},{28,20},{1,9},{5... | collective-permute-start | bytes 393224 | tf_op jit(solution)/shard_map/ppermute | solution.py:361
  81.6 0.5 collective-permute-start.29
  82.1 1.6 %collective-permute-start.30 = (bf16[4,128,128]{2,1,0:T(8,128)(2,1)S(1)}, bf16[4,128,128]{2,1,0:T(8,128)(2,1)S(1)}, u32[]{:S(2)}, u32[]{:S(2)}) collective-permute-start(bf16[4,128,128]{2,1,0:T(8,128)(2,1)S(1)} %get-tuple-element.41), channel_id=1, source_target_pairs={{0,24},{4,28},{8,16},{12,20},{16,8},{20,12},{24,0},{28,4},{1,25},{... | collective-permute-start | bytes 393224 | tf_op jit(solution)/shard_map/ppermute | solution.py:361
  83.7 2.5 %collective-permute-done.28 = bf16[4,128,128]{2,1,0:T(8,128)(2,1)S(1)} collective-permute-done((bf16[4,128,128]{2,1,0:T(8,128)(2,1)S(1)}, bf16[4,128,128]{2,1,0:T(8,128)(2,1)S(1)}, u32[]{:S(2)}, u32[]{:S(2)}) %collective-permute-start.28) | collective-permute-done | bytes 131104 | tf_op jit(solution)/shard_map/ppermute | solution.py:361
  86.2 3.5 %collective-permute-done.29 = bf16[4,128,128]{2,1,0:T(8,128)(2,1)S(1)} collective-permute-done((bf16[4,128,128]{2,1,0:T(8,128)(2,1)S(1)}, bf16[4,128,128]{2,1,0:T(8,128)(2,1)S(1)}, u32[]{:S(2)}, u32[]{:S(2)}) %collective-permute-start.29) | collective-permute-done | bytes 131104 | tf_op jit(solution)/shard_map/ppermute | solution.py:361
  89.9 0.7 collective-permute-start.32
  90.5 1.5 collective-permute-start.34
  92.0 1.4 collective-permute-start.36
  93.4 9.6 %collective-permute-done.24.refs_3_.refs_17_ = bf16[320,512]{1,0:T(8,128)(2,1)S(1)} collective-permute-done((bf16[320,512]{1,0:T(8,128)(2,1)S(1)}, bf16[320,512]{1,0:T(8,128)(2,1)S(1)}, u32[]{:S(2)}, u32[]{:S(2)}) %collective-permute-start.24) | collective-permute-done | bytes 327712 | tf_op jit(solution)/shard_map/ppermute | solution.py:364
  103.0 2.7 %collective-permute-done.41.refs_8_ = bf16[4,128,128]{2,1,0:T(8,128)(2,1)S(1)} collective-permute-done((bf16[4,128,128]{2,1,0:T(8,128)(2,1)S(1)}, bf16[4,128,128]{2,1,0:T(8,128)(2,1)S(1)}, u32[]{:S(2)}, u32[]{:S(2)}) %collective-permute-start.41) | collective-permute-done | bytes 131104 | tf_op jit(solution)/shard_map/ppermute | solution.py:364
  105.7 1.4 collective-permute-start.43
  107.1 0.7 collective-permute-start.45
  107.9 1.4 collective-permute-start.47
  109.2 0.5 collective-permute-start.35
  109.7 1.9 %collective-permute-done.43.refs_10_ = bf16[4,128,128]{2,1,0:T(8,128)(2,1)S(1)} collective-permute-done((bf16[4,128,128]{2,1,0:T(8,128)(2,1)S(1)}, bf16[4,128,128]{2,1,0:T(8,128)(2,1)S(1)}, u32[]{:S(2)}, u32[]{:S(2)}) %collective-permute-start.43) | collective-permute-done | bytes 131104 | tf_op jit(solution)/shard_map/ppermute | solution.py:361
  111.6 3.4 %collective-permute-done.45.refs_12_ = bf16[4,128,128]{2,1,0:T(8,128)(2,1)S(1)} collective-permute-done((bf16[4,128,128]{2,1,0:T(8,128)(2,1)S(1)}, bf16[4,128,128]{2,1,0:T(8,128)(2,1)S(1)}, u32[]{:S(2)}, u32[]{:S(2)}) %collective-permute-start.45) | collective-permute-done | bytes 131104 | tf_op jit(solution)/shard_map/ppermute | solution.py:361
  115.1 0.5 collective-permute-start.44
  116.4 0.7 collective-permute-start.25
  117.1 1.3 shard_map.129
  118.5 3.7 %collective-permute-start.49 = (bf16[4,10,32,128]{3,2,1,0:T(8,128)(2,1)S(1)}, bf16[4,10,32,128]{3,2,1,0:T(8,128)(2,1)S(1)}, u32[]{:S(2)}, u32[]{:S(2)}) collective-permute-start(bf16[4,10,32,128]{3,2,1,0:T(8,128)(2,1)S(1)} %get-tuple-element.34), channel_id=1, source_target_pairs={{0,1},{1,0},{2,3},{3,2},{4,5},{5,4},{6,7},{7,6},{8,9},{9,8},{10,11... | collective-permute-start | bytes 983048 | tf_op jit(solution)/shard_map/ppermute | solution.py:364
  122.3 1.3 collective-permute-start.26
  123.6 1.3 shard_map.127.refs_6_
  124.8 2.7 %collective-permute-start.38 = (bf16[128,512]{1,0:T(8,128)(2,1)S(1)}, bf16[128,512]{1,0:T(8,128)(2,1)S(1)}, u32[]{:S(2)}, u32[]{:S(2)}) collective-permute-start(bf16[128,512]{1,0:T(8,128)(2,1)S(1)} %shard_map.127.refs_6_), channel_id=1, source_target_pairs={{0,1},{1,0},{2,3},{3,2},{4,5},{5,4},{6,7},{7,6},{8,9},{9,8},{10,11... | collective-permute-start | bytes 393224 | tf_op jit(solution)/shard_map/ppermute | solution.py:364
  127.5 0.8 collective-permute-start.39
  128.4 1.6 %collective-permute-start.40 = (bf16[128,512]{1,0:T(8,128)(2,1)S(1)}, bf16[128,512]{1,0:T(8,128)(2,1)S(1)}, u32[]{:S(2)}, u32[]{:S(2)}) collective-permute-start(bf16[128,512]{1,0:T(8,128)(2,1)S(1)} %shard_map.127.refs_6_), channel_id=1, source_target_pairs={{0,3},{1,2},{2,1},{3,0},{4,7},{5,6},{6,5},{7,4},{8,11},{9,10},{10,... | collective-permute-start | bytes 393224 | tf_op jit(solution)/shard_map/ppermute | solution.py:364
  130.0 13.6 %collective-permute-done.26.refs_5_ = bf16[256,512]{1,0:T(8,128)(2,1)S(1)} collective-permute-done((bf16[256,512]{1,0:T(8,128)(2,1)S(1)}, bf16[256,512]{1,0:T(8,128)(2,1)S(1)}, u32[]{:S(2)}, u32[]{:S(2)}) %collective-permute-start.26) | collective-permute-done | bytes 262176 | tf_op jit(solution)/shard_map/ppermute | solution.py:367
  143.6 1.9 %collective-permute-done.38.refs_7_ = bf16[128,512]{1,0:T(8,128)(2,1)S(1)} collective-permute-done((bf16[128,512]{1,0:T(8,128)(2,1)S(1)}, bf16[128,512]{1,0:T(8,128)(2,1)S(1)}, u32[]{:S(2)}, u32[]{:S(2)}) %collective-permute-start.38) | collective-permute-done | bytes 131104 | tf_op jit(solution)/shard_map/ppermute | solution.py:364
  145.5 2.0 %shard_map.128 = (bf16[4,10,32,128]{3,2,1,0:T(8,128)(2,1)}, bf16[4,10,32,128]{3,2,1,0:T(8,128)(2,1)}) custom-call(s32[4]{0:T(128)S(1)} %copy-done.8, bf16[4,320,512]{2,1,0:T(8,128)(2,1)S(1)} %get-tuple-element.21.gathered.refs_0_, bf16[256,512]{1,0:T(8,128)(2,1)S(1)} %get-tuple-element.26.refs_1_, bf16[256,512]{1,0:T(8,128)(2,1)S(1)} %collective-permute-done.23.refs_2_, ...), custom_call_target="tpu_custom_call" | custom-call | flops 134217728 | bytes 3866640 | tf_op jit(solution)/shard_map/pallas_call | solution.py:23
  147.5 0.8 add_convert_fusion
  (73 shorter events, 2.7 us)
Async XLA Ops:
  0.6 1.2 copy-start
  2.2 2.1 %collective-permute-start = (bf16[4,512,128]{2,1,0:T(8,128)(2,1)S(1)}, bf16[4,512,128]{2,1,0:T(8,128)(2,1)S(1)}, u32[]{:S(2)}, u32[]{:S(2)}) collective-permute-start(bf16[4,512,128]{2,1,0:T(8,128)(2,1)S(1)} %get-tuple-element.20), channel_id=1, source_target_pairs={{0,4},{4,0},{8,12},{12,8},{16,20},{20,16},{24,28},{28,24},{1,5},{5... | collective-permute-start | bytes 1572872 | tf_op jit(solution)/shard_map/ppermute | solution.py:358
  4.3 27.4 %copy-start.2 = (bf16[4,10,32,128]{3,2,1,0:T(8,128)(2,1)S(1)}, bf16[4,10,32,128]{3,2,1,0:T(8,128)(2,1)}, u32[]{:S(2)}) copy-start(bf16[4,10,32,128]{3,2,1,0:T(8,128)(2,1)} %refs_0_.1) | copy-start | bytes 983044
  4.3 28.5 %copy-start.3 = (bf16[4,10,32,128]{3,2,1,0:T(8,128)(2,1)S(1)}, bf16[4,10,32,128]{3,2,1,0:T(8,128)(2,1)}, u32[]{:S(2)}) copy-start(bf16[4,10,32,128]{3,2,1,0:T(8,128)(2,1)} %gate.1) | copy-start | bytes 983044
  4.3 28.5 %copy-start.4 = (bf16[4,10,32,128]{3,2,1,0:T(8,128)(2,1)S(1)}, bf16[4,10,32,128]{3,2,1,0:T(8,128)(2,1)}, u32[]{:S(2)}) copy-start(bf16[4,10,32,128]{3,2,1,0:T(8,128)(2,1)} %up.1) | copy-start | bytes 983044
  4.3 28.5 %copy-start.8 = (s32[4]{0:T(128)S(1)}, s32[4]{0:T(128)}, u32[]{:S(2)}) copy-start(s32[4]{0:T(128)} %counts.6) | copy-start | bytes 52
  4.3 7.8 %collective-permute-start.1 = (bf16[512,128]{1,0:T(8,128)(2,1)S(1)}, bf16[512,128]{1,0:T(8,128)(2,1)S(1)}, u32[]{:S(2)}, u32[]{:S(2)}) collective-permute-start(bf16[512,128]{1,0:T(8,128)(2,1)S(1)} %get-tuple-element.39), channel_id=1, source_target_pairs={{0,24},{4,28},{8,16},{12,20},{16,8},{20,12},{24,0},{28,4},{1,25},{... | collective-permute-start | bytes 393224 | tf_op jit(solution)/shard_map/ppermute | solution.py:361
  8.2 6.6 %collective-permute-start.2 = (bf16[512,128]{1,0:T(8,128)(2,1)S(1)}, bf16[512,128]{1,0:T(8,128)(2,1)S(1)}, u32[]{:S(2)}, u32[]{:S(2)}) collective-permute-start(bf16[512,128]{1,0:T(8,128)(2,1)S(1)} %get-tuple-element.38), channel_id=1, source_target_pairs={{0,16},{4,20},{8,24},{12,28},{16,0},{20,4},{24,8},{28,12},{1,17},{... | collective-permute-start | bytes 393224 | tf_op jit(solution)/shard_map/ppermute | solution.py:361
  8.7 6.4 %collective-permute-start.3 = (bf16[512,128]{1,0:T(8,128)(2,1)S(1)}, bf16[512,128]{1,0:T(8,128)(2,1)S(1)}, u32[]{:S(2)}, u32[]{:S(2)}) collective-permute-start(bf16[512,128]{1,0:T(8,128)(2,1)S(1)} %get-tuple-element.37), channel_id=1, source_target_pairs={{0,8},{4,12},{8,0},{12,4},{16,24},{20,28},{24,16},{28,20},{1,9},{5... | collective-permute-start | bytes 393224 | tf_op jit(solution)/shard_map/ppermute | solution.py:361
  8.9 24.7 %copy-start.6 = (s32[4,10]{1,0:T(4,128)S(1)}, s32[4,10]{1,0:T(4,128)}, u32[]{:S(2)}) copy-start(s32[4,10]{1,0:T(4,128)} %lists.4) | copy-start | bytes 484
  15.2 5.2 %collective-permute-start.5 = (bf16[4,32,128]{2,1,0:T(8,128)(2,1)S(1)}, bf16[4,32,128]{2,1,0:T(8,128)(2,1)S(1)}, u32[]{:S(2)}, u32[]{:S(2)}) collective-permute-start(bf16[4,32,128]{2,1,0:T(8,128)(2,1)S(1)} %get-tuple-element.45), channel_id=1, source_target_pairs={{0,2},{1,3},{2,0},{3,1},{4,6},{5,7},{6,4},{7,5},{8,10},{9,11},{10,... | collective-permute-start | bytes 98312 | tf_op jit(solution)/shard_map/ppermute | solution.py:364
  17.8 5.7 %collective-permute-start.6 = (bf16[4,32,128]{2,1,0:T(8,128)(2,1)S(1)}, bf16[4,32,128]{2,1,0:T(8,128)(2,1)S(1)}, u32[]{:S(2)}, u32[]{:S(2)}) collective-permute-start(bf16[4,32,128]{2,1,0:T(8,128)(2,1)S(1)} %get-tuple-element.44), channel_id=1, source_target_pairs={{0,3},{1,2},{2,1},{3,0},{4,7},{5,6},{6,5},{7,4},{8,11},{9,10},{10,... | collective-permute-start | bytes 98312 | tf_op jit(solution)/shard_map/ppermute | solution.py:364
  19.2 4.4 %collective-permute-start.4 = (bf16[4,32,128]{2,1,0:T(8,128)(2,1)S(1)}, bf16[4,32,128]{2,1,0:T(8,128)(2,1)S(1)}, u32[]{:S(2)}, u32[]{:S(2)}) collective-permute-start(bf16[4,32,128]{2,1,0:T(8,128)(2,1)S(1)} %get-tuple-element.46), channel_id=1, source_target_pairs={{0,1},{1,0},{2,3},{3,2},{4,5},{5,4},{6,7},{7,6},{8,9},{9,8},{10,11... | collective-permute-start | bytes 98312 | tf_op jit(solution)/shard_map/ppermute | solution.py:364
  23.6 6.3 %collective-permute-start.10 = (bf16[4,128,128]{2,1,0:T(8,128)(2,1)S(1)}, bf16[4,128,128]{2,1,0:T(8,128)(2,1)S(1)}, u32[]{:S(2)}, u32[]{:S(2)}) collective-permute-start(bf16[4,128,128]{2,1,0:T(8,128)(2,1)S(1)} %pad_maximum_fusion.refs_0_), channel_id=1, source_target_pairs={{0,16},{4,20},{8,24},{12,28},{16,0},{20,4},{24,8},{28,12},{1,17},{... | collective-permute-start | bytes 393224 | tf_op jit(solution)/shard_map/ppermute | solution.py:361
  25.1 6.0 %collective-permute-start.12 = (bf16[4,128,128]{2,1,0:T(8,128)(2,1)S(1)}, bf16[4,128,128]{2,1,0:T(8,128)(2,1)S(1)}, u32[]{:S(2)}, u32[]{:S(2)}) collective-permute-start(bf16[4,128,128]{2,1,0:T(8,128)(2,1)S(1)} %pad_maximum_fusion.refs_0_), channel_id=1, source_target_pairs={{0,24},{4,28},{8,16},{12,20},{16,8},{20,12},{24,0},{28,4},{1,25},{... | collective-permute-start | bytes 393224 | tf_op jit(solution)/shard_map/ppermute | solution.py:361
  26.6 5.0 %collective-permute-start.8 = (bf16[4,128,128]{2,1,0:T(8,128)(2,1)S(1)}, bf16[4,128,128]{2,1,0:T(8,128)(2,1)S(1)}, u32[]{:S(2)}, u32[]{:S(2)}) collective-permute-start(bf16[4,128,128]{2,1,0:T(8,128)(2,1)S(1)} %pad_maximum_fusion.refs_0_), channel_id=1, source_target_pairs={{0,8},{4,12},{8,0},{12,4},{16,24},{20,28},{24,16},{28,20},{1,9},{5... | collective-permute-start | bytes 393224 | tf_op jit(solution)/shard_map/ppermute | solution.py:361
  27.1 6.4 %collective-permute-start.7 = (bf16[4,128,128]{2,1,0:T(8,128)(2,1)S(1)}, bf16[4,128,128]{2,1,0:T(8,128)(2,1)S(1)}, u32[]{:S(2)}, u32[]{:S(2)}) collective-permute-start(bf16[4,128,128]{2,1,0:T(8,128)(2,1)S(1)} %pad_maximum_fusion.refs_0_), channel_id=1, source_target_pairs={{0,4},{4,0},{8,12},{12,8},{16,20},{20,16},{24,28},{28,24},{1,5},{5... | collective-permute-start | bytes 393224 | tf_op jit(solution)/shard_map/ppermute | solution.py:358
  29.8 3.7 %collective-permute-start.11 = (bf16[4,128,128]{2,1,0:T(8,128)(2,1)S(1)}, bf16[4,128,128]{2,1,0:T(8,128)(2,1)S(1)}, u32[]{:S(2)}, u32[]{:S(2)}) collective-permute-start(bf16[4,128,128]{2,1,0:T(8,128)(2,1)S(1)} %collective-permute-done.10.refs_4_), channel_id=1, source_target_pairs={{0,4},{4,0},{8,12},{12,8},{16,20},{20,16},{24,28},{28,24},{1,5},{5... | collective-permute-start | bytes 393224 | tf_op jit(solution)/shard_map/ppermute | solution.py:358
  31.1 2.5 %collective-permute-start.13 = (bf16[4,128,128]{2,1,0:T(8,128)(2,1)S(1)}, bf16[4,128,128]{2,1,0:T(8,128)(2,1)S(1)}, u32[]{:S(2)}, u32[]{:S(2)}) collective-permute-start(bf16[4,128,128]{2,1,0:T(8,128)(2,1)S(1)} %collective-permute-done.12.refs_6_), channel_id=1, source_target_pairs={{0,4},{4,0},{8,12},{12,8},{16,20},{20,16},{24,28},{28,24},{1,5},{5... | collective-permute-start | bytes 393224 | tf_op jit(solution)/shard_map/ppermute | solution.py:358
  31.6 1.9 %collective-permute-start.9 = (bf16[4,128,128]{2,1,0:T(8,128)(2,1)S(1)}, bf16[4,128,128]{2,1,0:T(8,128)(2,1)S(1)}, u32[]{:S(2)}, u32[]{:S(2)}) collective-permute-start(bf16[4,128,128]{2,1,0:T(8,128)(2,1)S(1)} %collective-permute-done.8.refs_2_), channel_id=1, source_target_pairs={{0,4},{4,0},{8,12},{12,8},{16,20},{20,16},{24,28},{28,24},{1,5},{5... | collective-permute-start | bytes 393224 | tf_op jit(solution)/shard_map/ppermute | solution.py:358
  31.6 18.0 %collective-permute-start.20 = (bf16[4,10,32,128]{3,2,1,0:T(8,128)(2,1)S(1)}, bf16[4,10,32,128]{3,2,1,0:T(8,128)(2,1)S(1)}, u32[]{:S(2)}, u32[]{:S(2)}) collective-permute-start(bf16[4,10,32,128]{3,2,1,0:T(8,128)(2,1)S(1)} %copy-done.2), channel_id=1, source_target_pairs={{0,2},{1,3},{2,0},{3,1},{4,6},{5,7},{6,4},{7,5},{8,10},{9,11},{10,... | collective-permute-start | bytes 983048 | tf_op jit(solution)/shard_map/ppermute | solution.py:364
  34.9 19.4 %collective-permute-start.17 = (bf16[2,128,512]{2,1,0:T(8,128)(2,1)S(1)}, bf16[2,128,512]{2,1,0:T(8,128)(2,1)S(1)}, u32[]{:S(2)}, u32[]{:S(2)}) collective-permute-start(bf16[2,128,512]{2,1,0:T(8,128)(2,1)S(1)} %get-tuple-element.25), channel_id=1, source_target_pairs={{0,1},{3,2},{4,5},{7,6},{8,9},{11,10},{12,13},{15,14},{16,17},{19,... | collective-permute-start | bytes 786440 | tf_op jit(solution)/shard_map/ppermute | solution.py:367
  38.8 18.3 %collective-permute-start.19 = (bf16[4,10,32,128]{3,2,1,0:T(8,128)(2,1)S(1)}, bf16[4,10,32,128]{3,2,1,0:T(8,128)(2,1)S(1)}, u32[]{:S(2)}, u32[]{:S(2)}) collective-permute-start(bf16[4,10,32,128]{3,2,1,0:T(8,128)(2,1)S(1)} %copy-done.2), channel_id=1, source_target_pairs={{0,1},{1,0},{2,3},{3,2},{4,5},{5,4},{6,7},{7,6},{8,9},{9,8},{10,11... | collective-permute-start | bytes 983048 | tf_op jit(solution)/shard_map/ppermute | solution.py:364
  38.9 19.0 %collective-permute-start.21 = (bf16[4,10,32,128]{3,2,1,0:T(8,128)(2,1)S(1)}, bf16[4,10,32,128]{3,2,1,0:T(8,128)(2,1)S(1)}, u32[]{:S(2)}, u32[]{:S(2)}) collective-permute-start(bf16[4,10,32,128]{3,2,1,0:T(8,128)(2,1)S(1)} %copy-done.2), channel_id=1, source_target_pairs={{1,2},{2,1},{5,6},{6,5},{9,10},{10,9},{13,14},{14,13},{17,18},{18,... | collective-permute-start | bytes 983048 | tf_op jit(solution)/shard_map/ppermute | solution.py:367
  49.6 13.7 %collective-permute-start.22 = (bf16[4,10,32,128]{3,2,1,0:T(8,128)(2,1)S(1)}, bf16[4,10,32,128]{3,2,1,0:T(8,128)(2,1)S(1)}, u32[]{:S(2)}, u32[]{:S(2)}) collective-permute-start(bf16[4,10,32,128]{3,2,1,0:T(8,128)(2,1)S(1)} %collective-permute-done.20.refs_2_), channel_id=1, source_target_pairs={{1,0},{2,3},{5,4},{6,7},{9,8},{10,11},{13,12},{14,15},{17,16},{18,... | collective-permute-start | bytes 983048 | tf_op jit(solution)/shard_map/ppermute | solution.py:367
  50.9 12.4 %copy-start.7 = (s32[4]{0:T(128)S(1)}, s32[4]{0:T(128)}, u32[]{:S(2)}) copy-start(s32[4]{0:T(128)} %counts.7) | copy-start | bytes 52
  51.6 16.3 %collective-permute-start.14 = (bf16[2,128,512]{2,1,0:T(8,128)(2,1)S(1)}, bf16[2,128,512]{2,1,0:T(8,128)(2,1)S(1)}, u32[]{:S(2)}, u32[]{:S(2)}) collective-permute-start(bf16[2,128,512]{2,1,0:T(8,128)(2,1)S(1)} %get-tuple-element.23), channel_id=1, source_target_pairs={{0,1},{1,0},{2,3},{3,2},{4,5},{5,4},{6,7},{7,6},{8,9},{9,8},{10,11... | collective-permute-start | bytes 786440 | tf_op jit(solution)/shard_map/ppermute | solution.py:364
  54.3 13.6 %collective-permute-start.15 = (bf16[2,128,512]{2,1,0:T(8,128)(2,1)S(1)}, bf16[2,128,512]{2,1,0:T(8,128)(2,1)S(1)}, u32[]{:S(2)}, u32[]{:S(2)}) collective-permute-start(bf16[2,128,512]{2,1,0:T(8,128)(2,1)S(1)} %get-tuple-element.24), channel_id=1, source_target_pairs={{0,2},{3,1},{4,6},{7,5},{8,10},{11,9},{12,14},{15,13},{16,18},{19,... | collective-permute-start | bytes 786440 | tf_op jit(solution)/shard_map/ppermute | solution.py:367
  57.1 19.3 %copy-start.1 = (bf16[1,128,4096]{2,1,0:T(8,128)(2,1)S(1)}, bf16[1,128,4096]{2,1,0:T(8,128)(2,1)}, u32[]{:S(2)}) copy-start(bf16[1,128,4096]{2,1,0:T(8,128)(2,1)} %param.11) | copy-start | bytes 3145732
  57.1 19.3 %copy-start.5 = (s32[4,10]{1,0:T(4,128)S(1)}, s32[4,10]{1,0:T(4,128)}, u32[]{:S(2)}) copy-start(s32[4,10]{1,0:T(4,128)} %lists.7) | copy-start | bytes 484
  57.1 10.8 %collective-permute-start.16 = (bf16[2,128,512]{2,1,0:T(8,128)(2,1)S(1)}, bf16[2,128,512]{2,1,0:T(8,128)(2,1)S(1)}, u32[]{:S(2)}, u32[]{:S(2)}) collective-permute-start(bf16[2,128,512]{2,1,0:T(8,128)(2,1)S(1)} %get-tuple-element.25), channel_id=1, source_target_pairs={{1,2},{2,1},{5,6},{6,5},{9,10},{10,9},{13,14},{14,13},{17,18},{18,... | collective-permute-start | bytes 786440 | tf_op jit(solution)/shard_map/ppermute | solution.py:367
  57.9 18.4 %collective-permute-start.18 = (bf16[2,128,512]{2,1,0:T(8,128)(2,1)S(1)}, bf16[2,128,512]{2,1,0:T(8,128)(2,1)S(1)}, u32[]{:S(2)}, u32[]{:S(2)}) collective-permute-start(bf16[2,128,512]{2,1,0:T(8,128)(2,1)S(1)} %add_convert_fusion.1), channel_id=1, source_target_pairs={{2,0},{1,3},{6,4},{5,7},{10,8},{9,11},{14,12},{13,15},{18,16},{17,... | collective-permute-start | bytes 786440 | tf_op jit(solution)/shard_map/ppermute | solution.py:367
  77.9 2.0 %collective-permute-start.27 = (bf16[4,4,128,128]{3,2,1,0:T(8,128)(2,1)S(1)}, bf16[4,4,128,128]{3,2,1,0:T(8,128)(2,1)S(1)}, u32[]{:S(2)}, u32[]{:S(2)}) collective-permute-start(bf16[4,4,128,128]{3,2,1,0:T(8,128)(2,1)S(1)} %get-tuple-element.29), channel_id=1, source_target_pairs={{0,4},{4,0},{8,12},{12,8},{16,20},{20,16},{24,28},{28,24},{1,5},{5... | collective-permute-start | bytes 1572872 | tf_op jit(solution)/shard_map/ppermute | solution.py:358
  80.2 6.1 %collective-permute-start.28 = (bf16[4,128,128]{2,1,0:T(8,128)(2,1)S(1)}, bf16[4,128,128]{2,1,0:T(8,128)(2,1)S(1)}, u32[]{:S(2)}, u32[]{:S(2)}) collective-permute-start(bf16[4,128,128]{2,1,0:T(8,128)(2,1)S(1)} %get-tuple-element.40), channel_id=1, source_target_pairs={{0,8},{4,12},{8,0},{12,4},{16,24},{20,28},{24,16},{28,20},{1,9},{5... | collective-permute-start | bytes 393224 | tf_op jit(solution)/shard_map/ppermute | solution.py:361
  81.6 8.1 %collective-permute-start.29 = (bf16[4,128,128]{2,1,0:T(8,128)(2,1)S(1)}, bf16[4,128,128]{2,1,0:T(8,128)(2,1)S(1)}, u32[]{:S(2)}, u32[]{:S(2)}) collective-permute-start(bf16[4,128,128]{2,1,0:T(8,128)(2,1)S(1)} %get-tuple-element.42), channel_id=1, source_target_pairs={{0,16},{4,20},{8,24},{12,28},{16,0},{20,4},{24,8},{28,12},{1,17},{... | collective-permute-start | bytes 393224 | tf_op jit(solution)/shard_map/ppermute | solution.py:361
  82.1 7.6 %collective-permute-start.30 = (bf16[4,128,128]{2,1,0:T(8,128)(2,1)S(1)}, bf16[4,128,128]{2,1,0:T(8,128)(2,1)S(1)}, u32[]{:S(2)}, u32[]{:S(2)}) collective-permute-start(bf16[4,128,128]{2,1,0:T(8,128)(2,1)S(1)} %get-tuple-element.41), channel_id=1, source_target_pairs={{0,24},{4,28},{8,16},{12,20},{16,8},{20,12},{24,0},{28,4},{1,25},{... | collective-permute-start | bytes 393224 | tf_op jit(solution)/shard_map/ppermute | solution.py:361
  83.7 19.3 %collective-permute-start.24 = (bf16[320,512]{1,0:T(8,128)(2,1)S(1)}, bf16[320,512]{1,0:T(8,128)(2,1)S(1)}, u32[]{:S(2)}, u32[]{:S(2)}) collective-permute-start(bf16[320,512]{1,0:T(8,128)(2,1)S(1)} %get-tuple-element.27), channel_id=1, source_target_pairs={{0,2},{1,3},{2,0},{3,1},{4,6},{5,7},{6,4},{7,5},{8,10},{9,11},{10,... | collective-permute-start | bytes 983048 | tf_op jit(solution)/shard_map/ppermute | solution.py:364
  89.8 15.9 %collective-permute-start.41 = (bf16[4,128,128]{2,1,0:T(8,128)(2,1)S(1)}, bf16[4,128,128]{2,1,0:T(8,128)(2,1)S(1)}, u32[]{:S(2)}, u32[]{:S(2)}) collective-permute-start(bf16[4,128,128]{2,1,0:T(8,128)(2,1)S(1)} %fusion.4.refs_0_), channel_id=1, source_target_pairs={{0,2},{1,3},{2,0},{3,1},{4,6},{5,7},{6,4},{7,5},{8,10},{9,11},{10,... | collective-permute-start | bytes 393224 | tf_op jit(solution)/shard_map/ppermute | solution.py:364
  89.9 17.3 %collective-permute-start.32 = (bf16[4,128,128]{2,1,0:T(8,128)(2,1)S(1)}, bf16[4,128,128]{2,1,0:T(8,128)(2,1)S(1)}, u32[]{:S(2)}, u32[]{:S(2)}) collective-permute-start(bf16[4,128,128]{2,1,0:T(8,128)(2,1)S(1)} %fusion.4.refs_0_), channel_id=1, source_target_pairs={{0,8},{4,12},{8,0},{12,4},{16,24},{20,28},{24,16},{28,20},{1,9},{5... | collective-permute-start | bytes 393224 | tf_op jit(solution)/shard_map/ppermute | solution.py:361
  90.5 17.3 %collective-permute-start.34 = (bf16[4,128,128]{2,1,0:T(8,128)(2,1)S(1)}, bf16[4,128,128]{2,1,0:T(8,128)(2,1)S(1)}, u32[]{:S(2)}, u32[]{:S(2)}) collective-permute-start(bf16[4,128,128]{2,1,0:T(8,128)(2,1)S(1)} %fusion.4.refs_0_), channel_id=1, source_target_pairs={{0,16},{4,20},{8,24},{12,28},{16,0},{20,4},{24,8},{28,12},{1,17},{... | collective-permute-start | bytes 393224 | tf_op jit(solution)/shard_map/ppermute | solution.py:361
  92.0 17.2 %collective-permute-start.36 = (bf16[4,128,128]{2,1,0:T(8,128)(2,1)S(1)}, bf16[4,128,128]{2,1,0:T(8,128)(2,1)S(1)}, u32[]{:S(2)}, u32[]{:S(2)}) collective-permute-start(bf16[4,128,128]{2,1,0:T(8,128)(2,1)S(1)} %fusion.4.refs_0_), channel_id=1, source_target_pairs={{0,24},{4,28},{8,16},{12,20},{16,8},{20,12},{24,0},{28,4},{1,25},{... | collective-permute-start | bytes 393224 | tf_op jit(solution)/shard_map/ppermute | solution.py:361
  103.0 6.2 %collective-permute-start.31 = (bf16[4,128,128]{2,1,0:T(8,128)(2,1)S(1)}, bf16[4,128,128]{2,1,0:T(8,128)(2,1)S(1)}, u32[]{:S(2)}, u32[]{:S(2)}) collective-permute-start(bf16[4,128,128]{2,1,0:T(8,128)(2,1)S(1)} %fusion.4.refs_0_), channel_id=1, source_target_pairs={{0,4},{4,0},{8,12},{12,8},{16,20},{20,16},{24,28},{28,24},{1,5},{5... | collective-permute-start | bytes 393224 | tf_op jit(solution)/shard_map/ppermute | solution.py:358
  105.7 5.9 %collective-permute-start.43 = (bf16[4,128,128]{2,1,0:T(8,128)(2,1)S(1)}, bf16[4,128,128]{2,1,0:T(8,128)(2,1)S(1)}, u32[]{:S(2)}, u32[]{:S(2)}) collective-permute-start(bf16[4,128,128]{2,1,0:T(8,128)(2,1)S(1)} %collective-permute-done.41.refs_8_), channel_id=1, source_target_pairs={{0,8},{4,12},{8,0},{12,4},{16,24},{20,28},{24,16},{28,20},{1,9},{5... | collective-permute-start | bytes 393224 | tf_op jit(solution)/shard_map/ppermute | solution.py:361
  107.1 7.9 %collective-permute-start.45 = (bf16[4,128,128]{2,1,0:T(8,128)(2,1)S(1)}, bf16[4,128,128]{2,1,0:T(8,128)(2,1)S(1)}, u32[]{:S(2)}, u32[]{:S(2)}) collective-permute-start(bf16[4,128,128]{2,1,0:T(8,128)(2,1)S(1)} %collective-permute-done.41.refs_8_), channel_id=1, source_target_pairs={{0,16},{4,20},{8,24},{12,28},{16,0},{20,4},{24,8},{28,12},{1,17},{... | collective-permute-start | bytes 393224 | tf_op jit(solution)/shard_map/ppermute | solution.py:361
  107.9 7.2 %collective-permute-start.47 = (bf16[4,128,128]{2,1,0:T(8,128)(2,1)S(1)}, bf16[4,128,128]{2,1,0:T(8,128)(2,1)S(1)}, u32[]{:S(2)}, u32[]{:S(2)}) collective-permute-start(bf16[4,128,128]{2,1,0:T(8,128)(2,1)S(1)} %collective-permute-done.41.refs_8_), channel_id=1, source_target_pairs={{0,24},{4,28},{8,16},{12,20},{16,8},{20,12},{24,0},{28,4},{1,25},{... | collective-permute-start | bytes 393224 | tf_op jit(solution)/shard_map/ppermute | solution.py:361
  109.2 6.4 %collective-permute-start.33 = (bf16[4,128,128]{2,1,0:T(8,128)(2,1)S(1)}, bf16[4,128,128]{2,1,0:T(8,128)(2,1)S(1)}, u32[]{:S(2)}, u32[]{:S(2)}) collective-permute-start(bf16[4,128,128]{2,1,0:T(8,128)(2,1)S(1)} %collective-permute-done.32.refs_2_), channel_id=1, source_target_pairs={{0,4},{4,0},{8,12},{12,8},{16,20},{20,16},{24,28},{28,24},{1,5},{5... | collective-permute-start | bytes 393224 | tf_op jit(solution)/shard_map/ppermute | solution.py:358
  109.2 6.4 %collective-permute-start.35 = (bf16[4,128,128]{2,1,0:T(8,128)(2,1)S(1)}, bf16[4,128,128]{2,1,0:T(8,128)(2,1)S(1)}, u32[]{:S(2)}, u32[]{:S(2)}) collective-permute-start(bf16[4,128,128]{2,1,0:T(8,128)(2,1)S(1)} %collective-permute-done.34.refs_4_), channel_id=1, source_target_pairs={{0,4},{4,0},{8,12},{12,8},{16,20},{20,16},{24,28},{28,24},{1,5},{5... | collective-permute-start | bytes 393224 | tf_op jit(solution)/shard_map/ppermute | solution.py:358
  111.6 4.5 %collective-permute-start.37 = (bf16[4,128,128]{2,1,0:T(8,128)(2,1)S(1)}, bf16[4,128,128]{2,1,0:T(8,128)(2,1)S(1)}, u32[]{:S(2)}, u32[]{:S(2)}) collective-permute-start(bf16[4,128,128]{2,1,0:T(8,128)(2,1)S(1)} %collective-permute-done.36.refs_6_), channel_id=1, source_target_pairs={{0,4},{4,0},{8,12},{12,8},{16,20},{20,16},{24,28},{28,24},{1,5},{5... | collective-permute-start | bytes 393224 | tf_op jit(solution)/shard_map/ppermute | solution.py:358
  115.1 1.3 collective-permute-start.42
  115.1 2.0 %collective-permute-start.44 = (bf16[4,128,128]{2,1,0:T(8,128)(2,1)S(1)}, bf16[4,128,128]{2,1,0:T(8,128)(2,1)S(1)}, u32[]{:S(2)}, u32[]{:S(2)}) collective-permute-start(bf16[4,128,128]{2,1,0:T(8,128)(2,1)S(1)} %collective-permute-done.43.refs_10_), channel_id=1, source_target_pairs={{0,4},{4,0},{8,12},{12,8},{16,20},{20,16},{24,28},{28,24},{1,5},{5... | collective-permute-start | bytes 393224 | tf_op jit(solution)/shard_map/ppermute | solution.py:358
  115.6 1.5 %collective-permute-start.46 = (bf16[4,128,128]{2,1,0:T(8,128)(2,1)S(1)}, bf16[4,128,128]{2,1,0:T(8,128)(2,1)S(1)}, u32[]{:S(2)}, u32[]{:S(2)}) collective-permute-start(bf16[4,128,128]{2,1,0:T(8,128)(2,1)S(1)} %collective-permute-done.45.refs_12_), channel_id=1, source_target_pairs={{0,4},{4,0},{8,12},{12,8},{16,20},{20,16},{24,28},{28,24},{1,5},{5... | collective-permute-start | bytes 393224 | tf_op jit(solution)/shard_map/ppermute | solution.py:358
  115.7 1.5 collective-permute-start.48
  116.1 11.4 %collective-permute-start.23 = (bf16[256,512]{1,0:T(8,128)(2,1)S(1)}, bf16[256,512]{1,0:T(8,128)(2,1)S(1)}, u32[]{:S(2)}, u32[]{:S(2)}) collective-permute-start(bf16[256,512]{1,0:T(8,128)(2,1)S(1)} %get-tuple-element.26.refs_1_), channel_id=1, source_target_pairs={{0,1},{1,0},{2,3},{3,2},{4,5},{5,4},{6,7},{7,6},{8,9},{9,8},{10,11... | collective-permute-start | bytes 786440 | tf_op jit(solution)/shard_map/ppermute | solution.py:364
  116.4 11.9 %collective-permute-start.25 = (bf16[256,512]{1,0:T(8,128)(2,1)S(1)}, bf16[256,512]{1,0:T(8,128)(2,1)S(1)}, u32[]{:S(2)}, u32[]{:S(2)}) collective-permute-start(bf16[256,512]{1,0:T(8,128)(2,1)S(1)} %get-tuple-element.26.refs_1_), channel_id=1, source_target_pairs={{1,2},{2,1},{5,6},{6,5},{9,10},{10,9},{13,14},{14,13},{17,18},{18,... | collective-permute-start | bytes 786440 | tf_op jit(solution)/shard_map/ppermute | solution.py:367
  118.5 29.0 %collective-permute-start.49 = (bf16[4,10,32,128]{3,2,1,0:T(8,128)(2,1)S(1)}, bf16[4,10,32,128]{3,2,1,0:T(8,128)(2,1)S(1)}, u32[]{:S(2)}, u32[]{:S(2)}) collective-permute-start(bf16[4,10,32,128]{3,2,1,0:T(8,128)(2,1)S(1)} %get-tuple-element.34), channel_id=1, source_target_pairs={{0,1},{1,0},{2,3},{3,2},{4,5},{5,4},{6,7},{7,6},{8,9},{9,8},{10,11... | collective-permute-start | bytes 983048 | tf_op jit(solution)/shard_map/ppermute | solution.py:364
  122.3 21.3 %collective-permute-start.26 = (bf16[256,512]{1,0:T(8,128)(2,1)S(1)}, bf16[256,512]{1,0:T(8,128)(2,1)S(1)}, u32[]{:S(2)}, u32[]{:S(2)}) collective-permute-start(bf16[256,512]{1,0:T(8,128)(2,1)S(1)} %slice.59), channel_id=1, source_target_pairs={{1,0},{2,3},{5,4},{6,7},{9,8},{10,11},{13,12},{14,15},{17,16},{18,... | collective-permute-start | bytes 786440 | tf_op jit(solution)/shard_map/ppermute | solution.py:367
  124.8 20.7 %collective-permute-start.38 = (bf16[128,512]{1,0:T(8,128)(2,1)S(1)}, bf16[128,512]{1,0:T(8,128)(2,1)S(1)}, u32[]{:S(2)}, u32[]{:S(2)}) collective-permute-start(bf16[128,512]{1,0:T(8,128)(2,1)S(1)} %shard_map.127.refs_6_), channel_id=1, source_target_pairs={{0,1},{1,0},{2,3},{3,2},{4,5},{5,4},{6,7},{7,6},{8,9},{9,8},{10,11... | collective-permute-start | bytes 393224 | tf_op jit(solution)/shard_map/ppermute | solution.py:364
  127.5 17.9 %collective-permute-start.39 = (bf16[128,512]{1,0:T(8,128)(2,1)S(1)}, bf16[128,512]{1,0:T(8,128)(2,1)S(1)}, u32[]{:S(2)}, u32[]{:S(2)}) collective-permute-start(bf16[128,512]{1,0:T(8,128)(2,1)S(1)} %shard_map.127.refs_6_), channel_id=1, source_target_pairs={{0,2},{1,3},{2,0},{3,1},{4,6},{5,7},{6,4},{7,5},{8,10},{9,11},{10,... | collective-permute-start | bytes 393224 | tf_op jit(solution)/shard_map/ppermute | solution.py:364
  128.4 17.1 %collective-permute-start.40 = (bf16[128,512]{1,0:T(8,128)(2,1)S(1)}, bf16[128,512]{1,0:T(8,128)(2,1)S(1)}, u32[]{:S(2)}, u32[]{:S(2)}) collective-permute-start(bf16[128,512]{1,0:T(8,128)(2,1)S(1)} %shard_map.127.refs_6_), channel_id=1, source_target_pairs={{0,3},{1,2},{2,1},{3,0},{4,7},{5,6},{6,5},{7,4},{8,11},{9,10},{10,... | collective-permute-start | bytes 393224 | tf_op jit(solution)/shard_map/ppermute | solution.py:364

commit v5 on v4

--- a/solution.py
+++ b/solution.py
@@ -16,14 +16,14 @@
 NT = (((1,), (1,)), ((), ()))
 
 
-def call(kernel, outs, scratch, smem, *args):
+def call(kernel, outs, scratch, smem, *args, space=VM):
     nbytes = sum(a.size * a.dtype.itemsize for a in args) + sum(
         o.size * o.dtype.itemsize for o in outs
     )
     return pl.pallas_call(
         kernel,
         out_shape=tuple(outs),
-        in_specs=[SM] * smem + [VM] * (len(args) - smem),
+        in_specs=[SM] * smem + [space] * (len(args) - smem),
         out_specs=tuple(VM for _ in outs),
         scratch_shapes=scratch,
         compiler_params=pltpu.CompilerParams(vmem_limit_bytes=16 << 20),
@@ -39,14 +39,20 @@
     return jnp.logical_or(z == 0, z == zs - 1)
 
 
-def turn_kernel(tin, *outs, pieces, nb, edge):
+def turn_kernel(source, *refs, pieces, nb, edge):
+    outs, tin, sems = refs[:2], refs[2], refs[3]
     d = lax.axis_index("dp")
+    copies = []
     for r in range(pieces):
-        out = outs[r % 2]
-        base = lax.bitwise_xor(d, r) * (nb * edge)
+        at = pl.ds(pl.multiple_of(lax.bitwise_xor(d, r) * (nb * edge), edge), nb * edge)
+        copies.append(pltpu.make_async_copy(source.at[:, at], tin.at[r], sems.at[r]))
+    for r in list(range(1, pieces, 2)) + list(range(0, pieces, 2)):
+        copies[r].start()
+    for r in list(range(1, pieces, 2)) + list(range(0, pieces, 2)):
+        copies[r].wait()
         for j in range(nb):
-            lanes = pl.ds(pl.multiple_of(base + j * edge, edge), edge)
-            out[r // 2, j * edge : (j + 1) * edge, :] = tin[:, lanes].T
+            lanes = slice(j * edge, (j + 1) * edge)
+            outs[r % 2][r // 2, lanes, :] = tin[r, :, lanes].T
 
 
 def relative_block(block, d, nb):
@@ -391,7 +397,14 @@
     downs = [down_blocks] + gather(down_blocks, down_blocks)
 
     half = sds((chips, nb * edge, tok))
-    kept, sent = call(functools.partial(turn_kernel, **dims), [half, half], [], 0, tin)
+    kept, sent = call(
+        functools.partial(turn_kernel, **dims),
+        [half, half],
+        [pltpu.VMEM((pieces, tok, nb * edge), BF16), pltpu.SemaphoreType.DMA((pieces,))],
+        0,
+        tin,
+        space=pl.BlockSpec(memory_space=pl.ANY),
+    )
     met = partner(sent)
     is_owner = owner == d
     own_chip = lax.bitwise_xor(owner // 2, d // 2)

time: 149 us -> 149 us (level)
  transfers between devices with their start and end apart: 50 -> 50, of which waited for: 23 -> 23; matrix products, arithmetic and copies ran while one was open for 0% -> 0% of each run, Pallas kernels for 6% -> 5%
where the time goes in v5:
time: 149 us
  waiting for transfers between devices  83.4 us (56%)
  starting transfers between devices  50.7 us (34%)
  Pallas kernels  10.7 us (7%)
  between operations  1.62 us (1%)
    ppermute x13, waiting for transfers between devices, shift(): return lax.ppermute(a, 'fsdp', [(i, i ^ s) for i in range(zs)])  32 us
    ppermute x8, waiting for transfers between devices, move(): return lax.ppermute(a, 'fsdp', pairs)  26.2 us
    ppermute x15, waiting for transfers between devices, chip_swap(): return lax.ppermute(a, 'dp', [(i, i ^ 2 * c) for i in range(pieces)])  22.1 us
    ppermute x15, starting transfers between devices, chip_swap(): return lax.ppermute(a, 'dp', [(i, i ^ 2 * c) for i in range(pieces)])  18.7 us
    ppermute x13, starting transfers between devices, shift(): return lax.ppermute(a, 'fsdp', [(i, i ^ s) for i in range(zs)])  17.2 us
    ppermute x8, starting transfers between devices, move(): return lax.ppermute(a, 'fsdp', pairs)  12.6 us
    pallas_call x9, Pallas kernels, call(): pl.pallas_call(kernel, out_shape=tuple(outs), in_specs=[SM] * smem + [spa...  10.7 us
    ppermute x14, waiting for transfers between devices, partner(): return lax.ppermute(a, 'dp', [(i, i ^ 1) for i in range(pieces)])  3.13 us
  transfers between devices with their start and end apart: 50, of which 23 were waited for; matrix products, arithmetic and copies ran while one was open for 0% of the time, Pallas kernels for 5%

profile of v5, /device:TPU:0, one launch (start us, length us, event | category | flops | bytes accessed | tf_op | source)
XLA Modules:
  0.0 149.0 jit_solution(1875949277185880597)
XLA Ops:
  0.6 1.2 copy-done
  1.9 0.9 shard_map.121
  2.8 0.6 collective-permute-start
  4.0 0.9 collective-permute-done
  5.0 3.9 %collective-permute-start.1 = (bf16[512,128]{1,0:T(8,128)(2,1)S(1)}, bf16[512,128]{1,0:T(8,128)(2,1)S(1)}, u32[]{:S(2)}, u32[]{:S(2)}) collective-permute-start(bf16[512,128]{1,0:T(8,128)(2,1)S(1)} %get-tuple-element.39), channel_id=1, source_target_pairs={{0,24},{4,28},{8,16},{12,20},{16,8},{20,12},{24,0},{28,4},{1,25},{... | collective-permute-start | bytes 393224 | tf_op jit(solution)/shard_map/ppermute | solution.py:367
  8.8 0.5 collective-permute-start.2
  9.5 3.3 %collective-permute-done.1 = bf16[512,128]{1,0:T(8,128)(2,1)S(1)} collective-permute-done((bf16[512,128]{1,0:T(8,128)(2,1)S(1)}, bf16[512,128]{1,0:T(8,128)(2,1)S(1)}, u32[]{:S(2)}, u32[]{:S(2)}) %collective-permute-start.1) | collective-permute-done | bytes 131104 | tf_op jit(solution)/shard_map/ppermute | solution.py:367
  12.8 2.6 %collective-permute-done.2 = bf16[512,128]{1,0:T(8,128)(2,1)S(1)} collective-permute-done((bf16[512,128]{1,0:T(8,128)(2,1)S(1)}, bf16[512,128]{1,0:T(8,128)(2,1)S(1)}, u32[]{:S(2)}, u32[]{:S(2)}) %collective-permute-start.2) | collective-permute-done | bytes 131104 | tf_op jit(solution)/shard_map/ppermute | solution.py:367
  15.8 2.7 %collective-permute-start.5 = (bf16[4,32,128]{2,1,0:T(8,128)(2,1)S(1)}, bf16[4,32,128]{2,1,0:T(8,128)(2,1)S(1)}, u32[]{:S(2)}, u32[]{:S(2)}) collective-permute-start(bf16[4,32,128]{2,1,0:T(8,128)(2,1)S(1)} %get-tuple-element.45), channel_id=1, source_target_pairs={{0,2},{1,3},{2,0},{3,1},{4,6},{5,7},{6,4},{7,5},{8,10},{9,11},{10,... | collective-permute-start | bytes 98312 | tf_op jit(solution)/shard_map/ppermute | solution.py:370
  18.4 1.3 collective-permute-start.6
  20.0 1.0 collective-permute-done.5
  21.0 3.2 %collective-permute-done.6 = bf16[4,32,128]{2,1,0:T(8,128)(2,1)S(1)} collective-permute-done((bf16[4,32,128]{2,1,0:T(8,128)(2,1)S(1)}, bf16[4,32,128]{2,1,0:T(8,128)(2,1)S(1)}, u32[]{:S(2)}, u32[]{:S(2)}) %collective-permute-start.6) | collective-permute-done | bytes 32800 | tf_op jit(solution)/shard_map/ppermute | solution.py:370
  24.2 1.5 %collective-permute-start.10 = (bf16[4,128,128]{2,1,0:T(8,128)(2,1)S(1)}, bf16[4,128,128]{2,1,0:T(8,128)(2,1)S(1)}, u32[]{:S(2)}, u32[]{:S(2)}) collective-permute-start(bf16[4,128,128]{2,1,0:T(8,128)(2,1)S(1)} %pad_maximum_fusion.refs_0_), channel_id=1, source_target_pairs={{0,16},{4,20},{8,24},{12,28},{16,0},{20,4},{24,8},{28,12},{1,17},{... | collective-permute-start | bytes 393224 | tf_op jit(solution)/shard_map/ppermute | solution.py:367
  25.7 1.5 %collective-permute-start.12 = (bf16[4,128,128]{2,1,0:T(8,128)(2,1)S(1)}, bf16[4,128,128]{2,1,0:T(8,128)(2,1)S(1)}, u32[]{:S(2)}, u32[]{:S(2)}) collective-permute-start(bf16[4,128,128]{2,1,0:T(8,128)(2,1)S(1)} %pad_maximum_fusion.refs_0_), channel_id=1, source_target_pairs={{0,24},{4,28},{8,16},{12,20},{16,8},{20,12},{24,0},{28,4},{1,25},{... | collective-permute-start | bytes 393224 | tf_op jit(solution)/shard_map/ppermute | solution.py:367
  27.2 0.5 collective-permute-start.8
  27.7 2.7 %collective-permute-done.10.refs_4_ = bf16[4,128,128]{2,1,0:T(8,128)(2,1)S(1)} collective-permute-done((bf16[4,128,128]{2,1,0:T(8,128)(2,1)S(1)}, bf16[4,128,128]{2,1,0:T(8,128)(2,1)S(1)}, u32[]{:S(2)}, u32[]{:S(2)}) %collective-permute-start.10) | collective-permute-done | bytes 131104 | tf_op jit(solution)/shard_map/ppermute | solution.py:367
  30.4 1.3 collective-permute-done.12.refs_6_
  31.7 0.5 collective-permute-done.8.refs_2_
  32.2 1.2 collective-permute-start.20
  33.4 0.7 shard_map.122.refs_8_.weights
  34.2 1.3 shard_map.123
  35.5 3.9 %collective-permute-start.17 = (bf16[2,128,512]{2,1,0:T(8,128)(2,1)S(1)}, bf16[2,128,512]{2,1,0:T(8,128)(2,1)S(1)}, u32[]{:S(2)}, u32[]{:S(2)}) collective-permute-start(bf16[2,128,512]{2,1,0:T(8,128)(2,1)S(1)} %get-tuple-element.25), channel_id=1, source_target_pairs={{0,1},{3,2},{4,5},{7,6},{8,9},{11,10},{12,13},{15,14},{16,17},{19,... | collective-permute-start | bytes 786440 | tf_op jit(solution)/shard_map/ppermute | solution.py:373
  39.5 0.7 collective-permute-start.21
  40.2 10.1 %collective-permute-done.20.refs_2_ = bf16[4,10,32,128]{3,2,1,0:T(8,128)(2,1)S(1)} collective-permute-done((bf16[4,10,32,128]{3,2,1,0:T(8,128)(2,1)S(1)}, bf16[4,10,32,128]{3,2,1,0:T(8,128)(2,1)S(1)}, u32[]{:S(2)}, u32[]{:S(2)}) %collective-permute-start.20) | collective-permute-done | bytes 327712 | tf_op jit(solution)/shard_map/ppermute | solution.py:370
  50.3 1.3 collective-permute-start.22
  51.6 0.6 shard_map.124
  52.2 2.7 %collective-permute-start.14 = (bf16[2,128,512]{2,1,0:T(8,128)(2,1)S(1)}, bf16[2,128,512]{2,1,0:T(8,128)(2,1)S(1)}, u32[]{:S(2)}, u32[]{:S(2)}) collective-permute-start(bf16[2,128,512]{2,1,0:T(8,128)(2,1)S(1)} %get-tuple-element.23), channel_id=1, source_target_pairs={{0,1},{1,0},{2,3},{3,2},{4,5},{5,4},{6,7},{7,6},{8,9},{9,8},{10,11... | collective-permute-start | bytes 786440 | tf_op jit(solution)/shard_map/ppermute | solution.py:370
  54.9 2.7 %collective-permute-start.15 = (bf16[2,128,512]{2,1,0:T(8,128)(2,1)S(1)}, bf16[2,128,512]{2,1,0:T(8,128)(2,1)S(1)}, u32[]{:S(2)}, u32[]{:S(2)}) collective-permute-start(bf16[2,128,512]{2,1,0:T(8,128)(2,1)S(1)} %get-tuple-element.24), channel_id=1, source_target_pairs={{0,2},{3,1},{4,6},{7,5},{8,10},{11,9},{12,14},{15,13},{16,18},{19,... | collective-permute-start | bytes 786440 | tf_op jit(solution)/shard_map/ppermute | solution.py:373
  57.7 0.8 collective-permute-start.16
  58.6 1.3 collective-permute-start.18
  59.9 4.1 %collective-permute-done.22.refs_4_ = bf16[4,10,32,128]{3,2,1,0:T(8,128)(2,1)S(1)} collective-permute-done((bf16[4,10,32,128]{3,2,1,0:T(8,128)(2,1)S(1)}, bf16[4,10,32,128]{3,2,1,0:T(8,128)(2,1)S(1)}, u32[]{:S(2)}, u32[]{:S(2)}) %collective-permute-start.22) | collective-permute-done | bytes 327712 | tf_op jit(solution)/shard_map/ppermute | solution.py:373
  64.0 0.9 shard_map.125.refs_5_.refs_8_
  64.9 3.6 %collective-permute-done.14.refs_1_ = bf16[2,128,512]{2,1,0:T(8,128)(2,1)S(1)} collective-permute-done((bf16[2,128,512]{2,1,0:T(8,128)(2,1)S(1)}, bf16[2,128,512]{2,1,0:T(8,128)(2,1)S(1)}, u32[]{:S(2)}, u32[]{:S(2)}) %collective-permute-start.14) | collective-permute-done | bytes 262176 | tf_op jit(solution)/shard_map/ppermute | solution.py:370
  68.5 8.5 %collective-permute-done.18.refs_4_ = bf16[2,128,512]{2,1,0:T(8,128)(2,1)S(1)} collective-permute-done((bf16[2,128,512]{2,1,0:T(8,128)(2,1)S(1)}, bf16[2,128,512]{2,1,0:T(8,128)(2,1)S(1)}, u32[]{:S(2)}, u32[]{:S(2)}) %collective-permute-start.18) | collective-permute-done | bytes 262176 | tf_op jit(solution)/shard_map/ppermute | solution.py:373
  77.0 1.5 %shard_map.126 = (bf16[2,128,128]{2,1,0:T(8,128)(2,1)S(1)}, bf16[256,512]{1,0:T(8,128)(2,1)S(1)}, bf16[320,512]{1,0:T(8,128)(2,1)S(1)}, f32[4,4,128,128]{3,2,1,0:T(8,128)S(1)}, bf16[4,4,128,128]{3,2,1,0:T(8,128)(2,1)S(1)}) custom-call(s32[1]{0:T(128)} %copy.15.owners, s32[4,10]{1,0:T(4,128)S(1)} %copy-done.5, f32[2,128,512]{2,1,0:T(8,128)S(1)} %get-tuple-element.22.refs_0_, ...), custom_call_target="tpu_custom_call" | custom-call | flops 134217728 | bytes 6160548 | tf_op jit(solution)/shard_map/pallas_call | solution.py:23
  78.6 1.9 %collective-permute-done.27 = bf16[4,4,128,128]{3,2,1,0:T(8,128)(2,1)S(1)} collective-permute-done((bf16[4,4,128,128]{3,2,1,0:T(8,128)(2,1)S(1)}, bf16[4,4,128,128]{3,2,1,0:T(8,128)(2,1)S(1)}, u32[]{:S(2)}, u32[]{:S(2)}) %collective-permute-start.27) | collective-permute-done | bytes 524320 | tf_op jit(solution)/shard_map/ppermute | solution.py:364
  80.8 1.5 %collective-permute-start.28 = (bf16[4,128,128]{2,1,0:T(8,128)(2,1)S(1)}, bf16[4,128,128]{2,1,0:T(8,128)(2,1)S(1)}, u32[]{:S(2)}, u32[]{:S(2)}) collective-permute-start(bf16[4,128,128]{2,1,0:T(8,128)(2,1)S(1)} %get-tuple-element.40), channel_id=1, source_target_pairs={{0,8},{4,12},{8,0},{12,4},{16,24},{20,28},{24,16},{28,20},{1,9},{5... | collective-permute-start | bytes 393224 | tf_op jit(solution)/shard_map/ppermute | solution.py:367
  82.8 1.6 %collective-permute-start.30 = (bf16[4,128,128]{2,1,0:T(8,128)(2,1)S(1)}, bf16[4,128,128]{2,1,0:T(8,128)(2,1)S(1)}, u32[]{:S(2)}, u32[]{:S(2)}) collective-permute-start(bf16[4,128,128]{2,1,0:T(8,128)(2,1)S(1)} %get-tuple-element.41), channel_id=1, source_target_pairs={{0,24},{4,28},{8,16},{12,20},{16,8},{20,12},{24,0},{28,4},{1,25},{... | collective-permute-start | bytes 393224 | tf_op jit(solution)/shard_map/ppermute | solution.py:367
  84.3 2.5 %collective-permute-done.28 = bf16[4,128,128]{2,1,0:T(8,128)(2,1)S(1)} collective-permute-done((bf16[4,128,128]{2,1,0:T(8,128)(2,1)S(1)}, bf16[4,128,128]{2,1,0:T(8,128)(2,1)S(1)}, u32[]{:S(2)}, u32[]{:S(2)}) %collective-permute-start.28) | collective-permute-done | bytes 131104 | tf_op jit(solution)/shard_map/ppermute | solution.py:367
  86.8 3.5 %collective-permute-done.29 = bf16[4,128,128]{2,1,0:T(8,128)(2,1)S(1)} collective-permute-done((bf16[4,128,128]{2,1,0:T(8,128)(2,1)S(1)}, bf16[4,128,128]{2,1,0:T(8,128)(2,1)S(1)}, u32[]{:S(2)}, u32[]{:S(2)}) %collective-permute-start.29) | collective-permute-done | bytes 131104 | tf_op jit(solution)/shard_map/ppermute | solution.py:367
  90.5 0.7 collective-permute-start.32
  91.2 1.5 collective-permute-start.34
  92.6 1.4 collective-permute-start.36
  94.0 9.6 %collective-permute-done.24.refs_3_.refs_17_ = bf16[320,512]{1,0:T(8,128)(2,1)S(1)} collective-permute-done((bf16[320,512]{1,0:T(8,128)(2,1)S(1)}, bf16[320,512]{1,0:T(8,128)(2,1)S(1)}, u32[]{:S(2)}, u32[]{:S(2)}) %collective-permute-start.24) | collective-permute-done | bytes 327712 | tf_op jit(solution)/shard_map/ppermute | solution.py:370
  103.6 2.7 %collective-permute-done.41.refs_8_ = bf16[4,128,128]{2,1,0:T(8,128)(2,1)S(1)} collective-permute-done((bf16[4,128,128]{2,1,0:T(8,128)(2,1)S(1)}, bf16[4,128,128]{2,1,0:T(8,128)(2,1)S(1)}, u32[]{:S(2)}, u32[]{:S(2)}) %collective-permute-start.41) | collective-permute-done | bytes 131104 | tf_op jit(solution)/shard_map/ppermute | solution.py:370
  106.3 1.4 collective-permute-start.43
  107.8 0.7 collective-permute-start.45
  108.5 1.4 collective-permute-start.47
  109.8 0.5 collective-permute-start.35
  110.4 1.9 %collective-permute-done.43.refs_10_ = bf16[4,128,128]{2,1,0:T(8,128)(2,1)S(1)} collective-permute-done((bf16[4,128,128]{2,1,0:T(8,128)(2,1)S(1)}, bf16[4,128,128]{2,1,0:T(8,128)(2,1)S(1)}, u32[]{:S(2)}, u32[]{:S(2)}) %collective-permute-start.43) | collective-permute-done | bytes 131104 | tf_op jit(solution)/shard_map/ppermute | solution.py:367
  112.2 3.5 %collective-permute-done.45.refs_12_ = bf16[4,128,128]{2,1,0:T(8,128)(2,1)S(1)} collective-permute-done((bf16[4,128,128]{2,1,0:T(8,128)(2,1)S(1)}, bf16[4,128,128]{2,1,0:T(8,128)(2,1)S(1)}, u32[]{:S(2)}, u32[]{:S(2)}) %collective-permute-start.45) | collective-permute-done | bytes 131104 | tf_op jit(solution)/shard_map/ppermute | solution.py:367
  115.7 0.5 collective-permute-start.44
  117.1 0.7 collective-permute-start.25
  117.8 1.3 shard_map.129
  119.1 3.7 %collective-permute-start.49 = (bf16[4,10,32,128]{3,2,1,0:T(8,128)(2,1)S(1)}, bf16[4,10,32,128]{3,2,1,0:T(8,128)(2,1)S(1)}, u32[]{:S(2)}, u32[]{:S(2)}) collective-permute-start(bf16[4,10,32,128]{3,2,1,0:T(8,128)(2,1)S(1)} %get-tuple-element.34), channel_id=1, source_target_pairs={{0,1},{1,0},{2,3},{3,2},{4,5},{5,4},{6,7},{7,6},{8,9},{9,8},{10,11... | collective-permute-start | bytes 983048 | tf_op jit(solution)/shard_map/ppermute | solution.py:370
  122.9 1.3 collective-permute-start.26
  124.2 1.3 shard_map.127.refs_6_
  125.4 2.7 %collective-permute-start.38 = (bf16[128,512]{1,0:T(8,128)(2,1)S(1)}, bf16[128,512]{1,0:T(8,128)(2,1)S(1)}, u32[]{:S(2)}, u32[]{:S(2)}) collective-permute-start(bf16[128,512]{1,0:T(8,128)(2,1)S(1)} %shard_map.127.refs_6_), channel_id=1, source_target_pairs={{0,1},{1,0},{2,3},{3,2},{4,5},{5,4},{6,7},{7,6},{8,9},{9,8},{10,11... | collective-permute-start | bytes 393224 | tf_op jit(solution)/shard_map/ppermute | solution.py:370
  128.2 0.8 collective-permute-start.39
  129.0 1.6 %collective-permute-start.40 = (bf16[128,512]{1,0:T(8,128)(2,1)S(1)}, bf16[128,512]{1,0:T(8,128)(2,1)S(1)}, u32[]{:S(2)}, u32[]{:S(2)}) collective-permute-start(bf16[128,512]{1,0:T(8,128)(2,1)S(1)} %shard_map.127.refs_6_), channel_id=1, source_target_pairs={{0,3},{1,2},{2,1},{3,0},{4,7},{5,6},{6,5},{7,4},{8,11},{9,10},{10,... | collective-permute-start | bytes 393224 | tf_op jit(solution)/shard_map/ppermute | solution.py:370
  130.6 13.6 %collective-permute-done.26.refs_5_ = bf16[256,512]{1,0:T(8,128)(2,1)S(1)} collective-permute-done((bf16[256,512]{1,0:T(8,128)(2,1)S(1)}, bf16[256,512]{1,0:T(8,128)(2,1)S(1)}, u32[]{:S(2)}, u32[]{:S(2)}) %collective-permute-start.26) | collective-permute-done | bytes 262176 | tf_op jit(solution)/shard_map/ppermute | solution.py:373
  144.2 1.9 %collective-permute-done.38.refs_7_ = bf16[128,512]{1,0:T(8,128)(2,1)S(1)} collective-permute-done((bf16[128,512]{1,0:T(8,128)(2,1)S(1)}, bf16[128,512]{1,0:T(8,128)(2,1)S(1)}, u32[]{:S(2)}, u32[]{:S(2)}) %collective-permute-start.38) | collective-permute-done | bytes 131104 | tf_op jit(solution)/shard_map/ppermute | solution.py:370
  146.1 2.0 %shard_map.128 = (bf16[4,10,32,128]{3,2,1,0:T(8,128)(2,1)}, bf16[4,10,32,128]{3,2,1,0:T(8,128)(2,1)}) custom-call(s32[4]{0:T(128)S(1)} %copy-done.8, bf16[4,320,512]{2,1,0:T(8,128)(2,1)S(1)} %get-tuple-element.21.gathered.refs_0_, bf16[256,512]{1,0:T(8,128)(2,1)S(1)} %get-tuple-element.26.refs_1_, bf16[256,512]{1,0:T(8,128)(2,1)S(1)} %collective-permute-done.23.refs_2_, ...), custom_call_target="tpu_custom_call" | custom-call | flops 134217728 | bytes 3866640 | tf_op jit(solution)/shard_map/pallas_call | solution.py:23
  148.2 0.8 add_convert_fusion
  (73 shorter events, 2.8 us)
Async XLA Ops:
  0.6 1.2 copy-start
  2.8 2.1 %collective-permute-start = (bf16[4,512,128]{2,1,0:T(8,128)(2,1)S(1)}, bf16[4,512,128]{2,1,0:T(8,128)(2,1)S(1)}, u32[]{:S(2)}, u32[]{:S(2)}) collective-permute-start(bf16[4,512,128]{2,1,0:T(8,128)(2,1)S(1)} %get-tuple-element.20), channel_id=1, source_target_pairs={{0,4},{4,0},{8,12},{12,8},{16,20},{20,16},{24,28},{28,24},{1,5},{5... | collective-permute-start | bytes 1572872 | tf_op jit(solution)/shard_map/ppermute | solution.py:364
  4.9 27.4 %copy-start.2 = (bf16[4,10,32,128]{3,2,1,0:T(8,128)(2,1)S(1)}, bf16[4,10,32,128]{3,2,1,0:T(8,128)(2,1)}, u32[]{:S(2)}) copy-start(bf16[4,10,32,128]{3,2,1,0:T(8,128)(2,1)} %refs_0_.1) | copy-start | bytes 983044
  4.9 28.5 %copy-start.3 = (bf16[4,10,32,128]{3,2,1,0:T(8,128)(2,1)S(1)}, bf16[4,10,32,128]{3,2,1,0:T(8,128)(2,1)}, u32[]{:S(2)}) copy-start(bf16[4,10,32,128]{3,2,1,0:T(8,128)(2,1)} %gate.1) | copy-start | bytes 983044
  4.9 28.5 %copy-start.4 = (bf16[4,10,32,128]{3,2,1,0:T(8,128)(2,1)S(1)}, bf16[4,10,32,128]{3,2,1,0:T(8,128)(2,1)}, u32[]{:S(2)}) copy-start(bf16[4,10,32,128]{3,2,1,0:T(8,128)(2,1)} %up.1) | copy-start | bytes 983044
  4.9 28.5 %copy-start.8 = (s32[4]{0:T(128)S(1)}, s32[4]{0:T(128)}, u32[]{:S(2)}) copy-start(s32[4]{0:T(128)} %counts.6) | copy-start | bytes 52
  5.0 7.8 %collective-permute-start.1 = (bf16[512,128]{1,0:T(8,128)(2,1)S(1)}, bf16[512,128]{1,0:T(8,128)(2,1)S(1)}, u32[]{:S(2)}, u32[]{:S(2)}) collective-permute-start(bf16[512,128]{1,0:T(8,128)(2,1)S(1)} %get-tuple-element.39), channel_id=1, source_target_pairs={{0,24},{4,28},{8,16},{12,20},{16,8},{20,12},{24,0},{28,4},{1,25},{... | collective-permute-start | bytes 393224 | tf_op jit(solution)/shard_map/ppermute | solution.py:367
  8.8 6.6 %collective-permute-start.2 = (bf16[512,128]{1,0:T(8,128)(2,1)S(1)}, bf16[512,128]{1,0:T(8,128)(2,1)S(1)}, u32[]{:S(2)}, u32[]{:S(2)}) collective-permute-start(bf16[512,128]{1,0:T(8,128)(2,1)S(1)} %get-tuple-element.38), channel_id=1, source_target_pairs={{0,16},{4,20},{8,24},{12,28},{16,0},{20,4},{24,8},{28,12},{1,17},{... | collective-permute-start | bytes 393224 | tf_op jit(solution)/shard_map/ppermute | solution.py:367
  9.3 6.4 %collective-permute-start.3 = (bf16[512,128]{1,0:T(8,128)(2,1)S(1)}, bf16[512,128]{1,0:T(8,128)(2,1)S(1)}, u32[]{:S(2)}, u32[]{:S(2)}) collective-permute-start(bf16[512,128]{1,0:T(8,128)(2,1)S(1)} %get-tuple-element.37), channel_id=1, source_target_pairs={{0,8},{4,12},{8,0},{12,4},{16,24},{20,28},{24,16},{28,20},{1,9},{5... | collective-permute-start | bytes 393224 | tf_op jit(solution)/shard_map/ppermute | solution.py:367
  9.5 24.7 %copy-start.6 = (s32[4,10]{1,0:T(4,128)S(1)}, s32[4,10]{1,0:T(4,128)}, u32[]{:S(2)}) copy-start(s32[4,10]{1,0:T(4,128)} %lists.4) | copy-start | bytes 484
  15.8 5.2 %collective-permute-start.5 = (bf16[4,32,128]{2,1,0:T(8,128)(2,1)S(1)}, bf16[4,32,128]{2,1,0:T(8,128)(2,1)S(1)}, u32[]{:S(2)}, u32[]{:S(2)}) collective-permute-start(bf16[4,32,128]{2,1,0:T(8,128)(2,1)S(1)} %get-tuple-element.45), channel_id=1, source_target_pairs={{0,2},{1,3},{2,0},{3,1},{4,6},{5,7},{6,4},{7,5},{8,10},{9,11},{10,... | collective-permute-start | bytes 98312 | tf_op jit(solution)/shard_map/ppermute | solution.py:370
  18.4 5.7 %collective-permute-start.6 = (bf16[4,32,128]{2,1,0:T(8,128)(2,1)S(1)}, bf16[4,32,128]{2,1,0:T(8,128)(2,1)S(1)}, u32[]{:S(2)}, u32[]{:S(2)}) collective-permute-start(bf16[4,32,128]{2,1,0:T(8,128)(2,1)S(1)} %get-tuple-element.44), channel_id=1, source_target_pairs={{0,3},{1,2},{2,1},{3,0},{4,7},{5,6},{6,5},{7,4},{8,11},{9,10},{10,... | collective-permute-start | bytes 98312 | tf_op jit(solution)/shard_map/ppermute | solution.py:370
  19.8 4.4 %collective-permute-start.4 = (bf16[4,32,128]{2,1,0:T(8,128)(2,1)S(1)}, bf16[4,32,128]{2,1,0:T(8,128)(2,1)S(1)}, u32[]{:S(2)}, u32[]{:S(2)}) collective-permute-start(bf16[4,32,128]{2,1,0:T(8,128)(2,1)S(1)} %get-tuple-element.46), channel_id=1, source_target_pairs={{0,1},{1,0},{2,3},{3,2},{4,5},{5,4},{6,7},{7,6},{8,9},{9,8},{10,11... | collective-permute-start | bytes 98312 | tf_op jit(solution)/shard_map/ppermute | solution.py:370
  24.2 6.3 %collective-permute-start.10 = (bf16[4,128,128]{2,1,0:T(8,128)(2,1)S(1)}, bf16[4,128,128]{2,1,0:T(8,128)(2,1)S(1)}, u32[]{:S(2)}, u32[]{:S(2)}) collective-permute-start(bf16[4,128,128]{2,1,0:T(8,128)(2,1)S(1)} %pad_maximum_fusion.refs_0_), channel_id=1, source_target_pairs={{0,16},{4,20},{8,24},{12,28},{16,0},{20,4},{24,8},{28,12},{1,17},{... | collective-permute-start | bytes 393224 | tf_op jit(solution)/shard_map/ppermute | solution.py:367
  25.7 6.0 %collective-permute-start.12 = (bf16[4,128,128]{2,1,0:T(8,128)(2,1)S(1)}, bf16[4,128,128]{2,1,0:T(8,128)(2,1)S(1)}, u32[]{:S(2)}, u32[]{:S(2)}) collective-permute-start(bf16[4,128,128]{2,1,0:T(8,128)(2,1)S(1)} %pad_maximum_fusion.refs_0_), channel_id=1, source_target_pairs={{0,24},{4,28},{8,16},{12,20},{16,8},{20,12},{24,0},{28,4},{1,25},{... | collective-permute-start | bytes 393224 | tf_op jit(solution)/shard_map/ppermute | solution.py:367
  27.2 5.0 %collective-permute-start.8 = (bf16[4,128,128]{2,1,0:T(8,128)(2,1)S(1)}, bf16[4,128,128]{2,1,0:T(8,128)(2,1)S(1)}, u32[]{:S(2)}, u32[]{:S(2)}) collective-permute-start(bf16[4,128,128]{2,1,0:T(8,128)(2,1)S(1)} %pad_maximum_fusion.refs_0_), channel_id=1, source_target_pairs={{0,8},{4,12},{8,0},{12,4},{16,24},{20,28},{24,16},{28,20},{1,9},{5... | collective-permute-start | bytes 393224 | tf_op jit(solution)/shard_map/ppermute | solution.py:367
  27.7 6.4 %collective-permute-start.7 = (bf16[4,128,128]{2,1,0:T(8,128)(2,1)S(1)}, bf16[4,128,128]{2,1,0:T(8,128)(2,1)S(1)}, u32[]{:S(2)}, u32[]{:S(2)}) collective-permute-start(bf16[4,128,128]{2,1,0:T(8,128)(2,1)S(1)} %pad_maximum_fusion.refs_0_), channel_id=1, source_target_pairs={{0,4},{4,0},{8,12},{12,8},{16,20},{20,16},{24,28},{28,24},{1,5},{5... | collective-permute-start | bytes 393224 | tf_op jit(solution)/shard_map/ppermute | solution.py:364
  30.4 3.7 %collective-permute-start.11 = (bf16[4,128,128]{2,1,0:T(8,128)(2,1)S(1)}, bf16[4,128,128]{2,1,0:T(8,128)(2,1)S(1)}, u32[]{:S(2)}, u32[]{:S(2)}) collective-permute-start(bf16[4,128,128]{2,1,0:T(8,128)(2,1)S(1)} %collective-permute-done.10.refs_4_), channel_id=1, source_target_pairs={{0,4},{4,0},{8,12},{12,8},{16,20},{20,16},{24,28},{28,24},{1,5},{5... | collective-permute-start | bytes 393224 | tf_op jit(solution)/shard_map/ppermute | solution.py:364
  31.7 2.5 %collective-permute-start.13 = (bf16[4,128,128]{2,1,0:T(8,128)(2,1)S(1)}, bf16[4,128,128]{2,1,0:T(8,128)(2,1)S(1)}, u32[]{:S(2)}, u32[]{:S(2)}) collective-permute-start(bf16[4,128,128]{2,1,0:T(8,128)(2,1)S(1)} %collective-permute-done.12.refs_6_), channel_id=1, source_target_pairs={{0,4},{4,0},{8,12},{12,8},{16,20},{20,16},{24,28},{28,24},{1,5},{5... | collective-permute-start | bytes 393224 | tf_op jit(solution)/shard_map/ppermute | solution.py:364
  32.2 1.9 %collective-permute-start.9 = (bf16[4,128,128]{2,1,0:T(8,128)(2,1)S(1)}, bf16[4,128,128]{2,1,0:T(8,128)(2,1)S(1)}, u32[]{:S(2)}, u32[]{:S(2)}) collective-permute-start(bf16[4,128,128]{2,1,0:T(8,128)(2,1)S(1)} %collective-permute-done.8.refs_2_), channel_id=1, source_target_pairs={{0,4},{4,0},{8,12},{12,8},{16,20},{20,16},{24,28},{28,24},{1,5},{5... | collective-permute-start | bytes 393224 | tf_op jit(solution)/shard_map/ppermute | solution.py:364
  32.2 18.0 %collective-permute-start.20 = (bf16[4,10,32,128]{3,2,1,0:T(8,128)(2,1)S(1)}, bf16[4,10,32,128]{3,2,1,0:T(8,128)(2,1)S(1)}, u32[]{:S(2)}, u32[]{:S(2)}) collective-permute-start(bf16[4,10,32,128]{3,2,1,0:T(8,128)(2,1)S(1)} %copy-done.2), channel_id=1, source_target_pairs={{0,2},{1,3},{2,0},{3,1},{4,6},{5,7},{6,4},{7,5},{8,10},{9,11},{10,... | collective-permute-start | bytes 983048 | tf_op jit(solution)/shard_map/ppermute | solution.py:370
  35.5 19.4 %collective-permute-start.17 = (bf16[2,128,512]{2,1,0:T(8,128)(2,1)S(1)}, bf16[2,128,512]{2,1,0:T(8,128)(2,1)S(1)}, u32[]{:S(2)}, u32[]{:S(2)}) collective-permute-start(bf16[2,128,512]{2,1,0:T(8,128)(2,1)S(1)} %get-tuple-element.25), channel_id=1, source_target_pairs={{0,1},{3,2},{4,5},{7,6},{8,9},{11,10},{12,13},{15,14},{16,17},{19,... | collective-permute-start | bytes 786440 | tf_op jit(solution)/shard_map/ppermute | solution.py:373
  39.4 18.3 %collective-permute-start.19 = (bf16[4,10,32,128]{3,2,1,0:T(8,128)(2,1)S(1)}, bf16[4,10,32,128]{3,2,1,0:T(8,128)(2,1)S(1)}, u32[]{:S(2)}, u32[]{:S(2)}) collective-permute-start(bf16[4,10,32,128]{3,2,1,0:T(8,128)(2,1)S(1)} %copy-done.2), channel_id=1, source_target_pairs={{0,1},{1,0},{2,3},{3,2},{4,5},{5,4},{6,7},{7,6},{8,9},{9,8},{10,11... | collective-permute-start | bytes 983048 | tf_op jit(solution)/shard_map/ppermute | solution.py:370
  39.5 19.0 %collective-permute-start.21 = (bf16[4,10,32,128]{3,2,1,0:T(8,128)(2,1)S(1)}, bf16[4,10,32,128]{3,2,1,0:T(8,128)(2,1)S(1)}, u32[]{:S(2)}, u32[]{:S(2)}) collective-permute-start(bf16[4,10,32,128]{3,2,1,0:T(8,128)(2,1)S(1)} %copy-done.2), channel_id=1, source_target_pairs={{1,2},{2,1},{5,6},{6,5},{9,10},{10,9},{13,14},{14,13},{17,18},{18,... | collective-permute-start | bytes 983048 | tf_op jit(solution)/shard_map/ppermute | solution.py:373
  50.3 13.7 %collective-permute-start.22 = (bf16[4,10,32,128]{3,2,1,0:T(8,128)(2,1)S(1)}, bf16[4,10,32,128]{3,2,1,0:T(8,128)(2,1)S(1)}, u32[]{:S(2)}, u32[]{:S(2)}) collective-permute-start(bf16[4,10,32,128]{3,2,1,0:T(8,128)(2,1)S(1)} %collective-permute-done.20.refs_2_), channel_id=1, source_target_pairs={{1,0},{2,3},{5,4},{6,7},{9,8},{10,11},{13,12},{14,15},{17,16},{18,... | collective-permute-start | bytes 983048 | tf_op jit(solution)/shard_map/ppermute | solution.py:373
  51.5 12.4 %copy-start.7 = (s32[4]{0:T(128)S(1)}, s32[4]{0:T(128)}, u32[]{:S(2)}) copy-start(s32[4]{0:T(128)} %counts.7) | copy-start | bytes 52
  52.2 16.3 %collective-permute-start.14 = (bf16[2,128,512]{2,1,0:T(8,128)(2,1)S(1)}, bf16[2,128,512]{2,1,0:T(8,128)(2,1)S(1)}, u32[]{:S(2)}, u32[]{:S(2)}) collective-permute-start(bf16[2,128,512]{2,1,0:T(8,128)(2,1)S(1)} %get-tuple-element.23), channel_id=1, source_target_pairs={{0,1},{1,0},{2,3},{3,2},{4,5},{5,4},{6,7},{7,6},{8,9},{9,8},{10,11... | collective-permute-start | bytes 786440 | tf_op jit(solution)/shard_map/ppermute | solution.py:370
  54.9 13.6 %collective-permute-start.15 = (bf16[2,128,512]{2,1,0:T(8,128)(2,1)S(1)}, bf16[2,128,512]{2,1,0:T(8,128)(2,1)S(1)}, u32[]{:S(2)}, u32[]{:S(2)}) collective-permute-start(bf16[2,128,512]{2,1,0:T(8,128)(2,1)S(1)} %get-tuple-element.24), channel_id=1, source_target_pairs={{0,2},{3,1},{4,6},{7,5},{8,10},{11,9},{12,14},{15,13},{16,18},{19,... | collective-permute-start | bytes 786440 | tf_op jit(solution)/shard_map/ppermute | solution.py:373
  57.7 19.3 %copy-start.1 = (bf16[1,128,4096]{2,1,0:T(8,128)(2,1)S(1)}, bf16[1,128,4096]{2,1,0:T(8,128)(2,1)}, u32[]{:S(2)}) copy-start(bf16[1,128,4096]{2,1,0:T(8,128)(2,1)} %param.11) | copy-start | bytes 3145732
  57.7 19.3 %copy-start.5 = (s32[4,10]{1,0:T(4,128)S(1)}, s32[4,10]{1,0:T(4,128)}, u32[]{:S(2)}) copy-start(s32[4,10]{1,0:T(4,128)} %lists.7) | copy-start | bytes 484
  57.7 10.8 %collective-permute-start.16 = (bf16[2,128,512]{2,1,0:T(8,128)(2,1)S(1)}, bf16[2,128,512]{2,1,0:T(8,128)(2,1)S(1)}, u32[]{:S(2)}, u32[]{:S(2)}) collective-permute-start(bf16[2,128,512]{2,1,0:T(8,128)(2,1)S(1)} %get-tuple-element.25), channel_id=1, source_target_pairs={{1,2},{2,1},{5,6},{6,5},{9,10},{10,9},{13,14},{14,13},{17,18},{18,... | collective-permute-start | bytes 786440 | tf_op jit(solution)/shard_map/ppermute | solution.py:373
  58.6 18.4 %collective-permute-start.18 = (bf16[2,128,512]{2,1,0:T(8,128)(2,1)S(1)}, bf16[2,128,512]{2,1,0:T(8,128)(2,1)S(1)}, u32[]{:S(2)}, u32[]{:S(2)}) collective-permute-start(bf16[2,128,512]{2,1,0:T(8,128)(2,1)S(1)} %add_convert_fusion.1), channel_id=1, source_target_pairs={{2,0},{1,3},{6,4},{5,7},{10,8},{9,11},{14,12},{13,15},{18,16},{17,... | collective-permute-start | bytes 786440 | tf_op jit(solution)/shard_map/ppermute | solution.py:373
  78.5 2.0 %collective-permute-start.27 = (bf16[4,4,128,128]{3,2,1,0:T(8,128)(2,1)S(1)}, bf16[4,4,128,128]{3,2,1,0:T(8,128)(2,1)S(1)}, u32[]{:S(2)}, u32[]{:S(2)}) collective-permute-start(bf16[4,4,128,128]{3,2,1,0:T(8,128)(2,1)S(1)} %get-tuple-element.29), channel_id=1, source_target_pairs={{0,4},{4,0},{8,12},{12,8},{16,20},{20,16},{24,28},{28,24},{1,5},{5... | collective-permute-start | bytes 1572872 | tf_op jit(solution)/shard_map/ppermute | solution.py:364
  80.8 6.1 %collective-permute-start.28 = (bf16[4,128,128]{2,1,0:T(8,128)(2,1)S(1)}, bf16[4,128,128]{2,1,0:T(8,128)(2,1)S(1)}, u32[]{:S(2)}, u32[]{:S(2)}) collective-permute-start(bf16[4,128,128]{2,1,0:T(8,128)(2,1)S(1)} %get-tuple-element.40), channel_id=1, source_target_pairs={{0,8},{4,12},{8,0},{12,4},{16,24},{20,28},{24,16},{28,20},{1,9},{5... | collective-permute-start | bytes 393224 | tf_op jit(solution)/shard_map/ppermute | solution.py:367
  82.3 8.1 %collective-permute-start.29 = (bf16[4,128,128]{2,1,0:T(8,128)(2,1)S(1)}, bf16[4,128,128]{2,1,0:T(8,128)(2,1)S(1)}, u32[]{:S(2)}, u32[]{:S(2)}) collective-permute-start(bf16[4,128,128]{2,1,0:T(8,128)(2,1)S(1)} %get-tuple-element.42), channel_id=1, source_target_pairs={{0,16},{4,20},{8,24},{12,28},{16,0},{20,4},{24,8},{28,12},{1,17},{... | collective-permute-start | bytes 393224 | tf_op jit(solution)/shard_map/ppermute | solution.py:367
  82.8 7.6 %collective-permute-start.30 = (bf16[4,128,128]{2,1,0:T(8,128)(2,1)S(1)}, bf16[4,128,128]{2,1,0:T(8,128)(2,1)S(1)}, u32[]{:S(2)}, u32[]{:S(2)}) collective-permute-start(bf16[4,128,128]{2,1,0:T(8,128)(2,1)S(1)} %get-tuple-element.41), channel_id=1, source_target_pairs={{0,24},{4,28},{8,16},{12,20},{16,8},{20,12},{24,0},{28,4},{1,25},{... | collective-permute-start | bytes 393224 | tf_op jit(solution)/shard_map/ppermute | solution.py:367
  84.3 19.3 %collective-permute-start.24 = (bf16[320,512]{1,0:T(8,128)(2,1)S(1)}, bf16[320,512]{1,0:T(8,128)(2,1)S(1)}, u32[]{:S(2)}, u32[]{:S(2)}) collective-permute-start(bf16[320,512]{1,0:T(8,128)(2,1)S(1)} %get-tuple-element.27), channel_id=1, source_target_pairs={{0,2},{1,3},{2,0},{3,1},{4,6},{5,7},{6,4},{7,5},{8,10},{9,11},{10,... | collective-permute-start | bytes 983048 | tf_op jit(solution)/shard_map/ppermute | solution.py:370
  90.4 15.9 %collective-permute-start.41 = (bf16[4,128,128]{2,1,0:T(8,128)(2,1)S(1)}, bf16[4,128,128]{2,1,0:T(8,128)(2,1)S(1)}, u32[]{:S(2)}, u32[]{:S(2)}) collective-permute-start(bf16[4,128,128]{2,1,0:T(8,128)(2,1)S(1)} %fusion.4.refs_0_), channel_id=1, source_target_pairs={{0,2},{1,3},{2,0},{3,1},{4,6},{5,7},{6,4},{7,5},{8,10},{9,11},{10,... | collective-permute-start | bytes 393224 | tf_op jit(solution)/shard_map/ppermute | solution.py:370
  90.5 17.3 %collective-permute-start.32 = (bf16[4,128,128]{2,1,0:T(8,128)(2,1)S(1)}, bf16[4,128,128]{2,1,0:T(8,128)(2,1)S(1)}, u32[]{:S(2)}, u32[]{:S(2)}) collective-permute-start(bf16[4,128,128]{2,1,0:T(8,128)(2,1)S(1)} %fusion.4.refs_0_), channel_id=1, source_target_pairs={{0,8},{4,12},{8,0},{12,4},{16,24},{20,28},{24,16},{28,20},{1,9},{5... | collective-permute-start | bytes 393224 | tf_op jit(solution)/shard_map/ppermute | solution.py:367
  91.2 17.3 %collective-permute-start.34 = (bf16[4,128,128]{2,1,0:T(8,128)(2,1)S(1)}, bf16[4,128,128]{2,1,0:T(8,128)(2,1)S(1)}, u32[]{:S(2)}, u32[]{:S(2)}) collective-permute-start(bf16[4,128,128]{2,1,0:T(8,128)(2,1)S(1)} %fusion.4.refs_0_), channel_id=1, source_target_pairs={{0,16},{4,20},{8,24},{12,28},{16,0},{20,4},{24,8},{28,12},{1,17},{... | collective-permute-start | bytes 393224 | tf_op jit(solution)/shard_map/ppermute | solution.py:367
  92.6 17.2 %collective-permute-start.36 = (bf16[4,128,128]{2,1,0:T(8,128)(2,1)S(1)}, bf16[4,128,128]{2,1,0:T(8,128)(2,1)S(1)}, u32[]{:S(2)}, u32[]{:S(2)}) collective-permute-start(bf16[4,128,128]{2,1,0:T(8,128)(2,1)S(1)} %fusion.4.refs_0_), channel_id=1, source_target_pairs={{0,24},{4,28},{8,16},{12,20},{16,8},{20,12},{24,0},{28,4},{1,25},{... | collective-permute-start | bytes 393224 | tf_op jit(solution)/shard_map/ppermute | solution.py:367
  103.6 6.2 %collective-permute-start.31 = (bf16[4,128,128]{2,1,0:T(8,128)(2,1)S(1)}, bf16[4,128,128]{2,1,0:T(8,128)(2,1)S(1)}, u32[]{:S(2)}, u32[]{:S(2)}) collective-permute-start(bf16[4,128,128]{2,1,0:T(8,128)(2,1)S(1)} %fusion.4.refs_0_), channel_id=1, source_target_pairs={{0,4},{4,0},{8,12},{12,8},{16,20},{20,16},{24,28},{28,24},{1,5},{5... | collective-permute-start | bytes 393224 | tf_op jit(solution)/shard_map/ppermute | solution.py:364
  106.3 5.9 %collective-permute-start.43 = (bf16[4,128,128]{2,1,0:T(8,128)(2,1)S(1)}, bf16[4,128,128]{2,1,0:T(8,128)(2,1)S(1)}, u32[]{:S(2)}, u32[]{:S(2)}) collective-permute-start(bf16[4,128,128]{2,1,0:T(8,128)(2,1)S(1)} %collective-permute-done.41.refs_8_), channel_id=1, source_target_pairs={{0,8},{4,12},{8,0},{12,4},{16,24},{20,28},{24,16},{28,20},{1,9},{5... | collective-permute-start | bytes 393224 | tf_op jit(solution)/shard_map/ppermute | solution.py:367
  107.8 7.9 %collective-permute-start.45 = (bf16[4,128,128]{2,1,0:T(8,128)(2,1)S(1)}, bf16[4,128,128]{2,1,0:T(8,128)(2,1)S(1)}, u32[]{:S(2)}, u32[]{:S(2)}) collective-permute-start(bf16[4,128,128]{2,1,0:T(8,128)(2,1)S(1)} %collective-permute-done.41.refs_8_), channel_id=1, source_target_pairs={{0,16},{4,20},{8,24},{12,28},{16,0},{20,4},{24,8},{28,12},{1,17},{... | collective-permute-start | bytes 393224 | tf_op jit(solution)/shard_map/ppermute | solution.py:367
  108.5 7.2 %collective-permute-start.47 = (bf16[4,128,128]{2,1,0:T(8,128)(2,1)S(1)}, bf16[4,128,128]{2,1,0:T(8,128)(2,1)S(1)}, u32[]{:S(2)}, u32[]{:S(2)}) collective-permute-start(bf16[4,128,128]{2,1,0:T(8,128)(2,1)S(1)} %collective-permute-done.41.refs_8_), channel_id=1, source_target_pairs={{0,24},{4,28},{8,16},{12,20},{16,8},{20,12},{24,0},{28,4},{1,25},{... | collective-permute-start | bytes 393224 | tf_op jit(solution)/shard_map/ppermute | solution.py:367
  109.8 6.4 %collective-permute-start.33 = (bf16[4,128,128]{2,1,0:T(8,128)(2,1)S(1)}, bf16[4,128,128]{2,1,0:T(8,128)(2,1)S(1)}, u32[]{:S(2)}, u32[]{:S(2)}) collective-permute-start(bf16[4,128,128]{2,1,0:T(8,128)(2,1)S(1)} %collective-permute-done.32.refs_2_), channel_id=1, source_target_pairs={{0,4},{4,0},{8,12},{12,8},{16,20},{20,16},{24,28},{28,24},{1,5},{5... | collective-permute-start | bytes 393224 | tf_op jit(solution)/shard_map/ppermute | solution.py:364
  109.8 6.5 %collective-permute-start.35 = (bf16[4,128,128]{2,1,0:T(8,128)(2,1)S(1)}, bf16[4,128,128]{2,1,0:T(8,128)(2,1)S(1)}, u32[]{:S(2)}, u32[]{:S(2)}) collective-permute-start(bf16[4,128,128]{2,1,0:T(8,128)(2,1)S(1)} %collective-permute-done.34.refs_4_), channel_id=1, source_target_pairs={{0,4},{4,0},{8,12},{12,8},{16,20},{20,16},{24,28},{28,24},{1,5},{5... | collective-permute-start | bytes 393224 | tf_op jit(solution)/shard_map/ppermute | solution.py:364
  112.2 4.5 %collective-permute-start.37 = (bf16[4,128,128]{2,1,0:T(8,128)(2,1)S(1)}, bf16[4,128,128]{2,1,0:T(8,128)(2,1)S(1)}, u32[]{:S(2)}, u32[]{:S(2)}) collective-permute-start(bf16[4,128,128]{2,1,0:T(8,128)(2,1)S(1)} %collective-permute-done.36.refs_6_), channel_id=1, source_target_pairs={{0,4},{4,0},{8,12},{12,8},{16,20},{20,16},{24,28},{28,24},{1,5},{5... | collective-permute-start | bytes 393224 | tf_op jit(solution)/shard_map/ppermute | solution.py:364
  115.7 1.3 collective-permute-start.42
  115.7 2.0 %collective-permute-start.44 = (bf16[4,128,128]{2,1,0:T(8,128)(2,1)S(1)}, bf16[4,128,128]{2,1,0:T(8,128)(2,1)S(1)}, u32[]{:S(2)}, u32[]{:S(2)}) collective-permute-start(bf16[4,128,128]{2,1,0:T(8,128)(2,1)S(1)} %collective-permute-done.43.refs_10_), channel_id=1, source_target_pairs={{0,4},{4,0},{8,12},{12,8},{16,20},{20,16},{24,28},{28,24},{1,5},{5... | collective-permute-start | bytes 393224 | tf_op jit(solution)/shard_map/ppermute | solution.py:364
  116.2 1.5 %collective-permute-start.46 = (bf16[4,128,128]{2,1,0:T(8,128)(2,1)S(1)}, bf16[4,128,128]{2,1,0:T(8,128)(2,1)S(1)}, u32[]{:S(2)}, u32[]{:S(2)}) collective-permute-start(bf16[4,128,128]{2,1,0:T(8,128)(2,1)S(1)} %collective-permute-done.45.refs_12_), channel_id=1, source_target_pairs={{0,4},{4,0},{8,12},{12,8},{16,20},{20,16},{24,28},{28,24},{1,5},{5... | collective-permute-start | bytes 393224 | tf_op jit(solution)/shard_map/ppermute | solution.py:364
  116.3 1.5 collective-permute-start.48
  116.7 11.4 %collective-permute-start.23 = (bf16[256,512]{1,0:T(8,128)(2,1)S(1)}, bf16[256,512]{1,0:T(8,128)(2,1)S(1)}, u32[]{:S(2)}, u32[]{:S(2)}) collective-permute-start(bf16[256,512]{1,0:T(8,128)(2,1)S(1)} %get-tuple-element.26.refs_1_), channel_id=1, source_target_pairs={{0,1},{1,0},{2,3},{3,2},{4,5},{5,4},{6,7},{7,6},{8,9},{9,8},{10,11... | collective-permute-start | bytes 786440 | tf_op jit(solution)/shard_map/ppermute | solution.py:370
  117.1 11.9 %collective-permute-start.25 = (bf16[256,512]{1,0:T(8,128)(2,1)S(1)}, bf16[256,512]{1,0:T(8,128)(2,1)S(1)}, u32[]{:S(2)}, u32[]{:S(2)}) collective-permute-start(bf16[256,512]{1,0:T(8,128)(2,1)S(1)} %get-tuple-element.26.refs_1_), channel_id=1, source_target_pairs={{1,2},{2,1},{5,6},{6,5},{9,10},{10,9},{13,14},{14,13},{17,18},{18,... | collective-permute-start | bytes 786440 | tf_op jit(solution)/shard_map/ppermute | solution.py:373
  119.1 29.0 %collective-permute-start.49 = (bf16[4,10,32,128]{3,2,1,0:T(8,128)(2,1)S(1)}, bf16[4,10,32,128]{3,2,1,0:T(8,128)(2,1)S(1)}, u32[]{:S(2)}, u32[]{:S(2)}) collective-permute-start(bf16[4,10,32,128]{3,2,1,0:T(8,128)(2,1)S(1)} %get-tuple-element.34), channel_id=1, source_target_pairs={{0,1},{1,0},{2,3},{3,2},{4,5},{5,4},{6,7},{7,6},{8,9},{9,8},{10,11... | collective-permute-start | bytes 983048 | tf_op jit(solution)/shard_map/ppermute | solution.py:370
  122.9 21.3 %collective-permute-start.26 = (bf16[256,512]{1,0:T(8,128)(2,1)S(1)}, bf16[256,512]{1,0:T(8,128)(2,1)S(1)}, u32[]{:S(2)}, u32[]{:S(2)}) collective-permute-start(bf16[256,512]{1,0:T(8,128)(2,1)S(1)} %slice.59), channel_id=1, source_target_pairs={{1,0},{2,3},{5,4},{6,7},{9,8},{10,11},{13,12},{14,15},{17,16},{18,... | collective-permute-start | bytes 786440 | tf_op jit(solution)/shard_map/ppermute | solution.py:373
  125.4 20.7 %collective-permute-start.38 = (bf16[128,512]{1,0:T(8,128)(2,1)S(1)}, bf16[128,512]{1,0:T(8,128)(2,1)S(1)}, u32[]{:S(2)}, u32[]{:S(2)}) collective-permute-start(bf16[128,512]{1,0:T(8,128)(2,1)S(1)} %shard_map.127.refs_6_), channel_id=1, source_target_pairs={{0,1},{1,0},{2,3},{3,2},{4,5},{5,4},{6,7},{7,6},{8,9},{9,8},{10,11... | collective-permute-start | bytes 393224 | tf_op jit(solution)/shard_map/ppermute | solution.py:370
  128.2 17.9 %collective-permute-start.39 = (bf16[128,512]{1,0:T(8,128)(2,1)S(1)}, bf16[128,512]{1,0:T(8,128)(2,1)S(1)}, u32[]{:S(2)}, u32[]{:S(2)}) collective-permute-start(bf16[128,512]{1,0:T(8,128)(2,1)S(1)} %shard_map.127.refs_6_), channel_id=1, source_target_pairs={{0,2},{1,3},{2,0},{3,1},{4,6},{5,7},{6,4},{7,5},{8,10},{9,11},{10,... | collective-permute-start | bytes 393224 | tf_op jit(solution)/shard_map/ppermute | solution.py:370
  129.0 17.1 %collective-permute-start.40 = (bf16[128,512]{1,0:T(8,128)(2,1)S(1)}, bf16[128,512]{1,0:T(8,128)(2,1)S(1)}, u32[]{:S(2)}, u32[]{:S(2)}) collective-permute-start(bf16[128,512]{1,0:T(8,128)(2,1)S(1)} %shard_map.127.refs_6_), channel_id=1, source_target_pairs={{0,3},{1,2},{2,1},{3,0},{4,7},{5,6},{6,5},{7,4},{8,11},{9,10},{10,... | collective-permute-start | bytes 393224 | tf_op jit(solution)/shard_map/ppermute | solution.py:370
